TPU v7x, 32 devices: a whole 2x2x4 slice. The times are simulated.
32 devices in a mesh: dp: 4 (over y, x), seq: 8 (over z, core).
Axes of the slice: x: 2, y: 2, z: 4, core: 2. Of those that a mesh axis runs over, the one named last changes fastest.
Arguments:
- queries: bfloat16 [4, 2048, 1024], P('dp', 'seq'), may hold values from -8 to 8
- key_rows: bfloat16 [4, 2048, 512], P('dp', 'seq'), may hold values from -4 to 4
- values: bfloat16 [4, 2048, 512], P('dp', 'seq'), may hold values from -6 to 6
- out_weight: bfloat16 [2304, 1024], P(('dp', 'seq')), may hold values from -0.1875 to 0.1875
- out_grad: bfloat16 [4, 2048, 2304], P('dp', 'seq'), may hold values from -6 to 6
Outputs:
- layer_out: bfloat16 [4, 2048, 2304], P('dp', 'seq')
- query_grad: bfloat16 [4, 2048, 1024], P('dp', 'seq')
- key_grad: bfloat16 [4, 2048, 512], P('dp', 'seq')
- value_grad: bfloat16 [4, 2048, 512], P('dp', 'seq')
- weight_grad: float32 [2304, 1024], P(('dp', 'seq'))
All inputs are finite; a program needn't handle non-finite values.
Results may differ from a plain program's by a relative error of at most 0.024.
Values may be sent and summed in bfloat16 or wider, within the bound.
No kernel may reach another device: no remote copies, remote signals or barrier semaphores. Data moves between devices by JAX's collectives and lax.ppermute only.
A program may use at most 128 MiB of HBM per device.

v0:
```python
import math

import jax
import jax.numpy as jnp
from jax import lax
from jax.sharding import PartitionSpec as P

QH = 4
KH = 2
HD = 256
WINDOW = 2048


def passed_along(x, axis, by):
    length = lax.axis_size(axis)
    pairs = [(i, i + by) for i in range(length) if 0 <= i + by < length]
    return lax.ppermute(x, axis, pairs)


def on_device(queries, key_rows, values, out_weight, out_grad):
    tok_rows = queries.shape[1]
    seq_count = lax.axis_size("seq")
    prior = min(WINDOW // tok_rows, seq_count - 1)
    window = WINDOW
    groups = QH // KH
    score_scale = HD ** (-0.5)
    length = (prior + 1) * tok_rows
    shard_index = lax.axis_index("seq")
    own_keys = key_rows[0]
    own_values = values[0]
    blank = jnp.zeros((length, own_keys.shape[1]), own_keys.dtype)
    keys_start = lax.dynamic_update_slice_in_dim(blank, own_keys, prior * tok_rows, 0)
    values_start = lax.dynamic_update_slice_in_dim(blank, own_values, prior * tok_rows, 0)

    def fetch_one(number, carried):
        moving, keys_buf, values_buf = carried
        moving = passed_along((moving[0], moving[1]), "seq", 1)
        offset = (prior - number) * tok_rows
        keys_buf = lax.dynamic_update_slice_in_dim(keys_buf, moving[0], offset, 0)
        values_buf = lax.dynamic_update_slice_in_dim(values_buf, moving[1], offset, 0)
        return (moving, keys_buf, values_buf)

    carried = lax.fori_loop(
        1, prior + 1, fetch_one, ((own_keys, own_values), keys_start, values_start)
    )
    win_keys = carried[1]
    win_values = carried[2]
    query_pos = shard_index * tok_rows + jnp.arange(tok_rows, dtype=jnp.int32)
    key_pos = (shard_index - prior) * tok_rows + jnp.arange(length, dtype=jnp.int32)
    allowed = (
        (key_pos[None, :] <= query_pos[:, None])
        & (key_pos[None, :] > query_pos[:, None] - window)
        & (key_pos[None, :] >= 0)
    )
    query_heads = queries[0].reshape(tok_rows, KH, groups, HD)
    key_heads = win_keys.reshape(length, KH, HD)
    value_heads = win_values.reshape(length, KH, HD)
    scores = (
        jnp.einsum("qkgd,lkd->kgql", query_heads, key_heads, preferred_element_type=jnp.float32)
        * score_scale
    )
    scores = jnp.where(allowed, scores, -jnp.inf)
    maxima = jnp.max(scores, axis=-1, keepdims=True)
    weights = jnp.exp(scores - maxima)
    probs = weights / jnp.sum(weights, axis=-1, keepdims=True)
    probs_low = probs.astype(jnp.bfloat16)
    attended = jnp.einsum(
        "kgql,lkd->qkgd", probs_low, value_heads, preferred_element_type=jnp.float32
    ).astype(jnp.bfloat16)
    attended_flat = attended.reshape(tok_rows, QH * HD)
    full_weight = lax.all_gather(out_weight, ("dp", "seq"), axis=0, tiled=True)
    grad_rows = out_grad[0]
    layer_out = lax.dot_general(
        attended_flat, full_weight, (((1,), (1,)), ((), ())), preferred_element_type=jnp.float32
    ).astype(jnp.bfloat16)
    attended_grad = jnp.dot(grad_rows, full_weight, preferred_element_type=jnp.float32).astype(
        jnp.bfloat16
    )
    grad_heads = attended_grad.reshape(tok_rows, KH, groups, HD)
    prob_grad = jnp.einsum(
        "qkgd,lkd->kgql", grad_heads, value_heads, preferred_element_type=jnp.float32
    )
    delta = jnp.einsum("qkgd,qkgd->kgq", grad_heads, attended, preferred_element_type=jnp.float32)
    score_grad = (probs * (prob_grad - delta[..., None]) * score_scale).astype(jnp.bfloat16)
    query_grad = jnp.einsum(
        "kgql,lkd->qkgd", score_grad, key_heads, preferred_element_type=jnp.float32
    ).astype(jnp.bfloat16)
    key_terms = jnp.einsum(
        "kgql,qkgd->lkd", score_grad, query_heads, preferred_element_type=jnp.float32
    ).reshape(length, KH * HD)
    value_terms = jnp.einsum(
        "kgql,qkgd->lkd", probs_low, grad_heads, preferred_element_type=jnp.float32
    ).reshape(length, KH * HD)

    def return_one(number, carried):
        arrived = passed_along((carried[0], carried[1]), "seq", -1)
        offset = number * tok_rows
        key_part = lax.dynamic_slice_in_dim(key_terms, offset, tok_rows, 0)
        value_part = lax.dynamic_slice_in_dim(value_terms, offset, tok_rows, 0)
        return (arrived[0] + key_part, arrived[1] + value_part)

    totals = lax.fori_loop(1, prior + 1, return_one, (key_terms[:tok_rows], value_terms[:tok_rows]))
    key_total = totals[0]
    value_total = totals[1]
    total_tokens = lax.axis_size("dp") * seq_count * tok_rows
    grad_scale = 1.0 / math.sqrt(total_tokens)
    weight_grad = lax.psum_scatter(
        lax.dot_general(
            grad_rows, attended_flat, (((0,), (0,)), ((), ())), preferred_element_type=jnp.float32
        )
        * grad_scale,
        ("dp", "seq"),
        scatter_dimension=0,
        tiled=True,
    )
    return (
        layer_out[None],
        query_grad.reshape(1, tok_rows, QH * HD),
        key_total.astype(jnp.bfloat16)[None],
        value_total.astype(jnp.bfloat16)[None],
        weight_grad,
    )


def solution(mesh):
    in_specs = (
        P("dp", "seq", None),
        P("dp", "seq", None),
        P("dp", "seq", None),
        P(("dp", "seq"), None),
        P("dp", "seq", None),
    )
    out_specs = (
        P("dp", "seq", None),
        P("dp", "seq", None),
        P("dp", "seq", None),
        P("dp", "seq", None),
        P(("dp", "seq"), None),
    )
    return jax.shard_map(
        on_device, mesh=mesh, in_specs=in_specs, out_specs=out_specs, check_vma=False
    )
```

profile of v0, /device:TPU:9, one launch (start us, length us, event | category | flops | bytes accessed | tf_op | source)
XLA Modules:
  0.0 357.2 jit_solution(16437374752121823697)
XLA Ops:
  12.2 100.1 %while.34 = (s32[]{:T(128)}, bf16[256,512]{1,0:T(8,128)(2,1)S(1)}, bf16[256,512]{1,0:T(8,128)(2,1)S(1)}, bf16[2048,512]{1,0:T(8,128)(2,1)}, bf16[2048,512]{1,0:T...) while((s32[]{:T(128)}, bf16[256,512]{1,0:T(8,128)(2,1)S(1)}, ...), condition=%wide.region_1.0_spmd, body=%wide.region_0.0_spmd.sunk | while | flops 7 | bytes 4194551 | solution.py:43
  12.2 3.8 %collective-permute-start = (bf16[256,512]{1,0:T(8,128)(2,1)S(1)}, bf16[256,512]{1,0:T(8,128)(2,1)S(1)}, u32[]{:S(2)}, u32[]{:S(2)}) collective-permute-start(bf16[256,512]{1,0:T(8,128)(2,1)S(1)} %get-tuple-element.324), channel_id=1, source_target_pairs={{0,1},{1,2},{2,3},{3,4},{4,5},{5,6},{6,7},{8,9},{9,10},{10,11},{11... | collective-permute-start | bytes 786440 | tf_op jit(solution)/shard_map/while/body/eval_jaxpr/ppermute | solution.py:17
  16.0 1.9 collective-permute-start.1
  19.3 2.9 collective-permute-done.1
  23.6 5.0 %collective-permute-start = (bf16[256,512]{1,0:T(8,128)(2,1)S(1)}, bf16[256,512]{1,0:T(8,128)(2,1)S(1)}, u32[]{:S(2)}, u32[]{:S(2)}) collective-permute-start(bf16[256,512]{1,0:T(8,128)(2,1)S(1)} %get-tuple-element.324), channel_id=1, source_target_pairs={{0,1},{1,2},{2,3},{3,4},{4,5},{5,6},{6,7},{8,9},{9,10},{10,11},{11... | collective-permute-start | bytes 786440 | tf_op jit(solution)/shard_map/while/body/eval_jaxpr/ppermute | solution.py:17
  28.6 1.9 collective-permute-start.1
  30.5 2.0 collective-permute-done
  32.6 2.8 collective-permute-done.1
  36.8 4.4 %collective-permute-start = (bf16[256,512]{1,0:T(8,128)(2,1)S(1)}, bf16[256,512]{1,0:T(8,128)(2,1)S(1)}, u32[]{:S(2)}, u32[]{:S(2)}) collective-permute-start(bf16[256,512]{1,0:T(8,128)(2,1)S(1)} %get-tuple-element.324), channel_id=1, source_target_pairs={{0,1},{1,2},{2,3},{3,4},{4,5},{5,6},{6,7},{8,9},{9,10},{10,11},{11... | collective-permute-start | bytes 786440 | tf_op jit(solution)/shard_map/while/body/eval_jaxpr/ppermute | solution.py:17
  41.2 1.9 collective-permute-start.1
  43.1 4.6 %collective-permute-done = bf16[256,512]{1,0:T(8,128)(2,1)S(1)} collective-permute-done((bf16[256,512]{1,0:T(8,128)(2,1)S(1)}, bf16[256,512]{1,0:T(8,128)(2,1)S(1)}, u32[]{:S(2)}, u32[]{:S(2)}) %collective-permute-start) | collective-permute-done | bytes 262176 | tf_op jit(solution)/shard_map/while/body/eval_jaxpr/ppermute | solution.py:17
  47.8 3.6 %collective-permute-done.1 = bf16[256,512]{1,0:T(8,128)(2,1)S(1)} collective-permute-done((bf16[256,512]{1,0:T(8,128)(2,1)S(1)}, bf16[256,512]{1,0:T(8,128)(2,1)S(1)}, u32[]{:S(2)}, u32[]{:S(2)}) %collective-permute-start.1) | collective-permute-done | bytes 262176 | tf_op jit(solution)/shard_map/while/body/eval_jaxpr/ppermute | solution.py:17
  52.9 4.4 %collective-permute-start = (bf16[256,512]{1,0:T(8,128)(2,1)S(1)}, bf16[256,512]{1,0:T(8,128)(2,1)S(1)}, u32[]{:S(2)}, u32[]{:S(2)}) collective-permute-start(bf16[256,512]{1,0:T(8,128)(2,1)S(1)} %get-tuple-element.324), channel_id=1, source_target_pairs={{0,1},{1,2},{2,3},{3,4},{4,5},{5,6},{6,7},{8,9},{9,10},{10,11},{11... | collective-permute-start | bytes 786440 | tf_op jit(solution)/shard_map/while/body/eval_jaxpr/ppermute | solution.py:17
  57.3 1.9 collective-permute-start.1
  59.2 7.9 %collective-permute-done = bf16[256,512]{1,0:T(8,128)(2,1)S(1)} collective-permute-done((bf16[256,512]{1,0:T(8,128)(2,1)S(1)}, bf16[256,512]{1,0:T(8,128)(2,1)S(1)}, u32[]{:S(2)}, u32[]{:S(2)}) %collective-permute-start) | collective-permute-done | bytes 262176 | tf_op jit(solution)/shard_map/while/body/eval_jaxpr/ppermute | solution.py:17
  67.1 7.9 %collective-permute-done.1 = bf16[256,512]{1,0:T(8,128)(2,1)S(1)} collective-permute-done((bf16[256,512]{1,0:T(8,128)(2,1)S(1)}, bf16[256,512]{1,0:T(8,128)(2,1)S(1)}, u32[]{:S(2)}, u32[]{:S(2)}) %collective-permute-start.1) | collective-permute-done | bytes 262176 | tf_op jit(solution)/shard_map/while/body/eval_jaxpr/ppermute | solution.py:17
  76.5 4.4 %collective-permute-start = (bf16[256,512]{1,0:T(8,128)(2,1)S(1)}, bf16[256,512]{1,0:T(8,128)(2,1)S(1)}, u32[]{:S(2)}, u32[]{:S(2)}) collective-permute-start(bf16[256,512]{1,0:T(8,128)(2,1)S(1)} %get-tuple-element.324), channel_id=1, source_target_pairs={{0,1},{1,2},{2,3},{3,4},{4,5},{5,6},{6,7},{8,9},{9,10},{10,11},{11... | collective-permute-start | bytes 786440 | tf_op jit(solution)/shard_map/while/body/eval_jaxpr/ppermute | solution.py:17
  80.9 1.9 collective-permute-start.1
  84.2 2.8 collective-permute-done.1
  88.5 4.4 %collective-permute-start = (bf16[256,512]{1,0:T(8,128)(2,1)S(1)}, bf16[256,512]{1,0:T(8,128)(2,1)S(1)}, u32[]{:S(2)}, u32[]{:S(2)}) collective-permute-start(bf16[256,512]{1,0:T(8,128)(2,1)S(1)} %get-tuple-element.324), channel_id=1, source_target_pairs={{0,1},{1,2},{2,3},{3,4},{4,5},{5,6},{6,7},{8,9},{9,10},{10,11},{11... | collective-permute-start | bytes 786440 | tf_op jit(solution)/shard_map/while/body/eval_jaxpr/ppermute | solution.py:17
  92.8 1.9 collective-permute-start.1
  96.2 2.8 collective-permute-done.1
  100.4 4.4 %collective-permute-start = (bf16[256,512]{1,0:T(8,128)(2,1)S(1)}, bf16[256,512]{1,0:T(8,128)(2,1)S(1)}, u32[]{:S(2)}, u32[]{:S(2)}) collective-permute-start(bf16[256,512]{1,0:T(8,128)(2,1)S(1)} %get-tuple-element.324), channel_id=1, source_target_pairs={{0,1},{1,2},{2,3},{3,4},{4,5},{5,6},{6,7},{8,9},{9,10},{10,11},{11... | collective-permute-start | bytes 786440 | tf_op jit(solution)/shard_map/while/body/eval_jaxpr/ppermute | solution.py:17
  104.8 1.9 collective-permute-start.1
  108.1 2.8 collective-permute-done.1
  112.4 4.2 %reshape.53 = bf16[2048,2,256]{2,1,0:T(2,128)(2,1)} reshape(bf16[2048,512]{1,0:T(8,128)(2,1)} %get-tuple-element.196) | data formatting | bytes 4194304 | tf_op jit(solution)/shard_map/reshape | solution.py:56
  116.5 6.3 %copy.56 = bf16[2048,2,256,1]{0,2,3,1:T(8,128)(2,1)} copy(bf16[2048,2,256,1]{2,1,0,3:T(2,128)(2,1)} %bitcast.85) | data formatting | bytes 4194304 | tf_op jit(solution)/shard_map/reshape | solution.py:56
  122.8 2.1 copy.74
  124.9 2.1 reshape.52
  128.5 7.8 %fusion.22 = (f32[2,2,256]{2,1,0:T(2,128)S(1)}, f32[2,2,256,2048]{2,3,1,0:T(8,128)}) fusion(pred[256,2048]{0,1:T(8,128)(4,1)S(1)} %and_and_fusion, bf16[2048,2,256,1]{0,2,3,1:T(8,128)(2,1)} %copy.56, bf16[256,2,2,256]{0,3,2,1:T(8,128)(2,1)} %bitcast.86), kind=kOutput, calls=%fused_computation.40 | convolution fusion | flops 1082132480 | bytes 11538432 | tf_op jit(solution)/shard_map/sub | solution.py:64
  136.3 6.1 %fusion.9 = bf16[2,2,256,2048]{2,3,1,0:T(8,128)(2,1)} fusion(f32[2,2,256,2048]{2,3,1,0:T(8,128)} %get-tuple-element.242, f32[2,2,256]{2,1,0:T(2,128)S(1)} %get-tuple-element.241), kind=kLoop, calls=%fused_computation.19 | loop fusion | flops 4194304 | bytes 12587008 | tf_op jit(solution)/shard_map/convert_element_type | solution.py:66
  142.4 3.7 %convolution_convert_fusion.2 = bf16[256,1024]{1,0:T(8,128)(2,1)S(1)} fusion(bf16[2304,1024]{1,0:T(8,128)(2,1)} %all-gather.2.cloned.1.call-done, bf16[1,256,2304]{2,1,0:T(8,128)(2,1)S(1)} %copy-done), kind=kOutput, calls=%fused_computation.26 | convolution fusion | flops 1208221696 | bytes 6422528 | tf_op jit(solution)/shard_map/dot_general | solution.py:76
  148.3 4.4 %multiply_reduce_fusion = (f32[2,2,256]{2,1,0:T(2,128)S(1)}, bf16[2,256,2,256]{3,1,2,0:T(8,128)(2,1)S(1)}) fusion(f32[2,2,256,256]{2,3,1,0:T(8,128)} %copy.55, bf16[2,2,256,2048]{2,3,1,0:T(8,128)(2,1)} %fusion.9, bf16[2048,2,256,1]{2,1,0,3:T(2,128)(2,1)} %bitcast.88), kind=kOutput, calls=%fused_computation.29 | convolution fusion | flops 1074789376 | bytes 7868416 | tf_op jit(solution)/shard_map/kgql,lkd->qkgd/dot_general | solution.py:67
  153.5 5.0 %multiply_bitcast_fusion = f32[2304,1024]{0,1:T(8,128)} fusion(bf16[256,1024]{0,1:T(8,128)(2,1)S(1)} %bitcast.96, bf16[1,256,2304]{2,1,0:T(8,128)(2,1)S(1)} %copy-done), kind=kOutput, calls=%fused_computation.5 | convolution fusion | flops 1210318848 | bytes 11141120 | tf_op jit(solution)/shard_map/dot_general | solution.py:108
  158.5 9.7 %copy.70 = f32[2304,1024]{1,0:T(8,128)} copy(f32[2304,1024]{0,1:T(8,128)} %multiply_bitcast_fusion) | data formatting | bytes 18874368
  168.8 5.4 %fusion.3 = bf16[2,2,256,2048]{2,3,1,0:T(8,128)(2,1)S(1)} fusion(bf16[256,2,2,256]{0,3,2,1:T(8,128)(2,1)S(1)} %copy.38, f32[2,2,256]{2,1,0:T(2,128)S(1)} %get-tuple-element.243, f32[2,2,256,2048]{2,3,1,0:T(8,128)} %get-tuple-element.242, f32[2,2,256]{2,1,0:T(2,128)S(1)} %get-tuple-element.241, bf16[2048,2,256,1]{2,1,0,3:T(2,128)(2,1)} %bitcast.89), kind=kOutput, calls=%fused_computation.9 | convolution fusion | flops 1084227584 | bytes 15212544 | tf_op jit(solution)/shard_map/qkgd,lkd->kgql/dot_general | solution.py:80
  174.2 2.1 copy-done.5
  178.5 3.7 %fusion.23 = f32[2,2048,256,1]{1,2,3,0:T(8,128)S(1)} fusion(bf16[2,2,256,2048]{2,3,1,0:T(8,128)(2,1)} %copy-done.5, bf16[256,2,2,256]{0,3,2,1:T(8,128)(2,1)S(1)} %bitcast.87), kind=kOutput, calls=%fused_computation.41 | convolution fusion | flops 1073741824 | bytes 8912896 | tf_op jit(solution)/shard_map/kgql,qkgd->lkd/dot_general | solution.py:88
  182.2 2.1 copy-done.2
  184.6 3.7 %fusion.24 = f32[2,256,2048,1]{2,1,3,0:T(8,128)S(1)} fusion(bf16[256,2,2,256]{0,3,2,1:T(8,128)(2,1)S(1)} %copy.38, bf16[2,2,256,2048]{2,3,1,0:T(8,128)(2,1)} %fusion.9), kind=kOutput, calls=%fused_computation.42 | convolution fusion | flops 1073741824 | bytes 8912896 | tf_op jit(solution)/shard_map/kgql,qkgd->lkd/dot_general | solution.py:91
  188.3 1.9 copy-done.3
  191.3 151.5 %while.35 = (s32[]{:T(128)}, f32[256,512]{1,0:T(8,128)S(1)}, f32[256,512]{1,0:T(8,128)}, f32[2048,512]{0,1:T(8,128)}, f32[2048,512]{0,1:T(8,128)}, /*index=5*/s32[]{:T(128)}, s32[]{:T(128)}, s32[]{:T(128)}, s32[]{:T(128)}) while((s32[]{:T(128)}, f32[256,512]{1,0:T(8,128)S(1)}, f32[256,512]{1,0:T(8,128)}, f32[2048,512]{0,1:T(8,128)}, ...), condition=%wide.region_5.6_spmd, body=%wide.region_4.5_spmd.sunk | while | flops 262150 | bytes 11534559 | solution.py:102
  191.3 2.6 collective-permute-start.2
  193.8 1.9 collective-permute-start.3
  197.5 5.0 %collective-permute-done.2 = f32[256,512]{1,0:T(8,128)S(1)} collective-permute-done((f32[256,512]{1,0:T(8,128)S(1)}, f32[256,512]{1,0:T(8,128)S(1)}, u32[]{:S(2)}, u32[]{:S(2)}) %collective-permute-start.2) | collective-permute-done | bytes 524320 | tf_op jit(solution)/shard_map/while/body/eval_jaxpr/ppermute | solution.py:17
  202.6 5.5 %collective-permute-done.3 = f32[256,512]{1,0:T(8,128)S(1)} collective-permute-done((f32[256,512]{1,0:T(8,128)}, f32[256,512]{1,0:T(8,128)S(1)}, u32[]{:S(2)}, u32[]{:S(2)}) %collective-permute-start.3) | collective-permute-done | bytes 524320 | tf_op jit(solution)/shard_map/while/body/eval_jaxpr/ppermute | solution.py:17
  210.9 1.9 collective-permute-start.3
  214.5 4.9 %collective-permute-done.2 = f32[256,512]{1,0:T(8,128)S(1)} collective-permute-done((f32[256,512]{1,0:T(8,128)S(1)}, f32[256,512]{1,0:T(8,128)S(1)}, u32[]{:S(2)}, u32[]{:S(2)}) %collective-permute-start.2) | collective-permute-done | bytes 524320 | tf_op jit(solution)/shard_map/while/body/eval_jaxpr/ppermute | solution.py:17
  219.5 8.5 %collective-permute-done.3 = f32[256,512]{1,0:T(8,128)S(1)} collective-permute-done((f32[256,512]{1,0:T(8,128)}, f32[256,512]{1,0:T(8,128)S(1)}, u32[]{:S(2)}, u32[]{:S(2)}) %collective-permute-start.3) | collective-permute-done | bytes 524320 | tf_op jit(solution)/shard_map/while/body/eval_jaxpr/ppermute | solution.py:17
  230.8 1.9 collective-permute-start.3
  234.4 19.9 %collective-permute-done.2 = f32[256,512]{1,0:T(8,128)S(1)} collective-permute-done((f32[256,512]{1,0:T(8,128)S(1)}, f32[256,512]{1,0:T(8,128)S(1)}, u32[]{:S(2)}, u32[]{:S(2)}) %collective-permute-start.2) | collective-permute-done | bytes 524320 | tf_op jit(solution)/shard_map/while/body/eval_jaxpr/ppermute | solution.py:17
  254.4 7.2 %collective-permute-done.3 = f32[256,512]{1,0:T(8,128)S(1)} collective-permute-done((f32[256,512]{1,0:T(8,128)}, f32[256,512]{1,0:T(8,128)S(1)}, u32[]{:S(2)}, u32[]{:S(2)}) %collective-permute-start.3) | collective-permute-done | bytes 524320 | tf_op jit(solution)/shard_map/while/body/eval_jaxpr/ppermute | solution.py:17
  264.4 1.9 collective-permute-start.3
  268.1 4.9 %collective-permute-done.2 = f32[256,512]{1,0:T(8,128)S(1)} collective-permute-done((f32[256,512]{1,0:T(8,128)S(1)}, f32[256,512]{1,0:T(8,128)S(1)}, u32[]{:S(2)}, u32[]{:S(2)}) %collective-permute-start.2) | collective-permute-done | bytes 524320 | tf_op jit(solution)/shard_map/while/body/eval_jaxpr/ppermute | solution.py:17
  273.1 5.9 %collective-permute-done.3 = f32[256,512]{1,0:T(8,128)S(1)} collective-permute-done((f32[256,512]{1,0:T(8,128)}, f32[256,512]{1,0:T(8,128)S(1)}, u32[]{:S(2)}, u32[]{:S(2)}) %collective-permute-start.3) | collective-permute-done | bytes 524320 | tf_op jit(solution)/shard_map/while/body/eval_jaxpr/ppermute | solution.py:17
  285.5 12.9 %collective-permute-done.2 = f32[256,512]{1,0:T(8,128)S(1)} collective-permute-done((f32[256,512]{1,0:T(8,128)S(1)}, f32[256,512]{1,0:T(8,128)S(1)}, u32[]{:S(2)}, u32[]{:S(2)}) %collective-permute-start.2) | collective-permute-done | bytes 524320 | tf_op jit(solution)/shard_map/while/body/eval_jaxpr/ppermute | solution.py:17
  298.5 5.4 %collective-permute-done.3 = f32[256,512]{1,0:T(8,128)S(1)} collective-permute-done((f32[256,512]{1,0:T(8,128)}, f32[256,512]{1,0:T(8,128)S(1)}, u32[]{:S(2)}, u32[]{:S(2)}) %collective-permute-start.3) | collective-permute-done | bytes 524320 | tf_op jit(solution)/shard_map/while/body/eval_jaxpr/ppermute | solution.py:17
  306.6 1.9 collective-permute-start.3
  310.3 9.0 %collective-permute-done.2 = f32[256,512]{1,0:T(8,128)S(1)} collective-permute-done((f32[256,512]{1,0:T(8,128)S(1)}, f32[256,512]{1,0:T(8,128)S(1)}, u32[]{:S(2)}, u32[]{:S(2)}) %collective-permute-start.2) | collective-permute-done | bytes 524320 | tf_op jit(solution)/shard_map/while/body/eval_jaxpr/ppermute | solution.py:17
  319.4 5.5 %collective-permute-done.3 = f32[256,512]{1,0:T(8,128)S(1)} collective-permute-done((f32[256,512]{1,0:T(8,128)}, f32[256,512]{1,0:T(8,128)S(1)}, u32[]{:S(2)}, u32[]{:S(2)}) %collective-permute-start.3) | collective-permute-done | bytes 524320 | tf_op jit(solution)/shard_map/while/body/eval_jaxpr/ppermute | solution.py:17
  327.7 2.1 collective-permute-start.3
  331.5 4.8 %collective-permute-done.2 = f32[256,512]{1,0:T(8,128)S(1)} collective-permute-done((f32[256,512]{1,0:T(8,128)S(1)}, f32[256,512]{1,0:T(8,128)S(1)}, u32[]{:S(2)}, u32[]{:S(2)}) %collective-permute-start.2) | collective-permute-done | bytes 524320 | tf_op jit(solution)/shard_map/while/body/eval_jaxpr/ppermute | solution.py:17
  336.3 5.5 %collective-permute-done.3 = f32[256,512]{1,0:T(8,128)S(1)} collective-permute-done((f32[256,512]{1,0:T(8,128)}, f32[256,512]{1,0:T(8,128)S(1)}, u32[]{:S(2)}, u32[]{:S(2)}) %collective-permute-start.3) | collective-permute-done | bytes 524320 | tf_op jit(solution)/shard_map/while/body/eval_jaxpr/ppermute | solution.py:17
  345.4 5.0 %fusion.8 = bf16[1,256,2304]{2,1,0:T(8,128)(2,1)} fusion(bf16[256,1024]{0,1:T(8,128)(2,1)} %bitcast.97, bf16[2304,1024]{1,0:T(8,128)(2,1)} %all-gather.2.cloned.1.call-done), kind=kOutput, calls=%fused_computation.18 | convolution fusion | flops 1208549376 | bytes 6422528 | tf_op jit(solution)/shard_map/dot_general | solution.py:73
  (115 shorter events, 63.8 us)
Async XLA Ops:
  7.2 135.3 %copy-start = (bf16[1,256,2304]{2,1,0:T(8,128)(2,1)S(1)}, bf16[1,256,2304]{2,1,0:T(8,128)(2,1)}, u32[]{:S(2)}) copy-start(bf16[1,256,2304]{2,1,0:T(8,128)(2,1)} %param.13) | copy-start | bytes 3538948
  7.2 135.2 %all-gather.2.cloned.1.call-start = ((), (), s32[]{:S(2)}) async-start(), calls=%async_computation.1 | async-start | bytes 4866048 | tf_op jit(solution)/shard_map/all_gather | solution.py:71
  9.2 341.1 %reduce-scatter.4.cloned.1.call-start = ((), (), s32[]{:S(2)}) async-start(), calls=%async_computation.2 | async-start | bytes 9732096
  12.2 7.1 %collective-permute-start = (bf16[256,512]{1,0:T(8,128)(2,1)S(1)}, bf16[256,512]{1,0:T(8,128)(2,1)S(1)}, u32[]{:S(2)}, u32[]{:S(2)}) collective-permute-start(bf16[256,512]{1,0:T(8,128)(2,1)S(1)} %get-tuple-element.324), channel_id=1, source_target_pairs={{0,1},{1,2},{2,3},{3,4},{4,5},{5,6},{6,7},{8,9},{9,10},{10,11},{11... | collective-permute-start | bytes 786440 | tf_op jit(solution)/shard_map/while/body/eval_jaxpr/ppermute | solution.py:17
  16.0 6.2 %collective-permute-start.1 = (bf16[256,512]{1,0:T(8,128)(2,1)S(1)}, bf16[256,512]{1,0:T(8,128)(2,1)S(1)}, u32[]{:S(2)}, u32[]{:S(2)}) collective-permute-start(bf16[256,512]{1,0:T(8,128)(2,1)S(1)} %get-tuple-element.325), channel_id=1, source_target_pairs={{0,1},{1,2},{2,3},{3,4},{4,5},{5,6},{6,7},{8,9},{9,10},{10,11},{11... | collective-permute-start | bytes 786440 | tf_op jit(solution)/shard_map/while/body/eval_jaxpr/ppermute | solution.py:17
  23.6 8.9 %collective-permute-start = (bf16[256,512]{1,0:T(8,128)(2,1)S(1)}, bf16[256,512]{1,0:T(8,128)(2,1)S(1)}, u32[]{:S(2)}, u32[]{:S(2)}) collective-permute-start(bf16[256,512]{1,0:T(8,128)(2,1)S(1)} %get-tuple-element.324), channel_id=1, source_target_pairs={{0,1},{1,2},{2,3},{3,4},{4,5},{5,6},{6,7},{8,9},{9,10},{10,11},{11... | collective-permute-start | bytes 786440 | tf_op jit(solution)/shard_map/while/body/eval_jaxpr/ppermute | solution.py:17
  28.6 6.8 %collective-permute-start.1 = (bf16[256,512]{1,0:T(8,128)(2,1)S(1)}, bf16[256,512]{1,0:T(8,128)(2,1)S(1)}, u32[]{:S(2)}, u32[]{:S(2)}) collective-permute-start(bf16[256,512]{1,0:T(8,128)(2,1)S(1)} %get-tuple-element.325), channel_id=1, source_target_pairs={{0,1},{1,2},{2,3},{3,4},{4,5},{5,6},{6,7},{8,9},{9,10},{10,11},{11... | collective-permute-start | bytes 786440 | tf_op jit(solution)/shard_map/while/body/eval_jaxpr/ppermute | solution.py:17
  36.8 11.0 %collective-permute-start = (bf16[256,512]{1,0:T(8,128)(2,1)S(1)}, bf16[256,512]{1,0:T(8,128)(2,1)S(1)}, u32[]{:S(2)}, u32[]{:S(2)}) collective-permute-start(bf16[256,512]{1,0:T(8,128)(2,1)S(1)} %get-tuple-element.324), channel_id=1, source_target_pairs={{0,1},{1,2},{2,3},{3,4},{4,5},{5,6},{6,7},{8,9},{9,10},{10,11},{11... | collective-permute-start | bytes 786440 | tf_op jit(solution)/shard_map/while/body/eval_jaxpr/ppermute | solution.py:17
  41.2 10.2 %collective-permute-start.1 = (bf16[256,512]{1,0:T(8,128)(2,1)S(1)}, bf16[256,512]{1,0:T(8,128)(2,1)S(1)}, u32[]{:S(2)}, u32[]{:S(2)}) collective-permute-start(bf16[256,512]{1,0:T(8,128)(2,1)S(1)} %get-tuple-element.325), channel_id=1, source_target_pairs={{0,1},{1,2},{2,3},{3,4},{4,5},{5,6},{6,7},{8,9},{9,10},{10,11},{11... | collective-permute-start | bytes 786440 | tf_op jit(solution)/shard_map/while/body/eval_jaxpr/ppermute | solution.py:17
  52.9 14.3 %collective-permute-start = (bf16[256,512]{1,0:T(8,128)(2,1)S(1)}, bf16[256,512]{1,0:T(8,128)(2,1)S(1)}, u32[]{:S(2)}, u32[]{:S(2)}) collective-permute-start(bf16[256,512]{1,0:T(8,128)(2,1)S(1)} %get-tuple-element.324), channel_id=1, source_target_pairs={{0,1},{1,2},{2,3},{3,4},{4,5},{5,6},{6,7},{8,9},{9,10},{10,11},{11... | collective-permute-start | bytes 786440 | tf_op jit(solution)/shard_map/while/body/eval_jaxpr/ppermute | solution.py:17
  57.3 17.8 %collective-permute-start.1 = (bf16[256,512]{1,0:T(8,128)(2,1)S(1)}, bf16[256,512]{1,0:T(8,128)(2,1)S(1)}, u32[]{:S(2)}, u32[]{:S(2)}) collective-permute-start(bf16[256,512]{1,0:T(8,128)(2,1)S(1)} %get-tuple-element.325), channel_id=1, source_target_pairs={{0,1},{1,2},{2,3},{3,4},{4,5},{5,6},{6,7},{8,9},{9,10},{10,11},{11... | collective-permute-start | bytes 786440 | tf_op jit(solution)/shard_map/while/body/eval_jaxpr/ppermute | solution.py:17
  76.5 7.7 %collective-permute-start = (bf16[256,512]{1,0:T(8,128)(2,1)S(1)}, bf16[256,512]{1,0:T(8,128)(2,1)S(1)}, u32[]{:S(2)}, u32[]{:S(2)}) collective-permute-start(bf16[256,512]{1,0:T(8,128)(2,1)S(1)} %get-tuple-element.324), channel_id=1, source_target_pairs={{0,1},{1,2},{2,3},{3,4},{4,5},{5,6},{6,7},{8,9},{9,10},{10,11},{11... | collective-permute-start | bytes 786440 | tf_op jit(solution)/shard_map/while/body/eval_jaxpr/ppermute | solution.py:17
  80.9 6.1 %collective-permute-start.1 = (bf16[256,512]{1,0:T(8,128)(2,1)S(1)}, bf16[256,512]{1,0:T(8,128)(2,1)S(1)}, u32[]{:S(2)}, u32[]{:S(2)}) collective-permute-start(bf16[256,512]{1,0:T(8,128)(2,1)S(1)} %get-tuple-element.325), channel_id=1, source_target_pairs={{0,1},{1,2},{2,3},{3,4},{4,5},{5,6},{6,7},{8,9},{9,10},{10,11},{11... | collective-permute-start | bytes 786440 | tf_op jit(solution)/shard_map/while/body/eval_jaxpr/ppermute | solution.py:17
  88.5 7.7 %collective-permute-start = (bf16[256,512]{1,0:T(8,128)(2,1)S(1)}, bf16[256,512]{1,0:T(8,128)(2,1)S(1)}, u32[]{:S(2)}, u32[]{:S(2)}) collective-permute-start(bf16[256,512]{1,0:T(8,128)(2,1)S(1)} %get-tuple-element.324), channel_id=1, source_target_pairs={{0,1},{1,2},{2,3},{3,4},{4,5},{5,6},{6,7},{8,9},{9,10},{10,11},{11... | collective-permute-start | bytes 786440 | tf_op jit(solution)/shard_map/while/body/eval_jaxpr/ppermute | solution.py:17
  92.8 6.1 %collective-permute-start.1 = (bf16[256,512]{1,0:T(8,128)(2,1)S(1)}, bf16[256,512]{1,0:T(8,128)(2,1)S(1)}, u32[]{:S(2)}, u32[]{:S(2)}) collective-permute-start(bf16[256,512]{1,0:T(8,128)(2,1)S(1)} %get-tuple-element.325), channel_id=1, source_target_pairs={{0,1},{1,2},{2,3},{3,4},{4,5},{5,6},{6,7},{8,9},{9,10},{10,11},{11... | collective-permute-start | bytes 786440 | tf_op jit(solution)/shard_map/while/body/eval_jaxpr/ppermute | solution.py:17
  100.4 7.7 %collective-permute-start = (bf16[256,512]{1,0:T(8,128)(2,1)S(1)}, bf16[256,512]{1,0:T(8,128)(2,1)S(1)}, u32[]{:S(2)}, u32[]{:S(2)}) collective-permute-start(bf16[256,512]{1,0:T(8,128)(2,1)S(1)} %get-tuple-element.324), channel_id=1, source_target_pairs={{0,1},{1,2},{2,3},{3,4},{4,5},{5,6},{6,7},{8,9},{9,10},{10,11},{11... | collective-permute-start | bytes 786440 | tf_op jit(solution)/shard_map/while/body/eval_jaxpr/ppermute | solution.py:17
  104.8 6.1 %collective-permute-start.1 = (bf16[256,512]{1,0:T(8,128)(2,1)S(1)}, bf16[256,512]{1,0:T(8,128)(2,1)S(1)}, u32[]{:S(2)}, u32[]{:S(2)}) collective-permute-start(bf16[256,512]{1,0:T(8,128)(2,1)S(1)} %get-tuple-element.325), channel_id=1, source_target_pairs={{0,1},{1,2},{2,3},{3,4},{4,5},{5,6},{6,7},{8,9},{9,10},{10,11},{11... | collective-permute-start | bytes 786440 | tf_op jit(solution)/shard_map/while/body/eval_jaxpr/ppermute | solution.py:17
  112.4 12.5 %copy-start.4 = (bf16[2048,512]{1,0:T(8,128)(2,1)S(1)}, bf16[2048,512]{1,0:T(8,128)(2,1)}, u32[]{:S(2)}) copy-start(bf16[2048,512]{1,0:T(8,128)(2,1)} %get-tuple-element.195) | copy-start | bytes 6291460
  152.7 0.8 copy-start.8
  168.8 7.5 %copy-start.7 = (bf16[2048,2,256,1]{0,2,3,1:T(8,128)(2,1)S(1)}, bf16[2048,2,256,1]{0,2,3,1:T(8,128)(2,1)}, u32[]{:S(2)}) copy-start(bf16[2048,2,256,1]{0,2,3,1:T(8,128)(2,1)} %copy.56) | copy-start | bytes 6291460
  174.2 2.1 copy-start.5
  176.3 2.3 copy-start.6
  182.2 2.1 copy-start.2
  188.3 1.9 copy-start.3
  191.3 11.2 %collective-permute-start.2 = (f32[256,512]{1,0:T(8,128)S(1)}, f32[256,512]{1,0:T(8,128)S(1)}, u32[]{:S(2)}, u32[]{:S(2)}) collective-permute-start(f32[256,512]{1,0:T(8,128)S(1)} %get-tuple-element.353), channel_id=1, source_target_pairs={{1,0},{2,1},{3,2},{4,3},{5,4},{6,5},{7,6},{9,8},{10,9},{11,10},{12... | collective-permute-start | bytes 1572872 | tf_op jit(solution)/shard_map/while/body/eval_jaxpr/ppermute | solution.py:17
  193.8 14.3 %collective-permute-start.3 = (f32[256,512]{1,0:T(8,128)}, f32[256,512]{1,0:T(8,128)S(1)}, u32[]{:S(2)}, u32[]{:S(2)}) collective-permute-start(f32[256,512]{1,0:T(8,128)} %get-tuple-element.354), channel_id=1, source_target_pairs={{1,0},{2,1},{3,2},{4,3},{5,4},{6,5},{7,6},{9,8},{10,9},{11,10},{12... | collective-permute-start | bytes 1572872 | tf_op jit(solution)/shard_map/while/body/eval_jaxpr/ppermute | solution.py:17
  209.0 10.5 %collective-permute-start.2 = (f32[256,512]{1,0:T(8,128)S(1)}, f32[256,512]{1,0:T(8,128)S(1)}, u32[]{:S(2)}, u32[]{:S(2)}) collective-permute-start(f32[256,512]{1,0:T(8,128)S(1)} %get-tuple-element.353), channel_id=1, source_target_pairs={{1,0},{2,1},{3,2},{4,3},{5,4},{6,5},{7,6},{9,8},{10,9},{11,10},{12... | collective-permute-start | bytes 1572872 | tf_op jit(solution)/shard_map/while/body/eval_jaxpr/ppermute | solution.py:17
  210.9 17.1 %collective-permute-start.3 = (f32[256,512]{1,0:T(8,128)}, f32[256,512]{1,0:T(8,128)S(1)}, u32[]{:S(2)}, u32[]{:S(2)}) collective-permute-start(f32[256,512]{1,0:T(8,128)} %get-tuple-element.354), channel_id=1, source_target_pairs={{1,0},{2,1},{3,2},{4,3},{5,4},{6,5},{7,6},{9,8},{10,9},{11,10},{12... | collective-permute-start | bytes 1572872 | tf_op jit(solution)/shard_map/while/body/eval_jaxpr/ppermute | solution.py:17
  228.9 25.4 %collective-permute-start.2 = (f32[256,512]{1,0:T(8,128)S(1)}, f32[256,512]{1,0:T(8,128)S(1)}, u32[]{:S(2)}, u32[]{:S(2)}) collective-permute-start(f32[256,512]{1,0:T(8,128)S(1)} %get-tuple-element.353), channel_id=1, source_target_pairs={{1,0},{2,1},{3,2},{4,3},{5,4},{6,5},{7,6},{9,8},{10,9},{11,10},{12... | collective-permute-start | bytes 1572872 | tf_op jit(solution)/shard_map/while/body/eval_jaxpr/ppermute | solution.py:17
  230.8 30.8 %collective-permute-start.3 = (f32[256,512]{1,0:T(8,128)}, f32[256,512]{1,0:T(8,128)S(1)}, u32[]{:S(2)}, u32[]{:S(2)}) collective-permute-start(f32[256,512]{1,0:T(8,128)} %get-tuple-element.354), channel_id=1, source_target_pairs={{1,0},{2,1},{3,2},{4,3},{5,4},{6,5},{7,6},{9,8},{10,9},{11,10},{12... | collective-permute-start | bytes 1572872 | tf_op jit(solution)/shard_map/while/body/eval_jaxpr/ppermute | solution.py:17
  262.5 10.5 %collective-permute-start.2 = (f32[256,512]{1,0:T(8,128)S(1)}, f32[256,512]{1,0:T(8,128)S(1)}, u32[]{:S(2)}, u32[]{:S(2)}) collective-permute-start(f32[256,512]{1,0:T(8,128)S(1)} %get-tuple-element.353), channel_id=1, source_target_pairs={{1,0},{2,1},{3,2},{4,3},{5,4},{6,5},{7,6},{9,8},{10,9},{11,10},{12... | collective-permute-start | bytes 1572872 | tf_op jit(solution)/shard_map/while/body/eval_jaxpr/ppermute | solution.py:17
  264.4 14.6 %collective-permute-start.3 = (f32[256,512]{1,0:T(8,128)}, f32[256,512]{1,0:T(8,128)S(1)}, u32[]{:S(2)}, u32[]{:S(2)}) collective-permute-start(f32[256,512]{1,0:T(8,128)} %get-tuple-element.354), channel_id=1, source_target_pairs={{1,0},{2,1},{3,2},{4,3},{5,4},{6,5},{7,6},{9,8},{10,9},{11,10},{12... | collective-permute-start | bytes 1572872 | tf_op jit(solution)/shard_map/while/body/eval_jaxpr/ppermute | solution.py:17
  279.9 18.5 %collective-permute-start.2 = (f32[256,512]{1,0:T(8,128)S(1)}, f32[256,512]{1,0:T(8,128)S(1)}, u32[]{:S(2)}, u32[]{:S(2)}) collective-permute-start(f32[256,512]{1,0:T(8,128)S(1)} %get-tuple-element.353), channel_id=1, source_target_pairs={{1,0},{2,1},{3,2},{4,3},{5,4},{6,5},{7,6},{9,8},{10,9},{11,10},{12... | collective-permute-start | bytes 1572872 | tf_op jit(solution)/shard_map/while/body/eval_jaxpr/ppermute | solution.py:17
  281.8 22.0 %collective-permute-start.3 = (f32[256,512]{1,0:T(8,128)}, f32[256,512]{1,0:T(8,128)S(1)}, u32[]{:S(2)}, u32[]{:S(2)}) collective-permute-start(f32[256,512]{1,0:T(8,128)} %get-tuple-element.354), channel_id=1, source_target_pairs={{1,0},{2,1},{3,2},{4,3},{5,4},{6,5},{7,6},{9,8},{10,9},{11,10},{12... | collective-permute-start | bytes 1572872 | tf_op jit(solution)/shard_map/while/body/eval_jaxpr/ppermute | solution.py:17
  304.7 14.6 %collective-permute-start.2 = (f32[256,512]{1,0:T(8,128)S(1)}, f32[256,512]{1,0:T(8,128)S(1)}, u32[]{:S(2)}, u32[]{:S(2)}) collective-permute-start(f32[256,512]{1,0:T(8,128)S(1)} %get-tuple-element.353), channel_id=1, source_target_pairs={{1,0},{2,1},{3,2},{4,3},{5,4},{6,5},{7,6},{9,8},{10,9},{11,10},{12... | collective-permute-start | bytes 1572872 | tf_op jit(solution)/shard_map/while/body/eval_jaxpr/ppermute | solution.py:17
  306.6 18.3 %collective-permute-start.3 = (f32[256,512]{1,0:T(8,128)}, f32[256,512]{1,0:T(8,128)S(1)}, u32[]{:S(2)}, u32[]{:S(2)}) collective-permute-start(f32[256,512]{1,0:T(8,128)} %get-tuple-element.354), channel_id=1, source_target_pairs={{1,0},{2,1},{3,2},{4,3},{5,4},{6,5},{7,6},{9,8},{10,9},{11,10},{12... | collective-permute-start | bytes 1572872 | tf_op jit(solution)/shard_map/while/body/eval_jaxpr/ppermute | solution.py:17
  325.8 10.5 %collective-permute-start.2 = (f32[256,512]{1,0:T(8,128)S(1)}, f32[256,512]{1,0:T(8,128)S(1)}, u32[]{:S(2)}, u32[]{:S(2)}) collective-permute-start(f32[256,512]{1,0:T(8,128)S(1)} %get-tuple-element.353), channel_id=1, source_target_pairs={{1,0},{2,1},{3,2},{4,3},{5,4},{6,5},{7,6},{9,8},{10,9},{11,10},{12... | collective-permute-start | bytes 1572872 | tf_op jit(solution)/shard_map/while/body/eval_jaxpr/ppermute | solution.py:17
  327.7 14.2 %collective-permute-start.3 = (f32[256,512]{1,0:T(8,128)}, f32[256,512]{1,0:T(8,128)S(1)}, u32[]{:S(2)}, u32[]{:S(2)}) collective-permute-start(f32[256,512]{1,0:T(8,128)} %get-tuple-element.354), channel_id=1, source_target_pairs={{1,0},{2,1},{3,2},{4,3},{5,4},{6,5},{7,6},{9,8},{10,9},{11,10},{12... | collective-permute-start | bytes 1572872 | tf_op jit(solution)/shard_map/while/body/eval_jaxpr/ppermute | solution.py:17
  343.5 6.8 %copy-start.1 = (bf16[1,256,2304]{2,1,0:T(8,128)(2,1)S(1)}, bf16[1,256,2304]{2,1,0:T(8,128)(2,1)}, u32[]{:S(2)}) copy-start(bf16[1,256,2304]{2,1,0:T(8,128)(2,1)} %param.13) | copy-start | bytes 3538948
Sparse Core Ops, SparseCore 0:
  11.0 66.9 all-gather.1
  168.3 147.9 reduce-scatter.3
where the time goes:
time: 359 us; the launch traced here: 357 us
  waiting for transfers between devices  151 us (42%)
  starting transfers between devices  71.8 us (20%)
  local copies, waits for them, and re-layouts  62.9 us (18%)
  matrix products  40 us (11%)
  other arithmetic  17.2 us (5%)
  between operations  14.2 us (4%)
    ppermute x28, waiting for transfers between devices, passed_along(): return lax.ppermute(x, axis, pairs)  151 us
    ppermute x28, starting transfers between devices, passed_along(): return lax.ppermute(x, axis, pairs)  71.7 us
    unnamed x23, local copies, waits for them, and re-layouts  21 us
    dynamic_slice x14, local copies, waits for them, and re-layouts, return_one(): value_part = lax.dynamic_slice_in_dim(value_terms, offset, tok_rows, 0)  10.5 us
    reshape x2, local copies, waits for them, and re-layouts, on_device(): key_heads = win_keys.reshape(length, KH, HD)  10.4 us
    sub x1, matrix products, on_device(): weights = jnp.exp(scores - maxima)  7.85 us
  transfers between devices with their start and end apart: 30, of which 28 were waited for; matrix products, arithmetic and copies ran while one was open for 24% of the time, Pallas kernels for 0%

commit v1 on v0

v1 whole, which is shorter than its diff:
```python
import functools
import math

import jax
import jax.numpy as jnp
from jax import lax
from jax.experimental import pallas as pl
from jax.experimental.pallas import tpu as pltpu
from jax.sharding import Mesh
from jax.sharding import PartitionSpec as P

QH = 4
KH = 2
HD = 256
WINDOW = 2048
GROUPS = QH // KH
LANES = 128
NEG = -1e30
F32 = jnp.float32
BF16 = jnp.bfloat16
NT = (((1,), (1,)), ((), ()))
TN = (((0,), (0,)), ((), ()))


def dot(a, b, dims=(((1,), (0,)), ((), ()))):
    return lax.dot_general(a, b, dims, preferred_element_type=F32)


def admitted(step, rows, core, query_axis):
    if step > 0 and (step + 1) * rows <= WINDOW:
        return None
    shape = (rows, rows)
    half = rows // 2
    query = (lax.broadcasted_iota(jnp.int32, shape, query_axis) + core * half) % rows
    key = (lax.broadcasted_iota(jnp.int32, shape, 1 - query_axis) + core * half) % rows
    gap = key - query - step * rows
    return (gap <= 0) & (gap > -WINDOW)


def forward_kernel(steps, rows, first, last, info, q, *refs):
    chunks = refs[: len(steps)]
    refs = refs[len(steps) :]
    if not first:
        m_in, l_in, acc_in = refs[:3]
        refs = refs[3:]
    if last:
        out, lse_t, m_s, l_s, acc_s = refs
    else:
        m_s, l_s, acc_s = refs
    chip, core = info[0], info[1]
    if not first:
        m_s[...] = m_in[...]
        l_s[...] = l_in[...]
        acc_s[...] = acc_in[...]
    for at, step in enumerate(steps):
        mask = admitted(step, rows, core, 0)

        def block(at=at, step=step, mask=mask):
            keys = chunks[at][:, :HD]
            vals = chunks[at][:, HD:]
            for h in range(GROUPS):
                cols = slice(h * HD, (h + 1) * HD)
                stat = slice(h * LANES, (h + 1) * LANES)
                s = dot(q[:, cols], keys, NT)
                if mask is not None:
                    s = jnp.where(mask, s, NEG)
                top = jnp.max(s, axis=1, keepdims=True)
                if step == 0:
                    p = jnp.exp(s - top)
                    total = jnp.sum(p, axis=1, keepdims=True)
                    acc_s[:, cols] = dot(p.astype(BF16), vals)
                else:
                    before = m_s[:, stat][:, :1]
                    top = jnp.maximum(top, before)
                    p = jnp.exp(s - top)
                    keep = jnp.exp(before - top)
                    total = keep * l_s[:, stat][:, :1] + jnp.sum(p, axis=1, keepdims=True)
                    acc_s[:, cols] = keep * acc_s[:, cols] + dot(p.astype(BF16), vals)
                m_s[:, stat] = jnp.broadcast_to(top, (rows, LANES))
                l_s[:, stat] = jnp.broadcast_to(total, (rows, LANES))

        if step == 0:
            block()
        else:
            pl.when(chip >= step)(block)
    if last:
        for h in range(GROUPS):
            cols = slice(h * HD, (h + 1) * HD)
            stat = slice(h * LANES, (h + 1) * LANES)
            total = l_s[:, stat]
            out[:, cols] = (acc_s[:, cols] / total[:, :1]).astype(BF16)
            lse = m_s[:, stat] + jnp.log(total)
            lse_t[h * 8 : (h + 1) * 8, :] = jnp.transpose(lse)[:8, :]


def forward(info, q, chunks, steps, state, last):
    rows = q.shape[0]
    first = state is None
    stat = jax.ShapeDtypeStruct((rows, GROUPS * LANES), F32)
    acc = jax.ShapeDtypeStruct((rows, GROUPS * HD), F32)
    vmem = pl.BlockSpec(memory_space=pltpu.VMEM)
    smem = pl.BlockSpec(memory_space=pltpu.SMEM)
    scratch = []
    if last:
        outs = (
            jax.ShapeDtypeStruct((rows, GROUPS * HD), BF16),
            jax.ShapeDtypeStruct((GROUPS * 8, rows), F32),
        )
        scratch = [pltpu.VMEM(s.shape, F32) for s in (stat, stat, acc)]
    else:
        outs = (stat, stat, acc)
    args = [info, q, *chunks] + ([] if first else list(state))
    return pl.pallas_call(
        functools.partial(forward_kernel, steps, rows, first, last),
        out_shape=outs,
        in_specs=[smem] + [vmem] * (len(args) - 1),
        out_specs=tuple(vmem for _ in outs),
        scratch_shapes=scratch,
        cost_estimate=pl.CostEstimate(
            flops=len(steps) * GROUPS * rows * rows * HD * 4,
            bytes_accessed=4 * rows * rows * len(steps),
            transcendentals=len(steps) * GROUPS * rows * rows,
        ),
        compiler_params=pltpu.CompilerParams(vmem_limit_bytes=32 * 1024 * 1024),
        name="attend_forward",
    )(*args)


def backward_kernel(steps, rows, first, last, info, q, da, lse_t, *refs):
    chunks = refs[: len(steps)]
    refs = refs[len(steps) :]
    if first:
        att = refs[0]
        refs = refs[1:]
    else:
        delta_t, dq_in = refs[:2]
        refs = refs[2:]
    grads = refs[: len(steps)]
    refs = refs[len(steps) :]
    if last:
        dq_out = refs[0]
        refs = refs[1:]
    if first:
        delta_t = refs[0]
        refs = refs[1:]
    dq_s = refs[0]
    chip, core = info[0], info[1]
    if first:
        for h in range(GROUPS):
            cols = slice(h * HD, (h + 1) * HD)
            prod = da[:, cols].astype(F32) * att[:, cols].astype(F32)
            delta = jnp.sum(prod, axis=1, keepdims=True)
            wide = jnp.broadcast_to(delta, (rows, LANES))
            delta_t[h * 8 : (h + 1) * 8, :] = jnp.transpose(wide)[:8, :]
        dq_s[...] = jnp.zeros_like(dq_s)
    else:
        dq_s[...] = dq_in[...]
    for at, step in enumerate(steps):
        mask = admitted(step, rows, core, 1)

        def block(at=at, mask=mask):
            keys = chunks[at][:, :HD]
            vals = chunks[at][:, HD:]
            for h in range(GROUPS):
                cols = slice(h * HD, (h + 1) * HD)
                qh = q[:, cols]
                dah = da[:, cols]
                s = dot(keys, qh, NT)
                p = jnp.exp(s - lse_t[h * 8 : h * 8 + 1, :])
                if mask is not None:
                    p = jnp.where(mask, p, 0.0)
                dp = dot(vals, dah, NT)
                ds = (p * (dp - delta_t[h * 8 : h * 8 + 1, :])).astype(BF16)
                dk = dot(ds, qh)
                dv = dot(p.astype(BF16), dah)
                dq_s[:, cols] += dot(ds, keys, TN)
                if h == 0:
                    dk_sum, dv_sum = dk, dv
                else:
                    dk_sum, dv_sum = dk_sum + dk, dv_sum + dv
            grads[at][:, :HD] = dk_sum.astype(grads[at].dtype)
            grads[at][:, HD:] = dv_sum.astype(grads[at].dtype)

        if step == 0:
            block()
        else:

            def blank(at=at):
                grads[at][...] = jnp.zeros_like(grads[at])

            pl.when(chip >= step)(block)
            pl.when(chip < step)(blank)
    if last:
        dq_out[...] = (dq_s[...] * HD ** (-0.5)).astype(BF16)


def backward(info, q, da, lse_t, chunks, steps, att, carried, last):
    rows = q.shape[0]
    first = carried is None
    vmem = pl.BlockSpec(memory_space=pltpu.VMEM)
    smem = pl.BlockSpec(memory_space=pltpu.SMEM)
    wide = (rows, GROUPS * HD)
    outs = [jax.ShapeDtypeStruct((rows, 2 * HD), F32 if s == 0 else BF16) for s in steps]
    if last:
        outs.append(jax.ShapeDtypeStruct(wide, BF16))
    if first:
        outs.append(jax.ShapeDtypeStruct((GROUPS * 8, rows), F32))
    scratch = []
    if last:
        scratch = [pltpu.VMEM(wide, F32)]
    else:
        outs.append(jax.ShapeDtypeStruct(wide, F32))
    args = [info, q, da, lse_t, *chunks] + ([att] if first else list(carried))
    return pl.pallas_call(
        functools.partial(backward_kernel, steps, rows, first, last),
        out_shape=tuple(outs),
        in_specs=[smem] + [vmem] * (len(args) - 1),
        out_specs=tuple(vmem for _ in outs),
        scratch_shapes=scratch,
        cost_estimate=pl.CostEstimate(
            flops=len(steps) * GROUPS * rows * rows * HD * 10,
            bytes_accessed=6 * rows * rows * len(steps),
            transcendentals=len(steps) * GROUPS * rows * rows,
        ),
        compiler_params=pltpu.CompilerParams(vmem_limit_bytes=32 * 1024 * 1024),
        name="attend_backward",
    )(*args)


def on_device(queries, key_rows, values, out_weight, out_grad):
    chip = lax.axis_index("chip")
    core = lax.axis_index("core")
    row = lax.axis_index("dp")
    chips = lax.axis_size("chip")
    rows_dp = lax.axis_size("dp")
    tok = queries.shape[1]
    rows = 2 * tok
    prior = min(-(-WINDOW // rows), chips - 1)
    steps = tuple(range(prior + 1))
    low = core == 0
    info = jnp.stack([chip, core]).astype(jnp.int32)

    def own(x):
        half = x.shape[1] // 2
        return jnp.where(low, x[:, :half], x[:, half:])

    def other(x):
        half = x.shape[1] // 2
        return jnp.where(low, x[:, half:], x[:, :half])

    def swap(x):
        return lax.ppermute(x, "core", [(0, 1), (1, 0)])

    def in_order(mine, theirs, axis):
        return jnp.where(
            low,
            jnp.concatenate([mine, theirs], axis),
            jnp.concatenate([theirs, mine], axis),
        )

    block = in_order(own(out_weight), swap(other(out_weight)), 0)
    part = block.shape[0]
    if chips <= 4:
        weight_z = jnp.zeros((chips * part, block.shape[1]), BF16)
        weight_z = lax.dynamic_update_slice_in_dim(weight_z, block, chip * part, 0)
        for k in range(1, chips):
            got = lax.ppermute(block, "chip", [(i, (i + k) % chips) for i in range(chips)])
            source = lax.rem(chip - k + chips, chips)
            weight_z = lax.dynamic_update_slice_in_dim(weight_z, got, source * part, 0)
    else:
        weight_z = lax.all_gather(block, "chip", axis=0, tiled=True)
    share = weight_z.shape[0]

    k0, v0 = key_rows[0], values[0]
    kv = jnp.concatenate([own(k0), own(v0)], 1)
    kv = jnp.concatenate([kv, swap(jnp.concatenate([other(k0), other(v0)], 1))], 0)
    chunks = [kv]
    for k in steps[1:]:
        chunks.append(lax.ppermute(kv, "chip", [(i, i + k) for i in range(chips - k)]))

    q0 = queries[0]
    q = jnp.concatenate([own(q0), swap(other(q0))], 0) * jnp.asarray(HD ** (-0.5), BF16)
    grad = jnp.concatenate([out_grad[0], swap(out_grad[0])], 0)

    weight = jnp.zeros((rows_dp * share, block.shape[1]), BF16)
    weight = lax.dynamic_update_slice_in_dim(weight, weight_z, row * share, 0)
    for k in range(1, rows_dp):
        got = lax.ppermute(weight_z, "dp", [(i, i ^ k) for i in range(rows_dp)])
        weight = lax.dynamic_update_slice_in_dim(weight, got, (row ^ k) * share, 0)

    state = forward(info, q, chunks[:-1], steps[:-1], None, False)
    att, lse_t = forward(info, q, chunks[-1:], steps[-1:], state, True)

    dw = dot(grad, att, TN)
    mine = lax.dynamic_slice_in_dim(dw, row * share, share, 0)
    for k in range(1, rows_dp):
        sent = lax.dynamic_slice_in_dim(dw, (row ^ k) * share, share, 0).astype(BF16)
        mine = mine + lax.ppermute(sent, "dp", [(i, i ^ k) for i in range(rows_dp)]).astype(F32)
    if chips <= 4:
        final = lax.dynamic_slice_in_dim(mine, chip * part, part, 0)
        for k in range(1, chips):
            target = lax.rem(chip + k, chips)
            sent = lax.dynamic_slice_in_dim(mine, target * part, part, 0).astype(BF16)
            got = lax.ppermute(sent, "chip", [(i, (i + k) % chips) for i in range(chips)])
            final = final + got.astype(F32)
    else:
        final = lax.psum_scatter(mine, "chip", scatter_dimension=0, tiled=True)
    total_tokens = rows_dp * chips * rows
    final = final * (1.0 / math.sqrt(total_tokens))
    top, bottom = final[: part // 2], final[part // 2 :]
    weight_grad = in_order(jnp.where(low, top, bottom), swap(jnp.where(low, bottom, top)), 1)

    da = dot(grad, weight).astype(BF16)
    carried = None
    sums = {}
    for step in reversed(steps):
        last = step == 0
        res = backward(info, q, da, lse_t, [chunks[step]], (step,), att, carried, last)
        sums[step] = res[0]
        if carried is None:
            delta_t = res[1]
        if last:
            dq = res[1]
        else:
            carried = (delta_t, res[-1])
    kv_grad = sums[0]
    for k in reversed(steps[1:]):
        got = lax.ppermute(sums[k], "chip", [(i + k, i) for i in range(chips - k)])
        kv_grad = kv_grad + got.astype(F32)
    kv_grad = kv_grad.astype(BF16)

    weight_other = swap(weight)
    layer_out = (dot(att[:tok], weight, NT) + dot(swap(att[tok:]), weight_other, NT)).astype(BF16)

    query_grad = in_order(dq[:tok], swap(dq[tok:]), 1)
    theirs = swap(kv_grad[tok:])
    key_grad = in_order(kv_grad[:tok, :HD], theirs[:, :HD], 1)
    value_grad = in_order(kv_grad[:tok, HD:], theirs[:, HD:], 1)
    return (
        layer_out[None],
        query_grad[None],
        key_grad[None],
        value_grad[None],
        weight_grad,
    )


def solution(mesh):
    devices = mesh.devices
    pairs = Mesh(
        devices.reshape(devices.shape[0], devices.shape[1] // 2, 2), ("dp", "chip", "core")
    )
    tokens = P("dp", ("chip", "core"), None)
    features = P(("dp", "chip", "core"), None)
    return jax.shard_map(
        on_device,
        mesh=pairs,
        in_specs=(tokens, tokens, tokens, features, tokens),
        out_specs=(tokens, tokens, tokens, tokens, features),
        check_vma=False,
    )
```

time: 359 us -> 176 us (0.49)
  local copies, waits for them, and re-layouts: 62.9 us -> 1.99 us
  waiting for transfers between devices: 151 us -> 91.2 us
  matrix products: 40 us -> 8.03 us
  starting transfers between devices: 71.8 us -> 50.1 us
  between operations: 14.2 us -> 0.95 us
  Pallas kernels: 0 us -> 13 us
  other arithmetic: 17.2 us -> 8.27 us
    ppermute x28 -> x27, waiting for transfers between devices: 151 us -> 91.2 us  [the longest x3 39.5 us: on_device(): lax.ppermute(kv, 'chip', [(i, i + k) for i in range(chips - k)])]
    dot_general x8 -> x4, matrix products: 32.1 us -> 8.03 us  [dot(): return lax.dot_general(a, b, dims, preferred_element_type=F32)]
    ppermute x28 -> x27, starting transfers between devices: 71.7 us -> 50.1 us  [the longest x3 17.4 us: on_device(): lax.ppermute(sent, 'chip', [(i, (i + k) % chips) for i in range(chips)])]
    unnamed x23 -> x4, local copies, waits for them, and re-layouts: 21 us -> 0.01 us
    reshape x5 -> x0, local copies, waits for them, and re-layouts: 13.4 us -> none  [the longest x2 10.4 us: on_device(): key_heads = win_keys.reshape(length, KH, HD)]
    pallas_call x0 -> x6, Pallas kernels: none -> 13 us  [the longest x4 6.72 us: backward(): pl.pallas_call(functools.partial(backward_kernel, steps, rows, first, las...]
    dynamic_slice x21 -> x0, local copies, waits for them, and re-layouts: 11.8 us -> none  [the longest x14 10.5 us: return_one(): value_part = lax.dynamic_slice_in_dim(value_terms, offset, tok_rows, 0)]
    dynamic_update_slice x16 -> x7, local copies, waits for them, and re-layouts: 13.1 us -> 1.38 us  [the longest x3 1.29 us: on_device(): weight = lax.dynamic_update_slice_in_dim(weight, got, (row ^ k) * share, 0)]
  transfers between devices with their start and end apart: 30 -> 27, of which waited for: 28 -> 12; matrix products, arithmetic and copies ran while one was open for 24% -> 8% of each run, Pallas kernels for 0% -> 8%
where the time goes in v1:
time: 176 us; the launch traced here: 174 us
  waiting for transfers between devices  91.2 us (52%)
  starting transfers between devices  50.1 us (28%)
  Pallas kernels  13 us (7%)
  other arithmetic  8.27 us (5%)
  matrix products  8.03 us (5%)
  local copies, waits for them, and re-layouts  1.99 us (1%)
    ppermute x3, waiting for transfers between devices, on_device(): lax.ppermute(kv, 'chip', [(i, i + k) for i in range(chips - k)])  39.5 us
    ppermute x3, waiting for transfers between devices, on_device(): got = lax.ppermute(sums[k], 'chip', [(i + k, i) for i in range(chips - k)])  23.9 us
    ppermute x3, starting transfers between devices, on_device(): lax.ppermute(sent, 'chip', [(i, (i + k) % chips) for i in range(chips)])  17.4 us
    ppermute x3, waiting for transfers between devices, on_device(): lax.ppermute(sent, 'dp', [(i, i ^ k) for i in range(rows_dp)]).astype(F32)  11.1 us
    ppermute x9, starting transfers between devices, swap(): return lax.ppermute(x, 'core', [(0, 1), (1, 0)])  10.4 us
    dot_general x4, matrix products, dot(): return lax.dot_general(a, b, dims, preferred_element_type=F32)  8.03 us
    ppermute x3, waiting for transfers between devices, on_device(): lax.ppermute(sent, 'chip', [(i, (i + k) % chips) for i in range(chips)])  7.88 us
    pallas_call x4, Pallas kernels, backward(): pl.pallas_call(functools.partial(backward_kernel, steps, rows, first, las...  6.72 us
  transfers between devices with their start and end apart: 27, of which 12 were waited for; matrix products, arithmetic and copies ran while one was open for 8% of the time, Pallas kernels for 8%

profile of v1, /device:TPU:9, one launch (start us, length us, event | category | flops | bytes accessed | tf_op | source)
XLA Modules:
  0.0 173.6 jit_solution(11033637171679699813)
XLA Ops:
  0.6 1.0 broadcast_select_fusion.4
  1.7 1.0 broadcast_select_fusion.5
  2.7 0.7 collective-permute-start.1
  3.5 0.9 broadcast_select_fusion.6
  4.4 0.1 collective-permute-start.5
  4.5 1.2 collective-permute-done.5
  5.8 1.3 collective-permute-start.6
  7.2 1.1 collective-permute-start.7
  8.3 2.2 %collective-permute-start.3 = (bf16[512,512]{1,0:T(8,128)(2,1)S(1)}, bf16[512,512]{1,0:T(8,128)(2,1)S(1)}, u32[]{:S(2)}, u32[]{:S(2)}) collective-permute-start(bf16[512,512]{1,0:T(8,128)(2,1)S(1)} %pad_maximum_fusion.5.refs_0_), channel_id=1, source_target_pairs={{0,2},{2,4},{4,6},{1,3},{3,5},{5,7},{8,10},{10,12},{12,14},{9,11},... | collective-permute-start | bytes 1572872 | tf_op jit(solution)/shard_map/ppermute | solution.py:279
  10.5 2.3 %collective-permute-start.4 = (bf16[512,512]{1,0:T(8,128)(2,1)S(1)}, bf16[512,512]{1,0:T(8,128)(2,1)S(1)}, u32[]{:S(2)}, u32[]{:S(2)}) collective-permute-start(bf16[512,512]{1,0:T(8,128)(2,1)S(1)} %pad_maximum_fusion.5.refs_0_), channel_id=1, source_target_pairs={{0,4},{2,6},{1,5},{3,7},{8,12},{10,14},{9,13},{11,15},{16,20},{18,... | collective-permute-start | bytes 1572872 | tf_op jit(solution)/shard_map/ppermute | solution.py:279
  12.8 0.7 broadcast_select_fusion.1
  13.6 1.0 collective-permute-start
  14.6 2.4 %collective-permute-start.8 = (bf16[144,512]{1,0:T(8,128)(2,1)S(1)}, bf16[144,512]{1,0:T(8,128)(2,1)S(1)}, u32[]{:S(2)}, u32[]{:S(2)}) collective-permute-start(bf16[144,512]{1,0:T(8,128)(2,1)S(1)} %get-tuple-element.34), channel_id=1, source_target_pairs={{0,6},{2,0},{4,2},{6,4},{1,7},{3,1},{5,3},{7,5},{8,14},{10,8},{12,... | collective-permute-start | bytes 442376 | tf_op jit(solution)/shard_map/ppermute | solution.py:267
  17.0 1.2 collective-permute-start.14
  18.2 3.8 %collective-permute-done.8 = bf16[144,512]{1,0:T(8,128)(2,1)S(1)} collective-permute-done((bf16[144,512]{1,0:T(8,128)(2,1)S(1)}, bf16[144,512]{1,0:T(8,128)(2,1)S(1)}, u32[]{:S(2)}, u32[]{:S(2)}) %collective-permute-start.8) | collective-permute-done | bytes 147488 | tf_op jit(solution)/shard_map/ppermute | solution.py:267
  22.0 1.3 collective-permute-start.9
  23.3 0.7 collective-permute-start.2
  24.0 18.3 %collective-permute-done.3.refs_1_.refs_0_ = bf16[512,512]{1,0:T(8,128)(2,1)S(1)} collective-permute-done((bf16[512,512]{1,0:T(8,128)(2,1)S(1)}, bf16[512,512]{1,0:T(8,128)(2,1)S(1)}, u32[]{:S(2)}, u32[]{:S(2)}) %collective-permute-start.3) | collective-permute-done | bytes 524320 | tf_op jit(solution)/shard_map/ppermute | solution.py:279
  42.3 1.2 collective-permute-start.10
  43.5 0.1 pad_add_fusion.info
  43.6 21.2 %collective-permute-done.4.refs_2_.refs_0_ = bf16[512,512]{1,0:T(8,128)(2,1)S(1)} collective-permute-done((bf16[512,512]{1,0:T(8,128)(2,1)S(1)}, bf16[512,512]{1,0:T(8,128)(2,1)S(1)}, u32[]{:S(2)}, u32[]{:S(2)}) %collective-permute-start.4) | collective-permute-done | bytes 524320 | tf_op jit(solution)/shard_map/ppermute | solution.py:279
  64.7 2.2 %collective-permute-start.11 = (bf16[576,512]{1,0:T(8,128)(2,1)S(1)}, bf16[576,512]{1,0:T(8,128)(2,1)S(1)}, u32[]{:S(2)}, u32[]{:S(2)}) collective-permute-start(bf16[576,512]{1,0:T(8,128)(2,1)S(1)} %constant_dynamic-update-slice_fusion.4), channel_id=1, source_target_pairs={{0,24},{8,16},{16,8},{24,0},{1,25},{9,17},{17,9},{25,1},{2,26},{10... | collective-permute-start | bytes 1769480 | tf_op jit(solution)/shard_map/ppermute | solution.py:288
  66.9 0.2 broadcast_in_dim.12
  67.1 1.0 maximum_multiply_fusion.q
  68.2 5.3 %attend_forward.2 = (f32[512,256]{1,0:T(8,128)S(1)}, f32[512,256]{1,0:T(8,128)S(1)}, f32[512,512]{1,0:T(8,128)S(1)}) custom-call(s32[2]{0:T(128)S(1)} %pad_add_fusion.info, bf16[512,512]{1,0:T(8,128)(2,1)S(1)} %maximum_multiply_fusion.q, bf16[512,512]{1,0:T(8,128)(2,1)S(1)} %pad_maximum_fusion.5.refs_0_, ...), custom_call_target="tpu_custom_call" | custom-call | flops 1610612736 | bytes 3145728 | tf_op jit(solution)/shard_map/attend_forward/pallas_call | solution.py:113
  73.5 1.0 attend_forward.3
  74.6 1.2 constant_dynamic-update-slice_fusion.1
  75.8 3.7 %collective-permute-done.11 = bf16[576,512]{1,0:T(8,128)(2,1)S(1)} collective-permute-done((bf16[576,512]{1,0:T(8,128)(2,1)S(1)}, bf16[576,512]{1,0:T(8,128)(2,1)S(1)}, u32[]{:S(2)}, u32[]{:S(2)}) %collective-permute-start.11) | collective-permute-done | bytes 589856 | tf_op jit(solution)/shard_map/ppermute | solution.py:288
  79.6 1.9 %collective-permute-start.13 = (bf16[2304,512]{1,0:T(8,128)(2,1)S(1)}, bf16[2304,512]{1,0:T(8,128)(2,1)S(1)}, u32[]{:S(2)}, u32[]{:S(2)}) collective-permute-start(bf16[2304,512]{1,0:T(8,128)(2,1)S(1)} %constant_dynamic-update-slice_fusion), channel_id=1, source_target_pairs={{0,1},{1,0},{2,3},{3,2},{4,5},{5,4},{6,7},{7,6},{8,9},{9,8},{10,11... | collective-permute-start | bytes 7077896 | tf_op jit(solution)/shard_map/ppermute | solution.py:252
  81.5 2.6 %fusion.4.da = bf16[512,512]{1,0:T(8,128)(2,1)S(1)} fusion(bf16[2304,512]{1,0:T(8,128)(2,1)S(1)} %constant_dynamic-update-slice_fusion, bf16[256,2304]{1,0:T(8,128)(2,1)} %collective-permute-done.14, bf16[256,2304]{1,0:T(8,128)(2,1)S(1)} %bitcast.29), kind=kOutput, calls=%fused_computation.6 | convolution fusion | flops 1212940288 | bytes 5242880 | tf_op jit(solution)/shard_map/dot_general | solution.py:26
  84.2 1.1 attend_backward.4
  85.2 0.6 attend_backward.5
  85.9 2.5 %attend_backward.6 = (bf16[512,512]{1,0:T(8,128)(2,1)S(1)}, f32[512,512]{1,0:T(8,128)S(1)}) custom-call(s32[2]{0:T(128)S(1)} %pad_add_fusion.info, bf16[512,512]{1,0:T(8,128)(2,1)S(1)} %maximum_multiply_fusion.q, bf16[512,512]{1,0:T(8,128)(2,1)S(1)} %fusion.4.da, f32[16,512]{1,0:T(8,128)S(1)} %get-tuple-element.23.lse_t, ...), custom_call_target="tpu_custom_call" | custom-call | flops 1342177280 | bytes 1572864 | tf_op jit(solution)/shard_map/attend_backward/pallas_call | solution.py:214
  88.4 2.5 %attend_backward.7 = (f32[512,512]{1,0:T(8,128)S(1)}, bf16[512,512]{1,0:T(8,128)(2,1)S(1)}) custom-call(s32[2]{0:T(128)S(1)} %pad_add_fusion.info, bf16[512,512]{1,0:T(8,128)(2,1)S(1)} %maximum_multiply_fusion.q, bf16[512,512]{1,0:T(8,128)(2,1)S(1)} %fusion.4.da, f32[16,512]{1,0:T(8,128)S(1)} %get-tuple-element.23.lse_t, ...), custom_call_target="tpu_custom_call" | custom-call | flops 1342177280 | bytes 1572864 | tf_op jit(solution)/shard_map/attend_backward/pallas_call | solution.py:214
  90.9 1.9 %collective-permute-start.18 = (bf16[512,512]{1,0:T(8,128)(2,1)S(1)}, bf16[512,512]{1,0:T(8,128)(2,1)S(1)}, u32[]{:S(2)}, u32[]{:S(2)}) collective-permute-start(bf16[512,512]{1,0:T(8,128)(2,1)S(1)} %get-tuple-element.32), channel_id=1, source_target_pairs={{2,0},{4,2},{6,4},{3,1},{5,3},{7,5},{10,8},{12,10},{14,12},{11,9},... | collective-permute-start | bytes 1572872 | tf_op jit(solution)/shard_map/ppermute | solution.py:328
  92.8 1.3 collective-permute-start.17
  94.2 0.1 collective-permute-start.15
  94.3 0.7 collective-permute-start.16
  95.0 2.7 %fusion.2 = f32[2304,512]{1,0:T(8,128)S(1)} fusion(bf16[512,512]{1,0:T(8,128)(2,1)S(1)} %get-tuple-element.22.refs_1_, bf16[256,2304]{1,0:T(8,128)(2,1)} %collective-permute-done.14, bf16[256,2304]{1,0:T(8,128)(2,1)S(1)} %bitcast.30), kind=kOutput, calls=%fused_computation.4 | convolution fusion | flops 1212678144 | bytes 7602176 | tf_op jit(solution)/shard_map/dot_general | solution.py:26
  97.7 0.2 dynamic-slice_convert_fusion.2
  97.9 2.2 %collective-permute-start.22 = (bf16[576,512]{1,0:T(8,128)(2,1)S(1)}, bf16[576,512]{1,0:T(8,128)(2,1)S(1)}, u32[]{:S(2)}, u32[]{:S(2)}) collective-permute-start(bf16[576,512]{1,0:T(8,128)(2,1)S(1)} %get-tuple-element.36), channel_id=1, source_target_pairs={{0,24},{8,16},{16,8},{24,0},{1,25},{9,17},{17,9},{25,1},{2,26},{10... | collective-permute-start | bytes 1769480 | tf_op jit(solution)/shard_map/ppermute | solution.py:298
  100.2 6.2 %collective-permute-done.18 = bf16[512,512]{1,0:T(8,128)(2,1)S(1)} collective-permute-done((bf16[512,512]{1,0:T(8,128)(2,1)S(1)}, bf16[512,512]{1,0:T(8,128)(2,1)S(1)}, u32[]{:S(2)}, u32[]{:S(2)}) %collective-permute-start.18) | collective-permute-done | bytes 524320 | tf_op jit(solution)/shard_map/ppermute | solution.py:328
  106.3 1.2 collective-permute-start.21
  107.6 17.7 %collective-permute-done.17 = bf16[512,512]{1,0:T(8,128)(2,1)S(1)} collective-permute-done((bf16[512,512]{1,0:T(8,128)(2,1)S(1)}, bf16[512,512]{1,0:T(8,128)(2,1)S(1)}, u32[]{:S(2)}, u32[]{:S(2)}) %collective-permute-start.17) | collective-permute-done | bytes 524320 | tf_op jit(solution)/shard_map/ppermute | solution.py:328
  125.3 0.3 collective-permute-start.20
  125.5 1.0 maximum_select_fusion
  126.5 1.2 collective-permute-start.12
  127.7 0.3 add_convert_fusion
  128.1 11.1 %collective-permute-done.20 = bf16[576,512]{1,0:T(8,128)(2,1)S(1)} collective-permute-done((bf16[576,512]{1,0:T(8,128)(2,1)S(1)}, bf16[576,512]{1,0:T(8,128)(2,1)S(1)}, u32[]{:S(2)}, u32[]{:S(2)}) %collective-permute-start.20) | collective-permute-done | bytes 589856 | tf_op jit(solution)/shard_map/ppermute | solution.py:298
  139.2 0.3 convert_add_fusion
  139.5 0.1 dynamic-slice_convert_fusion.5
  139.6 16.1 %collective-permute-start.25 = (bf16[144,512]{1,0:T(8,128)(2,1)S(1)}, bf16[144,512]{1,0:T(8,128)(2,1)S(1)}, u32[]{:S(2)}, u32[]{:S(2)}) collective-permute-start(bf16[144,512]{1,0:T(8,128)(2,1)S(1)} %get-tuple-element.39), channel_id=1, source_target_pairs={{0,6},{2,0},{4,2},{6,4},{1,7},{3,1},{5,3},{7,5},{8,14},{10,8},{12,... | collective-permute-start | bytes 442376 | tf_op jit(solution)/shard_map/ppermute | solution.py:304
  155.7 1.3 collective-permute-start.23
  157.0 1.1 collective-permute-done.25
  158.1 3.6 %collective-permute-start.19 = (bf16[256,512]{1,0:T(8,128)(2,1)S(1)}, bf16[256,512]{1,0:T(8,128)(2,1)S(1)}, u32[]{:S(2)}, u32[]{:S(2)}) collective-permute-start(bf16[256,512]{1,0:T(8,128)(2,1)S(1)} %slice.91), channel_id=1, source_target_pairs={{0,1},{1,0},{2,3},{3,2},{4,5},{5,4},{6,7},{7,6},{8,9},{9,8},{10,11... | collective-permute-start | bytes 786440 | tf_op jit(solution)/shard_map/ppermute | solution.py:252
  161.7 3.6 %collective-permute-done.24 = bf16[144,512]{1,0:T(8,128)(2,1)S(1)} collective-permute-done((bf16[144,512]{1,0:T(8,128)(2,1)S(1)}, bf16[144,512]{1,0:T(8,128)(2,1)S(1)}, u32[]{:S(2)}, u32[]{:S(2)}) %collective-permute-start.24) | collective-permute-done | bytes 147488 | tf_op jit(solution)/shard_map/ppermute | solution.py:304
  165.3 3.2 %collective-permute-done.23 = bf16[144,512]{1,0:T(8,128)(2,1)S(1)} collective-permute-done((bf16[144,512]{1,0:T(8,128)(2,1)S(1)}, bf16[144,512]{1,0:T(8,128)(2,1)S(1)}, u32[]{:S(2)}, u32[]{:S(2)}) %collective-permute-start.23) | collective-permute-done | bytes 147488 | tf_op jit(solution)/shard_map/ppermute | solution.py:304
  168.5 0.1 add_multiply_fusion
  168.6 0.6 collective-permute-start.26
  169.2 0.9 maximum_select_fusion.2
  170.1 0.1 collective-permute-done.26
  170.2 0.7 maximum_select_fusion.1
  170.9 0.8 fusion.8
  171.7 1.9 %fusion.1 = bf16[1,256,2304]{2,1,0:T(8,128)(2,1)} fusion(f32[256,2304]{1,0:T(8,128)S(1)} %fusion.8, bf16[2304,512]{1,0:T(8,128)(2,1)S(1)} %constant_dynamic-update-slice_fusion, bf16[512,512]{1,0:T(8,128)(2,1)S(1)} %get-tuple-element.22.refs_1_), kind=kOutput, calls=%fused_computation.2 | convolution fusion | flops 605159424 | bytes 6160384 | tf_op jit(solution)/shard_map/dot_general | solution.py:26
  (36 shorter events, 0.5 us)
Async XLA Ops:
  0.6 12.2 %copy-start = (bf16[1,256,1024]{2,1,0:T(8,128)(2,1)S(1)}, bf16[1,256,1024]{2,1,0:T(8,128)(2,1)}, u32[]{:S(2)}) copy-start(bf16[1,256,1024]{2,1,0:T(8,128)(2,1)} %param.5) | copy-start | bytes 1572868
  2.7 5.5 %collective-permute-start.1 = (bf16[256,512]{1,0:T(8,128)(2,1)S(1)}, bf16[256,512]{1,0:T(8,128)(2,1)S(1)}, u32[]{:S(2)}, u32[]{:S(2)}) collective-permute-start(bf16[256,512]{1,0:T(8,128)(2,1)S(1)} %pad_maximum_fusion.6), channel_id=1, source_target_pairs={{0,1},{1,0},{2,3},{3,2},{4,5},{5,4},{6,7},{7,6},{8,9},{9,8},{10,11... | collective-permute-start | bytes 786440 | tf_op jit(solution)/shard_map/ppermute | solution.py:252
  4.4 1.3 collective-permute-start.5
  5.8 8.8 %collective-permute-start.6 = (bf16[144,512]{1,0:T(8,128)(2,1)S(1)}, bf16[144,512]{1,0:T(8,128)(2,1)S(1)}, u32[]{:S(2)}, u32[]{:S(2)}) collective-permute-start(bf16[144,512]{1,0:T(8,128)(2,1)S(1)} %get-tuple-element.34), channel_id=1, source_target_pairs={{0,2},{2,4},{4,6},{6,0},{1,3},{3,5},{5,7},{7,1},{8,10},{10,12},{12... | collective-permute-start | bytes 442376 | tf_op jit(solution)/shard_map/ppermute | solution.py:267
  7.2 9.8 %collective-permute-start.7 = (bf16[144,512]{1,0:T(8,128)(2,1)S(1)}, bf16[144,512]{1,0:T(8,128)(2,1)S(1)}, u32[]{:S(2)}, u32[]{:S(2)}) collective-permute-start(bf16[144,512]{1,0:T(8,128)(2,1)S(1)} %get-tuple-element.34), channel_id=1, source_target_pairs={{0,4},{2,6},{4,0},{6,2},{1,5},{3,7},{5,1},{7,3},{8,12},{10,14},{12... | collective-permute-start | bytes 442376 | tf_op jit(solution)/shard_map/ppermute | solution.py:267
  8.3 34.0 %collective-permute-start.3 = (bf16[512,512]{1,0:T(8,128)(2,1)S(1)}, bf16[512,512]{1,0:T(8,128)(2,1)S(1)}, u32[]{:S(2)}, u32[]{:S(2)}) collective-permute-start(bf16[512,512]{1,0:T(8,128)(2,1)S(1)} %pad_maximum_fusion.5.refs_0_), channel_id=1, source_target_pairs={{0,2},{2,4},{4,6},{1,3},{3,5},{5,7},{8,10},{10,12},{12,14},{9,11},... | collective-permute-start | bytes 1572872 | tf_op jit(solution)/shard_map/ppermute | solution.py:279
  10.5 54.3 %collective-permute-start.4 = (bf16[512,512]{1,0:T(8,128)(2,1)S(1)}, bf16[512,512]{1,0:T(8,128)(2,1)S(1)}, u32[]{:S(2)}, u32[]{:S(2)}) collective-permute-start(bf16[512,512]{1,0:T(8,128)(2,1)S(1)} %pad_maximum_fusion.5.refs_0_), channel_id=1, source_target_pairs={{0,4},{2,6},{1,5},{3,7},{8,12},{10,14},{9,13},{11,15},{16,20},{18,... | collective-permute-start | bytes 1572872 | tf_op jit(solution)/shard_map/ppermute | solution.py:279
  13.6 9.7 %collective-permute-start = (bf16[256,512]{1,0:T(8,128)(2,1)}, bf16[256,512]{1,0:T(8,128)(2,1)}, u32[]{:S(2)}, u32[]{:S(2)}) collective-permute-start(bf16[256,512]{1,0:T(8,128)(2,1)} %get-tuple-element.46), channel_id=1, source_target_pairs={{0,1},{1,0},{2,3},{3,2},{4,5},{5,4},{6,7},{7,6},{8,9},{9,8},{10,11... | collective-permute-start | bytes 786440 | tf_op jit(solution)/shard_map/ppermute | solution.py:252
  14.6 7.4 %collective-permute-start.8 = (bf16[144,512]{1,0:T(8,128)(2,1)S(1)}, bf16[144,512]{1,0:T(8,128)(2,1)S(1)}, u32[]{:S(2)}, u32[]{:S(2)}) collective-permute-start(bf16[144,512]{1,0:T(8,128)(2,1)S(1)} %get-tuple-element.34), channel_id=1, source_target_pairs={{0,6},{2,0},{4,2},{6,4},{1,7},{3,1},{5,3},{7,5},{8,14},{10,8},{12,... | collective-permute-start | bytes 442376 | tf_op jit(solution)/shard_map/ppermute | solution.py:267
  17.0 64.5 %collective-permute-start.14 = (bf16[256,2304]{1,0:T(8,128)(2,1)}, bf16[256,2304]{1,0:T(8,128)(2,1)}, u32[]{:S(2)}, u32[]{:S(2)}) collective-permute-start(bf16[256,2304]{1,0:T(8,128)(2,1)} %bitcast.28), channel_id=1, source_target_pairs={{0,1},{1,0},{2,3},{3,2},{4,5},{5,4},{6,7},{7,6},{8,9},{9,8},{10,11... | collective-permute-start | bytes 3538952 | tf_op jit(solution)/shard_map/ppermute | solution.py:252
  22.0 52.5 %collective-permute-start.9 = (bf16[576,512]{1,0:T(8,128)(2,1)S(1)}, bf16[576,512]{1,0:T(8,128)(2,1)S(1)}, u32[]{:S(2)}, u32[]{:S(2)}) collective-permute-start(bf16[576,512]{1,0:T(8,128)(2,1)S(1)} %constant_dynamic-update-slice_fusion.4), channel_id=1, source_target_pairs={{0,8},{8,0},{16,24},{24,16},{1,9},{9,1},{17,25},{25,17},{2,10},{10... | collective-permute-start | bytes 1769480 | tf_op jit(solution)/shard_map/ppermute | solution.py:288
  23.3 50.2 %collective-permute-start.2 = (bf16[512,512]{1,0:T(8,128)(2,1)S(1)}, bf16[512,512]{1,0:T(8,128)(2,1)S(1)}, u32[]{:S(2)}, u32[]{:S(2)}) collective-permute-start(bf16[512,512]{1,0:T(8,128)(2,1)S(1)} %pad_maximum_fusion.5.refs_0_), channel_id=1, source_target_pairs={{0,6},{1,7},{8,14},{9,15},{16,22},{17,23},{24,30},{25,31}} | collective-permute-start | bytes 1572872 | tf_op jit(solution)/shard_map/ppermute | solution.py:279
  42.3 32.3 %collective-permute-start.10 = (bf16[576,512]{1,0:T(8,128)(2,1)S(1)}, bf16[576,512]{1,0:T(8,128)(2,1)}, u32[]{:S(2)}, u32[]{:S(2)}) collective-permute-start(bf16[576,512]{1,0:T(8,128)(2,1)S(1)} %constant_dynamic-update-slice_fusion.4), channel_id=1, source_target_pairs={{0,16},{8,24},{16,0},{24,8},{1,17},{9,25},{17,1},{25,9},{2,18},{10... | collective-permute-start | bytes 1769480 | tf_op jit(solution)/shard_map/ppermute | solution.py:288
  64.7 14.8 %collective-permute-start.11 = (bf16[576,512]{1,0:T(8,128)(2,1)S(1)}, bf16[576,512]{1,0:T(8,128)(2,1)S(1)}, u32[]{:S(2)}, u32[]{:S(2)}) collective-permute-start(bf16[576,512]{1,0:T(8,128)(2,1)S(1)} %constant_dynamic-update-slice_fusion.4), channel_id=1, source_target_pairs={{0,24},{8,16},{16,8},{24,0},{1,25},{9,17},{17,9},{25,1},{2,26},{10... | collective-permute-start | bytes 1769480 | tf_op jit(solution)/shard_map/ppermute | solution.py:288
  74.5 7.0 %copy-start.1 = (bf16[1,256,2304]{2,1,0:T(8,128)(2,1)S(1)}, bf16[1,256,2304]{2,1,0:T(8,128)(2,1)}, u32[]{:S(2)}) copy-start(bf16[1,256,2304]{2,1,0:T(8,128)(2,1)} %param.9) | copy-start | bytes 3538948
  79.6 91.4 %collective-permute-start.13 = (bf16[2304,512]{1,0:T(8,128)(2,1)S(1)}, bf16[2304,512]{1,0:T(8,128)(2,1)S(1)}, u32[]{:S(2)}, u32[]{:S(2)}) collective-permute-start(bf16[2304,512]{1,0:T(8,128)(2,1)S(1)} %constant_dynamic-update-slice_fusion), channel_id=1, source_target_pairs={{0,1},{1,0},{2,3},{3,2},{4,5},{5,4},{6,7},{7,6},{8,9},{9,8},{10,11... | collective-permute-start | bytes 7077896 | tf_op jit(solution)/shard_map/ppermute | solution.py:252
  90.9 15.4 %collective-permute-start.18 = (bf16[512,512]{1,0:T(8,128)(2,1)S(1)}, bf16[512,512]{1,0:T(8,128)(2,1)S(1)}, u32[]{:S(2)}, u32[]{:S(2)}) collective-permute-start(bf16[512,512]{1,0:T(8,128)(2,1)S(1)} %get-tuple-element.32), channel_id=1, source_target_pairs={{2,0},{4,2},{6,4},{3,1},{5,3},{7,5},{10,8},{12,10},{14,12},{11,9},... | collective-permute-start | bytes 1572872 | tf_op jit(solution)/shard_map/ppermute | solution.py:328
  92.8 32.4 %collective-permute-start.17 = (bf16[512,512]{1,0:T(8,128)(2,1)S(1)}, bf16[512,512]{1,0:T(8,128)(2,1)S(1)}, u32[]{:S(2)}, u32[]{:S(2)}) collective-permute-start(bf16[512,512]{1,0:T(8,128)(2,1)S(1)} %get-tuple-element.31), channel_id=1, source_target_pairs={{4,0},{6,2},{5,1},{7,3},{12,8},{14,10},{13,9},{15,11},{20,16},{22,... | collective-permute-start | bytes 1572872 | tf_op jit(solution)/shard_map/ppermute | solution.py:328
  94.2 3.7 %collective-permute-start.15 = (bf16[256,512]{1,0:T(8,128)(2,1)S(1)}, bf16[256,512]{1,0:T(8,128)(2,1)S(1)}, u32[]{:S(2)}, u32[]{:S(2)}) collective-permute-start(bf16[256,512]{1,0:T(8,128)(2,1)S(1)} %get-tuple-element.44), channel_id=1, source_target_pairs={{0,1},{1,0},{2,3},{3,2},{4,5},{5,4},{6,7},{7,6},{8,9},{9,8},{10,11... | collective-permute-start | bytes 786440 | tf_op jit(solution)/shard_map/ppermute | solution.py:252
  94.3 32.2 %collective-permute-start.16 = (bf16[512,512]{1,0:T(8,128)(2,1)S(1)}, bf16[512,512]{1,0:T(8,128)(2,1)S(1)}, u32[]{:S(2)}, u32[]{:S(2)}) collective-permute-start(bf16[512,512]{1,0:T(8,128)(2,1)S(1)} %get-tuple-element.30), channel_id=1, source_target_pairs={{6,0},{7,1},{14,8},{15,9},{22,16},{23,17},{30,24},{31,25}} | collective-permute-start | bytes 1572872 | tf_op jit(solution)/shard_map/ppermute | solution.py:328
  97.9 30.1 %collective-permute-start.22 = (bf16[576,512]{1,0:T(8,128)(2,1)S(1)}, bf16[576,512]{1,0:T(8,128)(2,1)S(1)}, u32[]{:S(2)}, u32[]{:S(2)}) collective-permute-start(bf16[576,512]{1,0:T(8,128)(2,1)S(1)} %get-tuple-element.36), channel_id=1, source_target_pairs={{0,24},{8,16},{16,8},{24,0},{1,25},{9,17},{17,9},{25,1},{2,26},{10... | collective-permute-start | bytes 1769480 | tf_op jit(solution)/shard_map/ppermute | solution.py:298
  106.3 21.7 %collective-permute-start.21 = (bf16[576,512]{1,0:T(8,128)(2,1)S(1)}, bf16[576,512]{1,0:T(8,128)(2,1)S(1)}, u32[]{:S(2)}, u32[]{:S(2)}) collective-permute-start(bf16[576,512]{1,0:T(8,128)(2,1)S(1)} %get-tuple-element.37), channel_id=1, source_target_pairs={{0,16},{8,24},{16,0},{24,8},{1,17},{9,25},{17,1},{25,9},{2,18},{10... | collective-permute-start | bytes 1769480 | tf_op jit(solution)/shard_map/ppermute | solution.py:298
  125.3 13.9 %collective-permute-start.20 = (bf16[576,512]{1,0:T(8,128)(2,1)S(1)}, bf16[576,512]{1,0:T(8,128)(2,1)S(1)}, u32[]{:S(2)}, u32[]{:S(2)}) collective-permute-start(bf16[576,512]{1,0:T(8,128)(2,1)S(1)} %get-tuple-element.35), channel_id=1, source_target_pairs={{0,8},{8,0},{16,24},{24,16},{1,9},{9,1},{17,25},{25,17},{2,10},{10... | collective-permute-start | bytes 1769480 | tf_op jit(solution)/shard_map/ppermute | solution.py:298
  126.5 44.4 %collective-permute-start.12 = (bf16[256,512]{1,0:T(8,128)(2,1)S(1)}, bf16[256,512]{1,0:T(8,128)(2,1)S(1)}, u32[]{:S(2)}, u32[]{:S(2)}) collective-permute-start(bf16[256,512]{1,0:T(8,128)(2,1)S(1)} %slice.74), channel_id=1, source_target_pairs={{0,1},{1,0},{2,3},{3,2},{4,5},{5,4},{6,7},{7,6},{8,9},{9,8},{10,11... | collective-permute-start | bytes 786440 | tf_op jit(solution)/shard_map/ppermute | solution.py:252
  139.6 18.4 %collective-permute-start.25 = (bf16[144,512]{1,0:T(8,128)(2,1)S(1)}, bf16[144,512]{1,0:T(8,128)(2,1)S(1)}, u32[]{:S(2)}, u32[]{:S(2)}) collective-permute-start(bf16[144,512]{1,0:T(8,128)(2,1)S(1)} %get-tuple-element.39), channel_id=1, source_target_pairs={{0,6},{2,0},{4,2},{6,4},{1,7},{3,1},{5,3},{7,5},{8,14},{10,8},{12,... | collective-permute-start | bytes 442376 | tf_op jit(solution)/shard_map/ppermute | solution.py:304
  155.7 9.6 %collective-permute-start.24 = (bf16[144,512]{1,0:T(8,128)(2,1)S(1)}, bf16[144,512]{1,0:T(8,128)(2,1)S(1)}, u32[]{:S(2)}, u32[]{:S(2)}) collective-permute-start(bf16[144,512]{1,0:T(8,128)(2,1)S(1)} %get-tuple-element.40), channel_id=1, source_target_pairs={{0,4},{2,6},{4,0},{6,2},{1,5},{3,7},{5,1},{7,3},{8,12},{10,14},{12... | collective-permute-start | bytes 442376 | tf_op jit(solution)/shard_map/ppermute | solution.py:304
  155.7 12.8 %collective-permute-start.23 = (bf16[144,512]{1,0:T(8,128)(2,1)S(1)}, bf16[144,512]{1,0:T(8,128)(2,1)S(1)}, u32[]{:S(2)}, u32[]{:S(2)}) collective-permute-start(bf16[144,512]{1,0:T(8,128)(2,1)S(1)} %get-tuple-element.38), channel_id=1, source_target_pairs={{0,2},{2,4},{4,6},{6,0},{1,3},{3,5},{5,7},{7,1},{8,10},{10,12},{12... | collective-permute-start | bytes 442376 | tf_op jit(solution)/shard_map/ppermute | solution.py:304
  158.1 11.1 %collective-permute-start.19 = (bf16[256,512]{1,0:T(8,128)(2,1)S(1)}, bf16[256,512]{1,0:T(8,128)(2,1)S(1)}, u32[]{:S(2)}, u32[]{:S(2)}) collective-permute-start(bf16[256,512]{1,0:T(8,128)(2,1)S(1)} %slice.91), channel_id=1, source_target_pairs={{0,1},{1,0},{2,3},{3,2},{4,5},{5,4},{6,7},{7,6},{8,9},{9,8},{10,11... | collective-permute-start | bytes 786440 | tf_op jit(solution)/shard_map/ppermute | solution.py:252
  168.6 1.6 collective-permute-start.26

commit v2 on v1

--- a/solution.py
+++ b/solution.py
@@ -239,17 +239,30 @@
     steps = tuple(range(prior + 1))
     low = core == 0
     info = jnp.stack([chip, core]).astype(jnp.int32)
+    together = lax.optimization_barrier
 
     def own(x):
-        half = x.shape[1] // 2
-        return jnp.where(low, x[:, :half], x[:, half:])
+        half = x.shape[-1] // 2
+        return jnp.where(low, x[..., :half], x[..., half:])
 
     def other(x):
-        half = x.shape[1] // 2
-        return jnp.where(low, x[:, half:], x[:, :half])
+        half = x.shape[-1] // 2
+        return jnp.where(low, x[..., half:], x[..., :half])
 
     def swap(x):
         return lax.ppermute(x, "core", [(0, 1), (1, 0)])
+
+    def up(x, k):
+        return lax.ppermute(x, "chip", [(i, i + k) for i in range(chips - k)])
+
+    def down(x, k):
+        return lax.ppermute(x, "chip", [(i + k, i) for i in range(chips - k)])
+
+    def round_chips(x, k):
+        return lax.ppermute(x, "chip", [(i, (i + k) % chips) for i in range(chips)])
+
+    def across(x, k):
+        return lax.ppermute(x, "dp", [(i, i ^ k) for i in range(rows_dp)])
 
     def in_order(mine, theirs, axis):
         return jnp.where(
@@ -258,81 +271,118 @@
             jnp.concatenate([theirs, mine], axis),
         )
 
-    block = in_order(own(out_weight), swap(other(out_weight)), 0)
-    part = block.shape[0]
-    if chips <= 4:
-        weight_z = jnp.zeros((chips * part, block.shape[1]), BF16)
-        weight_z = lax.dynamic_update_slice_in_dim(weight_z, block, chip * part, 0)
-        for k in range(1, chips):
-            got = lax.ppermute(block, "chip", [(i, (i + k) % chips) for i in range(chips)])
+    k0, v0, q0, g0 = key_rows[0], values[0], queries[0], out_grad[0]
+    near = chips <= 4
+    moved = [round_chips(out_weight, k) for k in range(1, chips)] if near else []
+    kv_theirs = swap(jnp.concatenate([other(k0), other(v0)], 1))
+    grad_theirs = swap(g0)
+    kv_theirs, grad_theirs, *moved = together((kv_theirs, grad_theirs, *moved))
+
+    kv = jnp.concatenate([own(k0), own(v0)], 1)
+    kv = jnp.concatenate([kv, kv_theirs], 0)
+    chunks = [kv] + [up(kv, k) for k in steps[1:3]]
+    piece = out_weight.shape[0]
+    part = 2 * piece
+    if near:
+        column = jnp.zeros((chips, *out_weight.shape), BF16)
+        column = lax.dynamic_update_index_in_dim(column, out_weight, chip, 0)
+        for k, got in enumerate(moved, 1):
             source = lax.rem(chip - k + chips, chips)
-            weight_z = lax.dynamic_update_slice_in_dim(weight_z, got, source * part, 0)
-    else:
-        weight_z = lax.all_gather(block, "chip", axis=0, tiled=True)
-    share = weight_z.shape[0]
-
-    k0, v0 = key_rows[0], values[0]
-    kv = jnp.concatenate([own(k0), own(v0)], 1)
-    kv = jnp.concatenate([kv, swap(jnp.concatenate([other(k0), other(v0)], 1))], 0)
-    chunks = [kv]
-    for k in steps[1:]:
-        chunks.append(lax.ppermute(kv, "chip", [(i, i + k) for i in range(chips - k)]))
-
-    q0 = queries[0]
-    q = jnp.concatenate([own(q0), swap(other(q0))], 0) * jnp.asarray(HD ** (-0.5), BF16)
-    grad = jnp.concatenate([out_grad[0], swap(out_grad[0])], 0)
-
-    weight = jnp.zeros((rows_dp * share, block.shape[1]), BF16)
-    weight = lax.dynamic_update_slice_in_dim(weight, weight_z, row * share, 0)
-    for k in range(1, rows_dp):
-        got = lax.ppermute(weight_z, "dp", [(i, i ^ k) for i in range(rows_dp)])
-        weight = lax.dynamic_update_slice_in_dim(weight, got, (row ^ k) * share, 0)
-
+            column = lax.dynamic_update_index_in_dim(column, got, source, 0)
+    else:
+        column = lax.all_gather(out_weight, "chip", axis=0)
+    column_theirs, q_theirs = together((swap(other(column)), swap(other(q0))))
+    ours = in_order(own(column)[:, None], column_theirs[:, None], 1)
+    ours = ours.reshape(chips * part, ours.shape[-1])
+    share = ours.shape[0]
+    half = share // 2
+
+    by_x, by_y, *chunks = together((across(ours, 1), across(ours, 2), *chunks))
+    for k in steps[3:]:
+        chunks.append(up(chunks[-1], 1))
+    diagonal = [across(by_y[:half], 1), across(by_x[half:], 2)]
+    weight = jnp.zeros((rows_dp * share, ours.shape[1]), BF16)
+    for got, at in (
+        (ours, row * share),
+        (by_x, (row ^ 1) * share),
+        (by_y, (row ^ 2) * share),
+        (diagonal[0], (row ^ 3) * share),
+        (diagonal[1], (row ^ 3) * share + half),
+    ):
+        weight = lax.dynamic_update_slice_in_dim(weight, got, at, 0)
+
+    q = jnp.concatenate([own(q0), q_theirs], 0) * jnp.asarray(HD ** (-0.5), BF16)
+    grad = jnp.concatenate([g0, grad_theirs], 0)
+    turned = grad.T
+    blocks = [
+        lax.dynamic_slice_in_dim(turned, (row ^ k) * share, share, 0) for k in range(rows_dp)
+    ]
     state = forward(info, q, chunks[:-1], steps[:-1], None, False)
+    da = dot(grad, weight).astype(BF16)
+    da, chunks[-1], *blocks = together((da, chunks[-1], *blocks))
     att, lse_t = forward(info, q, chunks[-1:], steps[-1:], state, True)
 
-    dw = dot(grad, att, TN)
-    mine = lax.dynamic_slice_in_dim(dw, row * share, share, 0)
-    for k in range(1, rows_dp):
-        sent = lax.dynamic_slice_in_dim(dw, (row ^ k) * share, share, 0).astype(BF16)
-        mine = mine + lax.ppermute(sent, "dp", [(i, i ^ k) for i in range(rows_dp)]).astype(F32)
-    if chips <= 4:
-        final = lax.dynamic_slice_in_dim(mine, chip * part, part, 0)
-        for k in range(1, chips):
-            target = lax.rem(chip + k, chips)
-            sent = lax.dynamic_slice_in_dim(mine, target * part, part, 0).astype(BF16)
-            got = lax.ppermute(sent, "chip", [(i, (i + k) % chips) for i in range(chips)])
-            final = final + got.astype(F32)
-    else:
-        final = lax.psum_scatter(mine, "chip", scatter_dimension=0, tiled=True)
-    total_tokens = rows_dp * chips * rows
-    final = final * (1.0 / math.sqrt(total_tokens))
-    top, bottom = final[: part // 2], final[part // 2 :]
-    weight_grad = in_order(jnp.where(low, top, bottom), swap(jnp.where(low, bottom, top)), 1)
-
-    da = dot(grad, weight).astype(BF16)
+    dw = [dot(b, att) for b in blocks]
+    far = dw[3].astype(BF16)
+    far, da = together((far, da))
+    from_x, from_y = across(far[:half], 1), across(far[half:], 2)
     carried = None
-    sums = {}
-    for step in reversed(steps):
+    terms = {}
+    order = [*range(prior, 2, -1), *([1, 2] if prior >= 2 else [1][:prior]), 0]
+    for step in order:
         last = step == 0
         res = backward(info, q, da, lse_t, [chunks[step]], (step,), att, carried, last)
-        sums[step] = res[0]
+        terms[step] = res[0]
         if carried is None:
             delta_t = res[1]
         if last:
             dq = res[1]
         else:
             carried = (delta_t, res[-1])
-    kv_grad = sums[0]
-    for k in reversed(steps[1:]):
-        got = lax.ppermute(sums[k], "chip", [(i + k, i) for i in range(chips - k)])
-        kv_grad = kv_grad + got.astype(F32)
-    kv_grad = kv_grad.astype(BF16)
-
-    weight_other = swap(weight)
-    layer_out = (dot(att[:tok], weight, NT) + dot(swap(att[tok:]), weight_other, NT)).astype(BF16)
-
-    query_grad = in_order(dq[:tok], swap(dq[tok:]), 1)
+    to_x = jnp.concatenate([dw[1][:half], dw[1][half:] + from_y.astype(F32)], 0).astype(BF16)
+    to_y = jnp.concatenate([dw[2][:half] + from_x.astype(F32), dw[2][half:]], 0).astype(BF16)
+    coming = [down(terms[1], 1), down(terms[prior], 1)] if prior >= 2 else []
+    by_x, by_y, dq_theirs, *coming = together(
+        (across(to_x, 1), across(to_y, 2), swap(dq[tok:]), *coming)
+    )
+    mine = dw[0] + by_x.astype(F32) + by_y.astype(F32)
+
+    kv_grad = terms[0]
+    if prior >= 2:
+        far_term = coming[1]
+        for k in range(prior - 1, 2, -1):
+            far_term = down((terms[k].astype(F32) + far_term.astype(F32)).astype(BF16), 1)
+        passing = terms[2]
+        if prior >= 3:
+            passing = (passing.astype(F32) + far_term.astype(F32)).astype(BF16)
+        kv_grad = kv_grad + coming[0].astype(F32)
+        coming = down(passing, 2)
+    else:
+        coming = down(terms[1], 1)
+    att, mine = together((att, mine))
+    partial = dot(att, weight, NT)
+    layer_theirs = swap(partial[tok:].astype(BF16))
+    if near:
+        final = lax.dynamic_slice_in_dim(mine, chip * part, part, 0)
+        got = []
+        for k in range(1, chips):
+            target = lax.rem(chip + k, chips)
+            sent = lax.dynamic_slice_in_dim(mine, target * part, part, 0).astype(BF16)
+            got.append(round_chips(sent, k))
+        coming, layer_theirs, *got = together((coming, layer_theirs, *got))
+        for x in got:
+            final = final + x.astype(F32)
+    else:
+        final = lax.psum_scatter(mine, "chip", scatter_dimension=0, tiled=True)
+    layer_out = (partial[:tok] + layer_theirs.astype(F32)).astype(BF16)
+    total_tokens = rows_dp * chips * rows
+    final = final * (1.0 / math.sqrt(total_tokens))
+    first_rows, last_rows = final[:piece], final[piece:]
+    weight_grad = in_order(
+        jnp.where(low, first_rows, last_rows), swap(jnp.where(low, last_rows, first_rows)), 1
+    )
+    kv_grad = (kv_grad + coming.astype(F32)).astype(BF16)
+    query_grad = in_order(dq[:tok], dq_theirs, 1)
     theirs = swap(kv_grad[tok:])
     key_grad = in_order(kv_grad[:tok, :HD], theirs[:, :HD], 1)
     value_grad = in_order(kv_grad[:tok, HD:], theirs[:, HD:], 1)

time: 176 us -> 170 us (0.966); the launches traced: 174 us -> 170 us
  starting transfers between devices: 50.1 us -> 39.2 us
  other arithmetic: 8.27 us -> 18.7 us
  matrix products: 8.03 us -> 4.82 us
    ppermute x18 -> x20, starting transfers between devices: 39.7 us -> 29.7 us  [the longest x6 11.7 us: round_chips(): return lax.ppermute(x, 'chip', [(i, (i + k) % chips) for i in range(chips)])]
    ppermute x18 -> x20, waiting for transfers between devices: 89.9 us -> 85.5 us  [the longest x6 42.8 us: round_chips(): return lax.ppermute(x, 'chip', [(i, (i + k) % chips) for i in range(chips)])]
    broadcast_in_dim x0 -> x2, other arithmetic: none -> 3.29 us  [the longest x1 3.25 us: on_device(): layer_out[None]]
    dot_general x4 -> x6, matrix products: 8.03 us -> 4.82 us  [dot(): return lax.dot_general(a, b, dims, preferred_element_type=F32)]
    ppermute x9 -> x8, waiting for transfers between devices: 1.33 us -> 4.36 us  [swap(): return lax.ppermute(x, 'core', [(0, 1), (1, 0)])]
    select_n x3 -> x4, other arithmetic: 2.62 us -> 4.95 us  [in_order(): jnp.where(low, jnp.concatenate([mine, theirs], axis), jnp.concatenate([th...]
    dynamic_slice x0 -> x1, other arithmetic: none -> 2.15 us  [on_device(): lax.dynamic_slice_in_dim(turned, (row ^ k) * share, share, 0)]
    convert_element_type x1 -> x2, other arithmetic: 0.28 us -> 2.18 us  [the longest x1 1.25 us: on_device(): kv_grad = (kv_grad + coming.astype(F32)).astype(BF16)]
  transfers between devices with their start and end apart: 27 -> 28, of which waited for: 12 -> 13; matrix products, arithmetic and copies ran while one was open for 8% -> 9% of each run, Pallas kernels for 8% -> 7%
where the time goes in v2:
time: 170 us
  waiting for transfers between devices  89.8 us (53%)
  starting transfers between devices  39.2 us (23%)
  other arithmetic  18.7 us (11%)
  Pallas kernels  13.3 us (8%)
  matrix products  4.82 us (3%)
  local copies, waits for them, and re-layouts  3.03 us (2%)
    ppermute x6, waiting for transfers between devices, round_chips(): return lax.ppermute(x, 'chip', [(i, (i + k) % chips) for i in range(chips)])  42.8 us
    ppermute x3, waiting for transfers between devices, up(): return lax.ppermute(x, 'chip', [(i, i + k) for i in range(chips - k)])  31.9 us
    ppermute x6, starting transfers between devices, round_chips(): return lax.ppermute(x, 'chip', [(i, (i + k) % chips) for i in range(chips)])  11.7 us
    ppermute x3, waiting for transfers between devices, down(): return lax.ppermute(x, 'chip', [(i + k, i) for i in range(chips - k)])  10.8 us
    ppermute x8, starting transfers between devices, swap(): return lax.ppermute(x, 'core', [(0, 1), (1, 0)])  9.47 us
    pallas_call x4, Pallas kernels, backward(): pl.pallas_call(functools.partial(backward_kernel, steps, rows, first, las...  6.77 us
    pallas_call x2, Pallas kernels, forward(): pl.pallas_call(functools.partial(forward_kernel, steps, rows, first, last...  6.5 us
    ppermute x3, starting transfers between devices, up(): return lax.ppermute(x, 'chip', [(i, i + k) for i in range(chips - k)])  6.5 us
  transfers between devices with their start and end apart: 28, of which 13 were waited for; matrix products, arithmetic and copies ran while one was open for 9% of the time, Pallas kernels for 7%

profile of v2, /device:TPU:9, one launch (start us, length us, event | category | flops | bytes accessed | tf_op | source)
XLA Modules:
  0.0 169.9 jit_solution(5627880789711419489)
XLA Ops:
  0.6 0.7 collective-permute-start.1
  1.4 1.0 broadcast_select_fusion.3
  2.4 1.0 broadcast_select_fusion.4
  3.5 1.3 collective-permute-start.2
  4.8 1.1 collective-permute-start.3
  5.9 1.4 collective-permute-start.4
  7.4 1.1 collective-permute-done.2
  8.5 8.6 %collective-permute-done.3 = bf16[72,1024]{1,0:T(8,128)(2,1)S(1)} collective-permute-done((bf16[72,1024]{1,0:T(8,128)(2,1)S(1)}, bf16[72,1024]{1,0:T(8,128)(2,1)S(1)}, u32[]{:S(2)}, u32[]{:S(2)}) %collective-permute-start.3) | collective-permute-done | bytes 147488 | tf_op jit(solution)/shard_map/ppermute | solution.py:262
  17.1 2.5 %collective-permute-done.4 = bf16[72,1024]{1,0:T(8,128)(2,1)S(1)} collective-permute-done((bf16[72,1024]{1,0:T(8,128)(2,1)S(1)}, bf16[72,1024]{1,0:T(8,128)(2,1)S(1)}, u32[]{:S(2)}, u32[]{:S(2)}) %collective-permute-start.4) | collective-permute-done | bytes 147488 | tf_op jit(solution)/shard_map/ppermute | solution.py:262
  19.7 0.6 copy-done.5
  20.4 0.6 collective-permute-start.5
  21.0 0.7 broadcast_select_fusion.2
  21.7 1.9 %collective-permute-done.6 = bf16[256,512]{1,0:T(8,128)(2,1)} collective-permute-done((bf16[256,512]{1,0:T(8,128)(2,1)}, bf16[256,512]{1,0:T(8,128)(2,1)}, u32[]{:S(2)}, u32[]{:S(2)}) %collective-permute-start.6) | collective-permute-done | bytes 262176 | tf_op jit(solution)/shard_map/ppermute | solution.py:253
  23.6 1.1 maximum_select_fusion
  24.7 1.3 collective-permute-start.7
  26.0 1.2 collective-permute-start.8
  27.2 1.0 pad_maximum_fusion.6.refs_0_
  28.2 1.9 %collective-permute-start.9 = (bf16[512,512]{1,0:T(8,128)(2,1)S(1)}, bf16[512,512]{1,0:T(8,128)(2,1)S(1)}, u32[]{:S(2)}, u32[]{:S(2)}) collective-permute-start(bf16[512,512]{1,0:T(8,128)(2,1)S(1)} %pad_maximum_fusion.6.refs_0_), channel_id=1, source_target_pairs={{0,2},{2,4},{4,6},{1,3},{3,5},{5,7},{8,10},{10,12},{12,14},{9,11},... | collective-permute-start | bytes 1572872 | tf_op jit(solution)/shard_map/ppermute | solution.py:256
  30.2 2.7 %collective-permute-start.10 = (bf16[512,512]{1,0:T(8,128)(2,1)S(1)}, bf16[512,512]{1,0:T(8,128)(2,1)S(1)}, u32[]{:S(2)}, u32[]{:S(2)}) collective-permute-start(bf16[512,512]{1,0:T(8,128)(2,1)S(1)} %pad_maximum_fusion.6.refs_0_), channel_id=1, source_target_pairs={{0,4},{2,6},{1,5},{3,7},{8,12},{10,14},{9,13},{11,15},{16,20},{18,... | collective-permute-start | bytes 1572872 | tf_op jit(solution)/shard_map/ppermute | solution.py:256
  32.9 2.1 %fusion.12 = (bf16[576,512]{0,1:T(8,128)(2,1)S(1)}, bf16[576,512]{0,1:T(8,128)(2,1)S(1)}, bf16[576,512]{0,1:T(8,128)(2,1)S(1)}, bf16[576,512]{0,1:T(8,128)(2,1)S(1)}) fusion(s32[]{:T(128)S(6)} %select_n.180, bf16[256,2304]{1,0:T(8,128)(2,1)S(1)} %bitcast.54, bf16[256,2304]{1,0:T(8,128)(2,1)S(1)} %collective-permute-done.1, s32[]{:T(128)S(6)} %select_n.175, ...), kind=kLoop, calls=%fused_computation.27 | loop fusion | flops 4718592 | bytes 4718608 | tf_op jit(solution)/shard_map/dynamic_slice | solution.py:318
  35.1 1.0 maximum_multiply_fusion.q
  36.3 6.6 %collective-permute-done.9.refs_1_.refs_0_ = bf16[512,512]{1,0:T(8,128)(2,1)S(1)} collective-permute-done((bf16[512,512]{1,0:T(8,128)(2,1)S(1)}, bf16[512,512]{1,0:T(8,128)(2,1)S(1)}, u32[]{:S(2)}, u32[]{:S(2)}) %collective-permute-start.9) | collective-permute-done | bytes 524320 | tf_op jit(solution)/shard_map/ppermute | solution.py:256
  42.9 20.6 %collective-permute-done.10.refs_2_.refs_0_ = bf16[512,512]{1,0:T(8,128)(2,1)S(1)} collective-permute-done((bf16[512,512]{1,0:T(8,128)(2,1)S(1)}, bf16[512,512]{1,0:T(8,128)(2,1)S(1)}, u32[]{:S(2)}, u32[]{:S(2)}) %collective-permute-start.10) | collective-permute-done | bytes 524320 | tf_op jit(solution)/shard_map/ppermute | solution.py:256
  63.5 0.3 collective-permute-start.11
  64.2 1.9 %collective-permute-start.13 = (bf16[512,512]{1,0:T(8,128)(2,1)S(1)}, bf16[512,512]{1,0:T(8,128)(2,1)S(1)}, u32[]{:S(2)}, u32[]{:S(2)}) collective-permute-start(bf16[512,512]{1,0:T(8,128)(2,1)S(1)} %collective-permute-done.10.refs_2_.refs_0_), channel_id=1, source_target_pairs={{0,2},{2,4},{4,6},{1,3},{3,5},{5,7},{8,10},{10,12},{12,14},{9,11},... | collective-permute-start | bytes 1572872 | tf_op jit(solution)/shard_map/ppermute | solution.py:256
  66.2 5.3 %attend_forward.2 = (f32[512,256]{1,0:T(8,128)S(1)}, f32[512,256]{1,0:T(8,128)S(1)}, f32[512,512]{1,0:T(8,128)S(1)}) custom-call(s32[2]{0:T(128)S(1)} %pad_add_fusion.info, bf16[512,512]{1,0:T(8,128)(2,1)S(1)} %maximum_multiply_fusion.q, bf16[512,512]{1,0:T(8,128)(2,1)S(1)} %pad_maximum_fusion.6.refs_0_, ...), custom_call_target="tpu_custom_call" | custom-call | flops 1610612736 | bytes 3145728 | tf_op jit(solution)/shard_map/attend_forward/pallas_call | solution.py:113
  71.6 1.4 fusion.3.da
  73.0 4.7 %collective-permute-done.13.refs_0_ = bf16[512,512]{1,0:T(8,128)(2,1)S(1)} collective-permute-done((bf16[512,512]{1,0:T(8,128)(2,1)S(1)}, bf16[512,512]{1,0:T(8,128)(2,1)S(1)}, u32[]{:S(2)}, u32[]{:S(2)}) %collective-permute-start.13) | collective-permute-done | bytes 524320 | tf_op jit(solution)/shard_map/ppermute | solution.py:256
  77.7 1.2 attend_forward.3
  78.9 0.5 fusion.17
  79.4 0.5 convolution_convert_fusion
  80.0 1.3 collective-permute-start.14
  81.3 0.5 fusion.18
  81.9 1.3 collective-permute-start.16
  83.1 0.9 attend_backward.4
  84.0 2.5 %attend_backward.5 = (bf16[512,512]{1,0:T(8,128)(2,1)S(1)}, f32[512,512]{1,0:T(8,128)S(1)}) custom-call(s32[2]{0:T(128)S(1)} %pad_add_fusion.info, bf16[512,512]{1,0:T(8,128)(2,1)S(1)} %maximum_multiply_fusion.q, bf16[512,512]{1,0:T(8,128)(2,1)S(1)} %fusion.3.da, f32[16,512]{1,0:T(8,128)S(1)} %get-tuple-element.75.lse_t, ...), custom_call_target="tpu_custom_call" | custom-call | flops 1342177280 | bytes 1572864 | tf_op jit(solution)/shard_map/attend_backward/pallas_call | solution.py:214
  86.5 1.9 %collective-permute-start.19 = (bf16[512,512]{1,0:T(8,128)(2,1)S(1)}, bf16[512,512]{1,0:T(8,128)(2,1)S(1)}, u32[]{:S(2)}, u32[]{:S(2)}) collective-permute-start(bf16[512,512]{1,0:T(8,128)(2,1)S(1)} %get-tuple-element.81), channel_id=1, source_target_pairs={{2,0},{4,2},{6,4},{3,1},{5,3},{7,5},{10,8},{12,10},{14,12},{11,9},... | collective-permute-start | bytes 1572872 | tf_op jit(solution)/shard_map/ppermute | solution.py:259
  88.5 1.9 %collective-permute-start.20 = (bf16[512,512]{1,0:T(8,128)(2,1)S(1)}, bf16[512,512]{1,0:T(8,128)(2,1)S(1)}, u32[]{:S(2)}, u32[]{:S(2)}) collective-permute-start(bf16[512,512]{1,0:T(8,128)(2,1)S(1)} %get-tuple-element.82), channel_id=1, source_target_pairs={{2,0},{4,2},{6,4},{3,1},{5,3},{7,5},{10,8},{12,10},{14,12},{11,9},... | collective-permute-start | bytes 1572872 | tf_op jit(solution)/shard_map/ppermute | solution.py:259
  90.4 0.9 attend_backward.6
  91.4 0.3 collective-permute-start.15
  92.2 2.5 %attend_backward.7 = (f32[512,512]{1,0:T(8,128)S(1)}, bf16[512,512]{1,0:T(8,128)(2,1)S(1)}) custom-call(s32[2]{0:T(128)S(1)} %pad_add_fusion.info, bf16[512,512]{1,0:T(8,128)(2,1)S(1)} %maximum_multiply_fusion.q, bf16[512,512]{1,0:T(8,128)(2,1)S(1)} %fusion.3.da, f32[16,512]{1,0:T(8,128)S(1)} %get-tuple-element.75.lse_t, ...), custom_call_target="tpu_custom_call" | custom-call | flops 1342177280 | bytes 1572864 | tf_op jit(solution)/shard_map/attend_backward/pallas_call | solution.py:214
  94.7 0.7 slice_bitcast_fusion
  95.4 3.9 %collective-permute-start.18 = (bf16[256,512]{1,0:T(8,128)(2,1)S(1)}, bf16[256,512]{1,0:T(8,128)(2,1)S(1)}, u32[]{:S(2)}, u32[]{:S(2)}) collective-permute-start(bf16[256,512]{1,0:T(8,128)(2,1)S(1)} %get-tuple-element.111), channel_id=1, source_target_pairs={{0,1},{1,0},{2,3},{3,2},{4,5},{5,4},{6,7},{7,6},{8,9},{9,8},{10,11... | collective-permute-start | bytes 786440 | tf_op jit(solution)/shard_map/ppermute | solution.py:253
  99.3 1.2 collective-permute-done.18
  100.5 10.8 %collective-permute-done.20 = bf16[512,512]{1,0:T(8,128)(2,1)S(1)} collective-permute-done((bf16[512,512]{1,0:T(8,128)(2,1)S(1)}, bf16[512,512]{1,0:T(8,128)(2,1)S(1)}, u32[]{:S(2)}, u32[]{:S(2)}) %collective-permute-start.20) | collective-permute-done | bytes 524320 | tf_op jit(solution)/shard_map/ppermute | solution.py:259
  111.2 0.5 fusion.2
  111.8 1.4 fusion.19
  113.3 3.6 %collective-permute-start.22 = (bf16[256,2304]{1,0:T(8,128)(2,1)S(1)}, bf16[256,2304]{1,0:T(8,128)(2,1)}, u32[]{:S(2)}, u32[]{:S(2)}) collective-permute-start(bf16[256,2304]{1,0:T(8,128)(2,1)S(1)} %slice.179), channel_id=1, source_target_pairs={{0,1},{1,0},{2,3},{3,2},{4,5},{5,4},{6,7},{7,6},{8,9},{9,8},{10,11... | collective-permute-start | bytes 3538952 | tf_op jit(solution)/shard_map/ppermute | solution.py:253
  116.9 0.9 add_convert_fusion.1
  117.8 1.3 collective-permute-start.21
  119.1 0.8 dynamic-slice_convert_fusion
  120.0 6.7 %collective-permute-start.23 = (bf16[144,512]{1,0:T(8,128)(2,1)}, bf16[144,512]{1,0:T(8,128)(2,1)S(1)}, u32[]{:S(2)}, u32[]{:S(2)}) collective-permute-start(bf16[144,512]{1,0:T(8,128)(2,1)} %get-tuple-element.103), channel_id=1, source_target_pairs={{0,2},{2,4},{4,6},{6,0},{1,3},{3,5},{5,7},{7,1},{8,10},{10,12},{12... | collective-permute-start | bytes 442376 | tf_op jit(solution)/shard_map/ppermute | solution.py:262
  126.7 1.2 collective-permute-start.25
  127.9 2.2 %maximum_select_fusion.1 = bf16[1,256,1024]{2,1,0:T(8,128)(2,1)} fusion(bf16[1,256,512]{2,1,0:T(8,128)(2,1)} %bitcast.59, bf16[1,256,512]{2,1,0:T(8,128)(2,1)} %get-tuple-element.110, pred[]{:T(512)S(6)} %eq.3), kind=kLoop, calls=%fused_computation.39 | loop fusion | flops 2359296 | bytes 1048577 | tf_op jit(solution)/shard_map/jit(_where)/select_n | solution.py:268
  130.0 5.9 %collective-permute-done.23 = bf16[144,512]{1,0:T(8,128)(2,1)S(1)} collective-permute-done((bf16[144,512]{1,0:T(8,128)(2,1)}, bf16[144,512]{1,0:T(8,128)(2,1)S(1)}, u32[]{:S(2)}, u32[]{:S(2)}) %collective-permute-start.23) | collective-permute-done | bytes 147488 | tf_op jit(solution)/shard_map/ppermute | solution.py:262
  135.9 5.8 %collective-permute-done.24 = bf16[144,512]{1,0:T(8,128)(2,1)} collective-permute-done((bf16[144,512]{1,0:T(8,128)(2,1)}, bf16[144,512]{1,0:T(8,128)(2,1)}, u32[]{:S(2)}, u32[]{:S(2)}) %collective-permute-start.24) | collective-permute-done | bytes 147488 | tf_op jit(solution)/shard_map/ppermute | solution.py:262
  141.8 18.8 %collective-permute-done.25 = bf16[144,512]{1,0:T(8,128)(2,1)} collective-permute-done((bf16[144,512]{1,0:T(8,128)(2,1)}, bf16[144,512]{1,0:T(8,128)(2,1)}, u32[]{:S(2)}, u32[]{:S(2)}) %collective-permute-start.25) | collective-permute-done | bytes 147488 | tf_op jit(solution)/shard_map/ppermute | solution.py:262
  160.6 3.2 %fusion.4 = bf16[1,256,2304]{2,1,0:T(8,128)(2,1)} fusion(bf16[256,2304]{1,0:T(8,128)(2,1)} %collective-permute-done.22, f32[512,2304]{1,0:T(8,128)} %copy-done), kind=kLoop, calls=%fused_computation.17 | loop fusion | flops 1769472 | bytes 4718592 | tf_op jit(solution)/shard_map/broadcast_in_dim | solution.py:390
  163.9 1.3 add_convert_fusion
  165.2 0.6 collective-permute-start.26
  165.7 1.1 add_multiply_fusion
  166.9 1.3 collective-permute-done.27
  168.2 0.7 maximum_select_fusion.2
  169.0 0.9 maximum_select_fusion.3
  (64 shorter events, 2.1 us)
Async XLA Ops:
  0.6 2.9 %copy-start.7 = (bf16[72,1024]{1,0:T(8,128)(2,1)S(1)}, bf16[72,1024]{1,0:T(8,128)(2,1)}, u32[]{:S(2)}) copy-start(bf16[72,1024]{1,0:T(8,128)(2,1)} %param.8) | copy-start | bytes 442372
  0.6 19.0 %collective-permute-start.1 = (bf16[256,2304]{1,0:T(8,128)(2,1)}, bf16[256,2304]{1,0:T(8,128)(2,1)S(1)}, u32[]{:S(2)}, u32[]{:S(2)}) collective-permute-start(bf16[256,2304]{1,0:T(8,128)(2,1)} %bitcast.53), channel_id=1, source_target_pairs={{0,1},{1,0},{2,3},{3,2},{4,5},{5,4},{6,7},{7,6},{8,9},{9,8},{10,11... | collective-permute-start | bytes 3538952 | tf_op jit(solution)/shard_map/ppermute | solution.py:253
  3.4 16.2 %collective-permute-start = (bf16[256,512]{1,0:T(8,128)(2,1)S(1)}, bf16[256,512]{1,0:T(8,128)(2,1)S(1)}, u32[]{:S(2)}, u32[]{:S(2)}) collective-permute-start(bf16[256,512]{1,0:T(8,128)(2,1)S(1)} %pad_maximum_fusion.7), channel_id=1, source_target_pairs={{0,1},{1,0},{2,3},{3,2},{4,5},{5,4},{6,7},{7,6},{8,9},{9,8},{10,11... | collective-permute-start | bytes 786440 | tf_op jit(solution)/shard_map/ppermute | solution.py:253
  3.5 5.0 %collective-permute-start.2 = (bf16[72,1024]{1,0:T(8,128)(2,1)S(1)}, bf16[72,1024]{1,0:T(8,128)(2,1)S(1)}, u32[]{:S(2)}, u32[]{:S(2)}) collective-permute-start(bf16[72,1024]{1,0:T(8,128)(2,1)S(1)} %copy-done.7), channel_id=1, source_target_pairs={{0,2},{2,4},{4,6},{6,0},{1,3},{3,5},{5,7},{7,1},{8,10},{10,12},{12... | collective-permute-start | bytes 442376 | tf_op jit(solution)/shard_map/ppermute | solution.py:262
  4.8 12.3 %collective-permute-start.3 = (bf16[72,1024]{1,0:T(8,128)(2,1)S(1)}, bf16[72,1024]{1,0:T(8,128)(2,1)S(1)}, u32[]{:S(2)}, u32[]{:S(2)}) collective-permute-start(bf16[72,1024]{1,0:T(8,128)(2,1)S(1)} %copy-done.7), channel_id=1, source_target_pairs={{0,4},{2,6},{4,0},{6,2},{1,5},{3,7},{5,1},{7,3},{8,12},{10,14},{12... | collective-permute-start | bytes 442376 | tf_op jit(solution)/shard_map/ppermute | solution.py:262
  5.9 13.7 %collective-permute-start.4 = (bf16[72,1024]{1,0:T(8,128)(2,1)S(1)}, bf16[72,1024]{1,0:T(8,128)(2,1)S(1)}, u32[]{:S(2)}, u32[]{:S(2)}) collective-permute-start(bf16[72,1024]{1,0:T(8,128)(2,1)S(1)} %copy-done.7), channel_id=1, source_target_pairs={{0,6},{2,0},{4,2},{6,4},{1,7},{3,1},{5,3},{7,5},{8,14},{10,8},{12,... | collective-permute-start | bytes 442376 | tf_op jit(solution)/shard_map/ppermute | solution.py:262
  7.4 13.6 %copy-start.4 = (bf16[1,256,1024]{2,1,0:T(8,128)(2,1)S(1)}, bf16[1,256,1024]{2,1,0:T(8,128)(2,1)}, u32[]{:S(2)}) copy-start(bf16[1,256,1024]{2,1,0:T(8,128)(2,1)} %param.5) | copy-start | bytes 1572868
  19.6 0.7 copy-start.5
  20.4 3.2 %collective-permute-start.5 = (bf16[4,72,512]{2,1,0:T(8,128)(2,1)S(1)}, bf16[4,72,512]{2,1,0:T(8,128)(2,1)}, u32[]{:S(2)}, u32[]{:S(2)}) collective-permute-start(bf16[4,72,512]{2,1,0:T(8,128)(2,1)S(1)} %get-tuple-element.107), channel_id=1, source_target_pairs={{0,1},{1,0},{2,3},{3,2},{4,5},{5,4},{6,7},{7,6},{8,9},{9,8},{10,11... | collective-permute-start | bytes 884744 | tf_op jit(solution)/shard_map/ppermute | solution.py:253
  21.7 11.2 %copy-start.1 = (bf16[1,256,2304]{2,1,0:T(8,128)(2,1)S(1)}, bf16[1,256,2304]{2,1,0:T(8,128)(2,1)}, u32[]{:S(2)}) copy-start(bf16[1,256,2304]{2,1,0:T(8,128)(2,1)} %param.9) | copy-start | bytes 3538948
  21.7 1.9 %collective-permute-start.6 = (bf16[256,512]{1,0:T(8,128)(2,1)}, bf16[256,512]{1,0:T(8,128)(2,1)}, u32[]{:S(2)}, u32[]{:S(2)}) collective-permute-start(bf16[256,512]{1,0:T(8,128)(2,1)} %get-tuple-element.113), channel_id=1, source_target_pairs={{0,1},{1,0},{2,3},{3,2},{4,5},{5,4},{6,7},{7,6},{8,9},{9,8},{10,11... | collective-permute-start | bytes 786440 | tf_op jit(solution)/shard_map/ppermute | solution.py:253
  24.7 38.8 %collective-permute-start.7 = (bf16[576,512]{1,0:T(8,128)(2,1)S(1)}, bf16[576,512]{1,0:T(8,128)(2,1)S(1)}, u32[]{:S(2)}, u32[]{:S(2)}) collective-permute-start(bf16[576,512]{1,0:T(8,128)(2,1)S(1)} %bitcast.50), channel_id=1, source_target_pairs={{0,8},{8,0},{16,24},{24,16},{1,9},{9,1},{17,25},{25,17},{2,10},{10... | collective-permute-start | bytes 1769480 | tf_op jit(solution)/shard_map/ppermute | solution.py:265
  26.0 37.5 %collective-permute-start.8 = (bf16[576,512]{1,0:T(8,128)(2,1)S(1)}, bf16[576,512]{1,0:T(8,128)(2,1)S(1)}, u32[]{:S(2)}, u32[]{:S(2)}) collective-permute-start(bf16[576,512]{1,0:T(8,128)(2,1)S(1)} %bitcast.51), channel_id=1, source_target_pairs={{0,16},{8,24},{16,0},{24,8},{1,17},{9,25},{17,1},{25,9},{2,18},{10... | collective-permute-start | bytes 1769480 | tf_op jit(solution)/shard_map/ppermute | solution.py:265
  28.2 14.6 %collective-permute-start.9 = (bf16[512,512]{1,0:T(8,128)(2,1)S(1)}, bf16[512,512]{1,0:T(8,128)(2,1)S(1)}, u32[]{:S(2)}, u32[]{:S(2)}) collective-permute-start(bf16[512,512]{1,0:T(8,128)(2,1)S(1)} %pad_maximum_fusion.6.refs_0_), channel_id=1, source_target_pairs={{0,2},{2,4},{4,6},{1,3},{3,5},{5,7},{8,10},{10,12},{12,14},{9,11},... | collective-permute-start | bytes 1572872 | tf_op jit(solution)/shard_map/ppermute | solution.py:256
  30.2 33.3 %collective-permute-start.10 = (bf16[512,512]{1,0:T(8,128)(2,1)S(1)}, bf16[512,512]{1,0:T(8,128)(2,1)S(1)}, u32[]{:S(2)}, u32[]{:S(2)}) collective-permute-start(bf16[512,512]{1,0:T(8,128)(2,1)S(1)} %pad_maximum_fusion.6.refs_0_), channel_id=1, source_target_pairs={{0,4},{2,6},{1,5},{3,7},{8,12},{10,14},{9,13},{11,15},{16,20},{18,... | collective-permute-start | bytes 1572872 | tf_op jit(solution)/shard_map/ppermute | solution.py:256
  63.5 8.0 %collective-permute-start.11 = (bf16[288,512]{1,0:T(8,128)(2,1)S(1)}, bf16[288,512]{1,0:T(8,128)(2,1)S(1)}, u32[]{:S(2)}, u32[]{:S(2)}) collective-permute-start(bf16[288,512]{1,0:T(8,128)(2,1)S(1)} %slice.100), channel_id=1, source_target_pairs={{0,8},{8,0},{16,24},{24,16},{1,9},{9,1},{17,25},{25,17},{2,10},{10... | collective-permute-start | bytes 884744 | tf_op jit(solution)/shard_map/ppermute | solution.py:265
  63.9 7.6 %collective-permute-start.12 = (bf16[288,512]{1,0:T(8,128)(2,1)S(1)}, bf16[288,512]{1,0:T(8,128)(2,1)S(1)}, u32[]{:S(2)}, u32[]{:S(2)}) collective-permute-start(bf16[288,512]{1,0:T(8,128)(2,1)S(1)} %slice.101), channel_id=1, source_target_pairs={{0,16},{8,24},{16,0},{24,8},{1,17},{9,25},{17,1},{25,9},{2,18},{10... | collective-permute-start | bytes 884744 | tf_op jit(solution)/shard_map/ppermute | solution.py:265
  64.2 13.5 %collective-permute-start.13 = (bf16[512,512]{1,0:T(8,128)(2,1)S(1)}, bf16[512,512]{1,0:T(8,128)(2,1)S(1)}, u32[]{:S(2)}, u32[]{:S(2)}) collective-permute-start(bf16[512,512]{1,0:T(8,128)(2,1)S(1)} %collective-permute-done.10.refs_2_.refs_0_), channel_id=1, source_target_pairs={{0,2},{2,4},{4,6},{1,3},{3,5},{5,7},{8,10},{10,12},{12,14},{9,11},... | collective-permute-start | bytes 1572872 | tf_op jit(solution)/shard_map/ppermute | solution.py:256
  80.0 11.3 %collective-permute-start.14 = (bf16[288,512]{1,0:T(8,128)(2,1)S(1)}, bf16[288,512]{1,0:T(8,128)(2,1)S(1)}, u32[]{:S(2)}, u32[]{:S(2)}) collective-permute-start(bf16[288,512]{1,0:T(8,128)(2,1)S(1)} %get-tuple-element.105), channel_id=1, source_target_pairs={{0,16},{8,24},{16,0},{24,8},{1,17},{9,25},{17,1},{25,9},{2,18},{10... | collective-permute-start | bytes 884744 | tf_op jit(solution)/shard_map/ppermute | solution.py:265
  81.9 9.9 %collective-permute-start.16 = (bf16[288,512]{1,0:T(8,128)(2,1)S(1)}, bf16[288,512]{1,0:T(8,128)(2,1)S(1)}, u32[]{:S(2)}, u32[]{:S(2)}) collective-permute-start(bf16[288,512]{1,0:T(8,128)(2,1)S(1)} %get-tuple-element.104), channel_id=1, source_target_pairs={{0,8},{8,0},{16,24},{24,16},{1,9},{9,1},{17,25},{25,17},{2,10},{10... | collective-permute-start | bytes 884744 | tf_op jit(solution)/shard_map/ppermute | solution.py:265
  86.5 13.9 %collective-permute-start.19 = (bf16[512,512]{1,0:T(8,128)(2,1)S(1)}, bf16[512,512]{1,0:T(8,128)(2,1)S(1)}, u32[]{:S(2)}, u32[]{:S(2)}) collective-permute-start(bf16[512,512]{1,0:T(8,128)(2,1)S(1)} %get-tuple-element.81), channel_id=1, source_target_pairs={{2,0},{4,2},{6,4},{3,1},{5,3},{7,5},{10,8},{12,10},{14,12},{11,9},... | collective-permute-start | bytes 1572872 | tf_op jit(solution)/shard_map/ppermute | solution.py:259
  88.5 22.8 %collective-permute-start.20 = (bf16[512,512]{1,0:T(8,128)(2,1)S(1)}, bf16[512,512]{1,0:T(8,128)(2,1)S(1)}, u32[]{:S(2)}, u32[]{:S(2)}) collective-permute-start(bf16[512,512]{1,0:T(8,128)(2,1)S(1)} %get-tuple-element.82), channel_id=1, source_target_pairs={{2,0},{4,2},{6,4},{3,1},{5,3},{7,5},{10,8},{12,10},{14,12},{11,9},... | collective-permute-start | bytes 1572872 | tf_op jit(solution)/shard_map/ppermute | solution.py:259
  91.4 19.8 %collective-permute-start.15 = (bf16[576,512]{1,0:T(8,128)(2,1)S(1)}, bf16[576,512]{1,0:T(8,128)(2,1)S(1)}, u32[]{:S(2)}, u32[]{:S(2)}) collective-permute-start(bf16[576,512]{1,0:T(8,128)(2,1)S(1)} %pad_maximum_fusion.4), channel_id=1, source_target_pairs={{0,8},{8,0},{16,24},{24,16},{1,9},{9,1},{17,25},{25,17},{2,10},{10... | collective-permute-start | bytes 1769480 | tf_op jit(solution)/shard_map/ppermute | solution.py:265
  91.9 19.4 %collective-permute-start.17 = (bf16[576,512]{1,0:T(8,128)(2,1)S(1)}, bf16[576,512]{1,0:T(8,128)(2,1)S(1)}, u32[]{:S(2)}, u32[]{:S(2)}) collective-permute-start(bf16[576,512]{1,0:T(8,128)(2,1)S(1)} %pad_maximum_fusion.5), channel_id=1, source_target_pairs={{0,16},{8,24},{16,0},{24,8},{1,17},{9,25},{17,1},{25,9},{2,18},{10... | collective-permute-start | bytes 1769480 | tf_op jit(solution)/shard_map/ppermute | solution.py:265
  95.4 5.0 %collective-permute-start.18 = (bf16[256,512]{1,0:T(8,128)(2,1)S(1)}, bf16[256,512]{1,0:T(8,128)(2,1)S(1)}, u32[]{:S(2)}, u32[]{:S(2)}) collective-permute-start(bf16[256,512]{1,0:T(8,128)(2,1)S(1)} %get-tuple-element.111), channel_id=1, source_target_pairs={{0,1},{1,0},{2,3},{3,2},{4,5},{5,4},{6,7},{7,6},{8,9},{9,8},{10,11... | collective-permute-start | bytes 786440 | tf_op jit(solution)/shard_map/ppermute | solution.py:253
  100.5 11.3 %copy-start.6 = (bf16[256,512]{1,0:T(8,128)(2,1)}, bf16[256,512]{1,0:T(8,128)(2,1)S(1)}, u32[]{:S(2)}) copy-start(bf16[256,512]{1,0:T(8,128)(2,1)S(1)} %collective-permute-done.18) | copy-start | bytes 786436
  100.5 11.3 %copy-start.2 = (bf16[512,512]{1,0:T(8,128)(2,1)}, bf16[512,512]{1,0:T(8,128)(2,1)S(1)}, u32[]{:S(2)}) copy-start(bf16[512,512]{1,0:T(8,128)(2,1)S(1)} %collective-permute-done.19) | copy-start | bytes 1572868
  113.2 4.6 %copy-start = (f32[512,2304]{1,0:T(8,128)}, f32[512,2304]{1,0:T(8,128)S(1)}, u32[]{:S(2)}) copy-start(f32[512,2304]{1,0:T(8,128)S(1)} %fusion.19) | copy-start | bytes 14155780
  113.3 47.3 %collective-permute-start.22 = (bf16[256,2304]{1,0:T(8,128)(2,1)S(1)}, bf16[256,2304]{1,0:T(8,128)(2,1)}, u32[]{:S(2)}, u32[]{:S(2)}) collective-permute-start(bf16[256,2304]{1,0:T(8,128)(2,1)S(1)} %slice.179), channel_id=1, source_target_pairs={{0,1},{1,0},{2,3},{3,2},{4,5},{5,4},{6,7},{7,6},{8,9},{9,8},{10,11... | collective-permute-start | bytes 3538952 | tf_op jit(solution)/shard_map/ppermute | solution.py:253
  117.8 42.8 %collective-permute-start.21 = (bf16[512,512]{1,0:T(8,128)(2,1)}, bf16[512,512]{1,0:T(8,128)(2,1)}, u32[]{:S(2)}, u32[]{:S(2)}) collective-permute-start(bf16[512,512]{1,0:T(8,128)(2,1)} %add_convert_fusion.1), channel_id=1, source_target_pairs={{4,0},{6,2},{5,1},{7,3},{12,8},{14,10},{13,9},{15,11},{20,16},{22,... | collective-permute-start | bytes 1572872 | tf_op jit(solution)/shard_map/ppermute | solution.py:259
  120.0 16.0 %collective-permute-start.23 = (bf16[144,512]{1,0:T(8,128)(2,1)}, bf16[144,512]{1,0:T(8,128)(2,1)S(1)}, u32[]{:S(2)}, u32[]{:S(2)}) collective-permute-start(bf16[144,512]{1,0:T(8,128)(2,1)} %get-tuple-element.103), channel_id=1, source_target_pairs={{0,2},{2,4},{4,6},{6,0},{1,3},{3,5},{5,7},{7,1},{8,10},{10,12},{12... | collective-permute-start | bytes 442376 | tf_op jit(solution)/shard_map/ppermute | solution.py:262
  126.7 15.1 %collective-permute-start.24 = (bf16[144,512]{1,0:T(8,128)(2,1)}, bf16[144,512]{1,0:T(8,128)(2,1)}, u32[]{:S(2)}, u32[]{:S(2)}) collective-permute-start(bf16[144,512]{1,0:T(8,128)(2,1)} %get-tuple-element.102), channel_id=1, source_target_pairs={{0,4},{2,6},{4,0},{6,2},{1,5},{3,7},{5,1},{7,3},{8,12},{10,14},{12... | collective-permute-start | bytes 442376 | tf_op jit(solution)/shard_map/ppermute | solution.py:262
  126.7 33.9 %collective-permute-start.25 = (bf16[144,512]{1,0:T(8,128)(2,1)}, bf16[144,512]{1,0:T(8,128)(2,1)}, u32[]{:S(2)}, u32[]{:S(2)}) collective-permute-start(bf16[144,512]{1,0:T(8,128)(2,1)} %get-tuple-element.101), channel_id=1, source_target_pairs={{0,6},{2,0},{4,2},{6,4},{1,7},{3,1},{5,3},{7,5},{8,14},{10,8},{12,... | collective-permute-start | bytes 442376 | tf_op jit(solution)/shard_map/ppermute | solution.py:262
  130.0 33.8 %copy-start.3 = (bf16[512,512]{1,0:T(8,128)(2,1)S(1)}, bf16[512,512]{1,0:T(8,128)(2,1)}, u32[]{:S(2)}) copy-start(bf16[512,512]{1,0:T(8,128)(2,1)} %copy-done.2) | copy-start | bytes 1572868
  165.2 3.8 %collective-permute-start.26 = (bf16[256,512]{1,0:T(8,128)(2,1)S(1)}, bf16[256,512]{1,0:T(8,128)(2,1)S(1)}, u32[]{:S(2)}, u32[]{:S(2)}) collective-permute-start(bf16[256,512]{1,0:T(8,128)(2,1)S(1)} %slice.134), channel_id=1, source_target_pairs={{0,1},{1,0},{2,3},{3,2},{4,5},{5,4},{6,7},{7,6},{8,9},{9,8},{10,11... | collective-permute-start | bytes 786440 | tf_op jit(solution)/shard_map/ppermute | solution.py:253
  166.8 1.4 collective-permute-start.27

commit v3 on v2

--- a/solution.py
+++ b/solution.py
@@ -275,12 +275,12 @@
     near = chips <= 4
     moved = [round_chips(out_weight, k) for k in range(1, chips)] if near else []
     kv_theirs = swap(jnp.concatenate([other(k0), other(v0)], 1))
-    grad_theirs = swap(g0)
-    kv_theirs, grad_theirs, *moved = together((kv_theirs, grad_theirs, *moved))
-
     kv = jnp.concatenate([own(k0), own(v0)], 1)
     kv = jnp.concatenate([kv, kv_theirs], 0)
-    chunks = [kv] + [up(kv, k) for k in steps[1:3]]
+    hop = up(kv, 1)
+    hop, grad_theirs, *moved = together((hop, swap(g0), *moved))
+    chunks = [kv, hop]
+
     piece = out_weight.shape[0]
     part = 2 * piece
     if near:
@@ -297,10 +297,13 @@
     share = ours.shape[0]
     half = share // 2
 
-    by_x, by_y, *chunks = together((across(ours, 1), across(ours, 2), *chunks))
-    for k in steps[3:]:
+    by_x, by_y, hop = together((across(ours, 1), across(ours, 2), up(hop, 1)))
+    chunks.append(hop)
+    diagonal = [across(by_y[:half], 1), across(by_x[half:], 2)]
+    diagonal[0], diagonal[1], hop = together((*diagonal, up(hop, 1)))
+    chunks.append(hop)
+    for _ in steps[4:]:
         chunks.append(up(chunks[-1], 1))
-    diagonal = [across(by_y[:half], 1), across(by_x[half:], 2)]
     weight = jnp.zeros((rows_dp * share, ours.shape[1]), BF16)
     for got, at in (
         (ours, row * share),
@@ -317,10 +320,11 @@
     blocks = [
         lax.dynamic_slice_in_dim(turned, (row ^ k) * share, share, 0) for k in range(rows_dp)
     ]
-    state = forward(info, q, chunks[:-1], steps[:-1], None, False)
+    state = None
+    for step in steps:
+        state = forward(info, q, chunks[step : step + 1], (step,), state, step == prior)
+    att, lse_t = state
     da = dot(grad, weight).astype(BF16)
-    da, chunks[-1], *blocks = together((da, chunks[-1], *blocks))
-    att, lse_t = forward(info, q, chunks[-1:], steps[-1:], state, True)
 
     dw = [dot(b, att) for b in blocks]
     far = dw[3].astype(BF16)
@@ -328,8 +332,7 @@
     from_x, from_y = across(far[:half], 1), across(far[half:], 2)
     carried = None
     terms = {}
-    order = [*range(prior, 2, -1), *([1, 2] if prior >= 2 else [1][:prior]), 0]
-    for step in order:
+    for step in reversed(steps):
         last = step == 0
         res = backward(info, q, da, lse_t, [chunks[step]], (step,), att, carried, last)
         terms[step] = res[0]
@@ -339,26 +342,21 @@
             dq = res[1]
         else:
             carried = (delta_t, res[-1])
+
+    passing = terms[prior]
+    for step in range(prior - 1, 2, -1):
+        passing = (terms[step].astype(F32) + down(passing, 1).astype(F32)).astype(BF16)
+    from_x, from_y, got = together((from_x, from_y, down(passing, 1)))
+    passing = (terms[2].astype(F32) + got.astype(F32)).astype(BF16)
     to_x = jnp.concatenate([dw[1][:half], dw[1][half:] + from_y.astype(F32)], 0).astype(BF16)
     to_y = jnp.concatenate([dw[2][:half] + from_x.astype(F32), dw[2][half:]], 0).astype(BF16)
-    coming = [down(terms[1], 1), down(terms[prior], 1)] if prior >= 2 else []
-    by_x, by_y, dq_theirs, *coming = together(
-        (across(to_x, 1), across(to_y, 2), swap(dq[tok:]), *coming)
+    by_x, by_y, dq_theirs, got = together(
+        (across(to_x, 1), across(to_y, 2), swap(dq[tok:]), down(passing, 1))
     )
     mine = dw[0] + by_x.astype(F32) + by_y.astype(F32)
 
-    kv_grad = terms[0]
-    if prior >= 2:
-        far_term = coming[1]
-        for k in range(prior - 1, 2, -1):
-            far_term = down((terms[k].astype(F32) + far_term.astype(F32)).astype(BF16), 1)
-        passing = terms[2]
-        if prior >= 3:
-            passing = (passing.astype(F32) + far_term.astype(F32)).astype(BF16)
-        kv_grad = kv_grad + coming[0].astype(F32)
-        coming = down(passing, 2)
-    else:
-        coming = down(terms[1], 1)
+    passing = (terms[1].astype(F32) + got.astype(F32)).astype(BF16)
+    coming = down(passing, 1)
     att, mine = together((att, mine))
     partial = dot(att, weight, NT)
     layer_theirs = swap(partial[tok:].astype(BF16))
@@ -381,7 +379,7 @@
     weight_grad = in_order(
         jnp.where(low, first_rows, last_rows), swap(jnp.where(low, last_rows, first_rows)), 1
     )
-    kv_grad = (kv_grad + coming.astype(F32)).astype(BF16)
+    kv_grad = (terms[0] + coming.astype(F32)).astype(BF16)
     query_grad = in_order(dq[:tok], dq_theirs, 1)
     theirs = swap(kv_grad[tok:])
     key_grad = in_order(kv_grad[:tok, :HD], theirs[:, :HD], 1)

time: 170 us -> 153 us (0.900)
  waiting for transfers between devices: 89.8 us -> 65.5 us
  starting transfers between devices: 39.2 us -> 43.6 us
  other arithmetic: 18.7 us -> 14.4 us
  local copies, waits for them, and re-layouts: 3.03 us -> 6.5 us
    ppermute x3, waiting for transfers between devices: 31.9 us -> 11.5 us  [up(): return lax.ppermute(x, 'chip', [(i, i + k) for i in range(chips - k)])]
    ppermute x8, waiting for transfers between devices: 0.02 us -> 5.04 us  [across(): return lax.ppermute(x, 'dp', [(i, i ^ k) for i in range(rows_dp)])]
    ppermute x6, waiting for transfers between devices: 42.8 us -> 38.6 us  [round_chips(): return lax.ppermute(x, 'chip', [(i, (i + k) % chips) for i in range(chips)])]
    ppermute x3, waiting for transfers between devices: 10.8 us -> 6.99 us  [down(): return lax.ppermute(x, 'chip', [(i + k, i) for i in range(chips - k)])]
    ppermute x8, starting transfers between devices: 9.47 us -> 11.8 us  [swap(): return lax.ppermute(x, 'core', [(0, 1), (1, 0)])]
    dynamic_slice x1 -> x0, other arithmetic: 2.15 us -> none  [on_device(): lax.dynamic_slice_in_dim(turned, (row ^ k) * share, share, 0)]
    dynamic_update_slice x5, local copies, waits for them, and re-layouts: 0.18 us -> 2.32 us  [on_device(): weight = lax.dynamic_update_slice_in_dim(weight, got, at, 0)]
    slice x2, local copies, waits for them, and re-layouts: 0.04 us -> 1.96 us  [on_device(): diagonal = [across(by_y[:half], 1), across(by_x[half:], 2)]]
  transfers between devices with their start and end apart: 28 -> 28, of which waited for: 13 -> 14; matrix products, arithmetic and copies ran while one was open for 9% -> 13% of each run, Pallas kernels for 7% -> 8%
where the time goes in v3:
time: 153 us; the launch traced here: 152 us
  waiting for transfers between devices  65.5 us (43%)
  starting transfers between devices  43.6 us (28%)
  Pallas kernels  14.5 us (9%)
  other arithmetic  14.4 us (9%)
  local copies, waits for them, and re-layouts  6.5 us (4%)
  matrix products  6.45 us (4%)
    ppermute x6, waiting for transfers between devices, round_chips(): return lax.ppermute(x, 'chip', [(i, (i + k) % chips) for i in range(chips)])  38.6 us
    ppermute x8, starting transfers between devices, swap(): return lax.ppermute(x, 'core', [(0, 1), (1, 0)])  11.8 us
    ppermute x3, waiting for transfers between devices, up(): return lax.ppermute(x, 'chip', [(i, i + k) for i in range(chips - k)])  11.5 us
    ppermute x6, starting transfers between devices, round_chips(): return lax.ppermute(x, 'chip', [(i, (i + k) % chips) for i in range(chips)])  10.4 us
    ppermute x3, starting transfers between devices, up(): return lax.ppermute(x, 'chip', [(i, i + k) for i in range(chips - k)])  8.2 us
    pallas_call x4, Pallas kernels, forward(): pl.pallas_call(functools.partial(forward_kernel, steps, rows, first, last...  7.93 us
    ppermute x8, starting transfers between devices, across(): return lax.ppermute(x, 'dp', [(i, i ^ k) for i in range(rows_dp)])  7.23 us
    ppermute x3, waiting for transfers between devices, down(): return lax.ppermute(x, 'chip', [(i + k, i) for i in range(chips - k)])  6.99 us
  transfers between devices with their start and end apart: 28, of which 14 were waited for; matrix products, arithmetic and copies ran while one was open for 13% of the time, Pallas kernels for 8%

profile of v3, /device:TPU:9, one launch (start us, length us, event | category | flops | bytes accessed | tf_op | source)
XLA Modules:
  0.0 152.1 jit_solution(4933754595071833849)
XLA Ops:
  0.6 0.7 collective-permute-start.2
  1.4 1.0 broadcast_select_fusion.6
  2.4 1.0 broadcast_select_fusion.5
  3.5 1.5 collective-permute-done
  5.1 3.2 %collective-permute-start.1 = (bf16[512,512]{1,0:T(8,128)(2,1)S(1)}, bf16[512,512]{1,0:T(8,128)(2,1)S(1)}, u32[]{:S(2)}, u32[]{:S(2)}) collective-permute-start(bf16[512,512]{1,0:T(8,128)(2,1)S(1)} %pad_maximum_fusion.6.refs_0_), channel_id=1, source_target_pairs={{0,2},{2,4},{4,6},{1,3},{3,5},{5,7},{8,10},{10,12},{12,14},{9,11},... | collective-permute-start | bytes 1572872 | tf_op jit(solution)/shard_map/ppermute | solution.py:256
  8.3 1.3 collective-permute-start.3
  9.6 1.0 collective-permute-start.4
  11.0 12.5 %collective-permute-done.3 = bf16[72,1024]{1,0:T(8,128)(2,1)S(1)} collective-permute-done((bf16[72,1024]{1,0:T(8,128)(2,1)S(1)}, bf16[72,1024]{1,0:T(8,128)(2,1)S(1)}, u32[]{:S(2)}, u32[]{:S(2)}) %collective-permute-start.3) | collective-permute-done | bytes 147488 | tf_op jit(solution)/shard_map/ppermute | solution.py:262
  23.5 8.6 %collective-permute-done.4 = bf16[72,1024]{1,0:T(8,128)(2,1)S(1)} collective-permute-done((bf16[72,1024]{1,0:T(8,128)(2,1)S(1)}, bf16[72,1024]{1,0:T(8,128)(2,1)S(1)}, u32[]{:S(2)}, u32[]{:S(2)}) %collective-permute-start.4) | collective-permute-done | bytes 147488 | tf_op jit(solution)/shard_map/ppermute | solution.py:262
  32.2 1.0 collective-permute-start.6
  33.2 0.7 broadcast_select_fusion.2
  34.0 1.6 %collective-permute-done.7 = bf16[256,512]{1,0:T(8,128)(2,1)} collective-permute-done((bf16[256,512]{1,0:T(8,128)(2,1)S(1)}, bf16[256,512]{1,0:T(8,128)(2,1)}, u32[]{:S(2)}, u32[]{:S(2)}) %collective-permute-start.7) | collective-permute-done | bytes 262176 | tf_op jit(solution)/shard_map/ppermute | solution.py:253
  35.7 1.3 collective-permute-start.8
  37.0 1.2 collective-permute-start.9
  38.2 1.9 %collective-permute-start.10 = (bf16[512,512]{1,0:T(8,128)(2,1)S(1)}, bf16[512,512]{1,0:T(8,128)(2,1)S(1)}, u32[]{:S(2)}, u32[]{:S(2)}) collective-permute-start(bf16[512,512]{1,0:T(8,128)(2,1)S(1)} %collective-permute-done.1.refs_0_), channel_id=1, source_target_pairs={{0,2},{2,4},{4,6},{1,3},{3,5},{5,7},{8,10},{10,12},{12,14},{9,11},... | collective-permute-start | bytes 1572872 | tf_op jit(solution)/shard_map/ppermute | solution.py:256
  40.3 1.1 maximum_multiply_fusion.q
  41.4 11.5 %collective-permute-done.10.refs_0_ = bf16[512,512]{1,0:T(8,128)(2,1)S(1)} collective-permute-done((bf16[512,512]{1,0:T(8,128)(2,1)S(1)}, bf16[512,512]{1,0:T(8,128)(2,1)S(1)}, u32[]{:S(2)}, u32[]{:S(2)}) %collective-permute-start.10) | collective-permute-done | bytes 524320 | tf_op jit(solution)/shard_map/ppermute | solution.py:256
  52.9 3.1 %collective-permute-start.13 = (bf16[512,512]{1,0:T(8,128)(2,1)S(1)}, bf16[512,512]{1,0:T(8,128)(2,1)S(1)}, u32[]{:S(2)}, u32[]{:S(2)}) collective-permute-start(bf16[512,512]{1,0:T(8,128)(2,1)S(1)} %collective-permute-done.10.refs_0_), channel_id=1, source_target_pairs={{0,2},{2,4},{4,6},{1,3},{3,5},{5,7},{8,10},{10,12},{12,14},{9,11},... | collective-permute-start | bytes 1572872 | tf_op jit(solution)/shard_map/ppermute | solution.py:256
  56.0 1.8 %attend_forward.4 = (f32[512,256]{1,0:T(8,128)S(1)}, f32[512,256]{1,0:T(8,128)S(1)}, f32[512,512]{1,0:T(8,128)S(1)}) custom-call(s32[2]{0:T(128)S(1)} %pad_add_fusion.info, bf16[512,512]{1,0:T(8,128)(2,1)S(1)} %maximum_multiply_fusion.q, bf16[512,512]{1,0:T(8,128)(2,1)S(1)} %pad_maximum_fusion.6.refs_0_), custom_call_target="tpu_custom_call" | custom-call | flops 536870912 | bytes 1048576 | tf_op jit(solution)/shard_map/attend_forward/pallas_call | solution.py:113
  57.8 4.3 %attend_forward.5 = (f32[512,256]{1,0:T(8,128)S(1)}, f32[512,256]{1,0:T(8,128)S(1)}, f32[512,512]{1,0:T(8,128)S(1)}) custom-call(s32[2]{0:T(128)S(1)} %pad_add_fusion.info, bf16[512,512]{1,0:T(8,128)(2,1)S(1)} %maximum_multiply_fusion.q, bf16[512,512]{1,0:T(8,128)(2,1)S(1)} %collective-permute-done.1.refs_0_, f32[512,256]{1,0:T(8,128)S(1)} %get-tuple-element.64.refs_1_, ...), custom_call_target="tpu_custom_call" | custom-call | flops 536870912 | bytes 1048576 | tf_op jit(solution)/shard_map/attend_forward/pallas_call | solution.py:113
  62.3 1.0 slice.100
  63.6 1.0 slice.101
  64.8 0.7 attend_forward.6
  65.5 1.1 constant_dynamic-update-slice_fusion.3
  66.6 1.1 constant_dynamic-update-slice_fusion.2
  67.8 2.2 %collective-permute-done.11 = bf16[288,512]{1,0:T(8,128)(2,1)S(1)} collective-permute-done((bf16[288,512]{1,0:T(8,128)(2,1)S(1)}, bf16[288,512]{1,0:T(8,128)(2,1)S(1)}, u32[]{:S(2)}, u32[]{:S(2)}) %collective-permute-start.11) | collective-permute-done | bytes 294944 | tf_op jit(solution)/shard_map/ppermute | solution.py:265
  70.0 1.0 collective-permute-done.12
  71.0 1.2 attend_forward.7
  72.3 0.9 fusion.13
  73.2 0.9 convolution_convert_fusion
  74.2 1.4 fusion.2.da
  75.5 0.9 attend_backward.4
  76.5 1.9 %collective-permute-start.16 = (bf16[512,512]{1,0:T(8,128)(2,1)S(1)}, bf16[512,512]{1,0:T(8,128)(2,1)S(1)}, u32[]{:S(2)}, u32[]{:S(2)}) collective-permute-start(bf16[512,512]{1,0:T(8,128)(2,1)S(1)} %get-tuple-element.80), channel_id=1, source_target_pairs={{2,0},{4,2},{6,4},{3,1},{5,3},{7,5},{10,8},{12,10},{14,12},{11,9},... | collective-permute-start | bytes 1572872 | tf_op jit(solution)/shard_map/ppermute | solution.py:259
  78.4 1.3 collective-permute-start.14
  79.9 0.9 fusion.8
  80.9 0.6 attend_backward.5
  81.6 2.5 %attend_backward.6 = (bf16[512,512]{1,0:T(8,128)(2,1)S(1)}, f32[512,512]{1,0:T(8,128)S(1)}) custom-call(s32[2]{0:T(128)S(1)} %pad_add_fusion.info, bf16[512,512]{1,0:T(8,128)(2,1)S(1)} %maximum_multiply_fusion.q, bf16[512,512]{1,0:T(8,128)(2,1)S(1)} %fusion.2.da, f32[16,512]{1,0:T(8,128)S(1)} %get-tuple-element.79.lse_t, ...), custom_call_target="tpu_custom_call" | custom-call | flops 1342177280 | bytes 1572864 | tf_op jit(solution)/shard_map/attend_backward/pallas_call | solution.py:214
  84.1 1.5 collective-permute-done.15
  85.6 5.1 %collective-permute-done.16 = bf16[512,512]{1,0:T(8,128)(2,1)S(1)} collective-permute-done((bf16[512,512]{1,0:T(8,128)(2,1)S(1)}, bf16[512,512]{1,0:T(8,128)(2,1)S(1)}, u32[]{:S(2)}, u32[]{:S(2)}) %collective-permute-start.16) | collective-permute-done | bytes 524320 | tf_op jit(solution)/shard_map/ppermute | solution.py:259
  90.8 2.1 %collective-permute-start.20 = (bf16[512,512]{1,0:T(8,128)(2,1)S(1)}, bf16[512,512]{1,0:T(8,128)(2,1)S(1)}, u32[]{:S(2)}, u32[]{:S(2)}) collective-permute-start(bf16[512,512]{1,0:T(8,128)(2,1)S(1)} %add_convert_fusion.2), channel_id=1, source_target_pairs={{2,0},{4,2},{6,4},{3,1},{5,3},{7,5},{10,8},{12,10},{14,12},{11,9},... | collective-permute-start | bytes 1572872 | tf_op jit(solution)/shard_map/ppermute | solution.py:259
  93.1 1.4 collective-permute-start.18
  94.6 1.2 collective-permute-start.17
  95.9 2.6 %attend_backward.7 = (f32[512,512]{1,0:T(8,128)S(1)}, bf16[512,512]{1,0:T(8,128)(2,1)S(1)}) custom-call(s32[2]{0:T(128)S(1)} %pad_add_fusion.info, bf16[512,512]{1,0:T(8,128)(2,1)S(1)} %maximum_multiply_fusion.q, bf16[512,512]{1,0:T(8,128)(2,1)S(1)} %fusion.2.da, f32[16,512]{1,0:T(8,128)S(1)} %get-tuple-element.79.lse_t, ...), custom_call_target="tpu_custom_call" | custom-call | flops 1342177280 | bytes 1572864 | tf_op jit(solution)/shard_map/attend_backward/pallas_call | solution.py:214
  98.4 0.7 slice_bitcast_fusion
  99.2 3.6 %collective-permute-start.19 = (bf16[256,512]{1,0:T(8,128)(2,1)S(1)}, bf16[256,512]{1,0:T(8,128)(2,1)S(1)}, u32[]{:S(2)}, u32[]{:S(2)}) collective-permute-start(bf16[256,512]{1,0:T(8,128)(2,1)S(1)} %get-tuple-element.113), channel_id=1, source_target_pairs={{0,1},{1,0},{2,3},{3,2},{4,5},{5,4},{6,7},{7,6},{8,9},{9,8},{10,11... | collective-permute-start | bytes 786440 | tf_op jit(solution)/shard_map/ppermute | solution.py:253
  102.8 0.9 fusion.5
  104.0 1.9 %collective-permute-done.20 = bf16[512,512]{1,0:T(8,128)(2,1)S(1)} collective-permute-done((bf16[512,512]{1,0:T(8,128)(2,1)S(1)}, bf16[512,512]{1,0:T(8,128)(2,1)S(1)}, u32[]{:S(2)}, u32[]{:S(2)}) %collective-permute-start.20) | collective-permute-done | bytes 524320 | tf_op jit(solution)/shard_map/ppermute | solution.py:259
  106.4 1.4 fusion.27
  108.0 4.3 %collective-permute-start.22 = (bf16[256,2304]{1,0:T(8,128)(2,1)S(1)}, bf16[256,2304]{1,0:T(8,128)(2,1)}, u32[]{:S(2)}, u32[]{:S(2)}) collective-permute-start(bf16[256,2304]{1,0:T(8,128)(2,1)S(1)} %slice.179), channel_id=1, source_target_pairs={{0,1},{1,0},{2,3},{3,2},{4,5},{5,4},{6,7},{7,6},{8,9},{9,8},{10,11... | collective-permute-start | bytes 3538952 | tf_op jit(solution)/shard_map/ppermute | solution.py:253
  112.4 0.9 add_convert_fusion.1
  113.3 1.9 %collective-permute-start.21 = (bf16[512,512]{1,0:T(8,128)(2,1)}, bf16[512,512]{1,0:T(8,128)(2,1)}, u32[]{:S(2)}, u32[]{:S(2)}) collective-permute-start(bf16[512,512]{1,0:T(8,128)(2,1)} %add_convert_fusion.1), channel_id=1, source_target_pairs={{2,0},{4,2},{6,4},{3,1},{5,3},{7,5},{10,8},{12,10},{14,12},{11,9},... | collective-permute-start | bytes 1572872 | tf_op jit(solution)/shard_map/ppermute | solution.py:259
  115.2 0.8 dynamic-slice_convert_fusion
  116.0 4.4 %collective-permute-start.23 = (bf16[144,512]{1,0:T(8,128)(2,1)}, bf16[144,512]{1,0:T(8,128)(2,1)S(1)}, u32[]{:S(2)}, u32[]{:S(2)}) collective-permute-start(bf16[144,512]{1,0:T(8,128)(2,1)} %get-tuple-element.105), channel_id=1, source_target_pairs={{0,2},{2,4},{4,6},{6,0},{1,3},{3,5},{5,7},{7,1},{8,10},{10,12},{12... | collective-permute-start | bytes 442376 | tf_op jit(solution)/shard_map/ppermute | solution.py:262
  120.4 2.0 %collective-permute-start.24 = (bf16[144,512]{1,0:T(8,128)(2,1)}, bf16[144,512]{1,0:T(8,128)(2,1)}, u32[]{:S(2)}, u32[]{:S(2)}) collective-permute-start(bf16[144,512]{1,0:T(8,128)(2,1)} %get-tuple-element.104), channel_id=1, source_target_pairs={{0,4},{2,6},{4,0},{6,2},{1,5},{3,7},{5,1},{7,3},{8,12},{10,14},{12... | collective-permute-start | bytes 442376 | tf_op jit(solution)/shard_map/ppermute | solution.py:262
  122.3 1.5 collective-permute-start.25
  123.8 2.3 %maximum_select_fusion.1 = bf16[1,256,1024]{2,1,0:T(8,128)(2,1)} fusion(bf16[1,256,512]{2,1,0:T(8,128)(2,1)} %bitcast.51, bf16[1,256,512]{2,1,0:T(8,128)(2,1)} %get-tuple-element.112, pred[]{:T(512)S(6)} %eq.3), kind=kLoop, calls=%fused_computation.38 | loop fusion | flops 2359296 | bytes 1048577 | tf_op jit(solution)/shard_map/jit(_where)/select_n | solution.py:268
  126.1 11.8 %collective-permute-done.24 = bf16[144,512]{1,0:T(8,128)(2,1)} collective-permute-done((bf16[144,512]{1,0:T(8,128)(2,1)}, bf16[144,512]{1,0:T(8,128)(2,1)}, u32[]{:S(2)}, u32[]{:S(2)}) %collective-permute-start.24) | collective-permute-done | bytes 147488 | tf_op jit(solution)/shard_map/ppermute | solution.py:262
  137.9 5.6 %collective-permute-done.25 = bf16[144,512]{1,0:T(8,128)(2,1)} collective-permute-done((bf16[144,512]{1,0:T(8,128)(2,1)}, bf16[144,512]{1,0:T(8,128)(2,1)}, u32[]{:S(2)}, u32[]{:S(2)}) %collective-permute-start.25) | collective-permute-done | bytes 147488 | tf_op jit(solution)/shard_map/ppermute | solution.py:262
  143.6 1.1 add_multiply_fusion
  144.7 1.9 %collective-permute-start.27 = (f32[72,512]{1,0:T(8,128)S(1)}, f32[72,512]{1,0:T(8,128)S(1)}, u32[]{:S(2)}, u32[]{:S(2)}) collective-permute-start(f32[72,512]{1,0:T(8,128)S(1)} %get-tuple-element.117), channel_id=1, source_target_pairs={{0,1},{1,0},{2,3},{3,2},{4,5},{5,4},{6,7},{7,6},{8,9},{9,8},{10,11... | collective-permute-start | bytes 442376 | tf_op jit(solution)/shard_map/ppermute | solution.py:253
  146.5 1.2 add_convert_fusion
  147.9 2.5 %fusion.3 = bf16[1,256,2304]{2,1,0:T(8,128)(2,1)} fusion(bf16[256,2304]{1,0:T(8,128)(2,1)} %collective-permute-done.22, f32[512,2304]{1,0:T(8,128)S(1)} %copy-done.2), kind=kLoop, calls=%fused_computation.15 | loop fusion | flops 1769472 | bytes 4718592 | tf_op jit(solution)/shard_map/broadcast_in_dim | solution.py:388
  150.4 0.7 maximum_select_fusion.2
  151.2 0.9 maximum_select_fusion.3
  (63 shorter events, 3.6 us)
Async XLA Ops:
  0.6 31.5 %collective-permute-start.2 = (bf16[256,2304]{1,0:T(8,128)(2,1)}, bf16[256,2304]{1,0:T(8,128)(2,1)S(1)}, u32[]{:S(2)}, u32[]{:S(2)}) collective-permute-start(bf16[256,2304]{1,0:T(8,128)(2,1)} %bitcast.38), channel_id=1, source_target_pairs={{0,1},{1,0},{2,3},{3,2},{4,5},{5,4},{6,7},{7,6},{8,9},{9,8},{10,11... | collective-permute-start | bytes 3538952 | tf_op jit(solution)/shard_map/ppermute | solution.py:253
  1.4 6.9 %copy-start.5 = (bf16[72,1024]{1,0:T(8,128)(2,1)S(1)}, bf16[72,1024]{1,0:T(8,128)(2,1)}, u32[]{:S(2)}) copy-start(bf16[72,1024]{1,0:T(8,128)(2,1)} %param.8) | copy-start | bytes 442372
  3.4 1.6 %collective-permute-start = (bf16[256,512]{1,0:T(8,128)(2,1)S(1)}, bf16[256,512]{1,0:T(8,128)(2,1)S(1)}, u32[]{:S(2)}, u32[]{:S(2)}) collective-permute-start(bf16[256,512]{1,0:T(8,128)(2,1)S(1)} %pad_maximum_fusion.7), channel_id=1, source_target_pairs={{0,1},{1,0},{2,3},{3,2},{4,5},{5,4},{6,7},{7,6},{8,9},{9,8},{10,11... | collective-permute-start | bytes 786440 | tf_op jit(solution)/shard_map/ppermute | solution.py:253
  5.1 27.0 %collective-permute-start.1 = (bf16[512,512]{1,0:T(8,128)(2,1)S(1)}, bf16[512,512]{1,0:T(8,128)(2,1)S(1)}, u32[]{:S(2)}, u32[]{:S(2)}) collective-permute-start(bf16[512,512]{1,0:T(8,128)(2,1)S(1)} %pad_maximum_fusion.6.refs_0_), channel_id=1, source_target_pairs={{0,2},{2,4},{4,6},{1,3},{3,5},{5,7},{8,10},{10,12},{12,14},{9,11},... | collective-permute-start | bytes 1572872 | tf_op jit(solution)/shard_map/ppermute | solution.py:256
  8.3 15.2 %collective-permute-start.3 = (bf16[72,1024]{1,0:T(8,128)(2,1)S(1)}, bf16[72,1024]{1,0:T(8,128)(2,1)S(1)}, u32[]{:S(2)}, u32[]{:S(2)}) collective-permute-start(bf16[72,1024]{1,0:T(8,128)(2,1)S(1)} %copy-done.5), channel_id=1, source_target_pairs={{0,2},{2,4},{4,6},{6,0},{1,3},{3,5},{5,7},{7,1},{8,10},{10,12},{12... | collective-permute-start | bytes 442376 | tf_op jit(solution)/shard_map/ppermute | solution.py:262
  9.6 22.4 %collective-permute-start.4 = (bf16[72,1024]{1,0:T(8,128)(2,1)S(1)}, bf16[72,1024]{1,0:T(8,128)(2,1)S(1)}, u32[]{:S(2)}, u32[]{:S(2)}) collective-permute-start(bf16[72,1024]{1,0:T(8,128)(2,1)S(1)} %copy-done.5), channel_id=1, source_target_pairs={{0,4},{2,6},{4,0},{6,2},{1,5},{3,7},{5,1},{7,3},{8,12},{10,14},{12... | collective-permute-start | bytes 442376 | tf_op jit(solution)/shard_map/ppermute | solution.py:262
  10.6 21.5 %collective-permute-start.5 = (bf16[72,1024]{1,0:T(8,128)(2,1)S(1)}, bf16[72,1024]{1,0:T(8,128)(2,1)S(1)}, u32[]{:S(2)}, u32[]{:S(2)}) collective-permute-start(bf16[72,1024]{1,0:T(8,128)(2,1)S(1)} %copy-done.5), channel_id=1, source_target_pairs={{0,6},{2,0},{4,2},{6,4},{1,7},{3,1},{5,3},{7,5},{8,14},{10,8},{12,... | collective-permute-start | bytes 442376 | tf_op jit(solution)/shard_map/ppermute | solution.py:262
  11.0 22.3 %copy-start.3 = (bf16[1,256,1024]{2,1,0:T(8,128)(2,1)S(1)}, bf16[1,256,1024]{2,1,0:T(8,128)(2,1)}, u32[]{:S(2)}) copy-start(bf16[1,256,1024]{2,1,0:T(8,128)(2,1)} %param.5) | copy-start | bytes 1572868
  32.2 3.4 %collective-permute-start.6 = (bf16[4,72,512]{2,1,0:T(8,128)(2,1)S(1)}, bf16[4,72,512]{2,1,0:T(8,128)(2,1)S(1)}, u32[]{:S(2)}, u32[]{:S(2)}) collective-permute-start(bf16[4,72,512]{2,1,0:T(8,128)(2,1)S(1)} %get-tuple-element.109), channel_id=1, source_target_pairs={{0,1},{1,0},{2,3},{3,2},{4,5},{5,4},{6,7},{7,6},{8,9},{9,8},{10,11... | collective-permute-start | bytes 884744 | tf_op jit(solution)/shard_map/ppermute | solution.py:253
  34.0 1.7 %collective-permute-start.7 = (bf16[256,512]{1,0:T(8,128)(2,1)S(1)}, bf16[256,512]{1,0:T(8,128)(2,1)}, u32[]{:S(2)}, u32[]{:S(2)}) collective-permute-start(bf16[256,512]{1,0:T(8,128)(2,1)S(1)} %get-tuple-element.115), channel_id=1, source_target_pairs={{0,1},{1,0},{2,3},{3,2},{4,5},{5,4},{6,7},{7,6},{8,9},{9,8},{10,11... | collective-permute-start | bytes 786440 | tf_op jit(solution)/shard_map/ppermute | solution.py:253
  35.7 17.1 %collective-permute-start.8 = (bf16[576,512]{1,0:T(8,128)(2,1)S(1)}, bf16[576,512]{1,0:T(8,128)(2,1)}, u32[]{:S(2)}, u32[]{:S(2)}) collective-permute-start(bf16[576,512]{1,0:T(8,128)(2,1)S(1)} %bitcast.44), channel_id=1, source_target_pairs={{0,8},{8,0},{16,24},{24,16},{1,9},{9,1},{17,25},{25,17},{2,10},{10... | collective-permute-start | bytes 1769480 | tf_op jit(solution)/shard_map/ppermute | solution.py:265
  37.0 15.9 %collective-permute-start.9 = (bf16[576,512]{1,0:T(8,128)(2,1)S(1)}, bf16[576,512]{1,0:T(8,128)(2,1)}, u32[]{:S(2)}, u32[]{:S(2)}) collective-permute-start(bf16[576,512]{1,0:T(8,128)(2,1)S(1)} %bitcast.45), channel_id=1, source_target_pairs={{0,16},{8,24},{16,0},{24,8},{1,17},{9,25},{17,1},{25,9},{2,18},{10... | collective-permute-start | bytes 1769480 | tf_op jit(solution)/shard_map/ppermute | solution.py:265
  38.2 14.6 %collective-permute-start.10 = (bf16[512,512]{1,0:T(8,128)(2,1)S(1)}, bf16[512,512]{1,0:T(8,128)(2,1)S(1)}, u32[]{:S(2)}, u32[]{:S(2)}) collective-permute-start(bf16[512,512]{1,0:T(8,128)(2,1)S(1)} %collective-permute-done.1.refs_0_), channel_id=1, source_target_pairs={{0,2},{2,4},{4,6},{1,3},{3,5},{5,7},{8,10},{10,12},{12,14},{9,11},... | collective-permute-start | bytes 1572872 | tf_op jit(solution)/shard_map/ppermute | solution.py:256
  52.9 18.1 %collective-permute-start.13 = (bf16[512,512]{1,0:T(8,128)(2,1)S(1)}, bf16[512,512]{1,0:T(8,128)(2,1)S(1)}, u32[]{:S(2)}, u32[]{:S(2)}) collective-permute-start(bf16[512,512]{1,0:T(8,128)(2,1)S(1)} %collective-permute-done.10.refs_0_), channel_id=1, source_target_pairs={{0,2},{2,4},{4,6},{1,3},{3,5},{5,7},{8,10},{10,12},{12,14},{9,11},... | collective-permute-start | bytes 1572872 | tf_op jit(solution)/shard_map/ppermute | solution.py:256
  63.3 6.7 %collective-permute-start.11 = (bf16[288,512]{1,0:T(8,128)(2,1)S(1)}, bf16[288,512]{1,0:T(8,128)(2,1)S(1)}, u32[]{:S(2)}, u32[]{:S(2)}) collective-permute-start(bf16[288,512]{1,0:T(8,128)(2,1)S(1)} %slice.100), channel_id=1, source_target_pairs={{0,8},{8,0},{16,24},{24,16},{1,9},{9,1},{17,25},{25,17},{2,10},{10... | collective-permute-start | bytes 884744 | tf_op jit(solution)/shard_map/ppermute | solution.py:265
  64.6 6.4 %collective-permute-start.12 = (bf16[288,512]{1,0:T(8,128)(2,1)S(1)}, bf16[288,512]{1,0:T(8,128)(2,1)S(1)}, u32[]{:S(2)}, u32[]{:S(2)}) collective-permute-start(bf16[288,512]{1,0:T(8,128)(2,1)S(1)} %slice.101), channel_id=1, source_target_pairs={{0,16},{8,24},{16,0},{24,8},{1,17},{9,25},{17,1},{25,9},{2,18},{10... | collective-permute-start | bytes 884744 | tf_op jit(solution)/shard_map/ppermute | solution.py:265
  71.0 1.3 copy-start
  76.5 14.2 %collective-permute-start.16 = (bf16[512,512]{1,0:T(8,128)(2,1)S(1)}, bf16[512,512]{1,0:T(8,128)(2,1)S(1)}, u32[]{:S(2)}, u32[]{:S(2)}) collective-permute-start(bf16[512,512]{1,0:T(8,128)(2,1)S(1)} %get-tuple-element.80), channel_id=1, source_target_pairs={{2,0},{4,2},{6,4},{3,1},{5,3},{7,5},{10,8},{12,10},{14,12},{11,9},... | collective-permute-start | bytes 1572872 | tf_op jit(solution)/shard_map/ppermute | solution.py:259
  78.4 5.6 %collective-permute-start.14 = (bf16[288,512]{1,0:T(8,128)(2,1)S(1)}, bf16[288,512]{1,0:T(8,128)(2,1)S(1)}, u32[]{:S(2)}, u32[]{:S(2)}) collective-permute-start(bf16[288,512]{1,0:T(8,128)(2,1)S(1)} %get-tuple-element.107), channel_id=1, source_target_pairs={{0,8},{8,0},{16,24},{24,16},{1,9},{9,1},{17,25},{25,17},{2,10},{10... | collective-permute-start | bytes 884744 | tf_op jit(solution)/shard_map/ppermute | solution.py:265
  79.7 5.9 %collective-permute-start.15 = (bf16[288,512]{1,0:T(8,128)(2,1)S(1)}, bf16[288,512]{1,0:T(8,128)(2,1)S(1)}, u32[]{:S(2)}, u32[]{:S(2)}) collective-permute-start(bf16[288,512]{1,0:T(8,128)(2,1)S(1)} %get-tuple-element.106), channel_id=1, source_target_pairs={{0,16},{8,24},{16,0},{24,8},{1,17},{9,25},{17,1},{25,9},{2,18},{10... | collective-permute-start | bytes 884744 | tf_op jit(solution)/shard_map/ppermute | solution.py:265
  90.8 15.0 %collective-permute-start.20 = (bf16[512,512]{1,0:T(8,128)(2,1)S(1)}, bf16[512,512]{1,0:T(8,128)(2,1)S(1)}, u32[]{:S(2)}, u32[]{:S(2)}) collective-permute-start(bf16[512,512]{1,0:T(8,128)(2,1)S(1)} %add_convert_fusion.2), channel_id=1, source_target_pairs={{2,0},{4,2},{6,4},{3,1},{5,3},{7,5},{10,8},{12,10},{14,12},{11,9},... | collective-permute-start | bytes 1572872 | tf_op jit(solution)/shard_map/ppermute | solution.py:259
  93.1 12.7 %collective-permute-start.18 = (bf16[576,512]{1,0:T(8,128)(2,1)S(1)}, bf16[576,512]{1,0:T(8,128)(2,1)S(1)}, u32[]{:S(2)}, u32[]{:S(2)}) collective-permute-start(bf16[576,512]{1,0:T(8,128)(2,1)S(1)} %pad_maximum_fusion.5), channel_id=1, source_target_pairs={{0,16},{8,24},{16,0},{24,8},{1,17},{9,25},{17,1},{25,9},{2,18},{10... | collective-permute-start | bytes 1769480 | tf_op jit(solution)/shard_map/ppermute | solution.py:265
  94.6 11.5 %collective-permute-start.17 = (bf16[576,512]{1,0:T(8,128)(2,1)S(1)}, bf16[576,512]{1,0:T(8,128)(2,1)S(1)}, u32[]{:S(2)}, u32[]{:S(2)}) collective-permute-start(bf16[576,512]{1,0:T(8,128)(2,1)S(1)} %pad_maximum_fusion.4), channel_id=1, source_target_pairs={{0,8},{8,0},{16,24},{24,16},{1,9},{9,1},{17,25},{25,17},{2,10},{10... | collective-permute-start | bytes 1769480 | tf_op jit(solution)/shard_map/ppermute | solution.py:265
  99.2 4.8 %collective-permute-start.19 = (bf16[256,512]{1,0:T(8,128)(2,1)S(1)}, bf16[256,512]{1,0:T(8,128)(2,1)S(1)}, u32[]{:S(2)}, u32[]{:S(2)}) collective-permute-start(bf16[256,512]{1,0:T(8,128)(2,1)S(1)} %get-tuple-element.113), channel_id=1, source_target_pairs={{0,1},{1,0},{2,3},{3,2},{4,5},{5,4},{6,7},{7,6},{8,9},{9,8},{10,11... | collective-permute-start | bytes 786440 | tf_op jit(solution)/shard_map/ppermute | solution.py:253
  104.0 3.9 %copy-start.4 = (bf16[256,512]{1,0:T(8,128)(2,1)}, bf16[256,512]{1,0:T(8,128)(2,1)S(1)}, u32[]{:S(2)}) copy-start(bf16[256,512]{1,0:T(8,128)(2,1)S(1)} %collective-permute-done.19) | copy-start | bytes 786436
  107.9 5.4 %copy-start.1 = (f32[512,2304]{1,0:T(8,128)}, f32[512,2304]{1,0:T(8,128)S(1)}, u32[]{:S(2)}) copy-start(f32[512,2304]{1,0:T(8,128)S(1)} %fusion.27) | copy-start | bytes 14155780
  108.0 35.6 %collective-permute-start.22 = (bf16[256,2304]{1,0:T(8,128)(2,1)S(1)}, bf16[256,2304]{1,0:T(8,128)(2,1)}, u32[]{:S(2)}, u32[]{:S(2)}) collective-permute-start(bf16[256,2304]{1,0:T(8,128)(2,1)S(1)} %slice.179), channel_id=1, source_target_pairs={{0,1},{1,0},{2,3},{3,2},{4,5},{5,4},{6,7},{7,6},{8,9},{9,8},{10,11... | collective-permute-start | bytes 3538952 | tf_op jit(solution)/shard_map/ppermute | solution.py:253
  113.3 30.3 %collective-permute-start.21 = (bf16[512,512]{1,0:T(8,128)(2,1)}, bf16[512,512]{1,0:T(8,128)(2,1)}, u32[]{:S(2)}, u32[]{:S(2)}) collective-permute-start(bf16[512,512]{1,0:T(8,128)(2,1)} %add_convert_fusion.1), channel_id=1, source_target_pairs={{2,0},{4,2},{6,4},{3,1},{5,3},{7,5},{10,8},{12,10},{14,12},{11,9},... | collective-permute-start | bytes 1572872 | tf_op jit(solution)/shard_map/ppermute | solution.py:259
  116.0 10.1 %collective-permute-start.23 = (bf16[144,512]{1,0:T(8,128)(2,1)}, bf16[144,512]{1,0:T(8,128)(2,1)S(1)}, u32[]{:S(2)}, u32[]{:S(2)}) collective-permute-start(bf16[144,512]{1,0:T(8,128)(2,1)} %get-tuple-element.105), channel_id=1, source_target_pairs={{0,2},{2,4},{4,6},{6,0},{1,3},{3,5},{5,7},{7,1},{8,10},{10,12},{12... | collective-permute-start | bytes 442376 | tf_op jit(solution)/shard_map/ppermute | solution.py:262
  120.4 17.6 %collective-permute-start.24 = (bf16[144,512]{1,0:T(8,128)(2,1)}, bf16[144,512]{1,0:T(8,128)(2,1)}, u32[]{:S(2)}, u32[]{:S(2)}) collective-permute-start(bf16[144,512]{1,0:T(8,128)(2,1)} %get-tuple-element.104), channel_id=1, source_target_pairs={{0,4},{2,6},{4,0},{6,2},{1,5},{3,7},{5,1},{7,3},{8,12},{10,14},{12... | collective-permute-start | bytes 442376 | tf_op jit(solution)/shard_map/ppermute | solution.py:262
  122.3 21.2 %collective-permute-start.25 = (bf16[144,512]{1,0:T(8,128)(2,1)}, bf16[144,512]{1,0:T(8,128)(2,1)}, u32[]{:S(2)}, u32[]{:S(2)}) collective-permute-start(bf16[144,512]{1,0:T(8,128)(2,1)} %get-tuple-element.103), channel_id=1, source_target_pairs={{0,6},{2,0},{4,2},{6,4},{1,7},{3,1},{5,3},{7,5},{8,14},{10,8},{12,... | collective-permute-start | bytes 442376 | tf_op jit(solution)/shard_map/ppermute | solution.py:262
  123.8 24.1 %copy-start.2 = (f32[512,2304]{1,0:T(8,128)S(1)}, f32[512,2304]{1,0:T(8,128)}, u32[]{:S(2)}) copy-start(f32[512,2304]{1,0:T(8,128)} %copy-done.1) | copy-start | bytes 14155780
  144.7 5.8 %collective-permute-start.27 = (f32[72,512]{1,0:T(8,128)S(1)}, f32[72,512]{1,0:T(8,128)S(1)}, u32[]{:S(2)}, u32[]{:S(2)}) collective-permute-start(f32[72,512]{1,0:T(8,128)S(1)} %get-tuple-element.117), channel_id=1, source_target_pairs={{0,1},{1,0},{2,3},{3,2},{4,5},{5,4},{6,7},{7,6},{8,9},{9,8},{10,11... | collective-permute-start | bytes 442376 | tf_op jit(solution)/shard_map/ppermute | solution.py:253
  147.8 3.4 %collective-permute-start.26 = (bf16[256,512]{1,0:T(8,128)(2,1)S(1)}, bf16[256,512]{1,0:T(8,128)(2,1)S(1)}, u32[]{:S(2)}, u32[]{:S(2)}) collective-permute-start(bf16[256,512]{1,0:T(8,128)(2,1)S(1)} %slice.134), channel_id=1, source_target_pairs={{0,1},{1,0},{2,3},{3,2},{4,5},{5,4},{6,7},{7,6},{8,9},{9,8},{10,11... | collective-permute-start | bytes 786440 | tf_op jit(solution)/shard_map/ppermute | solution.py:253

commit v4 on v3

--- a/solution.py
+++ b/solution.py
@@ -278,7 +278,9 @@
     kv = jnp.concatenate([own(k0), own(v0)], 1)
     kv = jnp.concatenate([kv, kv_theirs], 0)
     hop = up(kv, 1)
-    hop, grad_theirs, *moved = together((hop, swap(g0), *moved))
+    q = jnp.concatenate([own(q0), swap(other(q0))], 0) * jnp.asarray(HD ** (-0.5), BF16)
+    state = forward(info, q, [kv], (0,), None, False)
+    hop, q, state, *moved = together((hop, q, state, *moved))
     chunks = [kv, hop]
 
     piece = out_weight.shape[0]
@@ -291,45 +293,53 @@
             column = lax.dynamic_update_index_in_dim(column, got, source, 0)
     else:
         column = lax.all_gather(out_weight, "chip", axis=0)
-    column_theirs, q_theirs = together((swap(other(column)), swap(other(q0))))
-    ours = in_order(own(column)[:, None], column_theirs[:, None], 1)
+    ours = in_order(own(column)[:, None], swap(other(column))[:, None], 1)
     ours = ours.reshape(chips * part, ours.shape[-1])
     share = ours.shape[0]
     half = share // 2
 
-    by_x, by_y, hop = together((across(ours, 1), across(ours, 2), up(hop, 1)))
+    lower, upper = ours[:half], ours[half:]
+    hop = up(hop, 1)
+    state = forward(info, q, chunks[1:2], (1,), state, False)
+    *by_plane, hop, state = together(
+        (across(lower, 1), across(upper, 1), across(lower, 2), across(upper, 2), hop, state)
+    )
     chunks.append(hop)
-    diagonal = [across(by_y[:half], 1), across(by_x[half:], 2)]
-    diagonal[0], diagonal[1], hop = together((*diagonal, up(hop, 1)))
-    chunks.append(hop)
-    for _ in steps[4:]:
-        chunks.append(up(chunks[-1], 1))
-    weight = jnp.zeros((rows_dp * share, ours.shape[1]), BF16)
-    for got, at in (
-        (ours, row * share),
-        (by_x, (row ^ 1) * share),
-        (by_y, (row ^ 2) * share),
-        (diagonal[0], (row ^ 3) * share),
-        (diagonal[1], (row ^ 3) * share + half),
-    ):
-        weight = lax.dynamic_update_slice_in_dim(weight, got, at, 0)
-
-    q = jnp.concatenate([own(q0), q_theirs], 0) * jnp.asarray(HD ** (-0.5), BF16)
-    grad = jnp.concatenate([g0, grad_theirs], 0)
+    diagonal = [across(by_plane[2], 1), across(by_plane[1], 2)]
+    grad = jnp.concatenate([g0, swap(g0)], 0)
     turned = grad.T
     blocks = [
-        lax.dynamic_slice_in_dim(turned, (row ^ k) * share, share, 0) for k in range(rows_dp)
+        lax.dynamic_slice_in_dim(turned, (row ^ k) * share + at, half, 0)
+        for k in range(rows_dp)
+        for at in (0, half)
     ]
-    state = None
-    for step in steps:
-        state = forward(info, q, chunks[step : step + 1], (step,), state, step == prior)
-    att, lse_t = state
+    last_hop = up(hop, 1)
+    for step in steps[2:prior]:
+        state = forward(info, q, [hop], (step,), state, False)
+        hop = last_hop
+        if step + 1 < prior:
+            chunks.append(hop)
+            last_hop = up(hop, 1)
+    weight = jnp.zeros((rows_dp * share, ours.shape[1]), BF16)
+    for got, k, at in (
+        (ours, 0, 0),
+        (by_plane[0], 1, 0),
+        (by_plane[1], 1, half),
+        (by_plane[2], 2, 0),
+        (by_plane[3], 2, half),
+        (diagonal[0], 3, 0),
+        (diagonal[1], 3, half),
+    ):
+        weight = lax.dynamic_update_slice_in_dim(weight, got, (row ^ k) * share + at, 0)
     da = dot(grad, weight).astype(BF16)
-
-    dw = [dot(b, att) for b in blocks]
-    far = dw[3].astype(BF16)
-    far, da = together((far, da))
-    from_x, from_y = across(far[:half], 1), across(far[half:], 2)
+    da, last_hop, state, *blocks = together((da, last_hop, state, *blocks))
+    chunks.append(last_hop)
+    att, lse_t = forward(info, q, [last_hop], (prior,), state, True)
+
+    to_x, to_y, far_x, far_y = [dot(blocks[i], att).astype(BF16) for i in (2, 5, 6, 7)]
+    to_x, to_y, far_x, far_y, da, att = together((to_x, to_y, far_x, far_y, da, att))
+    partial = dot(att, weight, NT)
+    part_mine, part_sent = partial[:tok], partial[tok:].astype(BF16)
     carried = None
     terms = {}
     for step in reversed(steps):
@@ -346,20 +356,34 @@
     passing = terms[prior]
     for step in range(prior - 1, 2, -1):
         passing = (terms[step].astype(F32) + down(passing, 1).astype(F32)).astype(BF16)
-    from_x, from_y, got = together((from_x, from_y, down(passing, 1)))
+    from_x, from_y, by_x0, by_y1, got, part_sent = together(
+        (
+            across(far_x, 1),
+            across(far_y, 2),
+            across(to_x, 1),
+            across(to_y, 2),
+            down(passing, 1),
+            part_sent,
+        )
+    )
     passing = (terms[2].astype(F32) + got.astype(F32)).astype(BF16)
-    to_x = jnp.concatenate([dw[1][:half], dw[1][half:] + from_y.astype(F32)], 0).astype(BF16)
-    to_y = jnp.concatenate([dw[2][:half] + from_x.astype(F32), dw[2][half:]], 0).astype(BF16)
-    by_x, by_y, dq_theirs, got = together(
-        (across(to_x, 1), across(to_y, 2), swap(dq[tok:]), down(passing, 1))
-    )
-    mine = dw[0] + by_x.astype(F32) + by_y.astype(F32)
-
+    to_x = (dot(blocks[3], att) + from_y.astype(F32)).astype(BF16)
+    to_y = (dot(blocks[4], att) + from_x.astype(F32)).astype(BF16)
+    by_x1, by_y0, dq_theirs, layer_theirs, got = together(
+        (across(to_x, 1), across(to_y, 2), swap(dq[tok:]), swap(part_sent), down(passing, 1))
+    )
     passing = (terms[1].astype(F32) + got.astype(F32)).astype(BF16)
     coming = down(passing, 1)
-    att, mine = together((att, mine))
-    partial = dot(att, weight, NT)
-    layer_theirs = swap(partial[tok:].astype(BF16))
+    mine = jnp.concatenate(
+        [
+            dot(blocks[0], att) + by_x0.astype(F32) + by_y0.astype(F32),
+            dot(blocks[1], att) + by_x1.astype(F32) + by_y1.astype(F32),
+        ],
+        0,
+    )
+
+    layer_out = (part_mine + layer_theirs.astype(F32)).astype(BF16)
+    query_grad = in_order(dq[:tok], dq_theirs, 1)
     if near:
         final = lax.dynamic_slice_in_dim(mine, chip * part, part, 0)
         got = []
@@ -367,12 +391,11 @@
             target = lax.rem(chip + k, chips)
             sent = lax.dynamic_slice_in_dim(mine, target * part, part, 0).astype(BF16)
             got.append(round_chips(sent, k))
-        coming, layer_theirs, *got = together((coming, layer_theirs, *got))
+        coming, layer_out, query_grad, *got = together((coming, layer_out, query_grad, *got))
         for x in got:
             final = final + x.astype(F32)
     else:
         final = lax.psum_scatter(mine, "chip", scatter_dimension=0, tiled=True)
-    layer_out = (partial[:tok] + layer_theirs.astype(F32)).astype(BF16)
     total_tokens = rows_dp * chips * rows
     final = final * (1.0 / math.sqrt(total_tokens))
     first_rows, last_rows = final[:piece], final[piece:]
@@ -380,7 +403,6 @@
         jnp.where(low, first_rows, last_rows), swap(jnp.where(low, last_rows, first_rows)), 1
     )
     kv_grad = (terms[0] + coming.astype(F32)).astype(BF16)
-    query_grad = in_order(dq[:tok], dq_theirs, 1)
     theirs = swap(kv_grad[tok:])
     key_grad = in_order(kv_grad[:tok, :HD], theirs[:, :HD], 1)
     value_grad = in_order(kv_grad[:tok, HD:], theirs[:, HD:], 1)

time: 153 us -> 154 us (level)
  waiting for transfers between devices: 65.5 us -> 58.8 us
  matrix products: 6.45 us -> 10.7 us
  other arithmetic: 14.4 us -> 18.6 us
  starting transfers between devices: 43.6 us -> 41.6 us
    ppermute x6, waiting for transfers between devices: 38.6 us -> 19.5 us  [round_chips(): return lax.ppermute(x, 'chip', [(i, (i + k) % chips) for i in range(chips)])]
    ppermute x8 -> x12, waiting for transfers between devices: 5.04 us -> 17.4 us  [across(): return lax.ppermute(x, 'dp', [(i, i ^ k) for i in range(rows_dp)])]
    dynamic_slice x0 -> x2, other arithmetic: none -> 5.75 us  [on_device(): lax.dynamic_slice_in_dim(turned, (row ^ k) * share + at, half, 0)]
    dot_general x6 -> x10, matrix products: 6.45 us -> 10.7 us  [dot(): return lax.dot_general(a, b, dims, preferred_element_type=F32)]
    convert_element_type x0 -> x2, other arithmetic: none -> 3.57 us  [the longest x1 3.19 us: on_device(): layer_out = (part_mine + layer_theirs.astype(F32)).astype(BF16)]
    unnamed x12 -> x26, local copies, waits for them, and re-layouts: 0.13 us -> 2.91 us
    ppermute x3, waiting for transfers between devices: 6.99 us -> 4.35 us  [down(): return lax.ppermute(x, 'chip', [(i + k, i) for i in range(chips - k)])]
    ppermute x8, starting transfers between devices: 11.8 us -> 9.2 us  [swap(): return lax.ppermute(x, 'core', [(0, 1), (1, 0)])]
  transfers between devices with their start and end apart: 28 -> 32, of which waited for: 14 -> 18; matrix products, arithmetic and copies ran while one was open for 13% -> 18% of each run, Pallas kernels for 8% -> 8%
where the time goes in v4:
time: 154 us; the launch traced here: 153 us
  waiting for transfers between devices  58.8 us (38%)
  starting transfers between devices  41.6 us (27%)
  other arithmetic  18.6 us (12%)
  Pallas kernels  14.8 us (10%)
  matrix products  10.7 us (7%)
  local copies, waits for them, and re-layouts  7.35 us (5%)
    ppermute x6, waiting for transfers between devices, round_chips(): return lax.ppermute(x, 'chip', [(i, (i + k) % chips) for i in range(chips)])  19.5 us
    ppermute x12, waiting for transfers between devices, across(): return lax.ppermute(x, 'dp', [(i, i ^ k) for i in range(rows_dp)])  17.4 us
    ppermute x3, waiting for transfers between devices, up(): return lax.ppermute(x, 'chip', [(i, i + k) for i in range(chips - k)])  13.9 us
    dot_general x10, matrix products, dot(): return lax.dot_general(a, b, dims, preferred_element_type=F32)  10.7 us
    ppermute x6, starting transfers between devices, round_chips(): return lax.ppermute(x, 'chip', [(i, (i + k) % chips) for i in range(chips)])  9.98 us
    ppermute x8, starting transfers between devices, swap(): return lax.ppermute(x, 'core', [(0, 1), (1, 0)])  9.2 us
    ppermute x3, starting transfers between devices, up(): return lax.ppermute(x, 'chip', [(i, i + k) for i in range(chips - k)])  8.25 us
    ppermute x12, starting transfers between devices, across(): return lax.ppermute(x, 'dp', [(i, i ^ k) for i in range(rows_dp)])  8.25 us
  transfers between devices with their start and end apart: 32, of which 18 were waited for; matrix products, arithmetic and copies ran while one was open for 18% of the time, Pallas kernels for 8%

profile of v4, /device:TPU:9, one launch (start us, length us, event | category | flops | bytes accessed | tf_op | source)
XLA Modules:
  0.0 152.9 jit_solution(3011156050810715260)
XLA Ops:
  0.7 1.1 broadcast_select_fusion.5
  1.7 1.0 broadcast_select_fusion.6
  3.5 1.3 collective-permute-start.3
  4.8 1.0 collective-permute-start.4
  5.8 1.5 collective-permute-start.5
  7.3 1.9 %collective-permute-start.1 = (bf16[512,512]{1,0:T(8,128)(2,1)S(1)}, bf16[512,512]{1,0:T(8,128)(2,1)S(1)}, u32[]{:S(2)}, u32[]{:S(2)}) collective-permute-start(bf16[512,512]{1,0:T(8,128)(2,1)S(1)} %pad_maximum_fusion.4.refs_0_), channel_id=1, source_target_pairs={{0,2},{2,4},{4,6},{1,3},{3,5},{5,7},{8,10},{10,12},{12,14},{9,11},... | collective-permute-start | bytes 1572872 | tf_op jit(solution)/shard_map/ppermute | solution.py:256
  9.3 1.1 collective-permute-start.2
  10.5 1.0 collective-permute-done.2
  12.0 1.8 %attend_forward.4 = (f32[512,256]{1,0:T(8,128)S(1)}, f32[512,256]{1,0:T(8,128)S(1)}, f32[512,512]{1,0:T(8,128)S(1)}) custom-call(s32[2]{0:T(128)S(1)} %pad_add_fusion.info, bf16[512,512]{1,0:T(8,128)(2,1)S(1)} %maximum_multiply_fusion.q, bf16[512,512]{1,0:T(8,128)(2,1)S(1)} %pad_maximum_fusion.4.refs_0_), custom_call_target="tpu_custom_call" | custom-call | flops 536870912 | bytes 1048576 | tf_op jit(solution)/shard_map/attend_forward/pallas_call | solution.py:113
  14.6 3.2 %collective-permute-done.4 = bf16[72,1024]{1,0:T(8,128)(2,1)} collective-permute-done((bf16[72,1024]{1,0:T(8,128)(2,1)}, bf16[72,1024]{1,0:T(8,128)(2,1)}, u32[]{:S(2)}, u32[]{:S(2)}) %collective-permute-start.4) | collective-permute-done | bytes 147488 | tf_op jit(solution)/shard_map/ppermute | solution.py:262
  17.8 2.1 %collective-permute-done.5 = bf16[72,1024]{1,0:T(8,128)(2,1)} collective-permute-done((bf16[72,1024]{1,0:T(8,128)(2,1)}, bf16[72,1024]{1,0:T(8,128)(2,1)}, u32[]{:S(2)}, u32[]{:S(2)}) %collective-permute-start.5) | collective-permute-done | bytes 147488 | tf_op jit(solution)/shard_map/ppermute | solution.py:262
  19.9 9.0 %collective-permute-done.1.refs_0_ = bf16[512,512]{1,0:T(8,128)(2,1)S(1)} collective-permute-done((bf16[512,512]{1,0:T(8,128)(2,1)S(1)}, bf16[512,512]{1,0:T(8,128)(2,1)S(1)}, u32[]{:S(2)}, u32[]{:S(2)}) %collective-permute-start.1) | collective-permute-done | bytes 524320 | tf_op jit(solution)/shard_map/ppermute | solution.py:256
  29.0 1.1 bitcast_dynamic-update-slice_fusion.1
  30.1 0.9 bitcast_dynamic-update-slice_fusion
  31.8 0.8 collective-permute-start.7
  32.6 4.1 %collective-permute-start.12 = (bf16[512,512]{1,0:T(8,128)(2,1)S(1)}, bf16[512,512]{1,0:T(8,128)(2,1)S(1)}, u32[]{:S(2)}, u32[]{:S(2)}) collective-permute-start(bf16[512,512]{1,0:T(8,128)(2,1)S(1)} %collective-permute-done.1.refs_0_), channel_id=1, source_target_pairs={{0,2},{2,4},{4,6},{1,3},{3,5},{5,7},{8,10},{10,12},{12,14},{9,11},... | collective-permute-start | bytes 1572872 | tf_op jit(solution)/shard_map/ppermute | solution.py:256
  36.8 1.0 copy-done.3
  37.8 1.0 copy-done.5
  38.8 4.3 %attend_forward.5 = (f32[512,256]{1,0:T(8,128)S(1)}, f32[512,256]{1,0:T(8,128)S(1)}, f32[512,512]{1,0:T(8,128)S(1)}) custom-call(s32[2]{0:T(128)S(1)} %pad_add_fusion.info, bf16[512,512]{1,0:T(8,128)(2,1)S(1)} %maximum_multiply_fusion.q, bf16[512,512]{1,0:T(8,128)(2,1)S(1)} %collective-permute-done.1.refs_0_, f32[512,256]{1,0:T(8,128)S(1)} %copy-done.3, ...), custom_call_target="tpu_custom_call" | custom-call | flops 536870912 | bytes 1048576 | tf_op jit(solution)/shard_map/attend_forward/pallas_call | solution.py:113
  43.1 1.1 maximum_select_fusion
  44.3 1.3 collective-permute-start.8
  45.6 1.2 collective-permute-start.10
  47.6 1.6 %fusion.20 = (bf16[288,512]{0,1:T(8,128)(2,1)S(1)}, bf16[288,512]{0,1:T(8,128)(2,1)S(1)}) fusion(s32[]{:T(128)S(6)} %select_n.187, bf16[256,2304]{1,0:T(8,128)(2,1)} %bitcast.5, bf16[256,2304]{1,0:T(8,128)(2,1)} %collective-permute-done.6, s32[]{:T(128)S(6)} %select_n.186), kind=kLoop, calls=%fused_computation.62 | loop fusion | flops 1179648 | bytes 2949128 | tf_op jit(solution)/shard_map/dynamic_slice | solution.py:312
  49.2 4.1 %fusion.22 = (bf16[288,512]{0,1:T(8,128)(2,1)S(1)}, bf16[288,512]{0,1:T(8,128)(2,1)}, bf16[288,512]{0,1:T(8,128)(2,1)S(1)}, bf16[288,512]{0,1:T(8,128)(2,1)S(1)}...) fusion(s32[]{:T(128)S(6)} %select_n.188, bf16[256,2304]{1,0:T(8,128)(2,1)} %bitcast.5, ...), kind=kLoop, calls=%fused_computation.64 | loop fusion | flops 3538944 | bytes 4128792 | tf_op jit(solution)/shard_map/dynamic_slice | solution.py:312
  53.3 5.7 %collective-permute-done.9 = bf16[288,512]{1,0:T(8,128)(2,1)S(1)} collective-permute-done((bf16[288,512]{1,0:T(8,128)(2,1)S(1)}, bf16[288,512]{1,0:T(8,128)(2,1)S(1)}, u32[]{:S(2)}, u32[]{:S(2)}) %collective-permute-start.9) | collective-permute-done | bytes 294944 | tf_op jit(solution)/shard_map/ppermute | solution.py:265
  59.0 0.9 collective-permute-done.11
  60.2 1.2 collective-permute-start.14
  61.6 2.2 %collective-permute-start.15 = (bf16[512,512]{1,0:T(8,128)(2,1)S(1)}, bf16[512,512]{1,0:T(8,128)(2,1)S(1)}, u32[]{:S(2)}, u32[]{:S(2)}) collective-permute-start(bf16[512,512]{1,0:T(8,128)(2,1)S(1)} %collective-permute-done.12.refs_0_), channel_id=1, source_target_pairs={{0,2},{2,4},{4,6},{1,3},{3,5},{5,7},{8,10},{10,12},{12,14},{9,11},... | collective-permute-start | bytes 1572872 | tf_op jit(solution)/shard_map/ppermute | solution.py:256
  64.5 2.5 %collective-permute-done.13 = bf16[288,512]{1,0:T(8,128)(2,1)S(1)} collective-permute-done((bf16[288,512]{1,0:T(8,128)(2,1)S(1)}, bf16[288,512]{1,0:T(8,128)(2,1)S(1)}, u32[]{:S(2)}, u32[]{:S(2)}) %collective-permute-start.13) | collective-permute-done | bytes 294944 | tf_op jit(solution)/shard_map/ppermute | solution.py:265
  67.1 3.0 %fusion.2.da = bf16[512,512]{1,0:T(8,128)(2,1)S(1)} fusion(bf16[2304,512]{1,0:T(8,128)(2,1)S(1)} %constant_dynamic-update-slice_fusion, bf16[256,2304]{1,0:T(8,128)(2,1)} %collective-permute-done.6, bf16[256,2304]{1,0:T(8,128)(2,1)} %bitcast.5), kind=kOutput, calls=%fused_computation.29 | convolution fusion | flops 1212940288 | bytes 5242880 | tf_op jit(solution)/shard_map/dot_general | solution.py:26
  70.1 4.8 %collective-permute-done.15.refs_0_ = bf16[512,512]{1,0:T(8,128)(2,1)S(1)} collective-permute-done((bf16[512,512]{1,0:T(8,128)(2,1)S(1)}, bf16[512,512]{1,0:T(8,128)(2,1)S(1)}, u32[]{:S(2)}, u32[]{:S(2)}) %collective-permute-start.15) | collective-permute-done | bytes 524320 | tf_op jit(solution)/shard_map/ppermute | solution.py:256
  75.0 1.2 attend_forward.7
  77.5 0.9 attend_backward.4
  78.5 1.9 %collective-permute-start.20 = (bf16[512,512]{1,0:T(8,128)(2,1)S(1)}, bf16[512,512]{1,0:T(8,128)(2,1)S(1)}, u32[]{:S(2)}, u32[]{:S(2)}) collective-permute-start(bf16[512,512]{1,0:T(8,128)(2,1)S(1)} %get-tuple-element.124), channel_id=1, source_target_pairs={{2,0},{4,2},{6,4},{3,1},{5,3},{7,5},{10,8},{12,10},{14,12},{11,9},... | collective-permute-start | bytes 1572872 | tf_op jit(solution)/shard_map/ppermute | solution.py:259
  80.4 1.4 fusion.37
  81.8 1.1 collective-permute-start.16
  83.6 1.2 collective-permute-start.19
  85.5 1.1 slice.148
  86.6 2.7 %attend_backward.6 = (bf16[512,512]{1,0:T(8,128)(2,1)S(1)}, f32[512,512]{1,0:T(8,128)S(1)}) custom-call(s32[2]{0:T(128)S(1)} %pad_add_fusion.info, bf16[512,512]{1,0:T(8,128)(2,1)S(1)} %maximum_multiply_fusion.q, bf16[512,512]{1,0:T(8,128)(2,1)S(1)} %fusion.2.da, f32[16,512]{1,0:T(8,128)S(1)} %get-tuple-element.113.lse_t, bf16[512,512]{1,0:T(8,128)(2,1)S(1)} %copy-done.1, ...), custom_call_target="tpu_custom_call" | custom-call | flops 1342177280 | bytes 1572864 | tf_op jit(solution)/shard_map/attend_backward/pallas_call | solution.py:214
  89.4 2.6 %attend_backward.7 = (f32[512,512]{1,0:T(8,128)S(1)}, bf16[512,512]{1,0:T(8,128)(2,1)S(1)}) custom-call(s32[2]{0:T(128)S(1)} %pad_add_fusion.info, bf16[512,512]{1,0:T(8,128)(2,1)S(1)} %maximum_multiply_fusion.q, bf16[512,512]{1,0:T(8,128)(2,1)S(1)} %fusion.2.da, f32[16,512]{1,0:T(8,128)S(1)} %get-tuple-element.113.lse_t, ...), custom_call_target="tpu_custom_call" | custom-call | flops 1342177280 | bytes 1572864 | tf_op jit(solution)/shard_map/attend_backward/pallas_call | solution.py:214
  92.0 1.9 %collective-permute-done.18 = bf16[288,512]{1,0:T(8,128)(2,1)S(1)} collective-permute-done((bf16[288,512]{1,0:T(8,128)(2,1)S(1)}, bf16[288,512]{1,0:T(8,128)(2,1)S(1)}, u32[]{:S(2)}, u32[]{:S(2)}) %collective-permute-start.18) | collective-permute-done | bytes 294944 | tf_op jit(solution)/shard_map/ppermute | solution.py:265
  94.6 4.1 %collective-permute-start.24 = (bf16[256,2304]{1,0:T(8,128)(2,1)}, bf16[256,2304]{1,0:T(8,128)(2,1)}, u32[]{:S(2)}, u32[]{:S(2)}) collective-permute-start(bf16[256,2304]{1,0:T(8,128)(2,1)} %slice.148), channel_id=1, source_target_pairs={{0,1},{1,0},{2,3},{3,2},{4,5},{5,4},{6,7},{7,6},{8,9},{9,8},{10,11... | collective-permute-start | bytes 3538952 | tf_op jit(solution)/shard_map/ppermute | solution.py:253
  98.7 1.1 fusion.5
  100.2 0.9 add_convert_fusion.2
  101.1 2.0 %collective-permute-start.25 = (bf16[512,512]{1,0:T(8,128)(2,1)}, bf16[512,512]{1,0:T(8,128)(2,1)}, u32[]{:S(2)}, u32[]{:S(2)}) collective-permute-start(bf16[512,512]{1,0:T(8,128)(2,1)} %add_convert_fusion.2), channel_id=1, source_target_pairs={{2,0},{4,2},{6,4},{3,1},{5,3},{7,5},{10,8},{12,10},{14,12},{11,9},... | collective-permute-start | bytes 1572872 | tf_op jit(solution)/shard_map/ppermute | solution.py:259
  103.2 1.1 fusion.6
  105.8 1.4 collective-permute-done.23
  107.1 1.6 %collective-permute-done.21 = bf16[288,512]{1,0:T(8,128)(2,1)} collective-permute-done((bf16[288,512]{1,0:T(8,128)(2,1)}, bf16[288,512]{1,0:T(8,128)(2,1)}, u32[]{:S(2)}, u32[]{:S(2)}) %collective-permute-start.21) | collective-permute-done | bytes 294944 | tf_op jit(solution)/shard_map/ppermute | solution.py:265
  108.7 4.1 %collective-permute-done.22 = bf16[288,512]{1,0:T(8,128)(2,1)} collective-permute-done((bf16[288,512]{1,0:T(8,128)(2,1)}, bf16[288,512]{1,0:T(8,128)(2,1)}, u32[]{:S(2)}, u32[]{:S(2)}) %collective-permute-start.22) | collective-permute-done | bytes 294944 | tf_op jit(solution)/shard_map/ppermute | solution.py:265
  112.9 4.3 %collective-permute-done.25 = bf16[512,512]{1,0:T(8,128)(2,1)} collective-permute-done((bf16[512,512]{1,0:T(8,128)(2,1)}, bf16[512,512]{1,0:T(8,128)(2,1)}, u32[]{:S(2)}, u32[]{:S(2)}) %collective-permute-start.25) | collective-permute-done | bytes 524320 | tf_op jit(solution)/shard_map/ppermute | solution.py:259
  117.2 1.2 add_convert_fusion.1
  118.4 1.9 %collective-permute-start.26 = (bf16[512,512]{1,0:T(8,128)(2,1)S(1)}, bf16[512,512]{1,0:T(8,128)(2,1)S(1)}, u32[]{:S(2)}, u32[]{:S(2)}) collective-permute-start(bf16[512,512]{1,0:T(8,128)(2,1)S(1)} %add_convert_fusion.1), channel_id=1, source_target_pairs={{2,0},{4,2},{6,4},{3,1},{5,3},{7,5},{10,8},{12,10},{14,12},{11,9},... | collective-permute-start | bytes 1572872 | tf_op jit(solution)/shard_map/ppermute | solution.py:259
  120.4 1.4 fusion.3
  121.8 1.3 fusion.4
  123.5 3.5 %collective-permute-start.27 = (bf16[144,512]{1,0:T(8,128)(2,1)S(1)}, bf16[144,512]{1,0:T(8,128)(2,1)S(1)}, u32[]{:S(2)}, u32[]{:S(2)}) collective-permute-start(bf16[144,512]{1,0:T(8,128)(2,1)S(1)} %get-tuple-element.158), channel_id=1, source_target_pairs={{0,2},{2,4},{4,6},{6,0},{1,3},{3,5},{5,7},{7,1},{8,10},{10,12},{12... | collective-permute-start | bytes 442376 | tf_op jit(solution)/shard_map/ppermute | solution.py:262
  127.0 1.3 collective-permute-start.28
  128.3 1.4 collective-permute-start.29
  129.7 3.2 %fusion.1 = bf16[256,2304]{1,0:T(8,128)(2,1)} fusion(f32[512,2304]{1,0:T(8,128)} %copy-done.6, bf16[256,2304]{1,0:T(8,128)(2,1)} %collective-permute-done.24), kind=kLoop, calls=%fused_computation.19 | loop fusion | flops 1769472 | bytes 4718592 | tf_op jit(solution)/shard_map/convert_element_type | solution.py:385
  132.9 0.9 maximum_select_fusion.1
  133.8 8.7 %collective-permute-done.28 = bf16[144,512]{1,0:T(8,128)(2,1)S(1)} collective-permute-done((bf16[144,512]{1,0:T(8,128)(2,1)S(1)}, bf16[144,512]{1,0:T(8,128)(2,1)S(1)}, u32[]{:S(2)}, u32[]{:S(2)}) %collective-permute-start.28) | collective-permute-done | bytes 147488 | tf_op jit(solution)/shard_map/ppermute | solution.py:262
  142.6 5.4 %collective-permute-done.29 = bf16[144,512]{1,0:T(8,128)(2,1)S(1)} collective-permute-done((bf16[144,512]{1,0:T(8,128)(2,1)S(1)}, bf16[144,512]{1,0:T(8,128)(2,1)S(1)}, u32[]{:S(2)}, u32[]{:S(2)}) %collective-permute-start.29) | collective-permute-done | bytes 147488 | tf_op jit(solution)/shard_map/ppermute | solution.py:262
  148.2 1.4 collective-permute-start.30
  149.9 1.3 collective-permute-done.31
  152.0 0.9 maximum_select_fusion.3
  (84 shorter events, 12.0 us)
Async XLA Ops:
  0.6 9.9 %copy-start.12 = (bf16[72,1024]{1,0:T(8,128)(2,1)S(1)}, bf16[72,1024]{1,0:T(8,128)(2,1)}, u32[]{:S(2)}) copy-start(bf16[72,1024]{1,0:T(8,128)(2,1)} %param.8) | copy-start | bytes 442372
  0.6 8.6 %copy-start.8 = (bf16[1,256,1024]{2,1,0:T(8,128)(2,1)S(1)}, bf16[1,256,1024]{2,1,0:T(8,128)(2,1)}, u32[]{:S(2)}) copy-start(bf16[1,256,1024]{2,1,0:T(8,128)(2,1)} %param.5) | copy-start | bytes 1572868
  2.7 4.5 %collective-permute-start = (bf16[256,512]{1,0:T(8,128)(2,1)S(1)}, bf16[256,512]{1,0:T(8,128)(2,1)S(1)}, u32[]{:S(2)}, u32[]{:S(2)}) collective-permute-start(bf16[256,512]{1,0:T(8,128)(2,1)S(1)} %pad_maximum_fusion.5), channel_id=1, source_target_pairs={{0,1},{1,0},{2,3},{3,2},{4,5},{5,4},{6,7},{7,6},{8,9},{9,8},{10,11... | collective-permute-start | bytes 786440 | tf_op jit(solution)/shard_map/ppermute | solution.py:253
  3.5 11.1 %collective-permute-start.3 = (bf16[72,1024]{1,0:T(8,128)(2,1)}, bf16[72,1024]{1,0:T(8,128)(2,1)S(1)}, u32[]{:S(2)}, u32[]{:S(2)}) collective-permute-start(bf16[72,1024]{1,0:T(8,128)(2,1)} %param.8), channel_id=1, source_target_pairs={{0,2},{2,4},{4,6},{6,0},{1,3},{3,5},{5,7},{7,1},{8,10},{10,12},{12... | collective-permute-start | bytes 442376 | tf_op jit(solution)/shard_map/ppermute | solution.py:262
  4.8 13.1 %collective-permute-start.4 = (bf16[72,1024]{1,0:T(8,128)(2,1)}, bf16[72,1024]{1,0:T(8,128)(2,1)}, u32[]{:S(2)}, u32[]{:S(2)}) collective-permute-start(bf16[72,1024]{1,0:T(8,128)(2,1)} %param.8), channel_id=1, source_target_pairs={{0,4},{2,6},{4,0},{6,2},{1,5},{3,7},{5,1},{7,3},{8,12},{10,14},{12... | collective-permute-start | bytes 442376 | tf_op jit(solution)/shard_map/ppermute | solution.py:262
  5.8 14.1 %collective-permute-start.5 = (bf16[72,1024]{1,0:T(8,128)(2,1)}, bf16[72,1024]{1,0:T(8,128)(2,1)}, u32[]{:S(2)}, u32[]{:S(2)}) collective-permute-start(bf16[72,1024]{1,0:T(8,128)(2,1)} %param.8), channel_id=1, source_target_pairs={{0,6},{2,0},{4,2},{6,4},{1,7},{3,1},{5,3},{7,5},{8,14},{10,8},{12,... | collective-permute-start | bytes 442376 | tf_op jit(solution)/shard_map/ppermute | solution.py:262
  7.3 21.7 %collective-permute-start.1 = (bf16[512,512]{1,0:T(8,128)(2,1)S(1)}, bf16[512,512]{1,0:T(8,128)(2,1)S(1)}, u32[]{:S(2)}, u32[]{:S(2)}) collective-permute-start(bf16[512,512]{1,0:T(8,128)(2,1)S(1)} %pad_maximum_fusion.4.refs_0_), channel_id=1, source_target_pairs={{0,2},{2,4},{4,6},{1,3},{3,5},{5,7},{8,10},{10,12},{12,14},{9,11},... | collective-permute-start | bytes 1572872 | tf_op jit(solution)/shard_map/ppermute | solution.py:256
  9.3 2.2 %collective-permute-start.2 = (bf16[256,512]{1,0:T(8,128)(2,1)S(1)}, bf16[256,512]{1,0:T(8,128)(2,1)S(1)}, u32[]{:S(2)}, u32[]{:S(2)}) collective-permute-start(bf16[256,512]{1,0:T(8,128)(2,1)S(1)} %get-tuple-element.169), channel_id=1, source_target_pairs={{0,1},{1,0},{2,3},{3,2},{4,5},{5,4},{6,7},{7,6},{8,9},{9,8},{10,11... | collective-permute-start | bytes 786440 | tf_op jit(solution)/shard_map/ppermute | solution.py:253
  11.5 35.8 %collective-permute-start.6 = (bf16[256,2304]{1,0:T(8,128)(2,1)}, bf16[256,2304]{1,0:T(8,128)(2,1)}, u32[]{:S(2)}, u32[]{:S(2)}) collective-permute-start(bf16[256,2304]{1,0:T(8,128)(2,1)} %bitcast.5), channel_id=1, source_target_pairs={{0,1},{1,0},{2,3},{3,2},{4,5},{5,4},{6,7},{7,6},{8,9},{9,8},{10,11... | collective-permute-start | bytes 3538952 | tf_op jit(solution)/shard_map/ppermute | solution.py:253
  13.8 0.8 copy-start.4
  14.6 18.0 %copy-start.2 = (f32[512,256]{1,0:T(8,128)}, f32[512,256]{1,0:T(8,128)S(1)}, u32[]{:S(2)}) copy-start(f32[512,256]{1,0:T(8,128)S(1)} %get-tuple-element.85.refs_1_) | copy-start | bytes 1572868
  29.0 14.1 %copy-start = (bf16[512,512]{1,0:T(8,128)(2,1)}, bf16[512,512]{1,0:T(8,128)(2,1)S(1)}, u32[]{:S(2)}) copy-start(bf16[512,512]{1,0:T(8,128)(2,1)S(1)} %collective-permute-done.1.refs_0_) | copy-start | bytes 1572868
  31.8 11.3 %collective-permute-start.7 = (bf16[4,72,512]{2,1,0:T(8,128)(2,1)}, bf16[4,72,512]{2,1,0:T(8,128)(2,1)}, u32[]{:S(2)}, u32[]{:S(2)}) collective-permute-start(bf16[4,72,512]{2,1,0:T(8,128)(2,1)} %get-tuple-element.163), channel_id=1, source_target_pairs={{0,1},{1,0},{2,3},{3,2},{4,5},{5,4},{6,7},{7,6},{8,9},{9,8},{10,11... | collective-permute-start | bytes 884744 | tf_op jit(solution)/shard_map/ppermute | solution.py:253
  32.6 20.7 %collective-permute-start.12 = (bf16[512,512]{1,0:T(8,128)(2,1)S(1)}, bf16[512,512]{1,0:T(8,128)(2,1)S(1)}, u32[]{:S(2)}, u32[]{:S(2)}) collective-permute-start(bf16[512,512]{1,0:T(8,128)(2,1)S(1)} %collective-permute-done.1.refs_0_), channel_id=1, source_target_pairs={{0,2},{2,4},{4,6},{1,3},{3,5},{5,7},{8,10},{10,12},{12,14},{9,11},... | collective-permute-start | bytes 1572872 | tf_op jit(solution)/shard_map/ppermute | solution.py:256
  36.7 1.0 copy-start.3
  37.8 1.0 copy-start.5
  44.3 9.0 %collective-permute-start.8 = (bf16[288,512]{1,0:T(8,128)(2,1)S(1)}, bf16[288,512]{1,0:T(8,128)(2,1)S(1)}, u32[]{:S(2)}, u32[]{:S(2)}) collective-permute-start(bf16[288,512]{1,0:T(8,128)(2,1)S(1)} %bitcast.71), channel_id=1, source_target_pairs={{0,8},{8,0},{16,24},{24,16},{1,9},{9,1},{17,25},{25,17},{2,10},{10... | collective-permute-start | bytes 884744 | tf_op jit(solution)/shard_map/ppermute | solution.py:265
  45.6 13.4 %collective-permute-start.10 = (bf16[288,512]{1,0:T(8,128)(2,1)S(1)}, bf16[288,512]{1,0:T(8,128)(2,1)S(1)}, u32[]{:S(2)}, u32[]{:S(2)}) collective-permute-start(bf16[288,512]{1,0:T(8,128)(2,1)S(1)} %bitcast.72), channel_id=1, source_target_pairs={{0,16},{8,24},{16,0},{24,8},{1,17},{9,25},{17,1},{25,9},{2,18},{10... | collective-permute-start | bytes 884744 | tf_op jit(solution)/shard_map/ppermute | solution.py:265
  46.8 12.2 %collective-permute-start.9 = (bf16[288,512]{1,0:T(8,128)(2,1)S(1)}, bf16[288,512]{1,0:T(8,128)(2,1)S(1)}, u32[]{:S(2)}, u32[]{:S(2)}) collective-permute-start(bf16[288,512]{1,0:T(8,128)(2,1)S(1)} %bitcast.69), channel_id=1, source_target_pairs={{0,8},{8,0},{16,24},{24,16},{1,9},{9,1},{17,25},{25,17},{2,10},{10... | collective-permute-start | bytes 884744 | tf_op jit(solution)/shard_map/ppermute | solution.py:265
  47.3 12.6 %collective-permute-start.11 = (bf16[288,512]{1,0:T(8,128)(2,1)S(1)}, bf16[288,512]{1,0:T(8,128)(2,1)S(1)}, u32[]{:S(2)}, u32[]{:S(2)}) collective-permute-start(bf16[288,512]{1,0:T(8,128)(2,1)S(1)} %bitcast.70), channel_id=1, source_target_pairs={{0,16},{8,24},{16,0},{24,8},{1,17},{9,25},{17,1},{25,9},{2,18},{10... | collective-permute-start | bytes 884744 | tf_op jit(solution)/shard_map/ppermute | solution.py:265
  59.9 7.1 %collective-permute-start.13 = (bf16[288,512]{1,0:T(8,128)(2,1)S(1)}, bf16[288,512]{1,0:T(8,128)(2,1)S(1)}, u32[]{:S(2)}, u32[]{:S(2)}) collective-permute-start(bf16[288,512]{1,0:T(8,128)(2,1)S(1)} %collective-permute-done.10), channel_id=1, source_target_pairs={{0,8},{8,0},{16,24},{24,16},{1,9},{9,1},{17,25},{25,17},{2,10},{10... | collective-permute-start | bytes 884744 | tf_op jit(solution)/shard_map/ppermute | solution.py:265
  60.2 6.9 %collective-permute-start.14 = (bf16[288,512]{1,0:T(8,128)(2,1)S(1)}, bf16[288,512]{1,0:T(8,128)(2,1)S(1)}, u32[]{:S(2)}, u32[]{:S(2)}) collective-permute-start(bf16[288,512]{1,0:T(8,128)(2,1)S(1)} %collective-permute-done.9), channel_id=1, source_target_pairs={{0,16},{8,24},{16,0},{24,8},{1,17},{9,25},{17,1},{25,9},{2,18},{10... | collective-permute-start | bytes 884744 | tf_op jit(solution)/shard_map/ppermute | solution.py:265
  61.6 13.4 %collective-permute-start.15 = (bf16[512,512]{1,0:T(8,128)(2,1)S(1)}, bf16[512,512]{1,0:T(8,128)(2,1)S(1)}, u32[]{:S(2)}, u32[]{:S(2)}) collective-permute-start(bf16[512,512]{1,0:T(8,128)(2,1)S(1)} %collective-permute-done.12.refs_0_), channel_id=1, source_target_pairs={{0,2},{2,4},{4,6},{1,3},{3,5},{5,7},{8,10},{10,12},{12,14},{9,11},... | collective-permute-start | bytes 1572872 | tf_op jit(solution)/shard_map/ppermute | solution.py:256
  78.5 16.2 %collective-permute-start.20 = (bf16[512,512]{1,0:T(8,128)(2,1)S(1)}, bf16[512,512]{1,0:T(8,128)(2,1)S(1)}, u32[]{:S(2)}, u32[]{:S(2)}) collective-permute-start(bf16[512,512]{1,0:T(8,128)(2,1)S(1)} %get-tuple-element.124), channel_id=1, source_target_pairs={{2,0},{4,2},{6,4},{3,1},{5,3},{7,5},{10,8},{12,10},{14,12},{11,9},... | collective-permute-start | bytes 1572872 | tf_op jit(solution)/shard_map/ppermute | solution.py:259
  81.8 3.7 %copy-start.6 = (f32[512,2304]{1,0:T(8,128)}, f32[512,2304]{1,0:T(8,128)S(1)}, u32[]{:S(2)}) copy-start(f32[512,2304]{1,0:T(8,128)S(1)} %fusion.37) | copy-start | bytes 14155780
  81.8 10.2 %collective-permute-start.16 = (bf16[288,512]{1,0:T(8,128)(2,1)S(1)}, bf16[288,512]{1,0:T(8,128)(2,1)S(1)}, u32[]{:S(2)}, u32[]{:S(2)}) collective-permute-start(bf16[288,512]{1,0:T(8,128)(2,1)S(1)} %convolution_convert_fusion.1), channel_id=1, source_target_pairs={{0,8},{8,0},{16,24},{24,16},{1,9},{9,1},{17,25},{25,17},{2,10},{10... | collective-permute-start | bytes 884744 | tf_op jit(solution)/shard_map/ppermute | solution.py:265
  83.0 9.0 %collective-permute-start.17 = (bf16[288,512]{1,0:T(8,128)(2,1)S(1)}, bf16[288,512]{1,0:T(8,128)(2,1)S(1)}, u32[]{:S(2)}, u32[]{:S(2)}) collective-permute-start(bf16[288,512]{1,0:T(8,128)(2,1)S(1)} %convolution_convert_fusion), channel_id=1, source_target_pairs={{0,16},{8,24},{16,0},{24,8},{1,17},{9,25},{17,1},{25,9},{2,18},{10... | collective-permute-start | bytes 884744 | tf_op jit(solution)/shard_map/ppermute | solution.py:265
  83.2 10.7 %collective-permute-start.18 = (bf16[288,512]{1,0:T(8,128)(2,1)S(1)}, bf16[288,512]{1,0:T(8,128)(2,1)S(1)}, u32[]{:S(2)}, u32[]{:S(2)}) collective-permute-start(bf16[288,512]{1,0:T(8,128)(2,1)S(1)} %convolution_convert_fusion.3), channel_id=1, source_target_pairs={{0,8},{8,0},{16,24},{24,16},{1,9},{9,1},{17,25},{25,17},{2,10},{10... | collective-permute-start | bytes 884744 | tf_op jit(solution)/shard_map/ppermute | solution.py:265
  83.6 11.0 %collective-permute-start.19 = (bf16[288,512]{1,0:T(8,128)(2,1)S(1)}, bf16[288,512]{1,0:T(8,128)(2,1)S(1)}, u32[]{:S(2)}, u32[]{:S(2)}) collective-permute-start(bf16[288,512]{1,0:T(8,128)(2,1)S(1)} %convolution_convert_fusion.2), channel_id=1, source_target_pairs={{0,16},{8,24},{16,0},{24,8},{1,17},{9,25},{17,1},{25,9},{2,18},{10... | collective-permute-start | bytes 884744 | tf_op jit(solution)/shard_map/ppermute | solution.py:265
  85.5 1.1 copy-start.1
  93.9 11.3 %copy-start.11 = (bf16[288,512]{1,0:T(8,128)(2,1)}, bf16[288,512]{1,0:T(8,128)(2,1)S(1)}, u32[]{:S(2)}) copy-start(bf16[288,512]{1,0:T(8,128)(2,1)S(1)} %collective-permute-done.18) | copy-start | bytes 884740
  94.6 10.6 %copy-start.9 = (bf16[288,512]{1,0:T(8,128)(2,1)}, bf16[288,512]{1,0:T(8,128)(2,1)S(1)}, u32[]{:S(2)}) copy-start(bf16[288,512]{1,0:T(8,128)(2,1)S(1)} %collective-permute-done.19) | copy-start | bytes 884740
  94.6 22.6 %collective-permute-start.24 = (bf16[256,2304]{1,0:T(8,128)(2,1)}, bf16[256,2304]{1,0:T(8,128)(2,1)}, u32[]{:S(2)}, u32[]{:S(2)}) collective-permute-start(bf16[256,2304]{1,0:T(8,128)(2,1)} %slice.148), channel_id=1, source_target_pairs={{0,1},{1,0},{2,3},{3,2},{4,5},{5,4},{6,7},{7,6},{8,9},{9,8},{10,11... | collective-permute-start | bytes 3538952 | tf_op jit(solution)/shard_map/ppermute | solution.py:253
  99.8 8.9 %collective-permute-start.21 = (bf16[288,512]{1,0:T(8,128)(2,1)}, bf16[288,512]{1,0:T(8,128)(2,1)}, u32[]{:S(2)}, u32[]{:S(2)}) collective-permute-start(bf16[288,512]{1,0:T(8,128)(2,1)} %fusion.5), channel_id=1, source_target_pairs={{0,8},{8,0},{16,24},{24,16},{1,9},{9,1},{17,25},{25,17},{2,10},{10... | collective-permute-start | bytes 884744 | tf_op jit(solution)/shard_map/ppermute | solution.py:265
  101.1 19.2 %copy-start.7 = (bf16[288,512]{0,1:T(8,128)(2,1)S(1)}, bf16[288,512]{0,1:T(8,128)(2,1)}, u32[]{:S(2)}) copy-start(bf16[288,512]{0,1:T(8,128)(2,1)} %get-tuple-element.136) | copy-start | bytes 884740
  101.1 16.1 %collective-permute-start.25 = (bf16[512,512]{1,0:T(8,128)(2,1)}, bf16[512,512]{1,0:T(8,128)(2,1)}, u32[]{:S(2)}, u32[]{:S(2)}) collective-permute-start(bf16[512,512]{1,0:T(8,128)(2,1)} %add_convert_fusion.2), channel_id=1, source_target_pairs={{2,0},{4,2},{6,4},{3,1},{5,3},{7,5},{10,8},{12,10},{14,12},{11,9},... | collective-permute-start | bytes 1572872 | tf_op jit(solution)/shard_map/ppermute | solution.py:259
  104.2 8.6 %collective-permute-start.22 = (bf16[288,512]{1,0:T(8,128)(2,1)}, bf16[288,512]{1,0:T(8,128)(2,1)}, u32[]{:S(2)}, u32[]{:S(2)}) collective-permute-start(bf16[288,512]{1,0:T(8,128)(2,1)} %fusion.6), channel_id=1, source_target_pairs={{0,16},{8,24},{16,0},{24,8},{1,17},{9,25},{17,1},{25,9},{2,18},{10... | collective-permute-start | bytes 884744 | tf_op jit(solution)/shard_map/ppermute | solution.py:265
  105.2 1.9 %collective-permute-start.23 = (bf16[256,512]{1,0:T(8,128)(2,1)}, bf16[256,512]{1,0:T(8,128)(2,1)S(1)}, u32[]{:S(2)}, u32[]{:S(2)}) collective-permute-start(bf16[256,512]{1,0:T(8,128)(2,1)} %get-tuple-element.167), channel_id=1, source_target_pairs={{0,1},{1,0},{2,3},{3,2},{4,5},{5,4},{6,7},{7,6},{8,9},{9,8},{10,11... | collective-permute-start | bytes 786440 | tf_op jit(solution)/shard_map/ppermute | solution.py:253
  105.8 16.0 %copy-start.10 = (bf16[288,512]{1,0:T(8,128)(2,1)S(1)}, bf16[288,512]{1,0:T(8,128)(2,1)}, u32[]{:S(2)}) copy-start(bf16[288,512]{1,0:T(8,128)(2,1)} %copy-done.9) | copy-start | bytes 884740
  118.4 29.5 %collective-permute-start.26 = (bf16[512,512]{1,0:T(8,128)(2,1)S(1)}, bf16[512,512]{1,0:T(8,128)(2,1)S(1)}, u32[]{:S(2)}, u32[]{:S(2)}) collective-permute-start(bf16[512,512]{1,0:T(8,128)(2,1)S(1)} %add_convert_fusion.1), channel_id=1, source_target_pairs={{2,0},{4,2},{6,4},{3,1},{5,3},{7,5},{10,8},{12,10},{14,12},{11,9},... | collective-permute-start | bytes 1572872 | tf_op jit(solution)/shard_map/ppermute | solution.py:259
  123.5 10.3 %collective-permute-start.27 = (bf16[144,512]{1,0:T(8,128)(2,1)S(1)}, bf16[144,512]{1,0:T(8,128)(2,1)S(1)}, u32[]{:S(2)}, u32[]{:S(2)}) collective-permute-start(bf16[144,512]{1,0:T(8,128)(2,1)S(1)} %get-tuple-element.158), channel_id=1, source_target_pairs={{0,2},{2,4},{4,6},{6,0},{1,3},{3,5},{5,7},{7,1},{8,10},{10,12},{12... | collective-permute-start | bytes 442376 | tf_op jit(solution)/shard_map/ppermute | solution.py:262
  127.0 15.5 %collective-permute-start.28 = (bf16[144,512]{1,0:T(8,128)(2,1)S(1)}, bf16[144,512]{1,0:T(8,128)(2,1)S(1)}, u32[]{:S(2)}, u32[]{:S(2)}) collective-permute-start(bf16[144,512]{1,0:T(8,128)(2,1)S(1)} %get-tuple-element.159), channel_id=1, source_target_pairs={{0,4},{2,6},{4,0},{6,2},{1,5},{3,7},{5,1},{7,3},{8,12},{10,14},{12... | collective-permute-start | bytes 442376 | tf_op jit(solution)/shard_map/ppermute | solution.py:262
  128.3 19.7 %collective-permute-start.29 = (bf16[144,512]{1,0:T(8,128)(2,1)S(1)}, bf16[144,512]{1,0:T(8,128)(2,1)S(1)}, u32[]{:S(2)}, u32[]{:S(2)}) collective-permute-start(bf16[144,512]{1,0:T(8,128)(2,1)S(1)} %get-tuple-element.157), channel_id=1, source_target_pairs={{0,6},{2,0},{4,2},{6,4},{1,7},{3,1},{5,3},{7,5},{8,14},{10,8},{12,... | collective-permute-start | bytes 442376 | tf_op jit(solution)/shard_map/ppermute | solution.py:262
  148.2 3.8 %collective-permute-start.30 = (bf16[256,512]{1,0:T(8,128)(2,1)S(1)}, bf16[256,512]{1,0:T(8,128)(2,1)S(1)}, u32[]{:S(2)}, u32[]{:S(2)}) collective-permute-start(bf16[256,512]{1,0:T(8,128)(2,1)S(1)} %slice.114), channel_id=1, source_target_pairs={{0,1},{1,0},{2,3},{3,2},{4,5},{5,4},{6,7},{7,6},{8,9},{9,8},{10,11... | collective-permute-start | bytes 786440 | tf_op jit(solution)/shard_map/ppermute | solution.py:253
  149.8 1.4 collective-permute-start.31

commit v5 on v4

--- a/solution.py
+++ b/solution.py
@@ -20,6 +20,7 @@
 BF16 = jnp.bfloat16
 NT = (((1,), (1,)), ((), ()))
 TN = (((0,), (0,)), ((), ()))
+FILLER = pl.CostEstimate(flops=1, bytes_accessed=1, transcendentals=0)
 
 
 def dot(a, b, dims=(((1,), (0,)), ((), ()))):
@@ -37,9 +38,7 @@
     return (gap <= 0) & (gap > -WINDOW)
 
 
-def forward_kernel(steps, rows, first, last, info, q, *refs):
-    chunks = refs[: len(steps)]
-    refs = refs[len(steps) :]
+def forward_kernel(step, rows, first, last, info, q, kv, *refs):
     if not first:
         m_in, l_in, acc_in = refs[:3]
         refs = refs[3:]
@@ -48,80 +47,74 @@
     else:
         m_s, l_s, acc_s = refs
     chip, core = info[0], info[1]
-    if not first:
-        m_s[...] = m_in[...]
-        l_s[...] = l_in[...]
-        acc_s[...] = acc_in[...]
-    for at, step in enumerate(steps):
-        mask = admitted(step, rows, core, 0)
-
-        def block(at=at, step=step, mask=mask):
-            keys = chunks[at][:, :HD]
-            vals = chunks[at][:, HD:]
-            for h in range(GROUPS):
-                cols = slice(h * HD, (h + 1) * HD)
-                stat = slice(h * LANES, (h + 1) * LANES)
-                s = dot(q[:, cols], keys, NT)
-                if mask is not None:
-                    s = jnp.where(mask, s, NEG)
-                top = jnp.max(s, axis=1, keepdims=True)
-                if step == 0:
-                    p = jnp.exp(s - top)
-                    total = jnp.sum(p, axis=1, keepdims=True)
-                    acc_s[:, cols] = dot(p.astype(BF16), vals)
-                else:
-                    before = m_s[:, stat][:, :1]
-                    top = jnp.maximum(top, before)
-                    p = jnp.exp(s - top)
-                    keep = jnp.exp(before - top)
-                    total = keep * l_s[:, stat][:, :1] + jnp.sum(p, axis=1, keepdims=True)
-                    acc_s[:, cols] = keep * acc_s[:, cols] + dot(p.astype(BF16), vals)
-                m_s[:, stat] = jnp.broadcast_to(top, (rows, LANES))
-                l_s[:, stat] = jnp.broadcast_to(total, (rows, LANES))
-
-        if step == 0:
-            block()
-        else:
-            pl.when(chip >= step)(block)
-    if last:
+    mask = admitted(step, rows, core, 1)
+
+    def block():
+        keys = kv[:, :HD]
+        vals_t = jnp.transpose(kv[:, HD:])
         for h in range(GROUPS):
             cols = slice(h * HD, (h + 1) * HD)
-            stat = slice(h * LANES, (h + 1) * LANES)
-            total = l_s[:, stat]
-            out[:, cols] = (acc_s[:, cols] / total[:, :1]).astype(BF16)
-            lse = m_s[:, stat] + jnp.log(total)
-            lse_t[h * 8 : (h + 1) * 8, :] = jnp.transpose(lse)[:8, :]
-
-
-def forward(info, q, chunks, steps, state, last):
+            stat = slice(h * 8, h * 8 + 1)
+            whole = slice(h * 8, (h + 1) * 8)
+            s = dot(keys, q[:, cols], NT)
+            if mask is not None:
+                s = jnp.where(mask, s, NEG)
+            top = jnp.max(s, axis=0, keepdims=True)
+            if first:
+                p = jnp.exp(s - top)
+                total = jnp.sum(p, axis=0, keepdims=True)
+                acc_s[cols, :] = dot(vals_t, p.astype(BF16))
+            else:
+                before = m_in[stat, :]
+                top = jnp.maximum(top, before)
+                p = jnp.exp(s - top)
+                keep = jnp.exp(before - top)
+                total = keep * l_in[stat, :] + jnp.sum(p, axis=0, keepdims=True)
+                acc_s[cols, :] = keep * acc_in[cols, :] + dot(vals_t, p.astype(BF16))
+            m_s[whole, :] = jnp.broadcast_to(top, (8, rows))
+            l_s[whole, :] = jnp.broadcast_to(total, (8, rows))
+
+    if first:
+        block()
+    else:
+
+        def keep_all():
+            m_s[...] = m_in[...]
+            l_s[...] = l_in[...]
+            acc_s[...] = acc_in[...]
+
+        pl.when(chip >= step)(block)
+        pl.when(chip < step)(keep_all)
+    if last:
+        for h in range(GROUPS):
+            cols = slice(h * HD, (h + 1) * HD)
+            total = l_s[h * 8 : h * 8 + 1, :]
+            out[:, cols] = jnp.transpose(acc_s[cols, :] / total).astype(BF16)
+        lse_t[...] = m_s[...] + jnp.log(l_s[...])
+
+
+def forward(info, q, kv, step, state, last):
     rows = q.shape[0]
     first = state is None
-    stat = jax.ShapeDtypeStruct((rows, GROUPS * LANES), F32)
-    acc = jax.ShapeDtypeStruct((rows, GROUPS * HD), F32)
+    stat = jax.ShapeDtypeStruct((GROUPS * 8, rows), F32)
+    acc = jax.ShapeDtypeStruct((GROUPS * HD, rows), F32)
     vmem = pl.BlockSpec(memory_space=pltpu.VMEM)
     smem = pl.BlockSpec(memory_space=pltpu.SMEM)
     scratch = []
     if last:
-        outs = (
-            jax.ShapeDtypeStruct((rows, GROUPS * HD), BF16),
-            jax.ShapeDtypeStruct((GROUPS * 8, rows), F32),
-        )
+        outs = (jax.ShapeDtypeStruct((rows, GROUPS * HD), BF16), stat)
         scratch = [pltpu.VMEM(s.shape, F32) for s in (stat, stat, acc)]
     else:
         outs = (stat, stat, acc)
-    args = [info, q, *chunks] + ([] if first else list(state))
+    args = [info, q, kv] + ([] if first else list(state))
     return pl.pallas_call(
-        functools.partial(forward_kernel, steps, rows, first, last),
+        functools.partial(forward_kernel, step, rows, first, last),
         out_shape=outs,
         in_specs=[smem] + [vmem] * (len(args) - 1),
         out_specs=tuple(vmem for _ in outs),
         scratch_shapes=scratch,
-        cost_estimate=pl.CostEstimate(
-            flops=len(steps) * GROUPS * rows * rows * HD * 4,
-            bytes_accessed=4 * rows * rows * len(steps),
-            transcendentals=len(steps) * GROUPS * rows * rows,
-        ),
-        compiler_params=pltpu.CompilerParams(vmem_limit_bytes=32 * 1024 * 1024),
+        cost_estimate=FILLER,
+        compiler_params=pltpu.CompilerParams(vmem_limit_bytes=16 * 1024 * 1024),
         name="attend_forward",
     )(*args)
 
@@ -160,6 +153,7 @@
 
         def block(at=at, mask=mask):
             keys = chunks[at][:, :HD]
+            keys_t = jnp.transpose(keys)
             vals = chunks[at][:, HD:]
             for h in range(GROUPS):
                 cols = slice(h * HD, (h + 1) * HD)
@@ -173,7 +167,7 @@
                 ds = (p * (dp - delta_t[h * 8 : h * 8 + 1, :])).astype(BF16)
                 dk = dot(ds, qh)
                 dv = dot(p.astype(BF16), dah)
-                dq_s[:, cols] += dot(ds, keys, TN)
+                dq_s[cols, :] += dot(keys_t, ds)
                 if h == 0:
                     dk_sum, dv_sum = dk, dv
                 else:
@@ -191,7 +185,9 @@
             pl.when(chip >= step)(block)
             pl.when(chip < step)(blank)
     if last:
-        dq_out[...] = (dq_s[...] * HD ** (-0.5)).astype(BF16)
+        for h in range(GROUPS):
+            cols = slice(h * HD, (h + 1) * HD)
+            dq_out[:, cols] = jnp.transpose(dq_s[cols, :] * HD ** (-0.5)).astype(BF16)
 
 
 def backward(info, q, da, lse_t, chunks, steps, att, carried, last):
@@ -200,6 +196,7 @@
     vmem = pl.BlockSpec(memory_space=pltpu.VMEM)
     smem = pl.BlockSpec(memory_space=pltpu.SMEM)
     wide = (rows, GROUPS * HD)
+    tall = (GROUPS * HD, rows)
     outs = [jax.ShapeDtypeStruct((rows, 2 * HD), F32 if s == 0 else BF16) for s in steps]
     if last:
         outs.append(jax.ShapeDtypeStruct(wide, BF16))
@@ -207,9 +204,9 @@
         outs.append(jax.ShapeDtypeStruct((GROUPS * 8, rows), F32))
     scratch = []
     if last:
-        scratch = [pltpu.VMEM(wide, F32)]
-    else:
-        outs.append(jax.ShapeDtypeStruct(wide, F32))
+        scratch = [pltpu.VMEM(tall, F32)]
+    else:
+        outs.append(jax.ShapeDtypeStruct(tall, F32))
     args = [info, q, da, lse_t, *chunks] + ([att] if first else list(carried))
     return pl.pallas_call(
         functools.partial(backward_kernel, steps, rows, first, last),
@@ -217,14 +214,61 @@
         in_specs=[smem] + [vmem] * (len(args) - 1),
         out_specs=tuple(vmem for _ in outs),
         scratch_shapes=scratch,
-        cost_estimate=pl.CostEstimate(
-            flops=len(steps) * GROUPS * rows * rows * HD * 10,
-            bytes_accessed=6 * rows * rows * len(steps),
-            transcendentals=len(steps) * GROUPS * rows * rows,
-        ),
-        compiler_params=pltpu.CompilerParams(vmem_limit_bytes=32 * 1024 * 1024),
+        cost_estimate=FILLER,
+        compiler_params=pltpu.CompilerParams(vmem_limit_bytes=16 * 1024 * 1024),
         name="attend_backward",
     )(*args)
+
+
+def product_kernel(x, w, *outs):
+    result = dot(x[...], w[...], NT if len(outs) == 2 else (((1,), (0,)), ((), ())))
+    if len(outs) == 2:
+        half = result.shape[0] // 2
+        outs[0][...] = result[:half]
+        outs[1][...] = result[half:].astype(BF16)
+    else:
+        outs[0][...] = result
+
+
+def layer_product(att, weight):
+    rows, depth = att.shape
+    features = weight.shape[0]
+    wide = 256
+    block = pl.BlockSpec((rows // 2, wide), lambda i: (0, i))
+    return pl.pallas_call(
+        product_kernel,
+        grid=(features // wide,),
+        out_shape=(
+            jax.ShapeDtypeStruct((rows // 2, features), F32),
+            jax.ShapeDtypeStruct((rows // 2, features), BF16),
+        ),
+        in_specs=[
+            pl.BlockSpec((rows, depth), lambda i: (0, 0)),
+            pl.BlockSpec((wide, depth), lambda i: (i, 0)),
+        ],
+        out_specs=(block, block),
+        cost_estimate=FILLER,
+        compiler_params=pltpu.CompilerParams(vmem_limit_bytes=16 * 1024 * 1024),
+        name="layer_product",
+    )(att, weight)
+
+
+def strip_product(strips, att):
+    rows, depth = strips.shape
+    tall = rows // 4
+    return pl.pallas_call(
+        product_kernel,
+        grid=(4,),
+        out_shape=jax.ShapeDtypeStruct((rows, att.shape[1]), F32),
+        in_specs=[
+            pl.BlockSpec((tall, depth), lambda i: (i, 0)),
+            pl.BlockSpec(att.shape, lambda i: (0, 0)),
+        ],
+        out_specs=pl.BlockSpec((tall, att.shape[1]), lambda i: (i, 0)),
+        cost_estimate=FILLER,
+        compiler_params=pltpu.CompilerParams(vmem_limit_bytes=16 * 1024 * 1024),
+        name="strip_product",
+    )(strips, att)
 
 
 def on_device(queries, key_rows, values, out_weight, out_grad):
@@ -279,8 +323,8 @@
     kv = jnp.concatenate([kv, kv_theirs], 0)
     hop = up(kv, 1)
     q = jnp.concatenate([own(q0), swap(other(q0))], 0) * jnp.asarray(HD ** (-0.5), BF16)
-    state = forward(info, q, [kv], (0,), None, False)
-    hop, q, state, *moved = together((hop, q, state, *moved))
+    state = forward(info, q, kv, 0, None, False)
+    hop, q, state, grad_theirs, *moved = together((hop, q, state, swap(g0), *moved))
     chunks = [kv, hop]
 
     piece = out_weight.shape[0]
@@ -297,25 +341,30 @@
     ours = ours.reshape(chips * part, ours.shape[-1])
     share = ours.shape[0]
     half = share // 2
+    ours, *state = together((ours, *state))
 
     lower, upper = ours[:half], ours[half:]
     hop = up(hop, 1)
-    state = forward(info, q, chunks[1:2], (1,), state, False)
+    state = forward(info, q, chunks[1], 1, state, False)
     *by_plane, hop, state = together(
         (across(lower, 1), across(upper, 1), across(lower, 2), across(upper, 2), hop, state)
     )
     chunks.append(hop)
     diagonal = [across(by_plane[2], 1), across(by_plane[1], 2)]
-    grad = jnp.concatenate([g0, swap(g0)], 0)
+    grad = jnp.concatenate([g0, grad_theirs], 0)
     turned = grad.T
-    blocks = [
-        lax.dynamic_slice_in_dim(turned, (row ^ k) * share + at, half, 0)
-        for k in range(rows_dp)
-        for at in (0, half)
+
+    def strip(k, at, size):
+        return lax.dynamic_slice_in_dim(turned, (row ^ k) * share + at, size, 0)
+
+    strips = [
+        jnp.concatenate([strip(3, 0, half), strip(1, 0, half)], 0),
+        jnp.concatenate([strip(3, half, half), strip(2, half, half)], 0),
+        jnp.concatenate([strip(1, half, half), strip(2, 0, half), strip(0, 0, share)], 0),
     ]
     last_hop = up(hop, 1)
     for step in steps[2:prior]:
-        state = forward(info, q, [hop], (step,), state, False)
+        state = forward(info, q, hop, step, state, False)
         hop = last_hop
         if step + 1 < prior:
             chunks.append(hop)
@@ -332,14 +381,13 @@
     ):
         weight = lax.dynamic_update_slice_in_dim(weight, got, (row ^ k) * share + at, 0)
     da = dot(grad, weight).astype(BF16)
-    da, last_hop, state, *blocks = together((da, last_hop, state, *blocks))
+    da, last_hop, state, *strips = together((da, last_hop, state, *strips))
     chunks.append(last_hop)
-    att, lse_t = forward(info, q, [last_hop], (prior,), state, True)
-
-    to_x, to_y, far_x, far_y = [dot(blocks[i], att).astype(BF16) for i in (2, 5, 6, 7)]
-    to_x, to_y, far_x, far_y, da, att = together((to_x, to_y, far_x, far_y, da, att))
-    partial = dot(att, weight, NT)
-    part_mine, part_sent = partial[:tok], partial[tok:].astype(BF16)
+    att, lse_t = forward(info, q, last_hop, prior, state, True)
+
+    to_x, to_y = [dot(x, att).astype(BF16) for x in strips[:2]]
+    to_x, to_y, da, att = together((to_x, to_y, da, att))
+    part_mine, part_sent = layer_product(att, weight)
     carried = None
     terms = {}
     for step in reversed(steps):
@@ -356,28 +404,23 @@
     passing = terms[prior]
     for step in range(prior - 1, 2, -1):
         passing = (terms[step].astype(F32) + down(passing, 1).astype(F32)).astype(BF16)
-    from_x, from_y, by_x0, by_y1, got, part_sent = together(
-        (
-            across(far_x, 1),
-            across(far_y, 2),
-            across(to_x, 1),
-            across(to_y, 2),
-            down(passing, 1),
-            part_sent,
-        )
-    )
+    rest = strip_product(strips[2], att)
+    from_x, from_y, got, part_sent, rest, terms, dq = together(
+        (across(to_x, 1), across(to_y, 2), down(passing, 1), part_sent, rest, terms, dq)
+    )
+    later_x, later_y, here = rest[:half], rest[half:share], rest[share:]
     passing = (terms[2].astype(F32) + got.astype(F32)).astype(BF16)
-    to_x = (dot(blocks[3], att) + from_y.astype(F32)).astype(BF16)
-    to_y = (dot(blocks[4], att) + from_x.astype(F32)).astype(BF16)
+    to_x = (later_x + from_y[:half].astype(F32)).astype(BF16)
+    to_y = (later_y + from_x[:half].astype(F32)).astype(BF16)
     by_x1, by_y0, dq_theirs, layer_theirs, got = together(
         (across(to_x, 1), across(to_y, 2), swap(dq[tok:]), swap(part_sent), down(passing, 1))
     )
     passing = (terms[1].astype(F32) + got.astype(F32)).astype(BF16)
     coming = down(passing, 1)
-    mine = jnp.concatenate(
+    mine = here + jnp.concatenate(
         [
-            dot(blocks[0], att) + by_x0.astype(F32) + by_y0.astype(F32),
-            dot(blocks[1], att) + by_x1.astype(F32) + by_y1.astype(F32),
+            from_x[half:].astype(F32) + by_y0.astype(F32),
+            by_x1.astype(F32) + from_y[half:].astype(F32),
         ],
         0,
     )

time: 154 us -> 152 us (0.987)
  matrix products: 10.7 us -> 3.96 us
  waiting for transfers between devices: 58.8 us -> 63.7 us
  Pallas kernels: 14.8 us -> 18.1 us
  other arithmetic: 18.6 us -> 15.3 us
  local copies, waits for them, and re-layouts: 7.35 us -> 10.3 us
  starting transfers between devices: 41.6 us -> 38.9 us
    ppermute x6, waiting for transfers between devices: 19.5 us -> 31.5 us  [round_chips(): return lax.ppermute(x, 'chip', [(i, (i + k) % chips) for i in range(chips)])]
    ppermute x12 -> x10, waiting for transfers between devices: 17.4 us -> 9.71 us  [across(): return lax.ppermute(x, 'dp', [(i, i ^ k) for i in range(rows_dp)])]
    dot_general x10 -> x3, matrix products: 10.7 us -> 3.96 us  [dot(): return lax.dot_general(a, b, dims, preferred_element_type=F32)]
    pallas_call x4 -> x6, Pallas kernels: 7.93 us -> 11.7 us  [the longest x4 5.53 us: forward(): pl.pallas_call(functools.partial(forward_kernel, step, rows, first, last)...]
    ppermute x3, waiting for transfers between devices: 13.9 us -> 10.7 us  [up(): return lax.ppermute(x, 'chip', [(i, i + k) for i in range(chips - k)])]
    dynamic_slice x2, other arithmetic: 5.75 us -> 2.76 us  [strip(): return lax.dynamic_slice_in_dim(turned, (row ^ k) * share + at, size, 0)]
    ppermute x6, starting transfers between devices: 9.98 us -> 6.99 us  [round_chips(): return lax.ppermute(x, 'chip', [(i, (i + k) % chips) for i in range(chips)])]
    add x0 -> x3, other arithmetic: none -> 2.4 us  [the longest x1 1.13 us: on_device(): by_x1.astype(F32) + from_y[half:].astype(F32)]
  transfers between devices with their start and end apart: 32 -> 30, of which waited for: 18 -> 13; matrix products, arithmetic and copies ran while one was open for 18% -> 12% of each run, Pallas kernels for 8% -> 11%
where the time goes in v5:
time: 152 us; the launch traced here: 151 us
  waiting for transfers between devices  63.7 us (42%)
  starting transfers between devices  38.9 us (26%)
  Pallas kernels  18.1 us (12%)
  other arithmetic  15.3 us (10%)
  local copies, waits for them, and re-layouts  10.3 us (7%)
  matrix products  3.96 us (3%)
    ppermute x6, waiting for transfers between devices, round_chips(): return lax.ppermute(x, 'chip', [(i, (i + k) % chips) for i in range(chips)])  31.5 us
    ppermute x3, waiting for transfers between devices, up(): return lax.ppermute(x, 'chip', [(i, i + k) for i in range(chips - k)])  10.7 us
    ppermute x3, starting transfers between devices, up(): return lax.ppermute(x, 'chip', [(i, i + k) for i in range(chips - k)])  10.3 us
    ppermute x10, waiting for transfers between devices, across(): return lax.ppermute(x, 'dp', [(i, i ^ k) for i in range(rows_dp)])  9.71 us
    ppermute x8, starting transfers between devices, swap(): return lax.ppermute(x, 'core', [(0, 1), (1, 0)])  8.22 us
    ppermute x10, starting transfers between devices, across(): return lax.ppermute(x, 'dp', [(i, i ^ k) for i in range(rows_dp)])  7.49 us
    ppermute x6, starting transfers between devices, round_chips(): return lax.ppermute(x, 'chip', [(i, (i + k) % chips) for i in range(chips)])  6.99 us
    pallas_call x4, Pallas kernels, backward(): pl.pallas_call(functools.partial(backward_kernel, steps, rows, first, las...  6.33 us
  transfers between devices with their start and end apart: 30, of which 13 were waited for; matrix products, arithmetic and copies ran while one was open for 12% of the time, Pallas kernels for 11%

profile of v5, /device:TPU:9, one launch (start us, length us, event | category | flops | bytes accessed | tf_op | source)
XLA Modules:
  0.0 151.4 jit_solution(16393368094038181893)
XLA Ops:
  0.7 2.5 %copy.10 = bf16[1,256,2304]{1,2,0:T(8,128)(2,1)} copy(bf16[1,256,2304]{2,1,0:T(8,128)(2,1)} %param.9) | data formatting | bytes 2359296 | tf_op args[4]
  3.1 0.7 collective-permute-start.3
  4.0 2.7 %collective-permute-done = bf16[256,512]{1,0:T(8,128)(2,1)S(1)} collective-permute-done((bf16[256,512]{1,0:T(8,128)(2,1)S(1)}, bf16[256,512]{1,0:T(8,128)(2,1)S(1)}, u32[]{:S(2)}, u32[]{:S(2)}) %collective-permute-start) | collective-permute-done | bytes 262176 | tf_op jit(solution)/shard_map/ppermute | solution.py:297
  6.7 3.2 %collective-permute-start.1 = (bf16[512,512]{1,0:T(8,128)(2,1)S(1)}, bf16[512,512]{1,0:T(8,128)(2,1)S(1)}, u32[]{:S(2)}, u32[]{:S(2)}) collective-permute-start(bf16[512,512]{1,0:T(8,128)(2,1)S(1)} %pad_maximum_fusion.7.kv.refs_0_), channel_id=1, source_target_pairs={{0,2},{2,4},{4,6},{1,3},{3,5},{5,7},{8,10},{10,12},{12,14},{9,11},... | collective-permute-start | bytes 1572872 | tf_op jit(solution)/shard_map/ppermute | solution.py:300
  10.0 0.7 collective-permute-start.2
  10.7 1.3 collective-permute-start.4
  12.0 1.0 collective-permute-start.5
  13.0 0.9 bitcast_dynamic-update-slice_fusion.3
  14.4 2.1 %attend_forward.4 = (f32[16,512]{1,0:T(8,128)S(1)}, f32[16,512]{1,0:T(8,128)S(1)}, f32[512,512]{1,0:T(8,128)S(1)}) custom-call(s32[2]{0:T(128)S(1)} %pad_add_fusion.info, bf16[512,512]{1,0:T(8,128)(2,1)S(1)} %maximum_multiply_fusion.q, bf16[512,512]{1,0:T(8,128)(2,1)S(1)} %pad_maximum_fusion.7.kv.refs_0_), custom_call_target="tpu_custom_call" | custom-call | flops 1 | bytes 1 | tf_op jit(solution)/shard_map/attend_forward/pallas_call | solution.py:110
  16.5 8.5 %collective-permute-done.4 = bf16[72,1024]{1,0:T(8,128)(2,1)} collective-permute-done((bf16[72,1024]{1,0:T(8,128)(2,1)}, bf16[72,1024]{1,0:T(8,128)(2,1)}, u32[]{:S(2)}, u32[]{:S(2)}) %collective-permute-start.4) | collective-permute-done | bytes 147488 | tf_op jit(solution)/shard_map/ppermute | solution.py:306
  25.0 8.6 %collective-permute-done.5 = bf16[72,1024]{1,0:T(8,128)(2,1)} collective-permute-done((bf16[72,1024]{1,0:T(8,128)(2,1)}, bf16[72,1024]{1,0:T(8,128)(2,1)}, u32[]{:S(2)}, u32[]{:S(2)}) %collective-permute-start.5) | collective-permute-done | bytes 147488 | tf_op jit(solution)/shard_map/ppermute | solution.py:306
  33.6 1.1 bitcast_dynamic-update-slice_fusion.2
  34.7 0.9 bitcast_dynamic-update-slice_fusion.1
  35.6 0.9 bitcast_dynamic-update-slice_fusion
  36.6 1.3 collective-permute-start.7
  37.8 1.9 %collective-permute-start.12 = (bf16[512,512]{1,0:T(8,128)(2,1)S(1)}, bf16[512,512]{1,0:T(8,128)(2,1)S(1)}, u32[]{:S(2)}, u32[]{:S(2)}) collective-permute-start(bf16[512,512]{1,0:T(8,128)(2,1)S(1)} %collective-permute-done.1.kv.refs_0_), channel_id=1, source_target_pairs={{0,2},{2,4},{4,6},{1,3},{3,5},{5,7},{8,10},{10,12},{12,14},{9,11},... | collective-permute-start | bytes 1572872 | tf_op jit(solution)/shard_map/ppermute | solution.py:300
  39.8 1.7 %fusion.11 = (bf16[288,512]{1,0:T(8,128)(2,1)S(1)}, bf16[288,512]{1,0:T(8,128)(2,1)S(1)}, bf16[288,512]{1,0:T(8,128)(2,1)S(1)}, bf16[288,512]{1,0:T(8,128)(2,1)S...) fusion(s32[]{:T(128)S(6)} %select_n.181, bf16[256,2304]{0,1:T(8,128)(2,1)} %collective-permute-done.3, ...), kind=kLoop, calls=%fused_computation.50 | loop fusion | flops 3538944 | bytes 4128792 | tf_op jit(solution)/shard_map/dynamic_slice | solution.py:358
  41.4 1.1 fusion.3
  42.7 1.3 collective-permute-start.8
  44.0 1.2 collective-permute-start.10
  45.8 1.9 %attend_forward.5 = (f32[16,512]{1,0:T(8,128)S(1)}, f32[16,512]{1,0:T(8,128)S(1)}, f32[512,512]{1,0:T(8,128)S(1)}) custom-call(s32[2]{0:T(128)S(1)} %pad_add_fusion.info, bf16[512,512]{1,0:T(8,128)(2,1)S(1)} %maximum_multiply_fusion.q, bf16[512,512]{1,0:T(8,128)(2,1)S(1)} %collective-permute-done.1.kv.refs_0_, f32[16,512]{1,0:T(8,128)S(1)} %get-tuple-element.93.refs_0_, ...), custom_call_target="tpu_custom_call" | custom-call | flops 1 | bytes 1 | tf_op jit(solution)/shard_map/attend_forward/pallas_call | solution.py:110
  48.0 5.2 %collective-permute-done.12.kv.refs_0_ = bf16[512,512]{1,0:T(8,128)(2,1)S(1)} collective-permute-done((bf16[512,512]{1,0:T(8,128)(2,1)S(1)}, bf16[512,512]{1,0:T(8,128)(2,1)S(1)}, u32[]{:S(2)}, u32[]{:S(2)}) %collective-permute-start.12) | collective-permute-done | bytes 524320 | tf_op jit(solution)/shard_map/ppermute | solution.py:300
  53.3 4.3 %collective-permute-done.9 = bf16[288,512]{1,0:T(8,128)(2,1)S(1)} collective-permute-done((bf16[288,512]{1,0:T(8,128)(2,1)S(1)}, bf16[288,512]{1,0:T(8,128)(2,1)S(1)}, u32[]{:S(2)}, u32[]{:S(2)}) %collective-permute-start.9) | collective-permute-done | bytes 294944 | tf_op jit(solution)/shard_map/ppermute | solution.py:309
  57.6 0.9 collective-permute-done.11
  58.8 1.2 collective-permute-start.14
  60.1 5.2 %collective-permute-start.15 = (bf16[512,512]{1,0:T(8,128)(2,1)S(1)}, bf16[512,512]{1,0:T(8,128)(2,1)S(1)}, u32[]{:S(2)}, u32[]{:S(2)}) collective-permute-start(bf16[512,512]{1,0:T(8,128)(2,1)S(1)} %collective-permute-done.12.kv.refs_0_), channel_id=1, source_target_pairs={{0,2},{2,4},{4,6},{1,3},{3,5},{5,7},{8,10},{10,12},{12,14},{9,11},... | collective-permute-start | bytes 1572872 | tf_op jit(solution)/shard_map/ppermute | solution.py:300
  66.1 3.0 %fusion.1.da = bf16[512,512]{1,0:T(8,128)(2,1)S(1)} fusion(bf16[2304,512]{1,0:T(8,128)(2,1)S(1)} %constant_dynamic-update-slice_fusion.w, bf16[256,2304]{0,1:T(8,128)(2,1)} %collective-permute-done.3, bf16[256,2304]{0,1:T(8,128)(2,1)} %bitcast), kind=kOutput, calls=%fused_computation.19 | convolution fusion | flops 1212940288 | bytes 5242880 | tf_op jit(solution)/shard_map/dot_general | solution.py:27
  69.1 5.5 %collective-permute-done.15.kv.refs_0_ = bf16[512,512]{1,0:T(8,128)(2,1)S(1)} collective-permute-done((bf16[512,512]{1,0:T(8,128)(2,1)S(1)}, bf16[512,512]{1,0:T(8,128)(2,1)S(1)}, u32[]{:S(2)}, u32[]{:S(2)}) %collective-permute-start.15) | collective-permute-done | bytes 524320 | tf_op jit(solution)/shard_map/ppermute | solution.py:300
  74.6 0.8 attend_forward.7
  76.3 1.1 collective-permute-start.16
  77.7 0.9 attend_backward.4
  78.6 2.1 %collective-permute-start.18 = (bf16[512,512]{1,0:T(8,128)(2,1)S(1)}, bf16[512,512]{1,0:T(8,128)(2,1)S(1)}, u32[]{:S(2)}, u32[]{:S(2)}) collective-permute-start(bf16[512,512]{1,0:T(8,128)(2,1)S(1)} %get-tuple-element.123), channel_id=1, source_target_pairs={{2,0},{4,2},{6,4},{3,1},{5,3},{7,5},{10,8},{12,10},{14,12},{11,9},... | collective-permute-start | bytes 1572872 | tf_op jit(solution)/shard_map/ppermute | solution.py:303
  80.7 4.9 %layer_product.1 = (f32[256,2304]{1,0:T(8,128)S(1)}, bf16[256,2304]{1,0:T(8,128)(2,1)}) custom-call(bf16[512,512]{1,0:T(8,128)(2,1)S(1)} %get-tuple-element.122.refs_1_.x.w, bf16[2304,512]{1,0:T(8,128)(2,1)S(1)} %constant_dynamic-update-slice_fusion.w), custom_call_target="tpu_custom_call" | custom-call | flops 1 | bytes 1 | tf_op jit(solution)/shard_map/layer_product/pallas_call | solution.py:238
  85.7 1.4 copy-done
  87.1 1.3 strip_product.1
  88.4 0.6 attend_backward.5
  89.4 2.3 %attend_backward.6 = (bf16[512,512]{1,0:T(8,128)(2,1)S(1)}, f32[512,512]{1,0:T(8,128)S(1)}) custom-call(s32[2]{0:T(128)S(1)} %pad_add_fusion.info, bf16[512,512]{1,0:T(8,128)(2,1)S(1)} %maximum_multiply_fusion.q, bf16[512,512]{1,0:T(8,128)(2,1)S(1)} %fusion.1.da, f32[16,512]{1,0:T(8,128)S(1)} %get-tuple-element.121.lse_t, bf16[512,512]{1,0:T(8,128)(2,1)S(1)} %copy-done.3, ...), custom_call_target="tpu_custom_call" | custom-call | flops 1 | bytes 1 | tf_op jit(solution)/shard_map/attend_backward/pallas_call | solution.py:211
  91.7 0.8 copy-done.6
  92.5 2.5 %attend_backward.7 = (f32[512,512]{1,0:T(8,128)S(1)}, bf16[512,512]{1,0:T(8,128)(2,1)S(1)}) custom-call(s32[2]{0:T(128)S(1)} %pad_add_fusion.info, bf16[512,512]{1,0:T(8,128)(2,1)S(1)} %maximum_multiply_fusion.q, bf16[512,512]{1,0:T(8,128)(2,1)S(1)} %fusion.1.da, f32[16,512]{1,0:T(8,128)S(1)} %get-tuple-element.121.lse_t, ...), custom_call_target="tpu_custom_call" | custom-call | flops 1 | bytes 1 | tf_op jit(solution)/shard_map/attend_backward/pallas_call | solution.py:211
  95.1 3.6 %collective-permute-start.22 = (bf16[256,2304]{1,0:T(8,128)(2,1)}, bf16[256,2304]{1,0:T(8,128)(2,1)}, u32[]{:S(2)}, u32[]{:S(2)}) collective-permute-start(bf16[256,2304]{1,0:T(8,128)(2,1)} %get-tuple-element.139), channel_id=1, source_target_pairs={{0,1},{1,0},{2,3},{3,2},{4,5},{5,4},{6,7},{7,6},{8,9},{9,8},{10,11... | collective-permute-start | bytes 3538952 | tf_op jit(solution)/shard_map/ppermute | solution.py:297
  98.7 0.9 add_convert_fusion.3
  99.6 1.9 %collective-permute-start.23 = (bf16[512,512]{1,0:T(8,128)(2,1)}, bf16[512,512]{1,0:T(8,128)(2,1)}, u32[]{:S(2)}, u32[]{:S(2)}) collective-permute-start(bf16[512,512]{1,0:T(8,128)(2,1)} %add_convert_fusion.3), channel_id=1, source_target_pairs={{2,0},{4,2},{6,4},{3,1},{5,3},{7,5},{10,8},{12,10},{14,12},{11,9},... | collective-permute-start | bytes 1572872 | tf_op jit(solution)/shard_map/ppermute | solution.py:303
  101.5 0.9 add_convert_fusion.4
  102.8 1.2 collective-permute-start.20
  104.0 0.7 fusion.18
  104.7 0.6 collective-permute-start.21
  105.4 1.5 collective-permute-done.21
  106.9 4.5 %collective-permute-done.19 = bf16[288,512]{1,0:T(8,128)(2,1)} collective-permute-done((bf16[288,512]{1,0:T(8,128)(2,1)}, bf16[288,512]{1,0:T(8,128)(2,1)}, u32[]{:S(2)}, u32[]{:S(2)}) %collective-permute-start.19) | collective-permute-done | bytes 294944 | tf_op jit(solution)/shard_map/ppermute | solution.py:309
  111.4 6.2 %collective-permute-done.23 = bf16[512,512]{1,0:T(8,128)(2,1)} collective-permute-done((bf16[512,512]{1,0:T(8,128)(2,1)}, bf16[512,512]{1,0:T(8,128)(2,1)}, u32[]{:S(2)}, u32[]{:S(2)}) %collective-permute-start.23) | collective-permute-done | bytes 524320 | tf_op jit(solution)/shard_map/ppermute | solution.py:303
  117.6 1.2 add_convert_fusion.2
  118.7 1.9 %collective-permute-start.24 = (bf16[512,512]{1,0:T(8,128)(2,1)S(1)}, bf16[512,512]{1,0:T(8,128)(2,1)S(1)}, u32[]{:S(2)}, u32[]{:S(2)}) collective-permute-start(bf16[512,512]{1,0:T(8,128)(2,1)S(1)} %add_convert_fusion.2), channel_id=1, source_target_pairs={{2,0},{4,2},{6,4},{3,1},{5,3},{7,5},{10,8},{12,10},{14,12},{11,9},... | collective-permute-start | bytes 1572872 | tf_op jit(solution)/shard_map/ppermute | solution.py:303
  120.7 1.1 convert_add_fusion
  121.8 1.0 convert_add_fusion.1
  123.2 1.8 %collective-permute-start.25 = (bf16[144,512]{1,0:T(8,128)(2,1)S(1)}, bf16[144,512]{1,0:T(8,128)(2,1)S(1)}, u32[]{:S(2)}, u32[]{:S(2)}) collective-permute-start(bf16[144,512]{1,0:T(8,128)(2,1)S(1)} %get-tuple-element.165), channel_id=1, source_target_pairs={{0,2},{2,4},{4,6},{6,0},{1,3},{3,5},{5,7},{7,1},{8,10},{10,12},{12... | collective-permute-start | bytes 442376 | tf_op jit(solution)/shard_map/ppermute | solution.py:306
  125.0 1.3 collective-permute-start.26
  126.3 1.4 collective-permute-start.27
  127.7 2.6 %add_convert_fusion = bf16[256,2304]{1,0:T(8,128)(2,1)} fusion(f32[256,2304]{1,0:T(8,128)S(1)} %copy-done.1, bf16[256,2304]{1,0:T(8,128)(2,1)} %collective-permute-done.22), kind=kLoop, calls=%fused_computation.16 | loop fusion | flops 1769472 | bytes 4718592 | tf_op jit(solution)/shard_map/convert_element_type | solution.py:428
  130.3 2.0 %maximum_select_fusion.1 = bf16[256,1024]{1,0:T(8,128)(2,1)} fusion(bf16[256,512]{1,0:T(8,128)(2,1)} %collective-permute-done.21, bf16[256,512]{1,0:T(8,128)(2,1)S(1)} %get-tuple-element.172, pred[]{:T(512)S(6)} %eq.3), kind=kLoop, calls=%fused_computation.36 | loop fusion | flops 2359296 | bytes 1048577 | tf_op jit(solution)/shard_map/jit(_where)/select_n | solution.py:312
  132.3 9.1 %collective-permute-done.26 = bf16[144,512]{1,0:T(8,128)(2,1)S(1)} collective-permute-done((bf16[144,512]{1,0:T(8,128)(2,1)S(1)}, bf16[144,512]{1,0:T(8,128)(2,1)S(1)}, u32[]{:S(2)}, u32[]{:S(2)}) %collective-permute-start.26) | collective-permute-done | bytes 147488 | tf_op jit(solution)/shard_map/ppermute | solution.py:306
  141.3 5.4 %collective-permute-done.27 = bf16[144,512]{1,0:T(8,128)(2,1)S(1)} collective-permute-done((bf16[144,512]{1,0:T(8,128)(2,1)S(1)}, bf16[144,512]{1,0:T(8,128)(2,1)S(1)}, u32[]{:S(2)}, u32[]{:S(2)}) %collective-permute-start.27) | collective-permute-done | bytes 147488 | tf_op jit(solution)/shard_map/ppermute | solution.py:306
  147.0 1.2 collective-permute-start.28
  148.4 1.3 collective-permute-done.29
  149.7 0.7 maximum_select_fusion.2
  150.5 0.9 maximum_select_fusion.3
  (84 shorter events, 5.5 us)
Async XLA Ops:
  0.6 3.2 %copy-start.12 = (bf16[1,256,512]{2,1,0:T(8,128)(2,1)S(1)}, bf16[1,256,512]{2,1,0:T(8,128)(2,1)}, u32[]{:S(2)}) copy-start(bf16[1,256,512]{2,1,0:T(8,128)(2,1)} %param.7) | copy-start | bytes 786436
  0.6 3.2 %copy-start.13 = (bf16[1,256,512]{2,1,0:T(8,128)(2,1)S(1)}, bf16[1,256,512]{2,1,0:T(8,128)(2,1)}, u32[]{:S(2)}) copy-start(bf16[1,256,512]{2,1,0:T(8,128)(2,1)} %param.6) | copy-start | bytes 786436
  0.7 9.2 %copy-start.11 = (bf16[1,256,1024]{2,1,0:T(8,128)(2,1)S(1)}, bf16[1,256,1024]{2,1,0:T(8,128)(2,1)}, u32[]{:S(2)}) copy-start(bf16[1,256,1024]{2,1,0:T(8,128)(2,1)} %param.5) | copy-start | bytes 1572868
  3.1 30.4 %collective-permute-start.3 = (bf16[256,2304]{0,1:T(8,128)(2,1)}, bf16[256,2304]{0,1:T(8,128)(2,1)}, u32[]{:S(2)}, u32[]{:S(2)}) collective-permute-start(bf16[256,2304]{0,1:T(8,128)(2,1)} %bitcast), channel_id=1, source_target_pairs={{0,1},{1,0},{2,3},{3,2},{4,5},{5,4},{6,7},{7,6},{8,9},{9,8},{10,11... | collective-permute-start | bytes 3538952 | tf_op jit(solution)/shard_map/ppermute | solution.py:297
  3.9 2.8 %collective-permute-start = (bf16[256,512]{1,0:T(8,128)(2,1)S(1)}, bf16[256,512]{1,0:T(8,128)(2,1)S(1)}, u32[]{:S(2)}, u32[]{:S(2)}) collective-permute-start(bf16[256,512]{1,0:T(8,128)(2,1)S(1)} %pad_maximum_fusion.8), channel_id=1, source_target_pairs={{0,1},{1,0},{2,3},{3,2},{4,5},{5,4},{6,7},{7,6},{8,9},{9,8},{10,11... | collective-permute-start | bytes 786440 | tf_op jit(solution)/shard_map/ppermute | solution.py:297
  6.7 26.9 %collective-permute-start.1 = (bf16[512,512]{1,0:T(8,128)(2,1)S(1)}, bf16[512,512]{1,0:T(8,128)(2,1)S(1)}, u32[]{:S(2)}, u32[]{:S(2)}) collective-permute-start(bf16[512,512]{1,0:T(8,128)(2,1)S(1)} %pad_maximum_fusion.7.kv.refs_0_), channel_id=1, source_target_pairs={{0,2},{2,4},{4,6},{1,3},{3,5},{5,7},{8,10},{10,12},{12,14},{9,11},... | collective-permute-start | bytes 1572872 | tf_op jit(solution)/shard_map/ppermute | solution.py:300
  10.0 4.0 %collective-permute-start.2 = (bf16[256,512]{1,0:T(8,128)(2,1)S(1)}, bf16[256,512]{1,0:T(8,128)(2,1)S(1)}, u32[]{:S(2)}, u32[]{:S(2)}) collective-permute-start(bf16[256,512]{1,0:T(8,128)(2,1)S(1)} %get-tuple-element.175), channel_id=1, source_target_pairs={{0,1},{1,0},{2,3},{3,2},{4,5},{5,4},{6,7},{7,6},{8,9},{9,8},{10,11... | collective-permute-start | bytes 786440 | tf_op jit(solution)/shard_map/ppermute | solution.py:297
  10.7 14.3 %collective-permute-start.4 = (bf16[72,1024]{1,0:T(8,128)(2,1)}, bf16[72,1024]{1,0:T(8,128)(2,1)}, u32[]{:S(2)}, u32[]{:S(2)}) collective-permute-start(bf16[72,1024]{1,0:T(8,128)(2,1)} %param.8), channel_id=1, source_target_pairs={{0,2},{2,4},{4,6},{6,0},{1,3},{3,5},{5,7},{7,1},{8,10},{10,12},{12... | collective-permute-start | bytes 442376 | tf_op jit(solution)/shard_map/ppermute | solution.py:306
  12.0 21.6 %collective-permute-start.5 = (bf16[72,1024]{1,0:T(8,128)(2,1)}, bf16[72,1024]{1,0:T(8,128)(2,1)}, u32[]{:S(2)}, u32[]{:S(2)}) collective-permute-start(bf16[72,1024]{1,0:T(8,128)(2,1)} %param.8), channel_id=1, source_target_pairs={{0,4},{2,6},{4,0},{6,2},{1,5},{3,7},{5,1},{7,3},{8,12},{10,14},{12... | collective-permute-start | bytes 442376 | tf_op jit(solution)/shard_map/ppermute | solution.py:306
  14.0 19.6 %collective-permute-start.6 = (bf16[72,1024]{1,0:T(8,128)(2,1)}, bf16[72,1024]{1,0:T(8,128)(2,1)}, u32[]{:S(2)}, u32[]{:S(2)}) collective-permute-start(bf16[72,1024]{1,0:T(8,128)(2,1)} %param.8), channel_id=1, source_target_pairs={{0,6},{2,0},{4,2},{6,4},{1,7},{3,1},{5,3},{7,5},{8,14},{10,8},{12,... | collective-permute-start | bytes 442376 | tf_op jit(solution)/shard_map/ppermute | solution.py:306
  33.6 12.3 %copy-start.2 = (bf16[512,512]{1,0:T(8,128)(2,1)}, bf16[512,512]{1,0:T(8,128)(2,1)S(1)}, u32[]{:S(2)}) copy-start(bf16[512,512]{1,0:T(8,128)(2,1)S(1)} %collective-permute-done.1.kv.refs_0_) | copy-start | bytes 1572868
  36.6 6.0 %collective-permute-start.7 = (bf16[4,72,512]{2,1,0:T(8,128)(2,1)S(1)}, bf16[4,72,512]{2,1,0:T(8,128)(2,1)S(1)}, u32[]{:S(2)}, u32[]{:S(2)}) collective-permute-start(bf16[4,72,512]{2,1,0:T(8,128)(2,1)S(1)} %get-tuple-element.169), channel_id=1, source_target_pairs={{0,1},{1,0},{2,3},{3,2},{4,5},{5,4},{6,7},{7,6},{8,9},{9,8},{10,11... | collective-permute-start | bytes 884744 | tf_op jit(solution)/shard_map/ppermute | solution.py:297
  37.8 15.4 %collective-permute-start.12 = (bf16[512,512]{1,0:T(8,128)(2,1)S(1)}, bf16[512,512]{1,0:T(8,128)(2,1)S(1)}, u32[]{:S(2)}, u32[]{:S(2)}) collective-permute-start(bf16[512,512]{1,0:T(8,128)(2,1)S(1)} %collective-permute-done.1.kv.refs_0_), channel_id=1, source_target_pairs={{0,2},{2,4},{4,6},{1,3},{3,5},{5,7},{8,10},{10,12},{12,14},{9,11},... | collective-permute-start | bytes 1572872 | tf_op jit(solution)/shard_map/ppermute | solution.py:300
  42.7 10.5 %collective-permute-start.8 = (bf16[288,512]{1,0:T(8,128)(2,1)S(1)}, bf16[288,512]{1,0:T(8,128)(2,1)S(1)}, u32[]{:S(2)}, u32[]{:S(2)}) collective-permute-start(bf16[288,512]{1,0:T(8,128)(2,1)S(1)} %get-tuple-element.167), channel_id=1, source_target_pairs={{0,8},{8,0},{16,24},{24,16},{1,9},{9,1},{17,25},{25,17},{2,10},{10... | collective-permute-start | bytes 884744 | tf_op jit(solution)/shard_map/ppermute | solution.py:309
  44.0 13.6 %collective-permute-start.10 = (bf16[288,512]{1,0:T(8,128)(2,1)S(1)}, bf16[288,512]{1,0:T(8,128)(2,1)S(1)}, u32[]{:S(2)}, u32[]{:S(2)}) collective-permute-start(bf16[288,512]{1,0:T(8,128)(2,1)S(1)} %get-tuple-element.167), channel_id=1, source_target_pairs={{0,16},{8,24},{16,0},{24,8},{1,17},{9,25},{17,1},{25,9},{2,18},{10... | collective-permute-start | bytes 884744 | tf_op jit(solution)/shard_map/ppermute | solution.py:309
  45.3 12.3 %collective-permute-start.9 = (bf16[288,512]{1,0:T(8,128)(2,1)S(1)}, bf16[288,512]{1,0:T(8,128)(2,1)S(1)}, u32[]{:S(2)}, u32[]{:S(2)}) collective-permute-start(bf16[288,512]{1,0:T(8,128)(2,1)S(1)} %get-tuple-element.166), channel_id=1, source_target_pairs={{0,8},{8,0},{16,24},{24,16},{1,9},{9,1},{17,25},{25,17},{2,10},{10... | collective-permute-start | bytes 884744 | tf_op jit(solution)/shard_map/ppermute | solution.py:309
  45.5 13.0 %collective-permute-start.11 = (bf16[288,512]{1,0:T(8,128)(2,1)S(1)}, bf16[288,512]{1,0:T(8,128)(2,1)S(1)}, u32[]{:S(2)}, u32[]{:S(2)}) collective-permute-start(bf16[288,512]{1,0:T(8,128)(2,1)S(1)} %get-tuple-element.166), channel_id=1, source_target_pairs={{0,16},{8,24},{16,0},{24,8},{1,17},{9,25},{17,1},{25,9},{2,18},{10... | collective-permute-start | bytes 884744 | tf_op jit(solution)/shard_map/ppermute | solution.py:309
  58.5 7.5 %collective-permute-start.13 = (bf16[288,512]{1,0:T(8,128)(2,1)S(1)}, bf16[288,512]{1,0:T(8,128)(2,1)S(1)}, u32[]{:S(2)}, u32[]{:S(2)}) collective-permute-start(bf16[288,512]{1,0:T(8,128)(2,1)S(1)} %collective-permute-done.10), channel_id=1, source_target_pairs={{0,8},{8,0},{16,24},{24,16},{1,9},{9,1},{17,25},{25,17},{2,10},{10... | collective-permute-start | bytes 884744 | tf_op jit(solution)/shard_map/ppermute | solution.py:309
  58.8 7.2 %collective-permute-start.14 = (bf16[288,512]{1,0:T(8,128)(2,1)S(1)}, bf16[288,512]{1,0:T(8,128)(2,1)S(1)}, u32[]{:S(2)}, u32[]{:S(2)}) collective-permute-start(bf16[288,512]{1,0:T(8,128)(2,1)S(1)} %collective-permute-done.9), channel_id=1, source_target_pairs={{0,16},{8,24},{16,0},{24,8},{1,17},{9,25},{17,1},{25,9},{2,18},{10... | collective-permute-start | bytes 884744 | tf_op jit(solution)/shard_map/ppermute | solution.py:309
  60.1 14.4 %collective-permute-start.15 = (bf16[512,512]{1,0:T(8,128)(2,1)S(1)}, bf16[512,512]{1,0:T(8,128)(2,1)S(1)}, u32[]{:S(2)}, u32[]{:S(2)}) collective-permute-start(bf16[512,512]{1,0:T(8,128)(2,1)S(1)} %collective-permute-done.12.kv.refs_0_), channel_id=1, source_target_pairs={{0,2},{2,4},{4,6},{1,3},{3,5},{5,7},{8,10},{10,12},{12,14},{9,11},... | collective-permute-start | bytes 1572872 | tf_op jit(solution)/shard_map/ppermute | solution.py:300
  76.3 18.7 %collective-permute-start.16 = (bf16[576,512]{1,0:T(8,128)(2,1)S(1)}, bf16[576,512]{1,0:T(8,128)(2,1)S(1)}, u32[]{:S(2)}, u32[]{:S(2)}) collective-permute-start(bf16[576,512]{1,0:T(8,128)(2,1)S(1)} %convolution_convert_fusion.1), channel_id=1, source_target_pairs={{0,8},{8,0},{16,24},{24,16},{1,9},{9,1},{17,25},{25,17},{2,10},{10... | collective-permute-start | bytes 1769480 | tf_op jit(solution)/shard_map/ppermute | solution.py:309
  77.5 17.6 %collective-permute-start.17 = (bf16[576,512]{1,0:T(8,128)(2,1)S(1)}, bf16[576,512]{1,0:T(8,128)(2,1)S(1)}, u32[]{:S(2)}, u32[]{:S(2)}) collective-permute-start(bf16[576,512]{1,0:T(8,128)(2,1)S(1)} %convolution_convert_fusion), channel_id=1, source_target_pairs={{0,16},{8,24},{16,0},{24,8},{1,17},{9,25},{17,1},{25,9},{2,18},{10... | collective-permute-start | bytes 1769480 | tf_op jit(solution)/shard_map/ppermute | solution.py:309
  78.6 16.4 %collective-permute-start.18 = (bf16[512,512]{1,0:T(8,128)(2,1)S(1)}, bf16[512,512]{1,0:T(8,128)(2,1)S(1)}, u32[]{:S(2)}, u32[]{:S(2)}) collective-permute-start(bf16[512,512]{1,0:T(8,128)(2,1)S(1)} %get-tuple-element.123), channel_id=1, source_target_pairs={{2,0},{4,2},{6,4},{3,1},{5,3},{7,5},{10,8},{12,10},{14,12},{11,9},... | collective-permute-start | bytes 1572872 | tf_op jit(solution)/shard_map/ppermute | solution.py:303
  85.7 1.4 copy-start
  88.4 1.0 copy-start.3
  91.7 0.8 copy-start.6
  95.0 9.7 %copy-start.4 = (f32[512,512]{1,0:T(8,128)}, f32[512,512]{1,0:T(8,128)S(1)}, u32[]{:S(2)}) copy-start(f32[512,512]{1,0:T(8,128)S(1)} %get-tuple-element.150) | copy-start | bytes 3145732
  95.1 9.7 %copy-start.8 = (bf16[576,512]{1,0:T(8,128)(2,1)}, bf16[576,512]{1,0:T(8,128)(2,1)S(1)}, u32[]{:S(2)}) copy-start(bf16[576,512]{1,0:T(8,128)(2,1)S(1)} %collective-permute-done.16) | copy-start | bytes 1769476
  95.1 9.7 %copy-start.10 = (bf16[576,512]{1,0:T(8,128)(2,1)}, bf16[576,512]{1,0:T(8,128)(2,1)S(1)}, u32[]{:S(2)}) copy-start(bf16[576,512]{1,0:T(8,128)(2,1)S(1)} %collective-permute-done.17) | copy-start | bytes 1769476
  95.1 22.5 %copy-start.7 = (bf16[512,512]{1,0:T(8,128)(2,1)S(1)}, bf16[512,512]{1,0:T(8,128)(2,1)}, u32[]{:S(2)}) copy-start(bf16[512,512]{1,0:T(8,128)(2,1)} %copy-done.6) | copy-start | bytes 1572868
  95.1 22.5 %collective-permute-start.22 = (bf16[256,2304]{1,0:T(8,128)(2,1)}, bf16[256,2304]{1,0:T(8,128)(2,1)}, u32[]{:S(2)}, u32[]{:S(2)}) collective-permute-start(bf16[256,2304]{1,0:T(8,128)(2,1)} %get-tuple-element.139), channel_id=1, source_target_pairs={{0,1},{1,0},{2,3},{3,2},{4,5},{5,4},{6,7},{7,6},{8,9},{9,8},{10,11... | collective-permute-start | bytes 3538952 | tf_op jit(solution)/shard_map/ppermute | solution.py:297
  99.6 18.0 %collective-permute-start.23 = (bf16[512,512]{1,0:T(8,128)(2,1)}, bf16[512,512]{1,0:T(8,128)(2,1)}, u32[]{:S(2)}, u32[]{:S(2)}) collective-permute-start(bf16[512,512]{1,0:T(8,128)(2,1)} %add_convert_fusion.3), channel_id=1, source_target_pairs={{2,0},{4,2},{6,4},{3,1},{5,3},{7,5},{10,8},{12,10},{14,12},{11,9},... | collective-permute-start | bytes 1572872 | tf_op jit(solution)/shard_map/ppermute | solution.py:303
  102.4 8.9 %collective-permute-start.19 = (bf16[288,512]{1,0:T(8,128)(2,1)}, bf16[288,512]{1,0:T(8,128)(2,1)}, u32[]{:S(2)}, u32[]{:S(2)}) collective-permute-start(bf16[288,512]{1,0:T(8,128)(2,1)} %get-tuple-element.156), channel_id=1, source_target_pairs={{0,8},{8,0},{16,24},{24,16},{1,9},{9,1},{17,25},{25,17},{2,10},{10... | collective-permute-start | bytes 884744 | tf_op jit(solution)/shard_map/ppermute | solution.py:309
  102.8 8.6 %collective-permute-start.20 = (bf16[288,512]{1,0:T(8,128)(2,1)S(1)}, bf16[288,512]{1,0:T(8,128)(2,1)}, u32[]{:S(2)}, u32[]{:S(2)}) collective-permute-start(bf16[288,512]{1,0:T(8,128)(2,1)S(1)} %get-tuple-element.155), channel_id=1, source_target_pairs={{0,16},{8,24},{16,0},{24,8},{1,17},{9,25},{17,1},{25,9},{2,18},{10... | collective-permute-start | bytes 884744 | tf_op jit(solution)/shard_map/ppermute | solution.py:309
  104.7 2.1 %collective-permute-start.21 = (bf16[256,512]{1,0:T(8,128)(2,1)}, bf16[256,512]{1,0:T(8,128)(2,1)}, u32[]{:S(2)}, u32[]{:S(2)}) collective-permute-start(bf16[256,512]{1,0:T(8,128)(2,1)} %get-tuple-element.173), channel_id=1, source_target_pairs={{0,1},{1,0},{2,3},{3,2},{4,5},{5,4},{6,7},{7,6},{8,9},{9,8},{10,11... | collective-permute-start | bytes 786440 | tf_op jit(solution)/shard_map/ppermute | solution.py:297
  105.4 16.4 %copy-start.9 = (bf16[576,512]{1,0:T(8,128)(2,1)S(1)}, bf16[576,512]{1,0:T(8,128)(2,1)}, u32[]{:S(2)}) copy-start(bf16[576,512]{1,0:T(8,128)(2,1)} %copy-done.8) | copy-start | bytes 1769476
  118.7 28.0 %collective-permute-start.24 = (bf16[512,512]{1,0:T(8,128)(2,1)S(1)}, bf16[512,512]{1,0:T(8,128)(2,1)S(1)}, u32[]{:S(2)}, u32[]{:S(2)}) collective-permute-start(bf16[512,512]{1,0:T(8,128)(2,1)S(1)} %add_convert_fusion.2), channel_id=1, source_target_pairs={{2,0},{4,2},{6,4},{3,1},{5,3},{7,5},{10,8},{12,10},{14,12},{11,9},... | collective-permute-start | bytes 1572872 | tf_op jit(solution)/shard_map/ppermute | solution.py:303
  122.9 4.8 %copy-start.1 = (f32[256,2304]{1,0:T(8,128)S(1)}, f32[256,2304]{1,0:T(8,128)}, u32[]{:S(2)}) copy-start(f32[256,2304]{1,0:T(8,128)} %copy-done) | copy-start | bytes 7077892
  123.2 9.1 %collective-permute-start.25 = (bf16[144,512]{1,0:T(8,128)(2,1)S(1)}, bf16[144,512]{1,0:T(8,128)(2,1)S(1)}, u32[]{:S(2)}, u32[]{:S(2)}) collective-permute-start(bf16[144,512]{1,0:T(8,128)(2,1)S(1)} %get-tuple-element.165), channel_id=1, source_target_pairs={{0,2},{2,4},{4,6},{6,0},{1,3},{3,5},{5,7},{7,1},{8,10},{10,12},{12... | collective-permute-start | bytes 442376 | tf_op jit(solution)/shard_map/ppermute | solution.py:306
  125.0 16.4 %collective-permute-start.26 = (bf16[144,512]{1,0:T(8,128)(2,1)S(1)}, bf16[144,512]{1,0:T(8,128)(2,1)S(1)}, u32[]{:S(2)}, u32[]{:S(2)}) collective-permute-start(bf16[144,512]{1,0:T(8,128)(2,1)S(1)} %get-tuple-element.164), channel_id=1, source_target_pairs={{0,4},{2,6},{4,0},{6,2},{1,5},{3,7},{5,1},{7,3},{8,12},{10,14},{12... | collective-permute-start | bytes 442376 | tf_op jit(solution)/shard_map/ppermute | solution.py:306
  126.3 20.5 %collective-permute-start.27 = (bf16[144,512]{1,0:T(8,128)(2,1)S(1)}, bf16[144,512]{1,0:T(8,128)(2,1)S(1)}, u32[]{:S(2)}, u32[]{:S(2)}) collective-permute-start(bf16[144,512]{1,0:T(8,128)(2,1)S(1)} %get-tuple-element.163), channel_id=1, source_target_pairs={{0,6},{2,0},{4,2},{6,4},{1,7},{3,1},{5,3},{7,5},{8,14},{10,8},{12,... | collective-permute-start | bytes 442376 | tf_op jit(solution)/shard_map/ppermute | solution.py:306
  127.7 19.1 %copy-start.5 = (f32[512,512]{1,0:T(8,128)S(1)}, f32[512,512]{1,0:T(8,128)}, u32[]{:S(2)}) copy-start(f32[512,512]{1,0:T(8,128)} %copy-done.4) | copy-start | bytes 3145732
  147.0 3.5 %collective-permute-start.28 = (bf16[256,512]{1,0:T(8,128)(2,1)S(1)}, bf16[256,512]{1,0:T(8,128)(2,1)S(1)}, u32[]{:S(2)}, u32[]{:S(2)}) collective-permute-start(bf16[256,512]{1,0:T(8,128)(2,1)S(1)} %slice.121), channel_id=1, source_target_pairs={{0,1},{1,0},{2,3},{3,2},{4,5},{5,4},{6,7},{7,6},{8,9},{9,8},{10,11... | collective-permute-start | bytes 786440 | tf_op jit(solution)/shard_map/ppermute | solution.py:297
  148.3 1.4 collective-permute-start.29

commit v6 on v5

--- a/solution.py
+++ b/solution.py
@@ -220,6 +220,65 @@
     )(*args)
 
 
+def column_kernel(info, *refs):
+    *pieces, own, other = refs
+    chip, core = info[0], info[1]
+    chips = len(pieces)
+    half = own.shape[2]
+    for k, ref in enumerate(pieces):
+        at = lax.rem(chip - k + chips, chips)
+        left, right = ref[:, :half], ref[:, half:]
+        own[at] = jnp.where(core == 0, left, right)
+        other[at] = jnp.where(core == 0, right, left)
+
+
+def column_halves(info, pieces):
+    rows, width = pieces[0].shape
+    shape = jax.ShapeDtypeStruct((len(pieces), rows, width // 2), BF16)
+    vmem = pl.BlockSpec(memory_space=pltpu.VMEM)
+    return pl.pallas_call(
+        column_kernel,
+        out_shape=(shape, shape),
+        in_specs=[pl.BlockSpec(memory_space=pltpu.SMEM)] + [vmem] * len(pieces),
+        out_specs=(vmem, vmem),
+        cost_estimate=pl.CostEstimate(flops=4 * 10**9, bytes_accessed=1, transcendentals=0),
+        compiler_params=pltpu.CompilerParams(vmem_limit_bytes=8 * 1024 * 1024),
+        name="column_halves",
+    )(info, *pieces)
+
+
+def into_heads_kernel(places, info, grad, *refs):
+    *pieces, weight, out = refs
+    half = pieces[0].shape[0]
+    for (k, at), ref in zip(places, pieces):
+        start = ((info[2] ^ k) * 2 + at) * half
+        weight[pl.ds(pl.multiple_of(start, half), half), :] = ref[...]
+    depth = weight.shape[0]
+    wide = 256
+    total = dot(grad[:, :wide], weight[:wide, :])
+    for i in range(wide, depth, wide):
+        total = total + dot(grad[:, i : i + wide], weight[i : i + wide, :])
+    out[...] = total.astype(BF16)
+
+
+def gradient_into_heads(info, grad, pieces):
+    arrays = [x for x, _, _ in pieces]
+    half, width = arrays[0].shape
+    vmem = pl.BlockSpec(memory_space=pltpu.VMEM)
+    return pl.pallas_call(
+        functools.partial(into_heads_kernel, [(k, at) for _, k, at in pieces]),
+        out_shape=(
+            jax.ShapeDtypeStruct((half * len(pieces), width), BF16),
+            jax.ShapeDtypeStruct((grad.shape[0], width), BF16),
+        ),
+        in_specs=[pl.BlockSpec(memory_space=pltpu.SMEM)] + [vmem] * (1 + len(pieces)),
+        out_specs=(vmem, vmem),
+        cost_estimate=FILLER,
+        compiler_params=pltpu.CompilerParams(vmem_limit_bytes=20 * 1024 * 1024),
+        name="gradient_into_heads",
+    )(info, grad, *arrays)
+
+
 def product_kernel(x, w, *outs):
     result = dot(x[...], w[...], NT if len(outs) == 2 else (((1,), (0,)), ((), ())))
     if len(outs) == 2:
@@ -282,7 +341,7 @@
     prior = min(-(-WINDOW // rows), chips - 1)
     steps = tuple(range(prior + 1))
     low = core == 0
-    info = jnp.stack([chip, core]).astype(jnp.int32)
+    info = jnp.stack([chip, core, row]).astype(jnp.int32)
     together = lax.optimization_barrier
 
     def own(x):
@@ -324,33 +383,30 @@
     hop = up(kv, 1)
     q = jnp.concatenate([own(q0), swap(other(q0))], 0) * jnp.asarray(HD ** (-0.5), BF16)
     state = forward(info, q, kv, 0, None, False)
-    hop, q, state, grad_theirs, *moved = together((hop, q, state, swap(g0), *moved))
-    chunks = [kv, hop]
-
     piece = out_weight.shape[0]
     part = 2 * piece
     if near:
-        column = jnp.zeros((chips, *out_weight.shape), BF16)
-        column = lax.dynamic_update_index_in_dim(column, out_weight, chip, 0)
-        for k, got in enumerate(moved, 1):
-            source = lax.rem(chip - k + chips, chips)
-            column = lax.dynamic_update_index_in_dim(column, got, source, 0)
+        column, column_theirs = column_halves(info, [out_weight, *moved])
     else:
         column = lax.all_gather(out_weight, "chip", axis=0)
-    ours = in_order(own(column)[:, None], swap(other(column))[:, None], 1)
+        column, column_theirs = own(column), other(column)
+    ours = in_order(column[:, None], swap(column_theirs)[:, None], 1)
     ours = ours.reshape(chips * part, ours.shape[-1])
     share = ours.shape[0]
     half = share // 2
-    ours, *state = together((ours, *state))
-
     lower, upper = ours[:half], ours[half:]
+    hop, q, state, lower, upper = together((hop, q, state, lower, upper))
+    chunks = [kv, hop]
+
     hop = up(hop, 1)
     state = forward(info, q, chunks[1], 1, state, False)
-    *by_plane, hop, state = together(
-        (across(lower, 1), across(upper, 1), across(lower, 2), across(upper, 2), hop, state)
+    upper_x, lower_y, grad_theirs, hop, state, lower, upper = together(
+        (across(upper, 1), across(lower, 2), swap(g0), hop, state, lower, upper)
     )
     chunks.append(hop)
-    diagonal = [across(by_plane[2], 1), across(by_plane[1], 2)]
+    last_hop = up(hop, 1)
+    lower_x, upper_y = across(lower, 1), across(upper, 2)
+    diagonal = [across(lower_y, 1), across(upper_x, 2)]
     grad = jnp.concatenate([g0, grad_theirs], 0)
     turned = grad.T
 
@@ -362,32 +418,24 @@
         jnp.concatenate([strip(3, half, half), strip(2, half, half)], 0),
         jnp.concatenate([strip(1, half, half), strip(2, 0, half), strip(0, 0, share)], 0),
     ]
-    last_hop = up(hop, 1)
     for step in steps[2:prior]:
         state = forward(info, q, hop, step, state, False)
         hop = last_hop
         if step + 1 < prior:
             chunks.append(hop)
             last_hop = up(hop, 1)
-    weight = jnp.zeros((rows_dp * share, ours.shape[1]), BF16)
-    for got, k, at in (
-        (ours, 0, 0),
-        (by_plane[0], 1, 0),
-        (by_plane[1], 1, half),
-        (by_plane[2], 2, 0),
-        (by_plane[3], 2, half),
-        (diagonal[0], 3, 0),
-        (diagonal[1], 3, half),
-    ):
-        weight = lax.dynamic_update_slice_in_dim(weight, got, (row ^ k) * share + at, 0)
-    da = dot(grad, weight).astype(BF16)
-    da, last_hop, state, *strips = together((da, last_hop, state, *strips))
+    last_hop, state, *strips = together((last_hop, state, *strips))
     chunks.append(last_hop)
     att, lse_t = forward(info, q, last_hop, prior, state, True)
 
     to_x, to_y = [dot(x, att).astype(BF16) for x in strips[:2]]
-    to_x, to_y, da, att = together((to_x, to_y, da, att))
-    part_mine, part_sent = layer_product(att, weight)
+    to_x, to_y, att, grad = together((to_x, to_y, att, grad))
+    weight, da = gradient_into_heads(
+        info,
+        grad,
+        [(lower, 0, 0), (upper, 0, 1), (lower_x, 1, 0), (upper_x, 1, 1), (lower_y, 2, 0)]
+        + [(upper_y, 2, 1), (diagonal[0], 3, 0), (diagonal[1], 3, 1)],
+    )
     carried = None
     terms = {}
     for step in reversed(steps):
@@ -405,15 +453,16 @@
     for step in range(prior - 1, 2, -1):
         passing = (terms[step].astype(F32) + down(passing, 1).astype(F32)).astype(BF16)
     rest = strip_product(strips[2], att)
-    from_x, from_y, got, part_sent, rest, terms, dq = together(
-        (across(to_x, 1), across(to_y, 2), down(passing, 1), part_sent, rest, terms, dq)
-    )
+    from_x, from_y, got, rest, terms, dq, att = together(
+        (across(to_x, 1), across(to_y, 2), down(passing, 1), rest, terms, dq, att)
+    )
+    part_mine, part_sent = layer_product(att, weight)
     later_x, later_y, here = rest[:half], rest[half:share], rest[share:]
     passing = (terms[2].astype(F32) + got.astype(F32)).astype(BF16)
     to_x = (later_x + from_y[:half].astype(F32)).astype(BF16)
     to_y = (later_y + from_x[:half].astype(F32)).astype(BF16)
-    by_x1, by_y0, dq_theirs, layer_theirs, got = together(
-        (across(to_x, 1), across(to_y, 2), swap(dq[tok:]), swap(part_sent), down(passing, 1))
+    by_x1, by_y0, dq_theirs, part_sent, got = together(
+        (across(to_x, 1), across(to_y, 2), swap(dq[tok:]), part_sent, down(passing, 1))
     )
     passing = (terms[1].astype(F32) + got.astype(F32)).astype(BF16)
     coming = down(passing, 1)
@@ -425,7 +474,7 @@
         0,
     )
 
-    layer_out = (part_mine + layer_theirs.astype(F32)).astype(BF16)
+    layer_out = (part_mine + swap(part_sent).astype(F32)).astype(BF16)
     query_grad = in_order(dq[:tok], dq_theirs, 1)
     if near:
         final = lax.dynamic_slice_in_dim(mine, chip * part, part, 0)

time: 152 us -> 143 us (0.941)
  waiting for transfers between devices: 63.7 us -> 43.1 us
  other arithmetic: 15.3 us -> 24.2 us
  Pallas kernels: 18.1 us -> 20 us
    ppermute x6, waiting for transfers between devices: 31.5 us -> 13.9 us  [round_chips(): return lax.ppermute(x, 'chip', [(i, (i + k) % chips) for i in range(chips)])]
    ppermute x3, waiting for transfers between devices: 6.18 us -> 13.5 us  [down(): return lax.ppermute(x, 'chip', [(i + k, i) for i in range(chips - k)])]
    ppermute x10, waiting for transfers between devices: 9.71 us -> 3.87 us  [across(): return lax.ppermute(x, 'dp', [(i, i ^ k) for i in range(rows_dp)])]
    ppermute x8, waiting for transfers between devices: 5.52 us -> 0.72 us  [swap(): return lax.ppermute(x, 'core', [(0, 1), (1, 0)])]
    dynamic_update_slice x11 -> x0, local copies, waits for them, and re-layouts: 4.08 us -> none  [the longest x3 2.95 us: on_device(): column = lax.dynamic_update_index_in_dim(column, got, source, 0)]
    ppermute x3, starting transfers between devices: 10.3 us -> 6.69 us  [up(): return lax.ppermute(x, 'chip', [(i, i + k) for i in range(chips - k)])]
    pallas_call x0 -> x2, Pallas kernels: none -> 3.54 us  [the longest x1 2.95 us: gradient_into_heads(): pl.pallas_call(functools.partial(into_heads_kernel, [(k, at) for _, k, at...]
    select_n x3, other arithmetic: 0.09 us -> 3.41 us  [own(): return jnp.where(low, x[..., :half], x[..., half:])]
  transfers between devices with their start and end apart: 30 -> 30, of which waited for: 13 -> 11; matrix products, arithmetic and copies ran while one was open for 12% -> 22% of each run, Pallas kernels for 11% -> 14%
where the time goes in v6:
time: 143 us; the launch traced here: 142 us
  waiting for transfers between devices  43.1 us (30%)
  starting transfers between devices  40.1 us (28%)
  other arithmetic  24.2 us (17%)
  Pallas kernels  20 us (14%)
  local copies, waits for them, and re-layouts  10.8 us (8%)
  matrix products  2.59 us (2%)
    ppermute x6, waiting for transfers between devices, round_chips(): return lax.ppermute(x, 'chip', [(i, (i + k) % chips) for i in range(chips)])  13.9 us
    ppermute x3, waiting for transfers between devices, down(): return lax.ppermute(x, 'chip', [(i + k, i) for i in range(chips - k)])  13.5 us
    ppermute x3, waiting for transfers between devices, up(): return lax.ppermute(x, 'chip', [(i, i + k) for i in range(chips - k)])  11.1 us
    ppermute x8, starting transfers between devices, swap(): return lax.ppermute(x, 'core', [(0, 1), (1, 0)])  9.57 us
    ppermute x6, starting transfers between devices, round_chips(): return lax.ppermute(x, 'chip', [(i, (i + k) % chips) for i in range(chips)])  8.84 us
    ppermute x10, starting transfers between devices, across(): return lax.ppermute(x, 'dp', [(i, i ^ k) for i in range(rows_dp)])  8.41 us
    ppermute x3, starting transfers between devices, up(): return lax.ppermute(x, 'chip', [(i, i + k) for i in range(chips - k)])  6.69 us
    ppermute x3, starting transfers between devices, down(): return lax.ppermute(x, 'chip', [(i + k, i) for i in range(chips - k)])  6.63 us
  transfers between devices with their start and end apart: 30, of which 11 were waited for; matrix products, arithmetic and copies ran while one was open for 22% of the time, Pallas kernels for 14%

profile of v6, /device:TPU:9, one launch (start us, length us, event | category | flops | bytes accessed | tf_op | source)
XLA Modules:
  0.0 142.1 jit_solution(10921592243799865531)
XLA Ops:
  0.6 1.3 collective-permute-start.3
  2.0 1.1 collective-permute-start.4
  3.1 1.4 collective-permute-start.5
  4.5 1.0 broadcast_select_fusion.5
  5.5 1.7 %broadcast_select_fusion.4 = (bf16[256,256]{1,0:T(8,128)(2,1)}, bf16[256,256]{1,0:T(8,128)(2,1)S(1)}) fusion(pred[]{:T(512)S(6)} %eq.3, bf16[256,512]{1,0:T(8,128)(2,1)} %bitcast.47), kind=kLoop, calls=%fused_computation.65 | loop fusion | flops 131072 | bytes 524289 | tf_op jit(solution)/shard_map/jit(_where)/select_n | solution.py:349
  7.9 1.5 %collective-permute-start = (bf16[256,512]{1,0:T(8,128)(2,1)}, bf16[256,512]{1,0:T(8,128)(2,1)S(1)}, u32[]{:S(2)}, u32[]{:S(2)}) collective-permute-start(bf16[256,512]{1,0:T(8,128)(2,1)} %pad_maximum_fusion.5), channel_id=1, source_target_pairs={{0,1},{1,0},{2,3},{3,2},{4,5},{5,4},{6,7},{7,6},{8,9},{9,8},{10,11... | collective-permute-start | bytes 786440 | tf_op jit(solution)/shard_map/ppermute | solution.py:356
  9.4 0.7 broadcast_select_fusion.1
  10.2 4.1 %collective-permute-done.4.refs_2_ = bf16[72,1024]{1,0:T(8,128)(2,1)S(1)} collective-permute-done((bf16[72,1024]{1,0:T(8,128)(2,1)}, bf16[72,1024]{1,0:T(8,128)(2,1)S(1)}, u32[]{:S(2)}, u32[]{:S(2)}) %collective-permute-start.4) | collective-permute-done | bytes 147488 | tf_op jit(solution)/shard_map/ppermute | solution.py:365
  14.3 2.7 %collective-permute-done.5.refs_3_ = bf16[72,1024]{1,0:T(8,128)(2,1)S(1)} collective-permute-done((bf16[72,1024]{1,0:T(8,128)(2,1)}, bf16[72,1024]{1,0:T(8,128)(2,1)S(1)}, u32[]{:S(2)}, u32[]{:S(2)}) %collective-permute-start.5) | collective-permute-done | bytes 147488 | tf_op jit(solution)/shard_map/ppermute | solution.py:365
  18.2 1.4 copy.12
  19.7 1.9 %collective-permute-start.1 = (bf16[512,512]{1,0:T(8,128)(2,1)S(1)}, bf16[512,512]{1,0:T(8,128)(2,1)S(1)}, u32[]{:S(2)}, u32[]{:S(2)}) collective-permute-start(bf16[512,512]{1,0:T(8,128)(2,1)S(1)} %pad_maximum_fusion.4.kv.refs_0_), channel_id=1, source_target_pairs={{0,2},{2,4},{4,6},{1,3},{3,5},{5,7},{8,10},{10,12},{12,14},{9,11},... | collective-permute-start | bytes 1572872 | tf_op jit(solution)/shard_map/ppermute | solution.py:359
  21.6 1.0 maximum_multiply_fusion.q
  22.7 2.1 %attend_forward.4 = (f32[16,512]{1,0:T(8,128)S(1)}, f32[16,512]{1,0:T(8,128)S(1)}, f32[512,512]{1,0:T(8,128)S(1)}) custom-call(s32[3]{0:T(128)S(1)} %pad_add_fusion.info, bf16[512,512]{1,0:T(8,128)(2,1)S(1)} %maximum_multiply_fusion.q, bf16[512,512]{1,0:T(8,128)(2,1)S(1)} %pad_maximum_fusion.4.kv.refs_0_), custom_call_target="tpu_custom_call" | custom-call | flops 1 | bytes 1 | tf_op jit(solution)/shard_map/attend_forward/pallas_call | solution.py:110
  24.8 1.1 maximum_select_fusion
  26.1 0.8 copy.11
  26.9 7.7 %collective-permute-done.1.kv.refs_0_ = bf16[512,512]{1,0:T(8,128)(2,1)S(1)} collective-permute-done((bf16[512,512]{1,0:T(8,128)(2,1)S(1)}, bf16[512,512]{1,0:T(8,128)(2,1)S(1)}, u32[]{:S(2)}, u32[]{:S(2)}) %collective-permute-start.1) | collective-permute-done | bytes 524320 | tf_op jit(solution)/shard_map/ppermute | solution.py:359
  34.6 2.2 %collective-permute-start.10 = (bf16[512,512]{1,0:T(8,128)(2,1)S(1)}, bf16[512,512]{1,0:T(8,128)(2,1)S(1)}, u32[]{:S(2)}, u32[]{:S(2)}) collective-permute-start(bf16[512,512]{1,0:T(8,128)(2,1)S(1)} %collective-permute-done.1.kv.refs_0_), channel_id=1, source_target_pairs={{0,2},{2,4},{4,6},{1,3},{3,5},{5,7},{8,10},{10,12},{12,14},{9,11},... | collective-permute-start | bytes 1572872 | tf_op jit(solution)/shard_map/ppermute | solution.py:359
  36.8 1.3 collective-permute-start.7
  38.1 1.2 collective-permute-start.8
  39.3 1.9 %attend_forward.5 = (f32[16,512]{1,0:T(8,128)S(1)}, f32[16,512]{1,0:T(8,128)S(1)}, f32[512,512]{1,0:T(8,128)S(1)}) custom-call(s32[3]{0:T(128)S(1)} %pad_add_fusion.info, bf16[512,512]{1,0:T(8,128)(2,1)S(1)} %maximum_multiply_fusion.q, bf16[512,512]{1,0:T(8,128)(2,1)S(1)} %collective-permute-done.1.kv.refs_0_, f32[16,512]{1,0:T(8,128)S(1)} %get-tuple-element.87.refs_0_, ...), custom_call_target="tpu_custom_call" | custom-call | flops 1 | bytes 1 | tf_op jit(solution)/shard_map/attend_forward/pallas_call | solution.py:110
  41.3 3.1 %collective-permute-done.7.refs_3_ = bf16[288,512]{1,0:T(8,128)(2,1)} collective-permute-done((bf16[288,512]{1,0:T(8,128)(2,1)}, bf16[288,512]{1,0:T(8,128)(2,1)}, u32[]{:S(2)}, u32[]{:S(2)}) %collective-permute-start.7) | collective-permute-done | bytes 294944 | tf_op jit(solution)/shard_map/ppermute | solution.py:368
  45.1 3.4 %collective-permute-done.10.kv.refs_0_ = bf16[512,512]{1,0:T(8,128)(2,1)S(1)} collective-permute-done((bf16[512,512]{1,0:T(8,128)(2,1)S(1)}, bf16[512,512]{1,0:T(8,128)(2,1)S(1)}, u32[]{:S(2)}, u32[]{:S(2)}) %collective-permute-start.10) | collective-permute-done | bytes 524320 | tf_op jit(solution)/shard_map/ppermute | solution.py:359
  48.6 2.5 %collective-permute-start.11 = (bf16[512,512]{1,0:T(8,128)(2,1)S(1)}, bf16[512,512]{1,0:T(8,128)(2,1)S(1)}, u32[]{:S(2)}, u32[]{:S(2)}) collective-permute-start(bf16[512,512]{1,0:T(8,128)(2,1)S(1)} %collective-permute-done.10.kv.refs_0_), channel_id=1, source_target_pairs={{0,2},{2,4},{4,6},{1,3},{3,5},{5,7},{8,10},{10,12},{12,14},{9,11},... | collective-permute-start | bytes 1572872 | tf_op jit(solution)/shard_map/ppermute | solution.py:359
  51.1 1.3 collective-permute-start.14
  52.4 1.2 collective-permute-start.15
  54.1 1.1 fusion.1
  55.2 1.6 %fusion.9 = (bf16[288,512]{1,0:T(8,128)(2,1)S(1)}, bf16[288,512]{1,0:T(8,128)(2,1)S(1)}, bf16[288,512]{1,0:T(8,128)(2,1)S(1)}, bf16[288,512]{1,0:T(8,128)(2,1)S(...) fusion(s32[]{:T(128)S(6)} %select_n.139, bf16[256,2304]{0,1:T(8,128)(2,1)} %collective-permute-done.9, ...), kind=kLoop, calls=%fused_computation.47 | loop fusion | flops 3538944 | bytes 4128792 | tf_op jit(solution)/shard_map/dynamic_slice | solution.py:414
  56.9 1.1 pad_maximum_fusion.1.x
  58.7 3.2 %pad_maximum_fusion = bf16[512,2304]{0,1:T(8,128)(2,1)} fusion(bf16[256,2304]{0,1:T(8,128)(2,1)} %collective-permute-done.9, bf16[256,2304]{0,1:T(8,128)(2,1)} %bitcast.10), kind=kLoop, calls=%fused_computation.7 | loop fusion | flops 4718592 | bytes 4718592 | tf_op jit(solution)/shard_map/concatenate | solution.py:410
  61.9 0.8 attend_forward.7
  62.7 1.3 convolution_convert_fusion
  64.0 1.3 convolution_convert_fusion.1
  65.3 1.2 collective-permute-start.12
  67.3 1.2 collective-permute-start.13
  68.5 2.8 %copy.13.grad = bf16[512,2304]{1,0:T(8,128)(2,1)S(1)} copy(bf16[512,2304]{0,1:T(8,128)(2,1)} %pad_maximum_fusion) | data formatting | bytes 4718592 | tf_op jit(solution)/shard_map/optimization_barrier | solution.py:432
  71.4 1.0 copy-done.12
  72.4 1.0 copy-done.18
  73.4 2.9 %gradient_into_heads.1 = (bf16[2304,512]{1,0:T(8,128)(2,1)S(1)}, bf16[512,512]{1,0:T(8,128)(2,1)S(1)}) custom-call(s32[3]{0:T(128)S(1)} %pad_add_fusion.info, bf16[512,2304]{1,0:T(8,128)(2,1)S(1)} %copy.13.grad, bf16[288,512]{1,0:T(8,128)(2,1)S(1)} %bitcast.41, bf16[288,512]{1,0:T(8,128)(2,1)} %bitcast.9.refs_1_, bf16[288,512]{1,0:T(8,128)(2,1)S(1)} %copy-done.18, ...), custom_call_target="tpu_custom_call" | custom-call | flops 1 | bytes 1 | tf_op jit(solution)/shard_map/gradient_into_heads/pallas_call | solution.py:268
  76.3 1.1 attend_backward.4
  77.4 2.8 %collective-permute-start.18 = (bf16[512,512]{1,0:T(8,128)(2,1)S(1)}, bf16[512,512]{1,0:T(8,128)(2,1)S(1)}, u32[]{:S(2)}, u32[]{:S(2)}) collective-permute-start(bf16[512,512]{1,0:T(8,128)(2,1)S(1)} %get-tuple-element.118), channel_id=1, source_target_pairs={{2,0},{4,2},{6,4},{3,1},{5,3},{7,5},{10,8},{12,10},{14,12},{11,9},... | collective-permute-start | bytes 1572872 | tf_op jit(solution)/shard_map/ppermute | solution.py:362
  81.3 2.3 %attend_backward.6 = (bf16[512,512]{1,0:T(8,128)(2,1)S(1)}, f32[512,512]{1,0:T(8,128)S(1)}) custom-call(s32[3]{0:T(128)S(1)} %pad_add_fusion.info, bf16[512,512]{1,0:T(8,128)(2,1)S(1)} %maximum_multiply_fusion.q, bf16[512,512]{1,0:T(8,128)(2,1)S(1)} %get-tuple-element.115.da, f32[16,512]{1,0:T(8,128)S(1)} %get-tuple-element.116.lse_t, ...), custom_call_target="tpu_custom_call" | custom-call | flops 1 | bytes 1 | tf_op jit(solution)/shard_map/attend_backward/pallas_call | solution.py:211
  83.6 2.5 %attend_backward.7 = (f32[512,512]{1,0:T(8,128)S(1)}, bf16[512,512]{1,0:T(8,128)(2,1)S(1)}) custom-call(s32[3]{0:T(128)S(1)} %pad_add_fusion.info, bf16[512,512]{1,0:T(8,128)(2,1)S(1)} %maximum_multiply_fusion.q, bf16[512,512]{1,0:T(8,128)(2,1)S(1)} %get-tuple-element.115.da, f32[16,512]{1,0:T(8,128)S(1)} %get-tuple-element.116.lse_t, ...), custom_call_target="tpu_custom_call" | custom-call | flops 1 | bytes 1 | tf_op jit(solution)/shard_map/attend_backward/pallas_call | solution.py:211
  86.1 1.3 strip_product.1
  87.4 2.2 %collective-permute-done.18 = bf16[512,512]{1,0:T(8,128)(2,1)S(1)} collective-permute-done((bf16[512,512]{1,0:T(8,128)(2,1)S(1)}, bf16[512,512]{1,0:T(8,128)(2,1)S(1)}, u32[]{:S(2)}, u32[]{:S(2)}) %collective-permute-start.18) | collective-permute-done | bytes 524320 | tf_op jit(solution)/shard_map/ppermute | solution.py:362
  89.7 0.9 add_convert_fusion.3
  90.6 1.9 %collective-permute-start.22 = (bf16[512,512]{1,0:T(8,128)(2,1)}, bf16[512,512]{1,0:T(8,128)(2,1)}, u32[]{:S(2)}, u32[]{:S(2)}) collective-permute-start(bf16[512,512]{1,0:T(8,128)(2,1)} %add_convert_fusion.3), channel_id=1, source_target_pairs={{2,0},{4,2},{6,4},{3,1},{5,3},{7,5},{10,8},{12,10},{14,12},{11,9},... | collective-permute-start | bytes 1572872 | tf_op jit(solution)/shard_map/ppermute | solution.py:362
  92.5 2.0 %add_convert_fusion.4 = (bf16[288,512]{1,0:T(8,128)(2,1)}, bf16[288,512]{1,0:T(8,128)(2,1)}) fusion(f32[1152,512]{1,0:T(8,128)S(1)} %strip_product.1, bf16[576,512]{1,0:T(8,128)(2,1)} %collective-permute-done.12, bf16[576,512]{1,0:T(8,128)(2,1)} %collective-permute-done.13), kind=kLoop, calls=%fused_computation.30 | loop fusion | flops 884736 | bytes 2359296 | tf_op jit(solution)/shard_map/convert_element_type | solution.py:463
  95.8 5.7 %collective-permute-start.21 = (bf16[256,512]{1,0:T(8,128)(2,1)}, bf16[256,512]{1,0:T(8,128)(2,1)S(1)}, u32[]{:S(2)}, u32[]{:S(2)}) collective-permute-start(bf16[256,512]{1,0:T(8,128)(2,1)} %get-tuple-element.167), channel_id=1, source_target_pairs={{0,1},{1,0},{2,3},{3,2},{4,5},{5,4},{6,7},{7,6},{8,9},{9,8},{10,11... | collective-permute-start | bytes 786440 | tf_op jit(solution)/shard_map/ppermute | solution.py:356
  101.5 1.7 %copy-done.4 = bf16[2304,512]{1,0:T(8,128)(2,1)S(1)} copy-done((bf16[2304,512]{1,0:T(8,128)(2,1)S(1)}, bf16[2304,512]{1,0:T(8,128)(2,1)}, u32[]{:S(2)}) %copy-start.4) | copy-done | bytes 2359320
  103.1 3.2 %layer_product.1 = (f32[256,2304]{1,0:T(8,128)S(1)}, bf16[256,2304]{1,0:T(8,128)(2,1)S(1)}) custom-call(bf16[512,512]{1,0:T(8,128)(2,1)S(1)} %get-tuple-element.133.refs_1_.w.x, bf16[2304,512]{1,0:T(8,128)(2,1)S(1)} %copy-done.4), custom_call_target="tpu_custom_call" | custom-call | flops 1 | bytes 1 | tf_op jit(solution)/shard_map/layer_product/pallas_call | solution.py:297
  106.3 1.1 collective-permute-start.24
  107.5 1.1 convert_add_fusion.1
  108.6 1.1 convert_add_fusion
  110.1 1.5 %collective-permute-start.25 = (bf16[144,512]{1,0:T(8,128)(2,1)S(1)}, bf16[144,512]{1,0:T(8,128)(2,1)S(1)}, u32[]{:S(2)}, u32[]{:S(2)}) collective-permute-start(bf16[144,512]{1,0:T(8,128)(2,1)S(1)} %get-tuple-element.161), channel_id=1, source_target_pairs={{0,2},{2,4},{4,6},{6,0},{1,3},{3,5},{5,7},{7,1},{8,10},{10,12},{12... | collective-permute-start | bytes 442376 | tf_op jit(solution)/shard_map/ppermute | solution.py:365
  111.6 2.1 %collective-permute-start.26 = (bf16[144,512]{1,0:T(8,128)(2,1)S(1)}, bf16[144,512]{1,0:T(8,128)(2,1)S(1)}, u32[]{:S(2)}, u32[]{:S(2)}) collective-permute-start(bf16[144,512]{1,0:T(8,128)(2,1)S(1)} %get-tuple-element.160), channel_id=1, source_target_pairs={{0,4},{2,6},{4,0},{6,2},{1,5},{3,7},{5,1},{7,3},{8,12},{10,14},{12... | collective-permute-start | bytes 442376 | tf_op jit(solution)/shard_map/ppermute | solution.py:365
  113.7 1.4 collective-permute-start.27
  115.1 1.2 add_convert_fusion.2
  116.3 2.0 %collective-permute-start.23 = (bf16[512,512]{1,0:T(8,128)(2,1)S(1)}, bf16[512,512]{1,0:T(8,128)(2,1)S(1)}, u32[]{:S(2)}, u32[]{:S(2)}) collective-permute-start(bf16[512,512]{1,0:T(8,128)(2,1)S(1)} %add_convert_fusion.2), channel_id=1, source_target_pairs={{2,0},{4,2},{6,4},{3,1},{5,3},{7,5},{10,8},{12,10},{14,12},{11,9},... | collective-permute-start | bytes 1572872 | tf_op jit(solution)/shard_map/ppermute | solution.py:362
  118.2 0.9 maximum_select_fusion.1
  119.2 1.2 add_convert_fusion
  120.4 4.0 %collective-permute-done.26 = bf16[144,512]{1,0:T(8,128)(2,1)S(1)} collective-permute-done((bf16[144,512]{1,0:T(8,128)(2,1)S(1)}, bf16[144,512]{1,0:T(8,128)(2,1)S(1)}, u32[]{:S(2)}, u32[]{:S(2)}) %collective-permute-start.26) | collective-permute-done | bytes 147488 | tf_op jit(solution)/shard_map/ppermute | solution.py:365
  124.4 3.2 %collective-permute-done.27 = bf16[144,512]{1,0:T(8,128)(2,1)S(1)} collective-permute-done((bf16[144,512]{1,0:T(8,128)(2,1)S(1)}, bf16[144,512]{1,0:T(8,128)(2,1)S(1)}, u32[]{:S(2)}, u32[]{:S(2)}) %collective-permute-start.27) | collective-permute-done | bytes 147488 | tf_op jit(solution)/shard_map/ppermute | solution.py:365
  127.5 11.2 %collective-permute-done.23 = bf16[512,512]{1,0:T(8,128)(2,1)S(1)} collective-permute-done((bf16[512,512]{1,0:T(8,128)(2,1)S(1)}, bf16[512,512]{1,0:T(8,128)(2,1)S(1)}, u32[]{:S(2)}, u32[]{:S(2)}) %collective-permute-start.23) | collective-permute-done | bytes 524320 | tf_op jit(solution)/shard_map/ppermute | solution.py:362
  141.2 0.9 maximum_select_fusion.3
  (93 shorter events, 9.7 us)
Async XLA Ops:
  0.6 8.8 %copy-start.21 = (bf16[1,256,1024]{2,1,0:T(8,128)(2,1)S(1)}, bf16[1,256,1024]{2,1,0:T(8,128)(2,1)}, u32[]{:S(2)}) copy-start(bf16[1,256,1024]{2,1,0:T(8,128)(2,1)} %param.5) | copy-start | bytes 1572868
  0.6 9.6 %collective-permute-start.3 = (bf16[72,1024]{1,0:T(8,128)(2,1)}, bf16[72,1024]{1,0:T(8,128)(2,1)S(1)}, u32[]{:S(2)}, u32[]{:S(2)}) collective-permute-start(bf16[72,1024]{1,0:T(8,128)(2,1)} %refs_0_.1), channel_id=1, source_target_pairs={{0,2},{2,4},{4,6},{6,0},{1,3},{3,5},{5,7},{7,1},{8,10},{10,12},{12... | collective-permute-start | bytes 442376 | tf_op jit(solution)/shard_map/ppermute | solution.py:365
  2.0 12.3 %collective-permute-start.4 = (bf16[72,1024]{1,0:T(8,128)(2,1)}, bf16[72,1024]{1,0:T(8,128)(2,1)S(1)}, u32[]{:S(2)}, u32[]{:S(2)}) collective-permute-start(bf16[72,1024]{1,0:T(8,128)(2,1)} %refs_0_.1), channel_id=1, source_target_pairs={{0,4},{2,6},{4,0},{6,2},{1,5},{3,7},{5,1},{7,3},{8,12},{10,14},{12... | collective-permute-start | bytes 442376 | tf_op jit(solution)/shard_map/ppermute | solution.py:365
  3.1 13.9 %collective-permute-start.5 = (bf16[72,1024]{1,0:T(8,128)(2,1)}, bf16[72,1024]{1,0:T(8,128)(2,1)S(1)}, u32[]{:S(2)}, u32[]{:S(2)}) collective-permute-start(bf16[72,1024]{1,0:T(8,128)(2,1)} %refs_0_.1), channel_id=1, source_target_pairs={{0,6},{2,0},{4,2},{6,4},{1,7},{3,1},{5,3},{7,5},{8,14},{10,8},{12,... | collective-permute-start | bytes 442376 | tf_op jit(solution)/shard_map/ppermute | solution.py:365
  5.5 11.5 %copy-start.19 = (bf16[72,1024]{1,0:T(8,128)(2,1)S(1)}, bf16[72,1024]{1,0:T(8,128)(2,1)}, u32[]{:S(2)}) copy-start(bf16[72,1024]{1,0:T(8,128)(2,1)} %refs_0_.1) | copy-start | bytes 442372
  7.9 11.7 %collective-permute-start = (bf16[256,512]{1,0:T(8,128)(2,1)}, bf16[256,512]{1,0:T(8,128)(2,1)S(1)}, u32[]{:S(2)}, u32[]{:S(2)}) collective-permute-start(bf16[256,512]{1,0:T(8,128)(2,1)} %pad_maximum_fusion.5), channel_id=1, source_target_pairs={{0,1},{1,0},{2,3},{3,2},{4,5},{5,4},{6,7},{7,6},{8,9},{9,8},{10,11... | collective-permute-start | bytes 786440 | tf_op jit(solution)/shard_map/ppermute | solution.py:356
  10.1 11.5 %collective-permute-start.2 = (bf16[256,512]{1,0:T(8,128)(2,1)}, bf16[256,512]{1,0:T(8,128)(2,1)}, u32[]{:S(2)}, u32[]{:S(2)}) collective-permute-start(bf16[256,512]{1,0:T(8,128)(2,1)} %get-tuple-element.169), channel_id=1, source_target_pairs={{0,1},{1,0},{2,3},{3,2},{4,5},{5,4},{6,7},{7,6},{8,9},{9,8},{10,11... | collective-permute-start | bytes 786440 | tf_op jit(solution)/shard_map/ppermute | solution.py:356
  10.2 8.0 %copy-start.20 = (bf16[1,256,2304]{2,1,0:T(8,128)(2,1)S(1)}, bf16[1,256,2304]{2,1,0:T(8,128)(2,1)}, u32[]{:S(2)}) copy-start(bf16[1,256,2304]{2,1,0:T(8,128)(2,1)} %param.9) | copy-start | bytes 3538948
  17.6 2.0 %copy-start.22 = (bf16[256,256]{1,0:T(8,128)(2,1)S(1)}, bf16[256,256]{1,0:T(8,128)(2,1)}, u32[]{:S(2)}) copy-start(bf16[256,256]{1,0:T(8,128)(2,1)} %get-tuple-element.176) | copy-start | bytes 393220
  17.6 7.2 %collective-permute-start.6 = (bf16[4,72,512]{2,1,0:T(8,128)(2,1)S(1)}, bf16[4,72,512]{2,1,0:T(8,128)(2,1)}, u32[]{:S(2)}, u32[]{:S(2)}) collective-permute-start(bf16[4,72,512]{2,1,0:T(8,128)(2,1)S(1)} %get-tuple-element.82), channel_id=1, source_target_pairs={{0,1},{1,0},{2,3},{3,2},{4,5},{5,4},{6,7},{7,6},{8,9},{9,8},{10,11... | collective-permute-start | bytes 884744 | tf_op jit(solution)/shard_map/ppermute | solution.py:356
  19.6 25.6 %collective-permute-start.9 = (bf16[256,2304]{0,1:T(8,128)(2,1)}, bf16[256,2304]{0,1:T(8,128)(2,1)}, u32[]{:S(2)}, u32[]{:S(2)}) collective-permute-start(bf16[256,2304]{0,1:T(8,128)(2,1)} %bitcast.10), channel_id=1, source_target_pairs={{0,1},{1,0},{2,3},{3,2},{4,5},{5,4},{6,7},{7,6},{8,9},{9,8},{10,11... | collective-permute-start | bytes 3538952 | tf_op jit(solution)/shard_map/ppermute | solution.py:356
  19.7 6.3 %copy-start.1 = (bf16[512,512]{1,0:T(8,128)(2,1)}, bf16[512,512]{1,0:T(8,128)(2,1)S(1)}, u32[]{:S(2)}) copy-start(bf16[512,512]{1,0:T(8,128)(2,1)S(1)} %pad_maximum_fusion.4.kv.refs_0_) | copy-start | bytes 1572868
  19.7 14.9 %collective-permute-start.1 = (bf16[512,512]{1,0:T(8,128)(2,1)S(1)}, bf16[512,512]{1,0:T(8,128)(2,1)S(1)}, u32[]{:S(2)}, u32[]{:S(2)}) collective-permute-start(bf16[512,512]{1,0:T(8,128)(2,1)S(1)} %pad_maximum_fusion.4.kv.refs_0_), channel_id=1, source_target_pairs={{0,2},{2,4},{4,6},{1,3},{3,5},{5,7},{8,10},{10,12},{12,14},{9,11},... | collective-permute-start | bytes 1572872 | tf_op jit(solution)/shard_map/ppermute | solution.py:359
  26.1 25.1 %copy-start.11 = (bf16[2,2,72,512]{3,2,1,0:T(8,128)(2,1)}, bf16[2,2,72,512]{3,2,1,0:T(8,128)(2,1)S(1)}, u32[]{:S(2)}) copy-start(bf16[2,2,72,512]{3,2,1,0:T(8,128)(2,1)S(1)} %copy.10) | copy-start | bytes 884740
  34.6 20.6 %copy-start.7 = (bf16[512,512]{1,0:T(8,128)(2,1)}, bf16[512,512]{1,0:T(8,128)(2,1)S(1)}, u32[]{:S(2)}) copy-start(bf16[512,512]{1,0:T(8,128)(2,1)S(1)} %collective-permute-done.1.kv.refs_0_) | copy-start | bytes 1572868
  34.6 14.0 %collective-permute-start.10 = (bf16[512,512]{1,0:T(8,128)(2,1)S(1)}, bf16[512,512]{1,0:T(8,128)(2,1)S(1)}, u32[]{:S(2)}, u32[]{:S(2)}) collective-permute-start(bf16[512,512]{1,0:T(8,128)(2,1)S(1)} %collective-permute-done.1.kv.refs_0_), channel_id=1, source_target_pairs={{0,2},{2,4},{4,6},{1,3},{3,5},{5,7},{8,10},{10,12},{12,14},{9,11},... | collective-permute-start | bytes 1572872 | tf_op jit(solution)/shard_map/ppermute | solution.py:359
  36.8 7.6 %collective-permute-start.7 = (bf16[288,512]{1,0:T(8,128)(2,1)}, bf16[288,512]{1,0:T(8,128)(2,1)}, u32[]{:S(2)}, u32[]{:S(2)}) collective-permute-start(bf16[288,512]{1,0:T(8,128)(2,1)} %bitcast.9.refs_1_), channel_id=1, source_target_pairs={{0,8},{8,0},{16,24},{24,16},{1,9},{9,1},{17,25},{25,17},{2,10},{10... | collective-permute-start | bytes 884744 | tf_op jit(solution)/shard_map/ppermute | solution.py:368
  38.1 7.0 %collective-permute-start.8 = (bf16[288,512]{1,0:T(8,128)(2,1)S(1)}, bf16[288,512]{1,0:T(8,128)(2,1)}, u32[]{:S(2)}, u32[]{:S(2)}) collective-permute-start(bf16[288,512]{1,0:T(8,128)(2,1)S(1)} %bitcast.39), channel_id=1, source_target_pairs={{0,16},{8,24},{16,0},{24,8},{1,17},{9,25},{17,1},{25,9},{2,18},{10... | collective-permute-start | bytes 884744 | tf_op jit(solution)/shard_map/ppermute | solution.py:368
  48.6 9.5 %copy-start.9 = (bf16[512,512]{1,0:T(8,128)(2,1)}, bf16[512,512]{1,0:T(8,128)(2,1)S(1)}, u32[]{:S(2)}) copy-start(bf16[512,512]{1,0:T(8,128)(2,1)S(1)} %collective-permute-done.10.kv.refs_0_) | copy-start | bytes 1572868
  48.6 13.3 %collective-permute-start.11 = (bf16[512,512]{1,0:T(8,128)(2,1)S(1)}, bf16[512,512]{1,0:T(8,128)(2,1)S(1)}, u32[]{:S(2)}, u32[]{:S(2)}) collective-permute-start(bf16[512,512]{1,0:T(8,128)(2,1)S(1)} %collective-permute-done.10.kv.refs_0_), channel_id=1, source_target_pairs={{0,2},{2,4},{4,6},{1,3},{3,5},{5,7},{8,10},{10,12},{12,14},{9,11},... | collective-permute-start | bytes 1572872 | tf_op jit(solution)/shard_map/ppermute | solution.py:359
  51.1 15.4 %collective-permute-start.14 = (bf16[288,512]{1,0:T(8,128)(2,1)S(1)}, bf16[288,512]{1,0:T(8,128)(2,1)S(1)}, u32[]{:S(2)}, u32[]{:S(2)}) collective-permute-start(bf16[288,512]{1,0:T(8,128)(2,1)S(1)} %bitcast.40), channel_id=1, source_target_pairs={{0,8},{8,0},{16,24},{24,16},{1,9},{9,1},{17,25},{25,17},{2,10},{10... | collective-permute-start | bytes 884744 | tf_op jit(solution)/shard_map/ppermute | solution.py:368
  52.4 19.0 %collective-permute-start.15 = (bf16[288,512]{1,0:T(8,128)(2,1)}, bf16[288,512]{1,0:T(8,128)(2,1)}, u32[]{:S(2)}, u32[]{:S(2)}) collective-permute-start(bf16[288,512]{1,0:T(8,128)(2,1)} %bitcast.9.refs_1_), channel_id=1, source_target_pairs={{0,16},{8,24},{16,0},{24,8},{1,17},{9,25},{17,1},{25,9},{2,18},{10... | collective-permute-start | bytes 884744 | tf_op jit(solution)/shard_map/ppermute | solution.py:368
  53.6 17.7 %collective-permute-start.16 = (bf16[288,512]{1,0:T(8,128)(2,1)}, bf16[288,512]{1,0:T(8,128)(2,1)}, u32[]{:S(2)}, u32[]{:S(2)}) collective-permute-start(bf16[288,512]{1,0:T(8,128)(2,1)} %collective-permute-done.8.refs_4_), channel_id=1, source_target_pairs={{0,8},{8,0},{16,24},{24,16},{1,9},{9,1},{17,25},{25,17},{2,10},{10... | collective-permute-start | bytes 884744 | tf_op jit(solution)/shard_map/ppermute | solution.py:368
  53.9 17.5 %collective-permute-start.17 = (bf16[288,512]{1,0:T(8,128)(2,1)}, bf16[288,512]{1,0:T(8,128)(2,1)}, u32[]{:S(2)}, u32[]{:S(2)}) collective-permute-start(bf16[288,512]{1,0:T(8,128)(2,1)} %collective-permute-done.7.refs_3_), channel_id=1, source_target_pairs={{0,16},{8,24},{16,0},{24,8},{1,17},{9,25},{17,1},{25,9},{2,18},{10... | collective-permute-start | bytes 884744 | tf_op jit(solution)/shard_map/ppermute | solution.py:368
  61.9 2.1 %copy-start.5 = (bf16[512,512]{1,0:T(8,128)(2,1)}, bf16[512,512]{1,0:T(8,128)(2,1)S(1)}, u32[]{:S(2)}) copy-start(bf16[512,512]{1,0:T(8,128)(2,1)S(1)} %collective-permute-done.11.kv.refs_0_) | copy-start | bytes 1572868
  65.3 24.4 %collective-permute-start.12 = (bf16[576,512]{1,0:T(8,128)(2,1)}, bf16[576,512]{1,0:T(8,128)(2,1)}, u32[]{:S(2)}, u32[]{:S(2)}) collective-permute-start(bf16[576,512]{1,0:T(8,128)(2,1)} %convolution_convert_fusion.1), channel_id=1, source_target_pairs={{0,8},{8,0},{16,24},{24,16},{1,9},{9,1},{17,25},{25,17},{2,10},{10... | collective-permute-start | bytes 1769480 | tf_op jit(solution)/shard_map/ppermute | solution.py:368
  66.5 0.7 copy-start.17
  67.3 22.4 %collective-permute-start.13 = (bf16[576,512]{1,0:T(8,128)(2,1)}, bf16[576,512]{1,0:T(8,128)(2,1)}, u32[]{:S(2)}, u32[]{:S(2)}) collective-permute-start(bf16[576,512]{1,0:T(8,128)(2,1)} %convolution_convert_fusion), channel_id=1, source_target_pairs={{0,16},{8,24},{16,0},{24,8},{1,17},{9,25},{17,1},{25,9},{2,18},{10... | collective-permute-start | bytes 1769480 | tf_op jit(solution)/shard_map/ppermute | solution.py:368
  71.3 5.0 %copy-start.6 = (bf16[512,512]{1,0:T(8,128)(2,1)S(1)}, bf16[512,512]{1,0:T(8,128)(2,1)}, u32[]{:S(2)}) copy-start(bf16[512,512]{1,0:T(8,128)(2,1)} %copy-done.5) | copy-start | bytes 1572868
  71.4 1.0 copy-start.12
  72.4 1.0 copy-start.18
  76.3 4.6 %copy-start.3 = (bf16[2304,512]{1,0:T(8,128)(2,1)}, bf16[2304,512]{1,0:T(8,128)(2,1)S(1)}, u32[]{:S(2)}) copy-start(bf16[2304,512]{1,0:T(8,128)(2,1)S(1)} %get-tuple-element.134.w) | copy-start | bytes 7077892
  76.3 3.9 %copy-start.10 = (bf16[512,512]{1,0:T(8,128)(2,1)S(1)}, bf16[512,512]{1,0:T(8,128)(2,1)}, u32[]{:S(2)}) copy-start(bf16[512,512]{1,0:T(8,128)(2,1)} %copy-done.9) | copy-start | bytes 1572868
  77.4 12.3 %collective-permute-start.18 = (bf16[512,512]{1,0:T(8,128)(2,1)S(1)}, bf16[512,512]{1,0:T(8,128)(2,1)S(1)}, u32[]{:S(2)}, u32[]{:S(2)}) collective-permute-start(bf16[512,512]{1,0:T(8,128)(2,1)S(1)} %get-tuple-element.118), channel_id=1, source_target_pairs={{2,0},{4,2},{6,4},{3,1},{5,3},{7,5},{10,8},{12,10},{14,12},{11,9},... | collective-permute-start | bytes 1572872 | tf_op jit(solution)/shard_map/ppermute | solution.py:362
  80.2 1.0 copy-start.8
  81.3 2.3 %copy-start.2 = (bf16[512,512]{1,0:T(8,128)(2,1)S(1)}, bf16[512,512]{1,0:T(8,128)(2,1)}, u32[]{:S(2)}) copy-start(bf16[512,512]{1,0:T(8,128)(2,1)} %copy-done.1) | copy-start | bytes 1572868
  83.5 2.6 %copy-start.15 = (bf16[512,512]{1,0:T(8,128)(2,1)}, bf16[512,512]{1,0:T(8,128)(2,1)S(1)}, u32[]{:S(2)}) copy-start(bf16[512,512]{1,0:T(8,128)(2,1)S(1)} %get-tuple-element.128) | copy-start | bytes 1572868
  83.6 2.6 %copy-start = (bf16[1152,512]{1,0:T(8,128)(2,1)S(1)}, bf16[1152,512]{1,0:T(8,128)(2,1)}, u32[]{:S(2)}) copy-start(bf16[1152,512]{1,0:T(8,128)(2,1)} %pad_maximum_fusion.1.x) | copy-start | bytes 3538948
  86.1 1.3 copy-start.13
  90.6 15.7 %collective-permute-start.22 = (bf16[512,512]{1,0:T(8,128)(2,1)}, bf16[512,512]{1,0:T(8,128)(2,1)}, u32[]{:S(2)}, u32[]{:S(2)}) collective-permute-start(bf16[512,512]{1,0:T(8,128)(2,1)} %add_convert_fusion.3), channel_id=1, source_target_pairs={{2,0},{4,2},{6,4},{3,1},{5,3},{7,5},{10,8},{12,10},{14,12},{11,9},... | collective-permute-start | bytes 1572872 | tf_op jit(solution)/shard_map/ppermute | solution.py:362
  94.6 11.7 %collective-permute-start.19 = (bf16[288,512]{1,0:T(8,128)(2,1)}, bf16[288,512]{1,0:T(8,128)(2,1)}, u32[]{:S(2)}, u32[]{:S(2)}) collective-permute-start(bf16[288,512]{1,0:T(8,128)(2,1)} %get-tuple-element.152), channel_id=1, source_target_pairs={{0,8},{8,0},{16,24},{24,16},{1,9},{9,1},{17,25},{25,17},{2,10},{10... | collective-permute-start | bytes 884744 | tf_op jit(solution)/shard_map/ppermute | solution.py:368
  94.8 11.5 %collective-permute-start.20 = (bf16[288,512]{1,0:T(8,128)(2,1)}, bf16[288,512]{1,0:T(8,128)(2,1)}, u32[]{:S(2)}, u32[]{:S(2)}) collective-permute-start(bf16[288,512]{1,0:T(8,128)(2,1)} %get-tuple-element.151), channel_id=1, source_target_pairs={{0,16},{8,24},{16,0},{24,8},{1,17},{9,25},{17,1},{25,9},{2,18},{10... | collective-permute-start | bytes 884744 | tf_op jit(solution)/shard_map/ppermute | solution.py:368
  95.8 10.5 %collective-permute-start.21 = (bf16[256,512]{1,0:T(8,128)(2,1)}, bf16[256,512]{1,0:T(8,128)(2,1)S(1)}, u32[]{:S(2)}, u32[]{:S(2)}) collective-permute-start(bf16[256,512]{1,0:T(8,128)(2,1)} %get-tuple-element.167), channel_id=1, source_target_pairs={{0,1},{1,0},{2,3},{3,2},{4,5},{5,4},{6,7},{7,6},{8,9},{9,8},{10,11... | collective-permute-start | bytes 786440 | tf_op jit(solution)/shard_map/ppermute | solution.py:356
  101.5 1.7 %copy-start.4 = (bf16[2304,512]{1,0:T(8,128)(2,1)S(1)}, bf16[2304,512]{1,0:T(8,128)(2,1)}, u32[]{:S(2)}) copy-start(bf16[2304,512]{1,0:T(8,128)(2,1)} %copy-done.3) | copy-start | bytes 7077892
  106.3 12.8 %collective-permute-start.24 = (bf16[256,2304]{1,0:T(8,128)(2,1)S(1)}, bf16[256,2304]{1,0:T(8,128)(2,1)S(1)}, u32[]{:S(2)}, u32[]{:S(2)}) collective-permute-start(bf16[256,2304]{1,0:T(8,128)(2,1)S(1)} %get-tuple-element.140), channel_id=1, source_target_pairs={{0,1},{1,0},{2,3},{3,2},{4,5},{5,4},{6,7},{7,6},{8,9},{9,8},{10,11... | collective-permute-start | bytes 3538952 | tf_op jit(solution)/shard_map/ppermute | solution.py:356
  110.0 5.1 %copy-start.16 = (bf16[512,512]{1,0:T(8,128)(2,1)S(1)}, bf16[512,512]{1,0:T(8,128)(2,1)}, u32[]{:S(2)}) copy-start(bf16[512,512]{1,0:T(8,128)(2,1)} %copy-done.15) | copy-start | bytes 1572868
  110.1 10.3 %collective-permute-start.25 = (bf16[144,512]{1,0:T(8,128)(2,1)S(1)}, bf16[144,512]{1,0:T(8,128)(2,1)S(1)}, u32[]{:S(2)}, u32[]{:S(2)}) collective-permute-start(bf16[144,512]{1,0:T(8,128)(2,1)S(1)} %get-tuple-element.161), channel_id=1, source_target_pairs={{0,2},{2,4},{4,6},{6,0},{1,3},{3,5},{5,7},{7,1},{8,10},{10,12},{12... | collective-permute-start | bytes 442376 | tf_op jit(solution)/shard_map/ppermute | solution.py:365
  111.6 12.8 %collective-permute-start.26 = (bf16[144,512]{1,0:T(8,128)(2,1)S(1)}, bf16[144,512]{1,0:T(8,128)(2,1)S(1)}, u32[]{:S(2)}, u32[]{:S(2)}) collective-permute-start(bf16[144,512]{1,0:T(8,128)(2,1)S(1)} %get-tuple-element.160), channel_id=1, source_target_pairs={{0,4},{2,6},{4,0},{6,2},{1,5},{3,7},{5,1},{7,3},{8,12},{10,14},{12... | collective-permute-start | bytes 442376 | tf_op jit(solution)/shard_map/ppermute | solution.py:365
  113.7 13.8 %collective-permute-start.27 = (bf16[144,512]{1,0:T(8,128)(2,1)S(1)}, bf16[144,512]{1,0:T(8,128)(2,1)S(1)}, u32[]{:S(2)}, u32[]{:S(2)}) collective-permute-start(bf16[144,512]{1,0:T(8,128)(2,1)S(1)} %get-tuple-element.159), channel_id=1, source_target_pairs={{0,6},{2,0},{4,2},{6,4},{1,7},{3,1},{5,3},{7,5},{8,14},{10,8},{12,... | collective-permute-start | bytes 442376 | tf_op jit(solution)/shard_map/ppermute | solution.py:365
  116.3 22.5 %collective-permute-start.23 = (bf16[512,512]{1,0:T(8,128)(2,1)S(1)}, bf16[512,512]{1,0:T(8,128)(2,1)S(1)}, u32[]{:S(2)}, u32[]{:S(2)}) collective-permute-start(bf16[512,512]{1,0:T(8,128)(2,1)S(1)} %add_convert_fusion.2), channel_id=1, source_target_pairs={{2,0},{4,2},{6,4},{3,1},{5,3},{7,5},{10,8},{12,10},{14,12},{11,9},... | collective-permute-start | bytes 1572872 | tf_op jit(solution)/shard_map/ppermute | solution.py:362
  120.4 19.0 %copy-start.14 = (f32[512,512]{1,0:T(8,128)S(1)}, f32[512,512]{1,0:T(8,128)}, u32[]{:S(2)}) copy-start(f32[512,512]{1,0:T(8,128)} %copy-done.13) | copy-start | bytes 3145732
  138.9 1.5 %collective-permute-start.29 = (f32[72,512]{1,0:T(8,128)S(1)}, f32[72,512]{1,0:T(8,128)S(1)}, u32[]{:S(2)}, u32[]{:S(2)}) collective-permute-start(f32[72,512]{1,0:T(8,128)S(1)} %get-tuple-element.171), channel_id=1, source_target_pairs={{0,1},{1,0},{2,3},{3,2},{4,5},{5,4},{6,7},{7,6},{8,9},{9,8},{10,11... | collective-permute-start | bytes 442376 | tf_op jit(solution)/shard_map/ppermute | solution.py:356
  139.6 1.6 %collective-permute-start.28 = (bf16[256,512]{1,0:T(8,128)(2,1)S(1)}, bf16[256,512]{1,0:T(8,128)(2,1)S(1)}, u32[]{:S(2)}, u32[]{:S(2)}) collective-permute-start(bf16[256,512]{1,0:T(8,128)(2,1)S(1)} %slice.119), channel_id=1, source_target_pairs={{0,1},{1,0},{2,3},{3,2},{4,5},{5,4},{6,7},{7,6},{8,9},{9,8},{10,11... | collective-permute-start | bytes 786440 | tf_op jit(solution)/shard_map/ppermute | solution.py:356

commit v7 on v6

--- a/solution.py
+++ b/solution.py
@@ -43,7 +43,7 @@
         m_in, l_in, acc_in = refs[:3]
         refs = refs[3:]
     if last:
-        out, lse_t, m_s, l_s, acc_s = refs
+        strip_x, strip_y, out, lse_t, to_x, to_y, m_s, l_s, acc_s = refs
     else:
         m_s, l_s, acc_s = refs
     chip, core = info[0], info[1]
@@ -91,11 +91,14 @@
             total = l_s[h * 8 : h * 8 + 1, :]
             out[:, cols] = jnp.transpose(acc_s[cols, :] / total).astype(BF16)
         lse_t[...] = m_s[...] + jnp.log(l_s[...])
-
-
-def forward(info, q, kv, step, state, last):
+        to_x[...] = dot(strip_x[...], out[...]).astype(BF16)
+        to_y[...] = dot(strip_y[...], out[...]).astype(BF16)
+
+
+def forward(info, q, kv, step, state, strips=()):
     rows = q.shape[0]
     first = state is None
+    last = len(strips) > 0
     stat = jax.ShapeDtypeStruct((GROUPS * 8, rows), F32)
     acc = jax.ShapeDtypeStruct((GROUPS * HD, rows), F32)
     vmem = pl.BlockSpec(memory_space=pltpu.VMEM)
@@ -103,10 +106,11 @@
     scratch = []
     if last:
         outs = (jax.ShapeDtypeStruct((rows, GROUPS * HD), BF16), stat)
+        outs += tuple(jax.ShapeDtypeStruct((x.shape[0], GROUPS * HD), BF16) for x in strips)
         scratch = [pltpu.VMEM(s.shape, F32) for s in (stat, stat, acc)]
     else:
         outs = (stat, stat, acc)
-    args = [info, q, kv] + ([] if first else list(state))
+    args = [info, q, kv] + ([] if first else list(state)) + list(strips)
     return pl.pallas_call(
         functools.partial(forward_kernel, step, rows, first, last),
         out_shape=outs,
@@ -247,7 +251,7 @@
     )(info, *pieces)
 
 
-def into_heads_kernel(places, info, grad, *refs):
+def into_heads_kernel(places, info, mine, theirs, *refs):
     *pieces, weight, out = refs
     half = pieces[0].shape[0]
     for (k, at), ref in zip(places, pieces):
@@ -255,13 +259,15 @@
         weight[pl.ds(pl.multiple_of(start, half), half), :] = ref[...]
     depth = weight.shape[0]
     wide = 256
-    total = dot(grad[:, :wide], weight[:wide, :])
-    for i in range(wide, depth, wide):
-        total = total + dot(grad[:, i : i + wide], weight[i : i + wide, :])
-    out[...] = total.astype(BF16)
-
-
-def gradient_into_heads(info, grad, pieces):
+    tok = mine.shape[0]
+    for at, grad in ((0, mine), (tok, theirs)):
+        total = dot(grad[:, :wide], weight[:wide, :])
+        for i in range(wide, depth, wide):
+            total = total + dot(grad[:, i : i + wide], weight[i : i + wide, :])
+        out[at : at + tok, :] = total.astype(BF16)
+
+
+def gradient_into_heads(info, mine, theirs, pieces):
     arrays = [x for x, _, _ in pieces]
     half, width = arrays[0].shape
     vmem = pl.BlockSpec(memory_space=pltpu.VMEM)
@@ -269,14 +275,14 @@
         functools.partial(into_heads_kernel, [(k, at) for _, k, at in pieces]),
         out_shape=(
             jax.ShapeDtypeStruct((half * len(pieces), width), BF16),
-            jax.ShapeDtypeStruct((grad.shape[0], width), BF16),
+            jax.ShapeDtypeStruct((2 * mine.shape[0], width), BF16),
         ),
-        in_specs=[pl.BlockSpec(memory_space=pltpu.SMEM)] + [vmem] * (1 + len(pieces)),
+        in_specs=[pl.BlockSpec(memory_space=pltpu.SMEM)] + [vmem] * (2 + len(pieces)),
         out_specs=(vmem, vmem),
         cost_estimate=FILLER,
         compiler_params=pltpu.CompilerParams(vmem_limit_bytes=20 * 1024 * 1024),
         name="gradient_into_heads",
-    )(info, grad, *arrays)
+    )(info, mine, theirs, *arrays)
 
 
 def product_kernel(x, w, *outs):
@@ -382,7 +388,7 @@
     kv = jnp.concatenate([kv, kv_theirs], 0)
     hop = up(kv, 1)
     q = jnp.concatenate([own(q0), swap(other(q0))], 0) * jnp.asarray(HD ** (-0.5), BF16)
-    state = forward(info, q, kv, 0, None, False)
+    state = forward(info, q, kv, 0, None)
     piece = out_weight.shape[0]
     part = 2 * piece
     if near:
@@ -395,20 +401,27 @@
     share = ours.shape[0]
     half = share // 2
     lower, upper = ours[:half], ours[half:]
-    hop, q, state, lower, upper = together((hop, q, state, lower, upper))
+    upper_x, lower_y = across(upper, 1), across(lower, 2)
+    hop, q, state, lower, upper, upper_x, lower_y, grad_theirs = together(
+        (hop, q, state, lower, upper, upper_x, lower_y, swap(g0))
+    )
     chunks = [kv, hop]
 
     hop = up(hop, 1)
-    state = forward(info, q, chunks[1], 1, state, False)
-    upper_x, lower_y, grad_theirs, hop, state, lower, upper = together(
-        (across(upper, 1), across(lower, 2), swap(g0), hop, state, lower, upper)
+    state = forward(info, q, chunks[1], 1, state)
+    lower_x, upper_y, diagonal_x, diagonal_y, hop, state = together(
+        (across(lower, 1), across(upper, 2), across(lower_y, 1), across(upper_x, 2), hop, state)
     )
     chunks.append(hop)
+
     last_hop = up(hop, 1)
-    lower_x, upper_y = across(lower, 1), across(upper, 2)
-    diagonal = [across(lower_y, 1), across(upper_x, 2)]
-    grad = jnp.concatenate([g0, grad_theirs], 0)
-    turned = grad.T
+    for step in steps[2:prior]:
+        state = forward(info, q, hop, step, state)
+        hop = last_hop
+        if step + 1 < prior:
+            chunks.append(hop)
+            last_hop = up(hop, 1)
+    turned = jnp.concatenate([g0.T, grad_theirs.T], 1)
 
     def strip(k, at, size):
         return lax.dynamic_slice_in_dim(turned, (row ^ k) * share + at, size, 0)
@@ -418,24 +431,17 @@
         jnp.concatenate([strip(3, half, half), strip(2, half, half)], 0),
         jnp.concatenate([strip(1, half, half), strip(2, 0, half), strip(0, 0, share)], 0),
     ]
-    for step in steps[2:prior]:
-        state = forward(info, q, hop, step, state, False)
-        hop = last_hop
-        if step + 1 < prior:
-            chunks.append(hop)
-            last_hop = up(hop, 1)
-    last_hop, state, *strips = together((last_hop, state, *strips))
-    chunks.append(last_hop)
-    att, lse_t = forward(info, q, last_hop, prior, state, True)
-
-    to_x, to_y = [dot(x, att).astype(BF16) for x in strips[:2]]
-    to_x, to_y, att, grad = together((to_x, to_y, att, grad))
     weight, da = gradient_into_heads(
         info,
-        grad,
+        g0,
+        grad_theirs,
         [(lower, 0, 0), (upper, 0, 1), (lower_x, 1, 0), (upper_x, 1, 1), (lower_y, 2, 0)]
-        + [(upper_y, 2, 1), (diagonal[0], 3, 0), (diagonal[1], 3, 1)],
-    )
+        + [(upper_y, 2, 1), (diagonal_x, 3, 0), (diagonal_y, 3, 1)],
+    )
+    da, last_hop, state, *strips = together((da, last_hop, state, *strips))
+    chunks.append(last_hop)
+    att, lse_t, to_x, to_y = forward(info, q, last_hop, prior, state, strips[:2])
+
     carried = None
     terms = {}
     for step in reversed(steps):

time: 143 us -> 133 us (0.930)
  other arithmetic: 24.2 us -> 17.3 us
  waiting for transfers between devices: 43.1 us -> 39.8 us
  Pallas kernels: 20 us -> 23 us
  matrix products: 2.59 us -> 0 us
    ppermute x10, waiting for transfers between devices: 3.87 us -> 8.61 us  [across(): return lax.ppermute(x, 'dp', [(i, i ^ k) for i in range(rows_dp)])]
    ppermute x3, waiting for transfers between devices: 11.1 us -> 6.66 us  [up(): return lax.ppermute(x, 'chip', [(i, i + k) for i in range(chips - k)])]
    dynamic_slice x2 -> x0, other arithmetic: 2.74 us -> none  [strip(): return lax.dynamic_slice_in_dim(turned, (row ^ k) * share + at, size, 0)]
    dot_general x2 -> x0, matrix products: 2.59 us -> none  [dot(): return lax.dot_general(a, b, dims, preferred_element_type=F32)]
    ppermute x6, waiting for transfers between devices: 13.9 us -> 11.9 us  [round_chips(): return lax.ppermute(x, 'chip', [(i, (i + k) % chips) for i in range(chips)])]
    pallas_call x4, Pallas kernels: 5.54 us -> 7.23 us  [forward(): pl.pallas_call(functools.partial(forward_kernel, step, rows, first, last)...]
    ppermute x3, waiting for transfers between devices: 13.5 us -> 11.9 us  [down(): return lax.ppermute(x, 'chip', [(i + k, i) for i in range(chips - k)])]
    concatenate x1 -> x2, other arithmetic: 3.18 us -> 2.58 us  [on_device(): turned = jnp.concatenate([g0.T, grad_theirs.T], 1)]
  transfers between devices with their start and end apart: 30 -> 30, of which waited for: 11 -> 13; matrix products, arithmetic and copies ran while one was open for 22% -> 16% of each run, Pallas kernels for 14% -> 16%
where the time goes in v7:
time: 133 us; the launch traced here: 132 us
  starting transfers between devices  40.6 us (31%)
  waiting for transfers between devices  39.8 us (30%)
  Pallas kernels  23 us (17%)
  other arithmetic  17.3 us (13%)
  local copies, waits for them, and re-layouts  10.2 us (8%)
    ppermute x6, waiting for transfers between devices, round_chips(): return lax.ppermute(x, 'chip', [(i, (i + k) % chips) for i in range(chips)])  11.9 us
    ppermute x3, waiting for transfers between devices, down(): return lax.ppermute(x, 'chip', [(i + k, i) for i in range(chips - k)])  11.9 us
    ppermute x8, starting transfers between devices, swap(): return lax.ppermute(x, 'core', [(0, 1), (1, 0)])  10.3 us
    ppermute x10, waiting for transfers between devices, across(): return lax.ppermute(x, 'dp', [(i, i ^ k) for i in range(rows_dp)])  8.61 us
    ppermute x10, starting transfers between devices, across(): return lax.ppermute(x, 'dp', [(i, i ^ k) for i in range(rows_dp)])  8.42 us
    ppermute x6, starting transfers between devices, round_chips(): return lax.ppermute(x, 'chip', [(i, (i + k) % chips) for i in range(chips)])  7.93 us
    pallas_call x4, Pallas kernels, backward(): pl.pallas_call(functools.partial(backward_kernel, steps, rows, first, las...  7.54 us
    pallas_call x4, Pallas kernels, forward(): pl.pallas_call(functools.partial(forward_kernel, step, rows, first, last)...  7.23 us
  transfers between devices with their start and end apart: 30, of which 13 were waited for; matrix products, arithmetic and copies ran while one was open for 16% of the time, Pallas kernels for 16%

profile of v7, /device:TPU:9, one launch (start us, length us, event | category | flops | bytes accessed | tf_op | source)
XLA Modules:
  0.0 132.0 jit_solution(18275090338376709711)
XLA Ops:
  0.6 1.3 %collective-permute-start.3 = (bf16[72,1024]{1,0:T(8,128)(2,1)}, bf16[72,1024]{1,0:T(8,128)(2,1)S(1)}, u32[]{:S(2)}, u32[]{:S(2)}) collective-permute-start(bf16[72,1024]{1,0:T(8,128)(2,1)} %refs_0_.1), channel_id=1, source_target_pairs={{0,2},{2,4},{4,6},{6,0},{1,3},{3,5},{5,7},{7,1},{8,10},{10,12},{12... | collective-permute-start | bytes 442376 | tf_op jit(solution)/shard_map/ppermute | solution.py:371
  2.0 1.1 collective-permute-start.4
  3.1 1.4 %collective-permute-start.5 = (bf16[72,1024]{1,0:T(8,128)(2,1)}, bf16[72,1024]{1,0:T(8,128)(2,1)S(1)}, u32[]{:S(2)}, u32[]{:S(2)}) collective-permute-start(bf16[72,1024]{1,0:T(8,128)(2,1)} %refs_0_.1), channel_id=1, source_target_pairs={{0,6},{2,0},{4,2},{6,4},{1,7},{3,1},{5,3},{7,5},{8,14},{10,8},{12,... | collective-permute-start | bytes 442376 | tf_op jit(solution)/shard_map/ppermute | solution.py:371
  4.5 1.0 broadcast_select_fusion.5
  5.5 1.6 %broadcast_select_fusion.4 = (bf16[256,256]{1,0:T(8,128)(2,1)}, bf16[256,256]{1,0:T(8,128)(2,1)S(1)}) fusion(pred[]{:T(512)S(6)} %eq.3, bf16[256,512]{1,0:T(8,128)(2,1)} %bitcast.35), kind=kLoop, calls=%fused_computation.55 | loop fusion | flops 131072 | bytes 524289 | tf_op jit(solution)/shard_map/jit(_where)/select_n | solution.py:355
  7.1 1.6 %collective-permute-start = (bf16[256,512]{1,0:T(8,128)(2,1)S(1)}, bf16[256,512]{1,0:T(8,128)(2,1)}, u32[]{:S(2)}, u32[]{:S(2)}) collective-permute-start(bf16[256,512]{1,0:T(8,128)(2,1)S(1)} %pad_maximum_fusion.4), channel_id=1, source_target_pairs={{0,1},{1,0},{2,3},{3,2},{4,5},{5,4},{6,7},{7,6},{8,9},{9,8},{10,11... | collective-permute-start | bytes 786440 | tf_op jit(solution)/shard_map/ppermute | solution.py:362
  8.7 1.4 %copy.12 = bf16[1,256,2304]{1,2,0:T(8,128)(2,1)} copy(bf16[1,256,2304]{2,1,0:T(8,128)(2,1)S(1)} %copy-done) | data formatting | bytes 2359296 | tf_op args[4]
  10.3 4.0 %collective-permute-done.4.refs_2_ = bf16[72,1024]{1,0:T(8,128)(2,1)S(1)} collective-permute-done((bf16[72,1024]{1,0:T(8,128)(2,1)}, bf16[72,1024]{1,0:T(8,128)(2,1)S(1)}, u32[]{:S(2)}, u32[]{:S(2)}) %collective-permute-start.4) | collective-permute-done | bytes 147488 | tf_op jit(solution)/shard_map/ppermute | solution.py:371
  14.3 2.7 %collective-permute-done.5.refs_3_ = bf16[72,1024]{1,0:T(8,128)(2,1)S(1)} collective-permute-done((bf16[72,1024]{1,0:T(8,128)(2,1)}, bf16[72,1024]{1,0:T(8,128)(2,1)S(1)}, u32[]{:S(2)}, u32[]{:S(2)}) %collective-permute-start.5) | collective-permute-done | bytes 147488 | tf_op jit(solution)/shard_map/ppermute | solution.py:371
  18.3 1.0 pad_maximum_fusion.3.kv.refs_0_
  19.3 1.9 %collective-permute-start.1 = (bf16[512,512]{1,0:T(8,128)(2,1)S(1)}, bf16[512,512]{1,0:T(8,128)(2,1)}, u32[]{:S(2)}, u32[]{:S(2)}) collective-permute-start(bf16[512,512]{1,0:T(8,128)(2,1)S(1)} %pad_maximum_fusion.3.kv.refs_0_), channel_id=1, source_target_pairs={{0,2},{2,4},{4,6},{1,3},{3,5},{5,7},{8,10},{10,12},{12,14},{9,11},... | collective-permute-start | bytes 1572872 | tf_op jit(solution)/shard_map/ppermute | solution.py:365
  21.4 0.7 copy.11
  22.1 1.2 collective-permute-start.7
  23.3 0.7 copy.10
  24.1 1.2 collective-permute-start.8
  25.4 2.1 %attend_forward.4 = (f32[16,512]{1,0:T(8,128)S(1)}, f32[16,512]{1,0:T(8,128)S(1)}, f32[512,512]{1,0:T(8,128)S(1)}) custom-call(s32[3]{0:T(128)S(1)} %pad_add_fusion.info, bf16[512,512]{1,0:T(8,128)(2,1)S(1)} %maximum_multiply_fusion.q, bf16[512,512]{1,0:T(8,128)(2,1)S(1)} %pad_maximum_fusion.3.kv.refs_0_), custom_call_target="tpu_custom_call" | custom-call | flops 1 | bytes 1 | tf_op jit(solution)/shard_map/attend_forward/pallas_call | solution.py:114
  27.5 3.0 %collective-permute-done.7.refs_3_ = bf16[288,512]{1,0:T(8,128)(2,1)} collective-permute-done((bf16[288,512]{1,0:T(8,128)(2,1)}, bf16[288,512]{1,0:T(8,128)(2,1)}, u32[]{:S(2)}, u32[]{:S(2)}) %collective-permute-start.7) | collective-permute-done | bytes 294944 | tf_op jit(solution)/shard_map/ppermute | solution.py:374
  30.5 1.6 %collective-permute-done.8.refs_4_ = bf16[288,512]{1,0:T(8,128)(2,1)} collective-permute-done((bf16[288,512]{1,0:T(8,128)(2,1)}, bf16[288,512]{1,0:T(8,128)(2,1)}, u32[]{:S(2)}, u32[]{:S(2)}) %collective-permute-start.8) | collective-permute-done | bytes 294944 | tf_op jit(solution)/shard_map/ppermute | solution.py:374
  32.2 2.1 %collective-permute-done.1.kv.refs_0_ = bf16[512,512]{1,0:T(8,128)(2,1)} collective-permute-done((bf16[512,512]{1,0:T(8,128)(2,1)S(1)}, bf16[512,512]{1,0:T(8,128)(2,1)}, u32[]{:S(2)}, u32[]{:S(2)}) %collective-permute-start.1) | collective-permute-done | bytes 524320 | tf_op jit(solution)/shard_map/ppermute | solution.py:365
  34.3 2.2 %collective-permute-start.14 = (bf16[512,512]{1,0:T(8,128)(2,1)}, bf16[512,512]{1,0:T(8,128)(2,1)}, u32[]{:S(2)}, u32[]{:S(2)}) collective-permute-start(bf16[512,512]{1,0:T(8,128)(2,1)} %collective-permute-done.1.kv.refs_0_), channel_id=1, source_target_pairs={{0,2},{2,4},{4,6},{1,3},{3,5},{5,7},{8,10},{10,12},{12,14},{9,11},... | collective-permute-start | bytes 1572872 | tf_op jit(solution)/shard_map/ppermute | solution.py:365
  36.5 1.3 collective-permute-start.10
  37.8 1.2 collective-permute-start.11
  39.5 2.5 %attend_forward.5 = (f32[16,512]{1,0:T(8,128)S(1)}, f32[16,512]{1,0:T(8,128)S(1)}, f32[512,512]{1,0:T(8,128)S(1)}) custom-call(s32[3]{0:T(128)S(1)} %pad_add_fusion.info, bf16[512,512]{1,0:T(8,128)(2,1)S(1)} %maximum_multiply_fusion.q, bf16[512,512]{1,0:T(8,128)(2,1)} %collective-permute-done.1.kv.refs_0_, f32[16,512]{1,0:T(8,128)S(1)} %get-tuple-element.91.refs_0_, ...), custom_call_target="tpu_custom_call" | custom-call | flops 1 | bytes 1 | tf_op jit(solution)/shard_map/attend_forward/pallas_call | solution.py:114
  42.0 1.0 copy-done.3
  43.0 1.6 %copy.14.theirs = bf16[256,2304]{1,0:T(8,128)(2,1)S(1)} copy(bf16[256,2304]{0,1:T(8,128)(2,1)} %collective-permute-done.9) | data formatting | bytes 2359296 | tf_op jit(solution)/shard_map/optimization_barrier | solution.py:405
  44.6 1.2 fusion
  46.0 1.4 %fusion.5 = (bf16[288,512]{1,0:T(8,128)(2,1)S(1)}, bf16[288,512]{1,0:T(8,128)(2,1)S(1)}, bf16[288,512]{1,0:T(8,128)(2,1)S(1)}, bf16[288,512]{1,0:T(8,128)(2,1)S(...) fusion(s32[]{:T(128)S(6)} %select_n.139, bf16[2304,256]{1,0:T(8,128)(2,1)S(1)} %bitcast.29, ...), kind=kLoop, calls=%fused_computation.35 | loop fusion | flops 3538944 | bytes 4128792 | tf_op jit(solution)/shard_map/concatenate | solution.py:424
  47.4 3.0 %collective-permute-done.12.refs_6_ = bf16[288,512]{1,0:T(8,128)(2,1)} collective-permute-done((bf16[288,512]{1,0:T(8,128)(2,1)}, bf16[288,512]{1,0:T(8,128)(2,1)}, u32[]{:S(2)}, u32[]{:S(2)}) %collective-permute-start.12) | collective-permute-done | bytes 294944 | tf_op jit(solution)/shard_map/ppermute | solution.py:374
  50.5 0.9 collective-permute-done.13.refs_7_
  51.4 2.9 %collective-permute-start.15 = (bf16[512,512]{1,0:T(8,128)(2,1)}, bf16[512,512]{1,0:T(8,128)(2,1)S(1)}, u32[]{:S(2)}, u32[]{:S(2)}) collective-permute-start(bf16[512,512]{1,0:T(8,128)(2,1)} %collective-permute-done.14.kv.refs_0_), channel_id=1, source_target_pairs={{0,2},{2,4},{4,6},{1,3},{3,5},{5,7},{8,10},{10,12},{12,14},{9,11},... | collective-permute-start | bytes 1572872 | tf_op jit(solution)/shard_map/ppermute | solution.py:365
  54.5 1.1 copy-done.4
  55.6 1.1 attend_forward.6
  56.7 3.1 %gradient_into_heads.1 = (bf16[2304,512]{1,0:T(8,128)(2,1)S(1)}, bf16[512,512]{1,0:T(8,128)(2,1)S(1)}) custom-call(s32[3]{0:T(128)S(1)} %pad_add_fusion.info, bf16[256,2304]{1,0:T(8,128)(2,1)S(1)} %bitcast.25, bf16[256,2304]{1,0:T(8,128)(2,1)S(1)} %copy.14.theirs, bf16[288,512]{1,0:T(8,128)(2,1)} %bitcast.8.refs_0_, bf16[288,512]{1,0:T(8,128)(2,1)} %bitcast.9.refs_1_, ...), custom_call_target="tpu_custom_call" | custom-call | flops 1 | bytes 1 | tf_op jit(solution)/shard_map/gradient_into_heads/pallas_call | solution.py:274
  59.9 4.5 %collective-permute-done.15.kv.refs_0_ = bf16[512,512]{1,0:T(8,128)(2,1)S(1)} collective-permute-done((bf16[512,512]{1,0:T(8,128)(2,1)}, bf16[512,512]{1,0:T(8,128)(2,1)S(1)}, u32[]{:S(2)}, u32[]{:S(2)}) %collective-permute-start.15) | collective-permute-done | bytes 524320 | tf_op jit(solution)/shard_map/ppermute | solution.py:365
  64.4 1.5 %attend_forward.7 = (bf16[512,512]{1,0:T(8,128)(2,1)S(1)}, f32[16,512]{1,0:T(8,128)S(1)}, bf16[576,512]{1,0:T(8,128)(2,1)S(1)}, bf16[576,512]{1,0:T(8,128)(2,1)S(1)}) custom-call(s32[3]{0:T(128)S(1)} %pad_add_fusion.info, bf16[512,512]{1,0:T(8,128)(2,1)S(1)} %maximum_multiply_fusion.q, bf16[512,512]{1,0:T(8,128)(2,1)S(1)} %collective-permute-done.15.kv.refs_0_, ...), custom_call_target="tpu_custom_call" | custom-call | flops 1 | bytes 1 | tf_op jit(solution)/shard_map/attend_forward/pallas_call | solution.py:114
  66.3 1.2 collective-permute-start.17
  67.6 0.9 attend_backward.4
  68.5 1.9 %collective-permute-start.18 = (bf16[512,512]{1,0:T(8,128)(2,1)S(1)}, bf16[512,512]{1,0:T(8,128)(2,1)S(1)}, u32[]{:S(2)}, u32[]{:S(2)}) collective-permute-start(bf16[512,512]{1,0:T(8,128)(2,1)S(1)} %get-tuple-element.120), channel_id=1, source_target_pairs={{2,0},{4,2},{6,4},{3,1},{5,3},{7,5},{10,8},{12,10},{14,12},{11,9},... | collective-permute-start | bytes 1572872 | tf_op jit(solution)/shard_map/ppermute | solution.py:368
  70.4 1.3 %attend_backward.5 = (bf16[512,512]{1,0:T(8,128)(2,1)S(1)}, f32[512,512]{1,0:T(8,128)S(1)}) custom-call(s32[3]{0:T(128)S(1)} %pad_add_fusion.info, bf16[512,512]{1,0:T(8,128)(2,1)S(1)} %maximum_multiply_fusion.q, bf16[512,512]{1,0:T(8,128)(2,1)S(1)} %get-tuple-element.117.da, f32[16,512]{1,0:T(8,128)S(1)} %get-tuple-element.118.lse_t, ...), custom_call_target="tpu_custom_call" | custom-call | flops 1 | bytes 1 | tf_op jit(solution)/shard_map/attend_backward/pallas_call | solution.py:215
  71.8 2.8 %attend_backward.6 = (bf16[512,512]{1,0:T(8,128)(2,1)S(1)}, f32[512,512]{1,0:T(8,128)S(1)}) custom-call(s32[3]{0:T(128)S(1)} %pad_add_fusion.info, bf16[512,512]{1,0:T(8,128)(2,1)S(1)} %maximum_multiply_fusion.q, bf16[512,512]{1,0:T(8,128)(2,1)S(1)} %get-tuple-element.117.da, f32[16,512]{1,0:T(8,128)S(1)} %get-tuple-element.118.lse_t, ...), custom_call_target="tpu_custom_call" | custom-call | flops 1 | bytes 1 | tf_op jit(solution)/shard_map/attend_backward/pallas_call | solution.py:215
  74.6 0.8 copy-done.7
  75.4 2.5 %attend_backward.7 = (f32[512,512]{1,0:T(8,128)S(1)}, bf16[512,512]{1,0:T(8,128)(2,1)S(1)}) custom-call(s32[3]{0:T(128)S(1)} %pad_add_fusion.info, bf16[512,512]{1,0:T(8,128)(2,1)S(1)} %maximum_multiply_fusion.q, bf16[512,512]{1,0:T(8,128)(2,1)S(1)} %get-tuple-element.117.da, f32[16,512]{1,0:T(8,128)S(1)} %get-tuple-element.118.lse_t, ...), custom_call_target="tpu_custom_call" | custom-call | flops 1 | bytes 1 | tf_op jit(solution)/shard_map/attend_backward/pallas_call | solution.py:215
  77.9 1.3 strip_product.1
  79.9 1.1 add_convert_fusion.3
  80.9 2.2 %collective-permute-start.22 = (bf16[512,512]{1,0:T(8,128)(2,1)}, bf16[512,512]{1,0:T(8,128)(2,1)}, u32[]{:S(2)}, u32[]{:S(2)}) collective-permute-start(bf16[512,512]{1,0:T(8,128)(2,1)} %add_convert_fusion.3), channel_id=1, source_target_pairs={{2,0},{4,2},{6,4},{3,1},{5,3},{7,5},{10,8},{12,10},{14,12},{11,9},... | collective-permute-start | bytes 1572872 | tf_op jit(solution)/shard_map/ppermute | solution.py:368
  83.1 0.9 add_convert_fusion.4
  84.1 1.1 collective-permute-start.19
  86.2 5.5 %collective-permute-start.21 = (bf16[256,512]{1,0:T(8,128)(2,1)}, bf16[256,512]{1,0:T(8,128)(2,1)}, u32[]{:S(2)}, u32[]{:S(2)}) collective-permute-start(bf16[256,512]{1,0:T(8,128)(2,1)} %get-tuple-element.169), channel_id=1, source_target_pairs={{0,1},{1,0},{2,3},{3,2},{4,5},{5,4},{6,7},{7,6},{8,9},{9,8},{10,11... | collective-permute-start | bytes 786440 | tf_op jit(solution)/shard_map/ppermute | solution.py:362
  91.6 1.7 %copy-done.2 = bf16[2304,512]{1,0:T(8,128)(2,1)S(1)} copy-done((bf16[2304,512]{1,0:T(8,128)(2,1)S(1)}, bf16[2304,512]{1,0:T(8,128)(2,1)}, u32[]{:S(2)}) %copy-start.2) | copy-done | bytes 2359320
  93.3 3.2 %layer_product.1 = (f32[256,2304]{1,0:T(8,128)S(1)}, bf16[256,2304]{1,0:T(8,128)(2,1)S(1)}) custom-call(bf16[512,512]{1,0:T(8,128)(2,1)S(1)} %get-tuple-element.135.refs_1_.w.x, bf16[2304,512]{1,0:T(8,128)(2,1)S(1)} %copy-done.2), custom_call_target="tpu_custom_call" | custom-call | flops 1 | bytes 1 | tf_op jit(solution)/shard_map/layer_product/pallas_call | solution.py:303
  96.5 1.9 %collective-permute-start.24 = (bf16[256,2304]{1,0:T(8,128)(2,1)S(1)}, bf16[256,2304]{1,0:T(8,128)(2,1)S(1)}, u32[]{:S(2)}, u32[]{:S(2)}) collective-permute-start(bf16[256,2304]{1,0:T(8,128)(2,1)S(1)} %get-tuple-element.142), channel_id=1, source_target_pairs={{0,1},{1,0},{2,3},{3,2},{4,5},{5,4},{6,7},{7,6},{8,9},{9,8},{10,11... | collective-permute-start | bytes 3538952 | tf_op jit(solution)/shard_map/ppermute | solution.py:362
  98.5 1.0 convert_add_fusion.1
  99.5 1.0 convert_add_fusion
  100.9 1.5 %collective-permute-start.25 = (bf16[144,512]{1,0:T(8,128)(2,1)S(1)}, bf16[144,512]{1,0:T(8,128)(2,1)S(1)}, u32[]{:S(2)}, u32[]{:S(2)}) collective-permute-start(bf16[144,512]{1,0:T(8,128)(2,1)S(1)} %get-tuple-element.163), channel_id=1, source_target_pairs={{0,2},{2,4},{4,6},{6,0},{1,3},{3,5},{5,7},{7,1},{8,10},{10,12},{12... | collective-permute-start | bytes 442376 | tf_op jit(solution)/shard_map/ppermute | solution.py:371
  102.4 1.2 collective-permute-start.26
  103.6 1.4 %collective-permute-start.27 = (bf16[144,512]{1,0:T(8,128)(2,1)S(1)}, bf16[144,512]{1,0:T(8,128)(2,1)S(1)}, u32[]{:S(2)}, u32[]{:S(2)}) collective-permute-start(bf16[144,512]{1,0:T(8,128)(2,1)S(1)} %get-tuple-element.161), channel_id=1, source_target_pairs={{0,6},{2,0},{4,2},{6,4},{1,7},{3,1},{5,3},{7,5},{8,14},{10,8},{12,... | collective-permute-start | bytes 442376 | tf_op jit(solution)/shard_map/ppermute | solution.py:371
  105.0 1.2 add_convert_fusion.2
  106.2 2.9 %collective-permute-start.23 = (bf16[512,512]{1,0:T(8,128)(2,1)S(1)}, bf16[512,512]{1,0:T(8,128)(2,1)S(1)}, u32[]{:S(2)}, u32[]{:S(2)}) collective-permute-start(bf16[512,512]{1,0:T(8,128)(2,1)S(1)} %add_convert_fusion.2), channel_id=1, source_target_pairs={{2,0},{4,2},{6,4},{3,1},{5,3},{7,5},{10,8},{12,10},{14,12},{11,9},... | collective-permute-start | bytes 1572872 | tf_op jit(solution)/shard_map/ppermute | solution.py:368
  109.1 2.0 %maximum_select_fusion.1 = bf16[256,1024]{1,0:T(8,128)(2,1)} fusion(bf16[256,512]{1,0:T(8,128)(2,1)} %collective-permute-done.21, bf16[256,512]{1,0:T(8,128)(2,1)S(1)} %get-tuple-element.168, pred[]{:T(512)S(6)} %eq.3), kind=kLoop, calls=%fused_computation.30 | loop fusion | flops 2359296 | bytes 1048577 | tf_op jit(solution)/shard_map/jit(_where)/select_n | solution.py:377
  111.0 1.2 add_convert_fusion
  112.3 2.9 %collective-permute-done.26 = bf16[144,512]{1,0:T(8,128)(2,1)S(1)} collective-permute-done((bf16[144,512]{1,0:T(8,128)(2,1)S(1)}, bf16[144,512]{1,0:T(8,128)(2,1)S(1)}, u32[]{:S(2)}, u32[]{:S(2)}) %collective-permute-start.26) | collective-permute-done | bytes 147488 | tf_op jit(solution)/shard_map/ppermute | solution.py:371
  115.2 2.3 %collective-permute-done.27 = bf16[144,512]{1,0:T(8,128)(2,1)S(1)} collective-permute-done((bf16[144,512]{1,0:T(8,128)(2,1)S(1)}, bf16[144,512]{1,0:T(8,128)(2,1)S(1)}, u32[]{:S(2)}, u32[]{:S(2)}) %collective-permute-start.27) | collective-permute-done | bytes 147488 | tf_op jit(solution)/shard_map/ppermute | solution.py:371
  117.4 11.2 %collective-permute-done.23 = bf16[512,512]{1,0:T(8,128)(2,1)S(1)} collective-permute-done((bf16[512,512]{1,0:T(8,128)(2,1)S(1)}, bf16[512,512]{1,0:T(8,128)(2,1)S(1)}, u32[]{:S(2)}, u32[]{:S(2)}) %collective-permute-start.23) | collective-permute-done | bytes 524320 | tf_op jit(solution)/shard_map/ppermute | solution.py:368
  131.1 0.9 maximum_select_fusion.3
  (78 shorter events, 7.3 us)
Async XLA Ops:
  0.6 8.1 %copy-start = (bf16[1,256,2304]{2,1,0:T(8,128)(2,1)S(1)}, bf16[1,256,2304]{2,1,0:T(8,128)(2,1)}, u32[]{:S(2)}) copy-start(bf16[1,256,2304]{2,1,0:T(8,128)(2,1)} %param.9) | copy-start | bytes 3538948
  0.6 9.6 %collective-permute-start.3 = (bf16[72,1024]{1,0:T(8,128)(2,1)}, bf16[72,1024]{1,0:T(8,128)(2,1)S(1)}, u32[]{:S(2)}, u32[]{:S(2)}) collective-permute-start(bf16[72,1024]{1,0:T(8,128)(2,1)} %refs_0_.1), channel_id=1, source_target_pairs={{0,2},{2,4},{4,6},{6,0},{1,3},{3,5},{5,7},{7,1},{8,10},{10,12},{12... | collective-permute-start | bytes 442376 | tf_op jit(solution)/shard_map/ppermute | solution.py:371
  2.0 12.3 %collective-permute-start.4 = (bf16[72,1024]{1,0:T(8,128)(2,1)}, bf16[72,1024]{1,0:T(8,128)(2,1)S(1)}, u32[]{:S(2)}, u32[]{:S(2)}) collective-permute-start(bf16[72,1024]{1,0:T(8,128)(2,1)} %refs_0_.1), channel_id=1, source_target_pairs={{0,4},{2,6},{4,0},{6,2},{1,5},{3,7},{5,1},{7,3},{8,12},{10,14},{12... | collective-permute-start | bytes 442376 | tf_op jit(solution)/shard_map/ppermute | solution.py:371
  3.1 13.9 %collective-permute-start.5 = (bf16[72,1024]{1,0:T(8,128)(2,1)}, bf16[72,1024]{1,0:T(8,128)(2,1)S(1)}, u32[]{:S(2)}, u32[]{:S(2)}) collective-permute-start(bf16[72,1024]{1,0:T(8,128)(2,1)} %refs_0_.1), channel_id=1, source_target_pairs={{0,6},{2,0},{4,2},{6,4},{1,7},{3,1},{5,3},{7,5},{8,14},{10,8},{12,... | collective-permute-start | bytes 442376 | tf_op jit(solution)/shard_map/ppermute | solution.py:371
  7.1 9.9 %copy-start.9 = (bf16[72,1024]{1,0:T(8,128)(2,1)S(1)}, bf16[72,1024]{1,0:T(8,128)(2,1)}, u32[]{:S(2)}) copy-start(bf16[72,1024]{1,0:T(8,128)(2,1)} %refs_0_.1) | copy-start | bytes 442372
  7.1 11.2 %collective-permute-start = (bf16[256,512]{1,0:T(8,128)(2,1)S(1)}, bf16[256,512]{1,0:T(8,128)(2,1)}, u32[]{:S(2)}, u32[]{:S(2)}) collective-permute-start(bf16[256,512]{1,0:T(8,128)(2,1)S(1)} %pad_maximum_fusion.4), channel_id=1, source_target_pairs={{0,1},{1,0},{2,3},{3,2},{4,5},{5,4},{6,7},{7,6},{8,9},{9,8},{10,11... | collective-permute-start | bytes 786440 | tf_op jit(solution)/shard_map/ppermute | solution.py:362
  10.1 24.2 %collective-permute-start.9 = (bf16[256,2304]{0,1:T(8,128)(2,1)}, bf16[256,2304]{0,1:T(8,128)(2,1)}, u32[]{:S(2)}, u32[]{:S(2)}) collective-permute-start(bf16[256,2304]{0,1:T(8,128)(2,1)} %bitcast.27), channel_id=1, source_target_pairs={{0,1},{1,0},{2,3},{3,2},{4,5},{5,4},{6,7},{7,6},{8,9},{9,8},{10,11... | collective-permute-start | bytes 3538952 | tf_op jit(solution)/shard_map/ppermute | solution.py:362
  10.2 7.9 %copy-start.15 = (bf16[1,256,1024]{2,1,0:T(8,128)(2,1)S(1)}, bf16[1,256,1024]{2,1,0:T(8,128)(2,1)}, u32[]{:S(2)}) copy-start(bf16[1,256,1024]{2,1,0:T(8,128)(2,1)} %param.5) | copy-start | bytes 1572868
  10.2 8.1 %copy-start.16 = (bf16[256,256]{1,0:T(8,128)(2,1)S(1)}, bf16[256,256]{1,0:T(8,128)(2,1)}, u32[]{:S(2)}) copy-start(bf16[256,256]{1,0:T(8,128)(2,1)} %get-tuple-element.178) | copy-start | bytes 393220
  17.6 3.6 %collective-permute-start.6 = (bf16[4,72,512]{2,1,0:T(8,128)(2,1)S(1)}, bf16[4,72,512]{2,1,0:T(8,128)(2,1)S(1)}, u32[]{:S(2)}, u32[]{:S(2)}) collective-permute-start(bf16[4,72,512]{2,1,0:T(8,128)(2,1)S(1)} %get-tuple-element.83), channel_id=1, source_target_pairs={{0,1},{1,0},{2,3},{3,2},{4,5},{5,4},{6,7},{7,6},{8,9},{9,8},{10,11... | collective-permute-start | bytes 884744 | tf_op jit(solution)/shard_map/ppermute | solution.py:362
  18.2 7.1 %collective-permute-start.2 = (bf16[256,512]{1,0:T(8,128)(2,1)S(1)}, bf16[256,512]{1,0:T(8,128)(2,1)S(1)}, u32[]{:S(2)}, u32[]{:S(2)}) collective-permute-start(bf16[256,512]{1,0:T(8,128)(2,1)S(1)} %get-tuple-element.171), channel_id=1, source_target_pairs={{0,1},{1,0},{2,3},{3,2},{4,5},{5,4},{6,7},{7,6},{8,9},{9,8},{10,11... | collective-permute-start | bytes 786440 | tf_op jit(solution)/shard_map/ppermute | solution.py:362
  19.3 15.0 %collective-permute-start.1 = (bf16[512,512]{1,0:T(8,128)(2,1)S(1)}, bf16[512,512]{1,0:T(8,128)(2,1)}, u32[]{:S(2)}, u32[]{:S(2)}) collective-permute-start(bf16[512,512]{1,0:T(8,128)(2,1)S(1)} %pad_maximum_fusion.3.kv.refs_0_), channel_id=1, source_target_pairs={{0,2},{2,4},{4,6},{1,3},{3,5},{5,7},{8,10},{10,12},{12,14},{9,11},... | collective-permute-start | bytes 1572872 | tf_op jit(solution)/shard_map/ppermute | solution.py:365
  22.1 8.4 %collective-permute-start.7 = (bf16[288,512]{1,0:T(8,128)(2,1)}, bf16[288,512]{1,0:T(8,128)(2,1)}, u32[]{:S(2)}, u32[]{:S(2)}) collective-permute-start(bf16[288,512]{1,0:T(8,128)(2,1)} %bitcast.9.refs_1_), channel_id=1, source_target_pairs={{0,8},{8,0},{16,24},{24,16},{1,9},{9,1},{17,25},{25,17},{2,10},{10... | collective-permute-start | bytes 884744 | tf_op jit(solution)/shard_map/ppermute | solution.py:374
  24.1 8.1 %collective-permute-start.8 = (bf16[288,512]{1,0:T(8,128)(2,1)}, bf16[288,512]{1,0:T(8,128)(2,1)}, u32[]{:S(2)}, u32[]{:S(2)}) collective-permute-start(bf16[288,512]{1,0:T(8,128)(2,1)} %bitcast.8.refs_0_), channel_id=1, source_target_pairs={{0,16},{8,24},{16,0},{24,8},{1,17},{9,25},{17,1},{25,9},{2,18},{10... | collective-permute-start | bytes 884744 | tf_op jit(solution)/shard_map/ppermute | solution.py:374
  34.3 17.1 %collective-permute-start.14 = (bf16[512,512]{1,0:T(8,128)(2,1)}, bf16[512,512]{1,0:T(8,128)(2,1)}, u32[]{:S(2)}, u32[]{:S(2)}) collective-permute-start(bf16[512,512]{1,0:T(8,128)(2,1)} %collective-permute-done.1.kv.refs_0_), channel_id=1, source_target_pairs={{0,2},{2,4},{4,6},{1,3},{3,5},{5,7},{8,10},{10,12},{12,14},{9,11},... | collective-permute-start | bytes 1572872 | tf_op jit(solution)/shard_map/ppermute | solution.py:365
  36.5 10.9 %collective-permute-start.10 = (bf16[288,512]{1,0:T(8,128)(2,1)}, bf16[288,512]{1,0:T(8,128)(2,1)}, u32[]{:S(2)}, u32[]{:S(2)}) collective-permute-start(bf16[288,512]{1,0:T(8,128)(2,1)} %bitcast.8.refs_0_), channel_id=1, source_target_pairs={{0,8},{8,0},{16,24},{24,16},{1,9},{9,1},{17,25},{25,17},{2,10},{10... | collective-permute-start | bytes 884744 | tf_op jit(solution)/shard_map/ppermute | solution.py:374
  37.8 9.6 %collective-permute-start.11 = (bf16[288,512]{1,0:T(8,128)(2,1)}, bf16[288,512]{1,0:T(8,128)(2,1)}, u32[]{:S(2)}, u32[]{:S(2)}) collective-permute-start(bf16[288,512]{1,0:T(8,128)(2,1)} %bitcast.9.refs_1_), channel_id=1, source_target_pairs={{0,16},{8,24},{16,0},{24,8},{1,17},{9,25},{17,1},{25,9},{2,18},{10... | collective-permute-start | bytes 884744 | tf_op jit(solution)/shard_map/ppermute | solution.py:374
  39.1 11.4 %collective-permute-start.12 = (bf16[288,512]{1,0:T(8,128)(2,1)}, bf16[288,512]{1,0:T(8,128)(2,1)}, u32[]{:S(2)}, u32[]{:S(2)}) collective-permute-start(bf16[288,512]{1,0:T(8,128)(2,1)} %collective-permute-done.8.refs_4_), channel_id=1, source_target_pairs={{0,8},{8,0},{16,24},{24,16},{1,9},{9,1},{17,25},{25,17},{2,10},{10... | collective-permute-start | bytes 884744 | tf_op jit(solution)/shard_map/ppermute | solution.py:374
  39.3 12.1 %collective-permute-start.13 = (bf16[288,512]{1,0:T(8,128)(2,1)}, bf16[288,512]{1,0:T(8,128)(2,1)}, u32[]{:S(2)}, u32[]{:S(2)}) collective-permute-start(bf16[288,512]{1,0:T(8,128)(2,1)} %collective-permute-done.7.refs_3_), channel_id=1, source_target_pairs={{0,16},{8,24},{16,0},{24,8},{1,17},{9,25},{17,1},{25,9},{2,18},{10... | collective-permute-start | bytes 884744 | tf_op jit(solution)/shard_map/ppermute | solution.py:374
  42.0 1.0 copy-start.3
  44.6 1.5 %copy-start.10 = (bf16[1,256,2304]{1,2,0:T(8,128)(2,1)S(1)}, bf16[1,256,2304]{1,2,0:T(8,128)(2,1)}, u32[]{:S(2)}) copy-start(bf16[1,256,2304]{1,2,0:T(8,128)(2,1)} %copy.12) | copy-start | bytes 3538948
  51.4 13.0 %collective-permute-start.15 = (bf16[512,512]{1,0:T(8,128)(2,1)}, bf16[512,512]{1,0:T(8,128)(2,1)S(1)}, u32[]{:S(2)}, u32[]{:S(2)}) collective-permute-start(bf16[512,512]{1,0:T(8,128)(2,1)} %collective-permute-done.14.kv.refs_0_), channel_id=1, source_target_pairs={{0,2},{2,4},{4,6},{1,3},{3,5},{5,7},{8,10},{10,12},{12,14},{9,11},... | collective-permute-start | bytes 1572872 | tf_op jit(solution)/shard_map/ppermute | solution.py:365
  54.4 1.2 copy-start.4
  59.9 6.1 %copy-start.1 = (bf16[2304,512]{1,0:T(8,128)(2,1)}, bf16[2304,512]{1,0:T(8,128)(2,1)S(1)}, u32[]{:S(2)}) copy-start(bf16[2304,512]{1,0:T(8,128)(2,1)S(1)} %get-tuple-element.136.w) | copy-start | bytes 7077892
  66.0 13.9 %collective-permute-start.16 = (bf16[576,512]{1,0:T(8,128)(2,1)S(1)}, bf16[576,512]{1,0:T(8,128)(2,1)S(1)}, u32[]{:S(2)}, u32[]{:S(2)}) collective-permute-start(bf16[576,512]{1,0:T(8,128)(2,1)S(1)} %get-tuple-element.115), channel_id=1, source_target_pairs={{0,8},{8,0},{16,24},{24,16},{1,9},{9,1},{17,25},{25,17},{2,10},{10... | collective-permute-start | bytes 1769480 | tf_op jit(solution)/shard_map/ppermute | solution.py:374
  66.3 13.5 %collective-permute-start.17 = (bf16[576,512]{1,0:T(8,128)(2,1)S(1)}, bf16[576,512]{1,0:T(8,128)(2,1)S(1)}, u32[]{:S(2)}, u32[]{:S(2)}) collective-permute-start(bf16[576,512]{1,0:T(8,128)(2,1)S(1)} %get-tuple-element.116), channel_id=1, source_target_pairs={{0,16},{8,24},{16,0},{24,8},{1,17},{9,25},{17,1},{25,9},{2,18},{10... | collective-permute-start | bytes 1769480 | tf_op jit(solution)/shard_map/ppermute | solution.py:374
  68.5 11.4 %collective-permute-start.18 = (bf16[512,512]{1,0:T(8,128)(2,1)S(1)}, bf16[512,512]{1,0:T(8,128)(2,1)S(1)}, u32[]{:S(2)}, u32[]{:S(2)}) collective-permute-start(bf16[512,512]{1,0:T(8,128)(2,1)S(1)} %get-tuple-element.120), channel_id=1, source_target_pairs={{2,0},{4,2},{6,4},{3,1},{5,3},{7,5},{10,8},{12,10},{14,12},{11,9},... | collective-permute-start | bytes 1572872 | tf_op jit(solution)/shard_map/ppermute | solution.py:368
  74.5 0.8 copy-start.7
  77.9 1.3 copy-start.5
  79.9 4.2 %copy-start.11 = (bf16[576,512]{1,0:T(8,128)(2,1)}, bf16[576,512]{1,0:T(8,128)(2,1)S(1)}, u32[]{:S(2)}) copy-start(bf16[576,512]{1,0:T(8,128)(2,1)S(1)} %collective-permute-done.16) | copy-start | bytes 1769476
  79.9 4.2 %copy-start.13 = (bf16[576,512]{1,0:T(8,128)(2,1)}, bf16[576,512]{1,0:T(8,128)(2,1)S(1)}, u32[]{:S(2)}) copy-start(bf16[576,512]{1,0:T(8,128)(2,1)S(1)} %collective-permute-done.17) | copy-start | bytes 1769476
  80.9 15.6 %collective-permute-start.22 = (bf16[512,512]{1,0:T(8,128)(2,1)}, bf16[512,512]{1,0:T(8,128)(2,1)}, u32[]{:S(2)}, u32[]{:S(2)}) collective-permute-start(bf16[512,512]{1,0:T(8,128)(2,1)} %add_convert_fusion.3), channel_id=1, source_target_pairs={{2,0},{4,2},{6,4},{3,1},{5,3},{7,5},{10,8},{12,10},{14,12},{11,9},... | collective-permute-start | bytes 1572872 | tf_op jit(solution)/shard_map/ppermute | solution.py:368
  84.1 12.4 %collective-permute-start.19 = (bf16[288,512]{1,0:T(8,128)(2,1)}, bf16[288,512]{1,0:T(8,128)(2,1)}, u32[]{:S(2)}, u32[]{:S(2)}) collective-permute-start(bf16[288,512]{1,0:T(8,128)(2,1)} %get-tuple-element.154), channel_id=1, source_target_pairs={{0,8},{8,0},{16,24},{24,16},{1,9},{9,1},{17,25},{25,17},{2,10},{10... | collective-permute-start | bytes 884744 | tf_op jit(solution)/shard_map/ppermute | solution.py:374
  85.2 11.3 %collective-permute-start.20 = (bf16[288,512]{1,0:T(8,128)(2,1)S(1)}, bf16[288,512]{1,0:T(8,128)(2,1)}, u32[]{:S(2)}, u32[]{:S(2)}) collective-permute-start(bf16[288,512]{1,0:T(8,128)(2,1)S(1)} %get-tuple-element.153), channel_id=1, source_target_pairs={{0,16},{8,24},{16,0},{24,8},{1,17},{9,25},{17,1},{25,9},{2,18},{10... | collective-permute-start | bytes 884744 | tf_op jit(solution)/shard_map/ppermute | solution.py:374
  86.2 10.3 %collective-permute-start.21 = (bf16[256,512]{1,0:T(8,128)(2,1)}, bf16[256,512]{1,0:T(8,128)(2,1)}, u32[]{:S(2)}, u32[]{:S(2)}) collective-permute-start(bf16[256,512]{1,0:T(8,128)(2,1)} %get-tuple-element.169), channel_id=1, source_target_pairs={{0,1},{1,0},{2,3},{3,2},{4,5},{5,4},{6,7},{7,6},{8,9},{9,8},{10,11... | collective-permute-start | bytes 786440 | tf_op jit(solution)/shard_map/ppermute | solution.py:362
  91.6 1.7 %copy-start.2 = (bf16[2304,512]{1,0:T(8,128)(2,1)S(1)}, bf16[2304,512]{1,0:T(8,128)(2,1)}, u32[]{:S(2)}) copy-start(bf16[2304,512]{1,0:T(8,128)(2,1)} %copy-done.1) | copy-start | bytes 7077892
  93.3 5.2 %copy-start.12 = (bf16[576,512]{1,0:T(8,128)(2,1)S(1)}, bf16[576,512]{1,0:T(8,128)(2,1)}, u32[]{:S(2)}) copy-start(bf16[576,512]{1,0:T(8,128)(2,1)} %copy-done.11) | copy-start | bytes 1769476
  96.5 3.0 %copy-start.14 = (bf16[576,512]{1,0:T(8,128)(2,1)S(1)}, bf16[576,512]{1,0:T(8,128)(2,1)}, u32[]{:S(2)}) copy-start(bf16[576,512]{1,0:T(8,128)(2,1)} %copy-done.13) | copy-start | bytes 1769476
  96.5 14.5 %collective-permute-start.24 = (bf16[256,2304]{1,0:T(8,128)(2,1)S(1)}, bf16[256,2304]{1,0:T(8,128)(2,1)S(1)}, u32[]{:S(2)}, u32[]{:S(2)}) collective-permute-start(bf16[256,2304]{1,0:T(8,128)(2,1)S(1)} %get-tuple-element.142), channel_id=1, source_target_pairs={{0,1},{1,0},{2,3},{3,2},{4,5},{5,4},{6,7},{7,6},{8,9},{9,8},{10,11... | collective-permute-start | bytes 3538952 | tf_op jit(solution)/shard_map/ppermute | solution.py:362
  100.8 4.2 %copy-start.8 = (bf16[512,512]{1,0:T(8,128)(2,1)S(1)}, bf16[512,512]{1,0:T(8,128)(2,1)}, u32[]{:S(2)}) copy-start(bf16[512,512]{1,0:T(8,128)(2,1)} %copy-done.7) | copy-start | bytes 1572868
  100.9 11.4 %collective-permute-start.25 = (bf16[144,512]{1,0:T(8,128)(2,1)S(1)}, bf16[144,512]{1,0:T(8,128)(2,1)S(1)}, u32[]{:S(2)}, u32[]{:S(2)}) collective-permute-start(bf16[144,512]{1,0:T(8,128)(2,1)S(1)} %get-tuple-element.163), channel_id=1, source_target_pairs={{0,2},{2,4},{4,6},{6,0},{1,3},{3,5},{5,7},{7,1},{8,10},{10,12},{12... | collective-permute-start | bytes 442376 | tf_op jit(solution)/shard_map/ppermute | solution.py:371
  102.4 12.8 %collective-permute-start.26 = (bf16[144,512]{1,0:T(8,128)(2,1)S(1)}, bf16[144,512]{1,0:T(8,128)(2,1)S(1)}, u32[]{:S(2)}, u32[]{:S(2)}) collective-permute-start(bf16[144,512]{1,0:T(8,128)(2,1)S(1)} %get-tuple-element.162), channel_id=1, source_target_pairs={{0,4},{2,6},{4,0},{6,2},{1,5},{3,7},{5,1},{7,3},{8,12},{10,14},{12... | collective-permute-start | bytes 442376 | tf_op jit(solution)/shard_map/ppermute | solution.py:371
  103.6 13.8 %collective-permute-start.27 = (bf16[144,512]{1,0:T(8,128)(2,1)S(1)}, bf16[144,512]{1,0:T(8,128)(2,1)S(1)}, u32[]{:S(2)}, u32[]{:S(2)}) collective-permute-start(bf16[144,512]{1,0:T(8,128)(2,1)S(1)} %get-tuple-element.161), channel_id=1, source_target_pairs={{0,6},{2,0},{4,2},{6,4},{1,7},{3,1},{5,3},{7,5},{8,14},{10,8},{12,... | collective-permute-start | bytes 442376 | tf_op jit(solution)/shard_map/ppermute | solution.py:371
  106.2 22.5 %collective-permute-start.23 = (bf16[512,512]{1,0:T(8,128)(2,1)S(1)}, bf16[512,512]{1,0:T(8,128)(2,1)S(1)}, u32[]{:S(2)}, u32[]{:S(2)}) collective-permute-start(bf16[512,512]{1,0:T(8,128)(2,1)S(1)} %add_convert_fusion.2), channel_id=1, source_target_pairs={{2,0},{4,2},{6,4},{3,1},{5,3},{7,5},{10,8},{12,10},{14,12},{11,9},... | collective-permute-start | bytes 1572872 | tf_op jit(solution)/shard_map/ppermute | solution.py:368
  112.3 17.0 %copy-start.6 = (f32[512,512]{1,0:T(8,128)S(1)}, f32[512,512]{1,0:T(8,128)}, u32[]{:S(2)}) copy-start(f32[512,512]{1,0:T(8,128)} %copy-done.5) | copy-start | bytes 3145732
  128.8 1.5 %collective-permute-start.29 = (f32[72,512]{1,0:T(8,128)S(1)}, f32[72,512]{1,0:T(8,128)S(1)}, u32[]{:S(2)}, u32[]{:S(2)}) collective-permute-start(f32[72,512]{1,0:T(8,128)S(1)} %get-tuple-element.173), channel_id=1, source_target_pairs={{0,1},{1,0},{2,3},{3,2},{4,5},{5,4},{6,7},{7,6},{8,9},{9,8},{10,11... | collective-permute-start | bytes 442376 | tf_op jit(solution)/shard_map/ppermute | solution.py:362
  129.5 1.6 %collective-permute-start.28 = (bf16[256,512]{1,0:T(8,128)(2,1)S(1)}, bf16[256,512]{1,0:T(8,128)(2,1)S(1)}, u32[]{:S(2)}, u32[]{:S(2)}) collective-permute-start(bf16[256,512]{1,0:T(8,128)(2,1)S(1)} %slice.119), channel_id=1, source_target_pairs={{0,1},{1,0},{2,3},{3,2},{4,5},{5,4},{6,7},{7,6},{8,9},{9,8},{10,11... | collective-permute-start | bytes 786440 | tf_op jit(solution)/shard_map/ppermute | solution.py:362

commit v8 on v7

--- a/solution.py
+++ b/solution.py
@@ -5,6 +5,7 @@
 import jax.numpy as jnp
 from jax import lax
 from jax.experimental import pallas as pl
+from jax.experimental.layout import Layout, with_layout_constraint
 from jax.experimental.pallas import tpu as pltpu
 from jax.sharding import Mesh
 from jax.sharding import PartitionSpec as P
@@ -245,7 +246,7 @@
         out_shape=(shape, shape),
         in_specs=[pl.BlockSpec(memory_space=pltpu.SMEM)] + [vmem] * len(pieces),
         out_specs=(vmem, vmem),
-        cost_estimate=pl.CostEstimate(flops=4 * 10**9, bytes_accessed=1, transcendentals=0),
+        cost_estimate=FILLER,
         compiler_params=pltpu.CompilerParams(vmem_limit_bytes=8 * 1024 * 1024),
         name="column_halves",
     )(info, *pieces)
@@ -389,6 +390,10 @@
     hop = up(kv, 1)
     q = jnp.concatenate([own(q0), swap(other(q0))], 0) * jnp.asarray(HD ** (-0.5), BF16)
     state = forward(info, q, kv, 0, None)
+    *moved, hop, q, m_s, l_s, acc_s = together((*moved, hop, q, *state))
+    state = (m_s, l_s, acc_s)
+    chunks = [kv, hop]
+
     piece = out_weight.shape[0]
     part = 2 * piece
     if near:
@@ -401,17 +406,13 @@
     share = ours.shape[0]
     half = share // 2
     lower, upper = ours[:half], ours[half:]
-    upper_x, lower_y = across(upper, 1), across(lower, 2)
-    hop, q, state, lower, upper, upper_x, lower_y, grad_theirs = together(
-        (hop, q, state, lower, upper, upper_x, lower_y, swap(g0))
-    )
-    chunks = [kv, hop]
-
+    lower, upper, *state = together((lower, upper, *state))
+    state = forward(info, q, hop, 1, state)
     hop = up(hop, 1)
-    state = forward(info, q, chunks[1], 1, state)
-    lower_x, upper_y, diagonal_x, diagonal_y, hop, state = together(
-        (across(lower, 1), across(upper, 2), across(lower_y, 1), across(upper_x, 2), hop, state)
-    )
+    upper_x, lower_y, lower, upper, hop, state, grad_theirs = together(
+        (across(upper, 1), across(lower, 2), lower, upper, hop, state, swap(g0))
+    )
+    grad_theirs = with_layout_constraint(grad_theirs, Layout(major_to_minor=(0, 1)))
     chunks.append(hop)
 
     last_hop = up(hop, 1)
@@ -431,6 +432,16 @@
         jnp.concatenate([strip(3, half, half), strip(2, half, half)], 0),
         jnp.concatenate([strip(1, half, half), strip(2, 0, half), strip(0, 0, share)], 0),
     ]
+    last_hop, state, grad_theirs, *strips = together((last_hop, state, grad_theirs, *strips))
+    lower_x, upper_y, diagonal_x, diagonal_y = (
+        across(lower, 1),
+        across(upper, 2),
+        across(lower_y, 1),
+        across(upper_x, 2),
+    )
+    chunks.append(last_hop)
+    att, lse_t, to_x, to_y = forward(info, q, last_hop, prior, state, strips[:2])
+    att, info = together((att, info))
     weight, da = gradient_into_heads(
         info,
         g0,
@@ -438,9 +449,6 @@
         [(lower, 0, 0), (upper, 0, 1), (lower_x, 1, 0), (upper_x, 1, 1), (lower_y, 2, 0)]
         + [(upper_y, 2, 1), (diagonal_x, 3, 0), (diagonal_y, 3, 1)],
     )
-    da, last_hop, state, *strips = together((da, last_hop, state, *strips))
-    chunks.append(last_hop)
-    att, lse_t, to_x, to_y = forward(info, q, last_hop, prior, state, strips[:2])
 
     carried = None
     terms = {}
@@ -489,7 +497,7 @@
             target = lax.rem(chip + k, chips)
             sent = lax.dynamic_slice_in_dim(mine, target * part, part, 0).astype(BF16)
             got.append(round_chips(sent, k))
-        coming, layer_out, query_grad, *got = together((coming, layer_out, query_grad, *got))
+        layer_out, query_grad, *got = together((layer_out, query_grad, *got))
         for x in got:
             final = final + x.astype(F32)
     else:
@@ -500,6 +508,7 @@
     weight_grad = in_order(
         jnp.where(low, first_rows, last_rows), swap(jnp.where(low, last_rows, first_rows)), 1
     )
+    coming, weight_grad = together((coming, weight_grad))
     kv_grad = (terms[0] + coming.astype(F32)).astype(BF16)
     theirs = swap(kv_grad[tok:])
     key_grad = in_order(kv_grad[:tok, :HD], theirs[:, :HD], 1)

time: 133 us -> 144 us (1.083)
  other arithmetic: 17.3 us -> 22 us
  starting transfers between devices: 40.6 us -> 43.5 us
  local copies, waits for them, and re-layouts: 10.2 us -> 12.1 us
    ppermute x10, waiting for transfers between devices: 8.61 us -> 0.03 us  [across(): return lax.ppermute(x, 'dp', [(i, i ^ k) for i in range(rows_dp)])]
    ppermute x6, waiting for transfers between devices: 11.9 us -> 18 us  [round_chips(): return lax.ppermute(x, 'chip', [(i, (i + k) % chips) for i in range(chips)])]
    ppermute x6, starting transfers between devices: 7.93 us -> 5.25 us  [round_chips(): return lax.ppermute(x, 'chip', [(i, (i + k) % chips) for i in range(chips)])]
    ppermute x8, waiting for transfers between devices: 0.73 us -> 3.32 us  [swap(): return lax.ppermute(x, 'core', [(0, 1), (1, 0)])]
    ppermute x3, starting transfers between devices: 6.97 us -> 9.46 us  [down(): return lax.ppermute(x, 'chip', [(i + k, i) for i in range(chips - k)])]
    ppermute x8, starting transfers between devices: 10.3 us -> 12.2 us  [swap(): return lax.ppermute(x, 'core', [(0, 1), (1, 0)])]
    unnamed x35 -> x63, local copies, waits for them, and re-layouts: 6.27 us -> 8.13 us
  transfers between devices with their start and end apart: 30 -> 30, of which waited for: 13 -> 10; matrix products, arithmetic and copies ran while one was open for 16% -> 16% of each run, Pallas kernels for 16% -> 16%
where the time goes in v8:
time: 144 us; the launch traced here: 143 us
  starting transfers between devices  43.5 us (30%)
  waiting for transfers between devices  40.8 us (28%)
  Pallas kernels  23.2 us (16%)
  other arithmetic  22 us (15%)
  local copies, waits for them, and re-layouts  12.1 us (8%)
    ppermute x6, waiting for transfers between devices, round_chips(): return lax.ppermute(x, 'chip', [(i, (i + k) % chips) for i in range(chips)])  18 us
    ppermute x3, waiting for transfers between devices, down(): return lax.ppermute(x, 'chip', [(i + k, i) for i in range(chips - k)])  13.1 us
    ppermute x8, starting transfers between devices, swap(): return lax.ppermute(x, 'core', [(0, 1), (1, 0)])  12.2 us
    ppermute x3, starting transfers between devices, down(): return lax.ppermute(x, 'chip', [(i + k, i) for i in range(chips - k)])  9.46 us
    ppermute x10, starting transfers between devices, across(): return lax.ppermute(x, 'dp', [(i, i ^ k) for i in range(rows_dp)])  8.51 us
    unnamed x63, local copies, waits for them, and re-layouts  8.13 us
    ppermute x3, starting transfers between devices, up(): return lax.ppermute(x, 'chip', [(i, i + k) for i in range(chips - k)])  8.09 us
    pallas_call x4, Pallas kernels, backward(): pl.pallas_call(functools.partial(backward_kernel, steps, rows, first, las...  7.81 us
  transfers between devices with their start and end apart: 30, of which 10 were waited for; matrix products, arithmetic and copies ran while one was open for 16% of the time, Pallas kernels for 16%

profile of v8, /device:TPU:9, one launch (start us, length us, event | category | flops | bytes accessed | tf_op | source)
XLA Modules:
  0.0 142.8 jit_solution(15489759340227783890)
XLA Ops:
  0.6 1.0 broadcast_select_fusion.4
  1.6 1.0 broadcast_select_fusion.5
  2.7 0.7 collective-permute-start.3
  3.5 1.2 collective-permute-done.3
  4.7 3.2 %collective-permute-start.4 = (bf16[512,512]{1,0:T(8,128)(2,1)S(1)}, bf16[512,512]{1,0:T(8,128)(2,1)S(1)}, u32[]{:S(2)}, u32[]{:S(2)}) collective-permute-start(bf16[512,512]{1,0:T(8,128)(2,1)S(1)} %pad_maximum_fusion.3.kv.refs_0_), channel_id=1, source_target_pairs={{0,2},{2,4},{4,6},{1,3},{3,5},{5,7},{8,10},{10,12},{12,14},{9,11},... | collective-permute-start | bytes 1572872 | tf_op jit(solution)/shard_map/ppermute | solution.py:366
  7.9 0.7 broadcast_select_fusion.1
  9.3 1.3 collective-permute-start
  10.6 1.0 collective-permute-start.1
  11.8 1.4 copy.12
  13.9 1.1 maximum_multiply_fusion.q
  15.1 2.1 %attend_forward.4 = (f32[16,512]{1,0:T(8,128)S(1)}, f32[16,512]{1,0:T(8,128)S(1)}, f32[512,512]{1,0:T(8,128)S(1)}) custom-call(s32[3]{0:T(128)S(1)} %pad_add_fusion.info, bf16[512,512]{1,0:T(8,128)(2,1)S(1)} %maximum_multiply_fusion.q, bf16[512,512]{1,0:T(8,128)(2,1)S(1)} %pad_maximum_fusion.3.kv.refs_0_), custom_call_target="tpu_custom_call" | custom-call | flops 1 | bytes 1 | tf_op jit(solution)/shard_map/attend_forward/pallas_call | solution.py:115
  17.8 5.1 %collective-permute-done.refs_1_ = bf16[72,1024]{1,0:T(8,128)(2,1)S(1)} collective-permute-done((bf16[72,1024]{1,0:T(8,128)(2,1)S(1)}, bf16[72,1024]{1,0:T(8,128)(2,1)S(1)}, u32[]{:S(2)}, u32[]{:S(2)}) %collective-permute-start) | collective-permute-done | bytes 147488 | tf_op jit(solution)/shard_map/ppermute | solution.py:372
  22.9 8.6 %collective-permute-done.1.refs_2_ = bf16[72,1024]{1,0:T(8,128)(2,1)S(1)} collective-permute-done((bf16[72,1024]{1,0:T(8,128)(2,1)S(1)}, bf16[72,1024]{1,0:T(8,128)(2,1)S(1)}, u32[]{:S(2)}, u32[]{:S(2)}) %collective-permute-start.1) | collective-permute-done | bytes 147488 | tf_op jit(solution)/shard_map/ppermute | solution.py:372
  32.1 1.1 copy-done.19
  33.8 1.3 collective-permute-start.6
  35.0 1.9 %collective-permute-start.9 = (bf16[512,512]{1,0:T(8,128)(2,1)S(1)}, bf16[512,512]{1,0:T(8,128)(2,1)}, u32[]{:S(2)}, u32[]{:S(2)}) collective-permute-start(bf16[512,512]{1,0:T(8,128)(2,1)S(1)} %collective-permute-done.4.kv.refs_0_), channel_id=1, source_target_pairs={{0,2},{2,4},{4,6},{1,3},{3,5},{5,7},{8,10},{10,12},{12,14},{9,11},... | collective-permute-start | bytes 1572872 | tf_op jit(solution)/shard_map/ppermute | solution.py:366
  38.6 1.2 collective-permute-start.7
  39.8 1.2 collective-permute-start.8
  41.1 1.2 copy-done.10
  42.3 1.9 %attend_forward.5 = (f32[16,512]{1,0:T(8,128)S(1)}, f32[16,512]{1,0:T(8,128)S(1)}, f32[512,512]{1,0:T(8,128)S(1)}) custom-call(s32[3]{0:T(128)S(1)} %pad_add_fusion.info, bf16[512,512]{1,0:T(8,128)(2,1)S(1)} %maximum_multiply_fusion.q, bf16[512,512]{1,0:T(8,128)(2,1)S(1)} %collective-permute-done.4.kv.refs_0_, f32[16,512]{1,0:T(8,128)S(1)} %get-tuple-element.101.refs_0_, ...), custom_call_target="tpu_custom_call" | custom-call | flops 1 | bytes 1 | tf_op jit(solution)/shard_map/attend_forward/pallas_call | solution.py:115
  44.3 6.3 %collective-permute-done.9.kv.refs_0_ = bf16[512,512]{1,0:T(8,128)(2,1)} collective-permute-done((bf16[512,512]{1,0:T(8,128)(2,1)S(1)}, bf16[512,512]{1,0:T(8,128)(2,1)}, u32[]{:S(2)}, u32[]{:S(2)}) %collective-permute-start.9) | collective-permute-done | bytes 524320 | tf_op jit(solution)/shard_map/ppermute | solution.py:366
  50.6 3.0 %collective-permute-start.11 = (bf16[512,512]{1,0:T(8,128)(2,1)}, bf16[512,512]{1,0:T(8,128)(2,1)}, u32[]{:S(2)}, u32[]{:S(2)}) collective-permute-start(bf16[512,512]{1,0:T(8,128)(2,1)} %collective-permute-done.9.kv.refs_0_), channel_id=1, source_target_pairs={{0,2},{2,4},{4,6},{1,3},{3,5},{5,7},{8,10},{10,12},{12,14},{9,11},... | collective-permute-start | bytes 1572872 | tf_op jit(solution)/shard_map/ppermute | solution.py:366
  53.6 1.3 collective-permute-start.14
  54.8 1.2 collective-permute-start.15
  56.6 1.8 %fusion = bf16[576,512]{1,0:T(8,128)(2,1)} fusion(s32[]{:T(128)S(6)} %select_n.141, bf16[2304,256]{1,0:T(8,128)(2,1)S(1)} %bitcast.28, bf16[2304,256]{1,0:T(8,128)(2,1)} %bitcast.12), kind=kLoop, calls=%fused_computation.20 | loop fusion | flops 1179648 | bytes 2949124 | tf_op jit(solution)/shard_map/concatenate | solution.py:425
  58.4 2.2 %fusion.5 = (bf16[288,512]{1,0:T(8,128)(2,1)}, bf16[288,512]{1,0:T(8,128)(2,1)S(1)}, bf16[288,512]{1,0:T(8,128)(2,1)S(1)}, bf16[288,512]{1,0:T(8,128)(2,1)S(1)},...) fusion(s32[]{:T(128)S(6)} %select_n.139, bf16[2304,256]{1,0:T(8,128)(2,1)S(1)} %bitcast.29, ...), kind=kLoop, calls=%fused_computation.35 | loop fusion | flops 3538944 | bytes 4128792 | tf_op jit(solution)/shard_map/concatenate | solution.py:425
  60.6 0.9 pad_maximum_fusion.1.refs_3_
  61.4 0.8 pad_maximum_fusion.2.refs_4_
  62.3 1.1 attend_forward.6
  63.4 1.0 copy-done.13
  64.4 1.6 %copy.13.theirs = bf16[256,2304]{1,0:T(8,128)(2,1)S(1)} copy(bf16[256,2304]{0,1:T(8,128)(2,1)} %collective-permute-done.10) | data formatting | bytes 2359296 | tf_op jit(solution)/shard_map/optimization_barrier | solution.py:412
  66.0 1.5 %pad_maximum_fusion.x = bf16[1152,512]{1,0:T(8,128)(2,1)S(1)} fusion(bf16[576,512]{1,0:T(8,128)(2,1)} %fusion, bf16[288,512]{1,0:T(8,128)(2,1)} %get-tuple-element.174, bf16[288,512]{1,0:T(8,128)(2,1)} %get-tuple-element.169), kind=kLoop, calls=%fused_computation.15 | loop fusion | flops 3538944 | bytes 2359296 | tf_op jit(solution)/shard_map/concatenate | solution.py:433
  67.9 2.0 %attend_forward.7 = (bf16[512,512]{1,0:T(8,128)(2,1)S(1)}, f32[16,512]{1,0:T(8,128)S(1)}, bf16[576,512]{1,0:T(8,128)(2,1)S(1)}, bf16[576,512]{1,0:T(8,128)(2,1)S(1)}) custom-call(s32[3]{0:T(128)S(1)} %copy-done.21, bf16[512,512]{1,0:T(8,128)(2,1)S(1)} %maximum_multiply_fusion.q, bf16[512,512]{1,0:T(8,128)(2,1)} %collective-permute-done.11.kv.refs_0_, ...), custom_call_target="tpu_custom_call" | custom-call | flops 1 | bytes 1 | tf_op jit(solution)/shard_map/attend_forward/pallas_call | solution.py:115
  70.0 1.3 collective-permute-start.12
  71.2 1.2 collective-permute-start.13
  72.5 3.1 %gradient_into_heads.1 = (bf16[2304,512]{1,0:T(8,128)(2,1)S(1)}, bf16[512,512]{1,0:T(8,128)(2,1)S(1)}) custom-call(s32[3]{0:T(128)S(1)} %copy-done.21, bf16[256,2304]{1,0:T(8,128)(2,1)S(1)} %bitcast.25, bf16[256,2304]{1,0:T(8,128)(2,1)S(1)} %copy.13.theirs, bf16[288,512]{1,0:T(8,128)(2,1)} %bitcast.8.refs_0_, bf16[288,512]{1,0:T(8,128)(2,1)} %bitcast.9.refs_1_, ...), custom_call_target="tpu_custom_call" | custom-call | flops 1 | bytes 1 | tf_op jit(solution)/shard_map/gradient_into_heads/pallas_call | solution.py:275
  75.6 1.8 %attend_backward.4 = (bf16[512,512]{1,0:T(8,128)(2,1)S(1)}, f32[16,512]{1,0:T(8,128)S(1)}, f32[512,512]{1,0:T(8,128)S(1)}) custom-call(s32[3]{0:T(128)S(1)} %copy-done.21, bf16[512,512]{1,0:T(8,128)(2,1)S(1)} %maximum_multiply_fusion.q, bf16[512,512]{1,0:T(8,128)(2,1)S(1)} %get-tuple-element.130.da, f32[16,512]{1,0:T(8,128)S(1)} %get-tuple-element.131.lse_t, ...), custom_call_target="tpu_custom_call" | custom-call | flops 1 | bytes 1 | tf_op jit(solution)/shard_map/attend_backward/pallas_call | solution.py:216
  77.4 3.2 %collective-permute-start.18 = (bf16[512,512]{1,0:T(8,128)(2,1)S(1)}, bf16[512,512]{1,0:T(8,128)(2,1)S(1)}, u32[]{:S(2)}, u32[]{:S(2)}) collective-permute-start(bf16[512,512]{1,0:T(8,128)(2,1)S(1)} %get-tuple-element.133), channel_id=1, source_target_pairs={{2,0},{4,2},{6,4},{3,1},{5,3},{7,5},{10,8},{12,10},{14,12},{11,9},... | collective-permute-start | bytes 1572872 | tf_op jit(solution)/shard_map/ppermute | solution.py:369
  80.7 1.3 strip_product.1
  82.0 1.2 attend_backward.5
  83.2 2.3 %attend_backward.6 = (bf16[512,512]{1,0:T(8,128)(2,1)S(1)}, f32[512,512]{1,0:T(8,128)S(1)}) custom-call(s32[3]{0:T(128)S(1)} %copy-done.21, bf16[512,512]{1,0:T(8,128)(2,1)S(1)} %maximum_multiply_fusion.q, bf16[512,512]{1,0:T(8,128)(2,1)S(1)} %get-tuple-element.130.da, f32[16,512]{1,0:T(8,128)S(1)} %get-tuple-element.131.lse_t, ...), custom_call_target="tpu_custom_call" | custom-call | flops 1 | bytes 1 | tf_op jit(solution)/shard_map/attend_backward/pallas_call | solution.py:216
  85.5 2.5 %attend_backward.7 = (f32[512,512]{1,0:T(8,128)S(1)}, bf16[512,512]{1,0:T(8,128)(2,1)S(1)}) custom-call(s32[3]{0:T(128)S(1)} %copy-done.21, bf16[512,512]{1,0:T(8,128)(2,1)S(1)} %maximum_multiply_fusion.q, bf16[512,512]{1,0:T(8,128)(2,1)S(1)} %get-tuple-element.130.da, f32[16,512]{1,0:T(8,128)S(1)} %get-tuple-element.131.lse_t, ...), custom_call_target="tpu_custom_call" | custom-call | flops 1 | bytes 1 | tf_op jit(solution)/shard_map/attend_backward/pallas_call | solution.py:216
  88.1 4.4 %collective-permute-done.18 = bf16[512,512]{1,0:T(8,128)(2,1)S(1)} collective-permute-done((bf16[512,512]{1,0:T(8,128)(2,1)S(1)}, bf16[512,512]{1,0:T(8,128)(2,1)S(1)}, u32[]{:S(2)}, u32[]{:S(2)}) %collective-permute-start.18) | collective-permute-done | bytes 524320 | tf_op jit(solution)/shard_map/ppermute | solution.py:369
  92.5 1.1 add_convert_fusion.3
  93.6 2.0 %collective-permute-start.22 = (bf16[512,512]{1,0:T(8,128)(2,1)}, bf16[512,512]{1,0:T(8,128)(2,1)}, u32[]{:S(2)}, u32[]{:S(2)}) collective-permute-start(bf16[512,512]{1,0:T(8,128)(2,1)} %add_convert_fusion.3), channel_id=1, source_target_pairs={{2,0},{4,2},{6,4},{3,1},{5,3},{7,5},{10,8},{12,10},{14,12},{11,9},... | collective-permute-start | bytes 1572872 | tf_op jit(solution)/shard_map/ppermute | solution.py:369
  95.6 0.9 add_convert_fusion.4
  97.8 4.0 %collective-permute-start.21 = (bf16[256,512]{1,0:T(8,128)(2,1)}, bf16[256,512]{1,0:T(8,128)(2,1)}, u32[]{:S(2)}, u32[]{:S(2)}) collective-permute-start(bf16[256,512]{1,0:T(8,128)(2,1)} %get-tuple-element.183), channel_id=1, source_target_pairs={{0,1},{1,0},{2,3},{3,2},{4,5},{5,4},{6,7},{7,6},{8,9},{9,8},{10,11... | collective-permute-start | bytes 786440 | tf_op jit(solution)/shard_map/ppermute | solution.py:363
  101.8 1.7 %copy-done.4 = bf16[2304,512]{1,0:T(8,128)(2,1)S(1)} copy-done((bf16[2304,512]{1,0:T(8,128)(2,1)S(1)}, bf16[2304,512]{1,0:T(8,128)(2,1)}, u32[]{:S(2)}) %copy-start.4) | copy-done | bytes 2359320
  103.5 3.2 %layer_product.1 = (f32[256,2304]{1,0:T(8,128)S(1)}, bf16[256,2304]{1,0:T(8,128)(2,1)S(1)}) custom-call(bf16[512,512]{1,0:T(8,128)(2,1)S(1)} %copy-done.2, bf16[2304,512]{1,0:T(8,128)(2,1)S(1)} %copy-done.4), custom_call_target="tpu_custom_call" | custom-call | flops 1 | bytes 1 | tf_op jit(solution)/shard_map/layer_product/pallas_call | solution.py:304
  106.7 3.8 %collective-permute-start.23 = (bf16[256,2304]{1,0:T(8,128)(2,1)S(1)}, bf16[256,2304]{1,0:T(8,128)(2,1)S(1)}, u32[]{:S(2)}, u32[]{:S(2)}) collective-permute-start(bf16[256,2304]{1,0:T(8,128)(2,1)S(1)} %get-tuple-element.153), channel_id=1, source_target_pairs={{0,1},{1,0},{2,3},{3,2},{4,5},{5,4},{6,7},{7,6},{8,9},{9,8},{10,11... | collective-permute-start | bytes 3538952 | tf_op jit(solution)/shard_map/ppermute | solution.py:363
  110.6 1.0 convert_add_fusion
  111.6 1.0 convert_add_fusion.1
  113.0 1.5 %collective-permute-start.24 = (bf16[144,512]{1,0:T(8,128)(2,1)S(1)}, bf16[144,512]{1,0:T(8,128)(2,1)S(1)}, u32[]{:S(2)}, u32[]{:S(2)}) collective-permute-start(bf16[144,512]{1,0:T(8,128)(2,1)S(1)} %get-tuple-element.177), channel_id=1, source_target_pairs={{0,2},{2,4},{4,6},{6,0},{1,3},{3,5},{5,7},{7,1},{8,10},{10,12},{12... | collective-permute-start | bytes 442376 | tf_op jit(solution)/shard_map/ppermute | solution.py:372
  114.8 0.9 collective-permute-start.26
  115.8 1.2 add_convert_fusion.2
  116.9 4.2 %collective-permute-start.27 = (bf16[512,512]{1,0:T(8,128)(2,1)S(1)}, bf16[512,512]{1,0:T(8,128)(2,1)S(1)}, u32[]{:S(2)}, u32[]{:S(2)}) collective-permute-start(bf16[512,512]{1,0:T(8,128)(2,1)S(1)} %add_convert_fusion.2), channel_id=1, source_target_pairs={{2,0},{4,2},{6,4},{3,1},{5,3},{7,5},{10,8},{12,10},{14,12},{11,9},... | collective-permute-start | bytes 1572872 | tf_op jit(solution)/shard_map/ppermute | solution.py:369
  121.2 2.0 %maximum_select_fusion.1 = bf16[256,1024]{1,0:T(8,128)(2,1)} fusion(bf16[256,512]{1,0:T(8,128)(2,1)} %collective-permute-done.21, bf16[256,512]{1,0:T(8,128)(2,1)S(1)} %get-tuple-element.182, pred[]{:T(512)S(6)} %eq.3), kind=kLoop, calls=%fused_computation.30 | loop fusion | flops 2359296 | bytes 1048577 | tf_op jit(solution)/shard_map/jit(_where)/select_n | solution.py:378
  123.2 1.2 add_convert_fusion
  124.4 2.9 %collective-permute-done.25 = bf16[144,512]{1,0:T(8,128)(2,1)S(1)} collective-permute-done((bf16[144,512]{1,0:T(8,128)(2,1)S(1)}, bf16[144,512]{1,0:T(8,128)(2,1)S(1)}, u32[]{:S(2)}, u32[]{:S(2)}) %collective-permute-start.25) | collective-permute-done | bytes 147488 | tf_op jit(solution)/shard_map/ppermute | solution.py:372
  127.3 1.5 %collective-permute-done.26 = bf16[144,512]{1,0:T(8,128)(2,1)S(1)} collective-permute-done((bf16[144,512]{1,0:T(8,128)(2,1)S(1)}, bf16[144,512]{1,0:T(8,128)(2,1)S(1)}, u32[]{:S(2)}, u32[]{:S(2)}) %collective-permute-start.26) | collective-permute-done | bytes 147488 | tf_op jit(solution)/shard_map/ppermute | solution.py:372
  129.4 1.0 collective-permute-done.28
  131.2 8.8 %collective-permute-done.27 = bf16[512,512]{1,0:T(8,128)(2,1)S(1)} collective-permute-done((bf16[512,512]{1,0:T(8,128)(2,1)S(1)}, bf16[512,512]{1,0:T(8,128)(2,1)S(1)}, u32[]{:S(2)}, u32[]{:S(2)}) %collective-permute-start.27) | collective-permute-done | bytes 524320 | tf_op jit(solution)/shard_map/ppermute | solution.py:369
  140.7 1.1 collective-permute-done.29
  141.9 0.9 maximum_select_fusion.3
  (106 shorter events, 10.3 us)
Async XLA Ops:
  1.6 6.3 %copy-start.29 = (bf16[1,256,1024]{2,1,0:T(8,128)(2,1)S(1)}, bf16[1,256,1024]{2,1,0:T(8,128)(2,1)}, u32[]{:S(2)}) copy-start(bf16[1,256,1024]{2,1,0:T(8,128)(2,1)} %param.5) | copy-start | bytes 1572868
  2.7 6.6 %copy-start.17 = (bf16[72,1024]{1,0:T(8,128)(2,1)S(1)}, bf16[72,1024]{1,0:T(8,128)(2,1)}, u32[]{:S(2)}) copy-start(bf16[72,1024]{1,0:T(8,128)(2,1)} %refs_0_.1) | copy-start | bytes 442372
  2.7 9.1 %copy-start = (bf16[1,256,2304]{2,1,0:T(8,128)(2,1)S(1)}, bf16[1,256,2304]{2,1,0:T(8,128)(2,1)}, u32[]{:S(2)}) copy-start(bf16[1,256,2304]{2,1,0:T(8,128)(2,1)} %param.9) | copy-start | bytes 3538948
  2.7 1.9 %collective-permute-start.3 = (bf16[256,512]{1,0:T(8,128)(2,1)S(1)}, bf16[256,512]{1,0:T(8,128)(2,1)S(1)}, u32[]{:S(2)}, u32[]{:S(2)}) collective-permute-start(bf16[256,512]{1,0:T(8,128)(2,1)S(1)} %pad_maximum_fusion.4), channel_id=1, source_target_pairs={{0,1},{1,0},{2,3},{3,2},{4,5},{5,4},{6,7},{7,6},{8,9},{9,8},{10,11... | collective-permute-start | bytes 786440 | tf_op jit(solution)/shard_map/ppermute | solution.py:363
  4.7 27.4 %collective-permute-start.4 = (bf16[512,512]{1,0:T(8,128)(2,1)S(1)}, bf16[512,512]{1,0:T(8,128)(2,1)S(1)}, u32[]{:S(2)}, u32[]{:S(2)}) collective-permute-start(bf16[512,512]{1,0:T(8,128)(2,1)S(1)} %pad_maximum_fusion.3.kv.refs_0_), channel_id=1, source_target_pairs={{0,2},{2,4},{4,6},{1,3},{3,5},{5,7},{8,10},{10,12},{12,14},{9,11},... | collective-permute-start | bytes 1572872 | tf_op jit(solution)/shard_map/ppermute | solution.py:366
  8.7 4.6 %collective-permute-start.5 = (bf16[256,512]{1,0:T(8,128)(2,1)S(1)}, bf16[256,512]{1,0:T(8,128)(2,1)S(1)}, u32[]{:S(2)}, u32[]{:S(2)}) collective-permute-start(bf16[256,512]{1,0:T(8,128)(2,1)S(1)} %get-tuple-element.185), channel_id=1, source_target_pairs={{0,1},{1,0},{2,3},{3,2},{4,5},{5,4},{6,7},{7,6},{8,9},{9,8},{10,11... | collective-permute-start | bytes 786440 | tf_op jit(solution)/shard_map/ppermute | solution.py:363
  9.3 13.6 %collective-permute-start = (bf16[72,1024]{1,0:T(8,128)(2,1)S(1)}, bf16[72,1024]{1,0:T(8,128)(2,1)S(1)}, u32[]{:S(2)}, u32[]{:S(2)}) collective-permute-start(bf16[72,1024]{1,0:T(8,128)(2,1)S(1)} %copy-done.17), channel_id=1, source_target_pairs={{0,2},{2,4},{4,6},{6,0},{1,3},{3,5},{5,7},{7,1},{8,10},{10,12},{12... | collective-permute-start | bytes 442376 | tf_op jit(solution)/shard_map/ppermute | solution.py:372
  10.6 20.8 %collective-permute-start.1 = (bf16[72,1024]{1,0:T(8,128)(2,1)S(1)}, bf16[72,1024]{1,0:T(8,128)(2,1)S(1)}, u32[]{:S(2)}, u32[]{:S(2)}) collective-permute-start(bf16[72,1024]{1,0:T(8,128)(2,1)S(1)} %copy-done.17), channel_id=1, source_target_pairs={{0,4},{2,6},{4,0},{6,2},{1,5},{3,7},{5,1},{7,3},{8,12},{10,14},{12... | collective-permute-start | bytes 442376 | tf_op jit(solution)/shard_map/ppermute | solution.py:372
  11.6 19.9 %collective-permute-start.2 = (bf16[72,1024]{1,0:T(8,128)(2,1)S(1)}, bf16[72,1024]{1,0:T(8,128)(2,1)S(1)}, u32[]{:S(2)}, u32[]{:S(2)}) collective-permute-start(bf16[72,1024]{1,0:T(8,128)(2,1)S(1)} %copy-done.17), channel_id=1, source_target_pairs={{0,6},{2,0},{4,2},{6,4},{1,7},{3,1},{5,3},{7,5},{8,14},{10,8},{12,... | collective-permute-start | bytes 442376 | tf_op jit(solution)/shard_map/ppermute | solution.py:372
  13.2 0.7 copy-start.30
  13.2 31.0 %collective-permute-start.10 = (bf16[256,2304]{0,1:T(8,128)(2,1)}, bf16[256,2304]{0,1:T(8,128)(2,1)}, u32[]{:S(2)}, u32[]{:S(2)}) collective-permute-start(bf16[256,2304]{0,1:T(8,128)(2,1)} %bitcast.27), channel_id=1, source_target_pairs={{0,1},{1,0},{2,3},{3,2},{4,5},{5,4},{6,7},{7,6},{8,9},{9,8},{10,11... | collective-permute-start | bytes 3538952 | tf_op jit(solution)/shard_map/ppermute | solution.py:363
  13.9 48.4 %copy-start.20 = (s32[3]{0:T(128)}, s32[3]{0:T(128)S(1)}, u32[]{:S(2)}) copy-start(s32[3]{0:T(128)S(1)} %pad_add_fusion.info) | copy-start | bytes 40
  17.2 0.6 copy-start.22
  17.8 19.3 %copy-start.9 = (f32[512,512]{1,0:T(8,128)}, f32[512,512]{1,0:T(8,128)S(1)}, u32[]{:S(2)}) copy-start(f32[512,512]{1,0:T(8,128)S(1)} %get-tuple-element.103.refs_2_) | copy-start | bytes 3145732
  31.5 0.7 copy-start.18
  32.1 8.9 %copy-start.7 = (bf16[512,512]{1,0:T(8,128)(2,1)}, bf16[512,512]{1,0:T(8,128)(2,1)S(1)}, u32[]{:S(2)}) copy-start(bf16[512,512]{1,0:T(8,128)(2,1)S(1)} %collective-permute-done.4.kv.refs_0_) | copy-start | bytes 1572868
  32.1 1.1 copy-start.19
  33.8 3.2 %collective-permute-start.6 = (bf16[4,72,512]{2,1,0:T(8,128)(2,1)S(1)}, bf16[4,72,512]{2,1,0:T(8,128)(2,1)S(1)}, u32[]{:S(2)}, u32[]{:S(2)}) collective-permute-start(bf16[4,72,512]{2,1,0:T(8,128)(2,1)S(1)} %get-tuple-element.94), channel_id=1, source_target_pairs={{0,1},{1,0},{2,3},{3,2},{4,5},{5,4},{6,7},{7,6},{8,9},{9,8},{10,11... | collective-permute-start | bytes 884744 | tf_op jit(solution)/shard_map/ppermute | solution.py:363
  35.0 15.5 %collective-permute-start.9 = (bf16[512,512]{1,0:T(8,128)(2,1)S(1)}, bf16[512,512]{1,0:T(8,128)(2,1)}, u32[]{:S(2)}, u32[]{:S(2)}) collective-permute-start(bf16[512,512]{1,0:T(8,128)(2,1)S(1)} %collective-permute-done.4.kv.refs_0_), channel_id=1, source_target_pairs={{0,2},{2,4},{4,6},{1,3},{3,5},{5,7},{8,10},{10,12},{12,14},{9,11},... | collective-permute-start | bytes 1572872 | tf_op jit(solution)/shard_map/ppermute | solution.py:366
  37.1 4.0 %copy-start.23 = (f32[16,512]{1,0:T(8,128)S(1)}, f32[16,512]{1,0:T(8,128)}, u32[]{:S(2)}) copy-start(f32[16,512]{1,0:T(8,128)} %copy-done.22) | copy-start | bytes 98308
  38.6 12.0 %collective-permute-start.7 = (bf16[288,512]{1,0:T(8,128)(2,1)}, bf16[288,512]{1,0:T(8,128)(2,1)}, u32[]{:S(2)}, u32[]{:S(2)}) collective-permute-start(bf16[288,512]{1,0:T(8,128)(2,1)} %bitcast.9.refs_1_), channel_id=1, source_target_pairs={{0,8},{8,0},{16,24},{24,16},{1,9},{9,1},{17,25},{25,17},{2,10},{10... | collective-permute-start | bytes 884744 | tf_op jit(solution)/shard_map/ppermute | solution.py:375
  39.8 10.7 %collective-permute-start.8 = (bf16[288,512]{1,0:T(8,128)(2,1)}, bf16[288,512]{1,0:T(8,128)(2,1)}, u32[]{:S(2)}, u32[]{:S(2)}) collective-permute-start(bf16[288,512]{1,0:T(8,128)(2,1)} %bitcast.8.refs_0_), channel_id=1, source_target_pairs={{0,16},{8,24},{16,0},{24,8},{1,17},{9,25},{17,1},{25,9},{2,18},{10... | collective-permute-start | bytes 884744 | tf_op jit(solution)/shard_map/ppermute | solution.py:375
  41.1 1.2 copy-start.10
  42.3 14.3 %copy-start.24 = (bf16[1,256,2304]{1,2,0:T(8,128)(2,1)S(1)}, bf16[1,256,2304]{1,2,0:T(8,128)(2,1)}, u32[]{:S(2)}) copy-start(bf16[1,256,2304]{1,2,0:T(8,128)(2,1)} %copy.12) | copy-start | bytes 3538948
  50.6 16.9 %collective-permute-start.11 = (bf16[512,512]{1,0:T(8,128)(2,1)}, bf16[512,512]{1,0:T(8,128)(2,1)}, u32[]{:S(2)}, u32[]{:S(2)}) collective-permute-start(bf16[512,512]{1,0:T(8,128)(2,1)} %collective-permute-done.9.kv.refs_0_), channel_id=1, source_target_pairs={{0,2},{2,4},{4,6},{1,3},{3,5},{5,7},{8,10},{10,12},{12,14},{9,11},... | collective-permute-start | bytes 1572872 | tf_op jit(solution)/shard_map/ppermute | solution.py:366
  53.6 17.7 %collective-permute-start.14 = (bf16[288,512]{1,0:T(8,128)(2,1)}, bf16[288,512]{1,0:T(8,128)(2,1)}, u32[]{:S(2)}, u32[]{:S(2)}) collective-permute-start(bf16[288,512]{1,0:T(8,128)(2,1)} %bitcast.8.refs_0_), channel_id=1, source_target_pairs={{0,8},{8,0},{16,24},{24,16},{1,9},{9,1},{17,25},{25,17},{2,10},{10... | collective-permute-start | bytes 884744 | tf_op jit(solution)/shard_map/ppermute | solution.py:375
  54.8 17.7 %collective-permute-start.15 = (bf16[288,512]{1,0:T(8,128)(2,1)}, bf16[288,512]{1,0:T(8,128)(2,1)}, u32[]{:S(2)}, u32[]{:S(2)}) collective-permute-start(bf16[288,512]{1,0:T(8,128)(2,1)} %bitcast.9.refs_1_), channel_id=1, source_target_pairs={{0,16},{8,24},{16,0},{24,8},{1,17},{9,25},{17,1},{25,9},{2,18},{10... | collective-permute-start | bytes 884744 | tf_op jit(solution)/shard_map/ppermute | solution.py:375
  56.1 16.4 %collective-permute-start.16 = (bf16[288,512]{1,0:T(8,128)(2,1)}, bf16[288,512]{1,0:T(8,128)(2,1)}, u32[]{:S(2)}, u32[]{:S(2)}) collective-permute-start(bf16[288,512]{1,0:T(8,128)(2,1)} %collective-permute-done.8.refs_4_), channel_id=1, source_target_pairs={{0,8},{8,0},{16,24},{24,16},{1,9},{9,1},{17,25},{25,17},{2,10},{10... | collective-permute-start | bytes 884744 | tf_op jit(solution)/shard_map/ppermute | solution.py:375
  56.3 16.2 %collective-permute-start.17 = (bf16[288,512]{1,0:T(8,128)(2,1)}, bf16[288,512]{1,0:T(8,128)(2,1)}, u32[]{:S(2)}, u32[]{:S(2)}) collective-permute-start(bf16[288,512]{1,0:T(8,128)(2,1)} %collective-permute-done.7.refs_3_), channel_id=1, source_target_pairs={{0,16},{8,24},{16,0},{24,8},{1,17},{9,25},{17,1},{25,9},{2,18},{10... | collective-permute-start | bytes 884744 | tf_op jit(solution)/shard_map/ppermute | solution.py:375
  63.4 1.0 copy-start.13
  66.0 1.5 %copy-start.5 = (bf16[576,512]{1,0:T(8,128)(2,1)S(1)}, bf16[576,512]{1,0:T(8,128)(2,1)}, u32[]{:S(2)}) copy-start(bf16[576,512]{1,0:T(8,128)(2,1)} %pad_maximum_fusion.1.refs_3_) | copy-start | bytes 1769476
  66.0 1.6 %copy-start.6 = (bf16[576,512]{1,0:T(8,128)(2,1)S(1)}, bf16[576,512]{1,0:T(8,128)(2,1)}, u32[]{:S(2)}) copy-start(bf16[576,512]{1,0:T(8,128)(2,1)} %pad_maximum_fusion.2.refs_4_) | copy-start | bytes 1769476
  66.0 1.9 %copy-start.14 = (f32[512,512]{1,0:T(8,128)S(1)}, f32[512,512]{1,0:T(8,128)}, u32[]{:S(2)}) copy-start(f32[512,512]{1,0:T(8,128)} %copy-done.13) | copy-start | bytes 3145732
  66.0 1.9 %copy-start.21 = (s32[3]{0:T(128)S(1)}, s32[3]{0:T(128)}, u32[]{:S(2)}) copy-start(s32[3]{0:T(128)} %copy-done.20) | copy-start | bytes 40
  69.9 10.7 %copy-start.1 = (bf16[512,512]{1,0:T(8,128)(2,1)}, bf16[512,512]{1,0:T(8,128)(2,1)S(1)}, u32[]{:S(2)}) copy-start(bf16[512,512]{1,0:T(8,128)(2,1)S(1)} %get-tuple-element.143.refs_1_.w.x) | copy-start | bytes 1572868
  70.0 22.5 %collective-permute-start.12 = (bf16[576,512]{1,0:T(8,128)(2,1)S(1)}, bf16[576,512]{1,0:T(8,128)(2,1)S(1)}, u32[]{:S(2)}, u32[]{:S(2)}) collective-permute-start(bf16[576,512]{1,0:T(8,128)(2,1)S(1)} %get-tuple-element.121), channel_id=1, source_target_pairs={{0,8},{8,0},{16,24},{24,16},{1,9},{9,1},{17,25},{25,17},{2,10},{10... | collective-permute-start | bytes 1769480 | tf_op jit(solution)/shard_map/ppermute | solution.py:375
  71.2 21.2 %collective-permute-start.13 = (bf16[576,512]{1,0:T(8,128)(2,1)S(1)}, bf16[576,512]{1,0:T(8,128)(2,1)S(1)}, u32[]{:S(2)}, u32[]{:S(2)}) collective-permute-start(bf16[576,512]{1,0:T(8,128)(2,1)S(1)} %get-tuple-element.122), channel_id=1, source_target_pairs={{0,16},{8,24},{16,0},{24,8},{1,17},{9,25},{17,1},{25,9},{2,18},{10... | collective-permute-start | bytes 1769480 | tf_op jit(solution)/shard_map/ppermute | solution.py:375
  75.6 6.4 %copy-start.3 = (bf16[2304,512]{1,0:T(8,128)(2,1)}, bf16[2304,512]{1,0:T(8,128)(2,1)S(1)}, u32[]{:S(2)}) copy-start(bf16[2304,512]{1,0:T(8,128)(2,1)S(1)} %get-tuple-element.144.w) | copy-start | bytes 7077892
  77.4 15.0 %collective-permute-start.18 = (bf16[512,512]{1,0:T(8,128)(2,1)S(1)}, bf16[512,512]{1,0:T(8,128)(2,1)S(1)}, u32[]{:S(2)}, u32[]{:S(2)}) collective-permute-start(bf16[512,512]{1,0:T(8,128)(2,1)S(1)} %get-tuple-element.133), channel_id=1, source_target_pairs={{2,0},{4,2},{6,4},{3,1},{5,3},{7,5},{10,8},{12,10},{14,12},{11,9},... | collective-permute-start | bytes 1572872 | tf_op jit(solution)/shard_map/ppermute | solution.py:369
  82.0 1.2 copy-start.8
  85.5 2.5 %copy-start.15 = (bf16[512,512]{1,0:T(8,128)(2,1)}, bf16[512,512]{1,0:T(8,128)(2,1)S(1)}, u32[]{:S(2)}) copy-start(bf16[512,512]{1,0:T(8,128)(2,1)S(1)} %get-tuple-element.160) | copy-start | bytes 1572868
  88.1 8.5 %copy-start.11 = (f32[512,512]{1,0:T(8,128)}, f32[512,512]{1,0:T(8,128)S(1)}, u32[]{:S(2)}) copy-start(f32[512,512]{1,0:T(8,128)S(1)} %get-tuple-element.159) | copy-start | bytes 3145732
  92.5 4.1 %copy-start.25 = (bf16[576,512]{1,0:T(8,128)(2,1)}, bf16[576,512]{1,0:T(8,128)(2,1)S(1)}, u32[]{:S(2)}) copy-start(bf16[576,512]{1,0:T(8,128)(2,1)S(1)} %collective-permute-done.12) | copy-start | bytes 1769476
  92.5 4.1 %copy-start.27 = (bf16[576,512]{1,0:T(8,128)(2,1)}, bf16[576,512]{1,0:T(8,128)(2,1)S(1)}, u32[]{:S(2)}) copy-start(bf16[576,512]{1,0:T(8,128)(2,1)S(1)} %collective-permute-done.13) | copy-start | bytes 1769476
  93.6 8.2 %copy-start.2 = (bf16[512,512]{1,0:T(8,128)(2,1)S(1)}, bf16[512,512]{1,0:T(8,128)(2,1)}, u32[]{:S(2)}) copy-start(bf16[512,512]{1,0:T(8,128)(2,1)} %copy-done.1) | copy-start | bytes 1572868
  93.6 13.1 %collective-permute-start.22 = (bf16[512,512]{1,0:T(8,128)(2,1)}, bf16[512,512]{1,0:T(8,128)(2,1)}, u32[]{:S(2)}, u32[]{:S(2)}) collective-permute-start(bf16[512,512]{1,0:T(8,128)(2,1)} %add_convert_fusion.3), channel_id=1, source_target_pairs={{2,0},{4,2},{6,4},{3,1},{5,3},{7,5},{10,8},{12,10},{14,12},{11,9},... | collective-permute-start | bytes 1572872 | tf_op jit(solution)/shard_map/ppermute | solution.py:369
  96.5 10.1 %collective-permute-start.19 = (bf16[288,512]{1,0:T(8,128)(2,1)}, bf16[288,512]{1,0:T(8,128)(2,1)}, u32[]{:S(2)}, u32[]{:S(2)}) collective-permute-start(bf16[288,512]{1,0:T(8,128)(2,1)} %get-tuple-element.168), channel_id=1, source_target_pairs={{0,8},{8,0},{16,24},{24,16},{1,9},{9,1},{17,25},{25,17},{2,10},{10... | collective-permute-start | bytes 884744 | tf_op jit(solution)/shard_map/ppermute | solution.py:375
  96.9 9.8 %collective-permute-start.20 = (bf16[288,512]{1,0:T(8,128)(2,1)S(1)}, bf16[288,512]{1,0:T(8,128)(2,1)}, u32[]{:S(2)}, u32[]{:S(2)}) collective-permute-start(bf16[288,512]{1,0:T(8,128)(2,1)S(1)} %get-tuple-element.167), channel_id=1, source_target_pairs={{0,16},{8,24},{16,0},{24,8},{1,17},{9,25},{17,1},{25,9},{2,18},{10... | collective-permute-start | bytes 884744 | tf_op jit(solution)/shard_map/ppermute | solution.py:375
  97.8 8.8 %collective-permute-start.21 = (bf16[256,512]{1,0:T(8,128)(2,1)}, bf16[256,512]{1,0:T(8,128)(2,1)}, u32[]{:S(2)}, u32[]{:S(2)}) collective-permute-start(bf16[256,512]{1,0:T(8,128)(2,1)} %get-tuple-element.183), channel_id=1, source_target_pairs={{0,1},{1,0},{2,3},{3,2},{4,5},{5,4},{6,7},{7,6},{8,9},{9,8},{10,11... | collective-permute-start | bytes 786440 | tf_op jit(solution)/shard_map/ppermute | solution.py:363
  101.8 1.7 %copy-start.4 = (bf16[2304,512]{1,0:T(8,128)(2,1)S(1)}, bf16[2304,512]{1,0:T(8,128)(2,1)}, u32[]{:S(2)}) copy-start(bf16[2304,512]{1,0:T(8,128)(2,1)} %copy-done.3) | copy-start | bytes 7077892
  103.5 7.1 %copy-start.28 = (bf16[576,512]{1,0:T(8,128)(2,1)S(1)}, bf16[576,512]{1,0:T(8,128)(2,1)}, u32[]{:S(2)}) copy-start(bf16[576,512]{1,0:T(8,128)(2,1)} %copy-done.27) | copy-start | bytes 1769476
  106.7 4.9 %copy-start.26 = (bf16[576,512]{1,0:T(8,128)(2,1)S(1)}, bf16[576,512]{1,0:T(8,128)(2,1)}, u32[]{:S(2)}) copy-start(bf16[576,512]{1,0:T(8,128)(2,1)} %copy-done.25) | copy-start | bytes 1769476
  106.7 16.5 %collective-permute-start.23 = (bf16[256,2304]{1,0:T(8,128)(2,1)S(1)}, bf16[256,2304]{1,0:T(8,128)(2,1)S(1)}, u32[]{:S(2)}, u32[]{:S(2)}) collective-permute-start(bf16[256,2304]{1,0:T(8,128)(2,1)S(1)} %get-tuple-element.153), channel_id=1, source_target_pairs={{0,1},{1,0},{2,3},{3,2},{4,5},{5,4},{6,7},{7,6},{8,9},{9,8},{10,11... | collective-permute-start | bytes 3538952 | tf_op jit(solution)/shard_map/ppermute | solution.py:363
  112.9 2.9 %copy-start.16 = (bf16[512,512]{1,0:T(8,128)(2,1)S(1)}, bf16[512,512]{1,0:T(8,128)(2,1)}, u32[]{:S(2)}) copy-start(bf16[512,512]{1,0:T(8,128)(2,1)} %copy-done.15) | copy-start | bytes 1572868
  113.0 11.4 %collective-permute-start.24 = (bf16[144,512]{1,0:T(8,128)(2,1)S(1)}, bf16[144,512]{1,0:T(8,128)(2,1)S(1)}, u32[]{:S(2)}, u32[]{:S(2)}) collective-permute-start(bf16[144,512]{1,0:T(8,128)(2,1)S(1)} %get-tuple-element.177), channel_id=1, source_target_pairs={{0,2},{2,4},{4,6},{6,0},{1,3},{3,5},{5,7},{7,1},{8,10},{10,12},{12... | collective-permute-start | bytes 442376 | tf_op jit(solution)/shard_map/ppermute | solution.py:372
  114.5 12.8 %collective-permute-start.25 = (bf16[144,512]{1,0:T(8,128)(2,1)S(1)}, bf16[144,512]{1,0:T(8,128)(2,1)S(1)}, u32[]{:S(2)}, u32[]{:S(2)}) collective-permute-start(bf16[144,512]{1,0:T(8,128)(2,1)S(1)} %get-tuple-element.176), channel_id=1, source_target_pairs={{0,4},{2,6},{4,0},{6,2},{1,5},{3,7},{5,1},{7,3},{8,12},{10,14},{12... | collective-permute-start | bytes 442376 | tf_op jit(solution)/shard_map/ppermute | solution.py:372
  114.8 13.9 %collective-permute-start.26 = (bf16[144,512]{1,0:T(8,128)(2,1)S(1)}, bf16[144,512]{1,0:T(8,128)(2,1)S(1)}, u32[]{:S(2)}, u32[]{:S(2)}) collective-permute-start(bf16[144,512]{1,0:T(8,128)(2,1)S(1)} %get-tuple-element.175), channel_id=1, source_target_pairs={{0,6},{2,0},{4,2},{6,4},{1,7},{3,1},{5,3},{7,5},{8,14},{10,8},{12,... | collective-permute-start | bytes 442376 | tf_op jit(solution)/shard_map/ppermute | solution.py:372
  116.9 23.0 %collective-permute-start.27 = (bf16[512,512]{1,0:T(8,128)(2,1)S(1)}, bf16[512,512]{1,0:T(8,128)(2,1)S(1)}, u32[]{:S(2)}, u32[]{:S(2)}) collective-permute-start(bf16[512,512]{1,0:T(8,128)(2,1)S(1)} %add_convert_fusion.2), channel_id=1, source_target_pairs={{2,0},{4,2},{6,4},{3,1},{5,3},{7,5},{10,8},{12,10},{14,12},{11,9},... | collective-permute-start | bytes 1572872 | tf_op jit(solution)/shard_map/ppermute | solution.py:369
  124.4 15.6 %copy-start.12 = (f32[512,512]{1,0:T(8,128)S(1)}, f32[512,512]{1,0:T(8,128)}, u32[]{:S(2)}) copy-start(f32[512,512]{1,0:T(8,128)} %copy-done.11) | copy-start | bytes 3145732
  128.8 1.6 %collective-permute-start.28 = (f32[72,512]{1,0:T(8,128)S(1)}, f32[72,512]{1,0:T(8,128)S(1)}, u32[]{:S(2)}, u32[]{:S(2)}) collective-permute-start(f32[72,512]{1,0:T(8,128)S(1)} %get-tuple-element.187), channel_id=1, source_target_pairs={{0,1},{1,0},{2,3},{3,2},{4,5},{5,4},{6,7},{7,6},{8,9},{9,8},{10,11... | collective-permute-start | bytes 442376 | tf_op jit(solution)/shard_map/ppermute | solution.py:363
  140.2 1.7 %collective-permute-start.29 = (bf16[256,512]{1,0:T(8,128)(2,1)S(1)}, bf16[256,512]{1,0:T(8,128)(2,1)S(1)}, u32[]{:S(2)}, u32[]{:S(2)}) collective-permute-start(bf16[256,512]{1,0:T(8,128)(2,1)S(1)} %slice.121), channel_id=1, source_target_pairs={{0,1},{1,0},{2,3},{3,2},{4,5},{5,4},{6,7},{7,6},{8,9},{9,8},{10,11... | collective-permute-start | bytes 786440 | tf_op jit(solution)/shard_map/ppermute | solution.py:363

commit v9 on v7

--- a/solution.py
+++ b/solution.py
@@ -489,7 +489,7 @@
             target = lax.rem(chip + k, chips)
             sent = lax.dynamic_slice_in_dim(mine, target * part, part, 0).astype(BF16)
             got.append(round_chips(sent, k))
-        coming, layer_out, query_grad, *got = together((coming, layer_out, query_grad, *got))
+        *got, layer_out, query_grad, coming = together((*got, layer_out, query_grad, coming))
         for x in got:
             final = final + x.astype(F32)
     else:

time: 133 us -> 132 us (level)
    ppermute x3, waiting for transfers between devices: 11.9 us -> 0.66 us  [down(): return lax.ppermute(x, 'chip', [(i + k, i) for i in range(chips - k)])]
    ppermute x6, waiting for transfers between devices: 11.9 us -> 23 us  [round_chips(): return lax.ppermute(x, 'chip', [(i, (i + k) % chips) for i in range(chips)])]
  transfers between devices with their start and end apart: 30 -> 30, of which waited for: 13 -> 12; matrix products, arithmetic and copies ran while one was open for 16% -> 16% of each run, Pallas kernels for 16% -> 16%
where the time goes in v9:
time: 132 us; the launch traced here: 131 us
  starting transfers between devices  40.1 us (30%)
  waiting for transfers between devices  39.7 us (30%)
  Pallas kernels  23 us (17%)
  other arithmetic  17.3 us (13%)
  local copies, waits for them, and re-layouts  10.2 us (8%)
    ppermute x6, waiting for transfers between devices, round_chips(): return lax.ppermute(x, 'chip', [(i, (i + k) % chips) for i in range(chips)])  23 us
    ppermute x8, starting transfers between devices, swap(): return lax.ppermute(x, 'core', [(0, 1), (1, 0)])  10.7 us
    ppermute x10, waiting for transfers between devices, across(): return lax.ppermute(x, 'dp', [(i, i ^ k) for i in range(rows_dp)])  8.61 us
    ppermute x10, starting transfers between devices, across(): return lax.ppermute(x, 'dp', [(i, i ^ k) for i in range(rows_dp)])  8.42 us
    ppermute x6, starting transfers between devices, round_chips(): return lax.ppermute(x, 'chip', [(i, (i + k) % chips) for i in range(chips)])  8 us
    pallas_call x4, Pallas kernels, backward(): pl.pallas_call(functools.partial(backward_kernel, steps, rows, first, las...  7.54 us
    pallas_call x4, Pallas kernels, forward(): pl.pallas_call(functools.partial(forward_kernel, step, rows, first, last)...  7.23 us
    ppermute x3, starting transfers between devices, up(): return lax.ppermute(x, 'chip', [(i, i + k) for i in range(chips - k)])  7.03 us
  transfers between devices with their start and end apart: 30, of which 12 were waited for; matrix products, arithmetic and copies ran while one was open for 16% of the time, Pallas kernels for 16%

profile of v9, /device:TPU:9, one launch (start us, length us, event | category | flops | bytes accessed | tf_op | source)
XLA Modules:
  0.0 131.5 jit_solution(1834900874097208330)
XLA Ops:
  0.6 1.3 %collective-permute-start.3 = (bf16[72,1024]{1,0:T(8,128)(2,1)}, bf16[72,1024]{1,0:T(8,128)(2,1)S(1)}, u32[]{:S(2)}, u32[]{:S(2)}) collective-permute-start(bf16[72,1024]{1,0:T(8,128)(2,1)} %refs_0_.1), channel_id=1, source_target_pairs={{0,2},{2,4},{4,6},{6,0},{1,3},{3,5},{5,7},{7,1},{8,10},{10,12},{12... | collective-permute-start | bytes 442376 | tf_op jit(solution)/shard_map/ppermute | solution.py:371
  2.0 1.1 collective-permute-start.4
  3.1 1.4 %collective-permute-start.5 = (bf16[72,1024]{1,0:T(8,128)(2,1)}, bf16[72,1024]{1,0:T(8,128)(2,1)S(1)}, u32[]{:S(2)}, u32[]{:S(2)}) collective-permute-start(bf16[72,1024]{1,0:T(8,128)(2,1)} %refs_0_.1), channel_id=1, source_target_pairs={{0,6},{2,0},{4,2},{6,4},{1,7},{3,1},{5,3},{7,5},{8,14},{10,8},{12,... | collective-permute-start | bytes 442376 | tf_op jit(solution)/shard_map/ppermute | solution.py:371
  4.5 1.0 broadcast_select_fusion.5
  5.5 1.6 %broadcast_select_fusion.4 = (bf16[256,256]{1,0:T(8,128)(2,1)}, bf16[256,256]{1,0:T(8,128)(2,1)S(1)}) fusion(pred[]{:T(512)S(6)} %eq.3, bf16[256,512]{1,0:T(8,128)(2,1)} %bitcast.35), kind=kLoop, calls=%fused_computation.55 | loop fusion | flops 131072 | bytes 524289 | tf_op jit(solution)/shard_map/jit(_where)/select_n | solution.py:355
  7.1 1.6 %collective-permute-start = (bf16[256,512]{1,0:T(8,128)(2,1)S(1)}, bf16[256,512]{1,0:T(8,128)(2,1)}, u32[]{:S(2)}, u32[]{:S(2)}) collective-permute-start(bf16[256,512]{1,0:T(8,128)(2,1)S(1)} %pad_maximum_fusion.4), channel_id=1, source_target_pairs={{0,1},{1,0},{2,3},{3,2},{4,5},{5,4},{6,7},{7,6},{8,9},{9,8},{10,11... | collective-permute-start | bytes 786440 | tf_op jit(solution)/shard_map/ppermute | solution.py:362
  8.7 1.4 %copy.12 = bf16[1,256,2304]{1,2,0:T(8,128)(2,1)} copy(bf16[1,256,2304]{2,1,0:T(8,128)(2,1)S(1)} %copy-done) | data formatting | bytes 2359296 | tf_op args[4]
  10.3 4.0 %collective-permute-done.4.refs_2_ = bf16[72,1024]{1,0:T(8,128)(2,1)S(1)} collective-permute-done((bf16[72,1024]{1,0:T(8,128)(2,1)}, bf16[72,1024]{1,0:T(8,128)(2,1)S(1)}, u32[]{:S(2)}, u32[]{:S(2)}) %collective-permute-start.4) | collective-permute-done | bytes 147488 | tf_op jit(solution)/shard_map/ppermute | solution.py:371
  14.3 2.7 %collective-permute-done.5.refs_3_ = bf16[72,1024]{1,0:T(8,128)(2,1)S(1)} collective-permute-done((bf16[72,1024]{1,0:T(8,128)(2,1)}, bf16[72,1024]{1,0:T(8,128)(2,1)S(1)}, u32[]{:S(2)}, u32[]{:S(2)}) %collective-permute-start.5) | collective-permute-done | bytes 147488 | tf_op jit(solution)/shard_map/ppermute | solution.py:371
  18.3 1.0 pad_maximum_fusion.3.kv.refs_0_
  19.3 1.9 %collective-permute-start.1 = (bf16[512,512]{1,0:T(8,128)(2,1)S(1)}, bf16[512,512]{1,0:T(8,128)(2,1)}, u32[]{:S(2)}, u32[]{:S(2)}) collective-permute-start(bf16[512,512]{1,0:T(8,128)(2,1)S(1)} %pad_maximum_fusion.3.kv.refs_0_), channel_id=1, source_target_pairs={{0,2},{2,4},{4,6},{1,3},{3,5},{5,7},{8,10},{10,12},{12,14},{9,11},... | collective-permute-start | bytes 1572872 | tf_op jit(solution)/shard_map/ppermute | solution.py:365
  21.4 0.7 copy.11
  22.1 1.2 collective-permute-start.7
  23.3 0.7 copy.10
  24.1 1.2 collective-permute-start.8
  25.4 2.1 %attend_forward.4 = (f32[16,512]{1,0:T(8,128)S(1)}, f32[16,512]{1,0:T(8,128)S(1)}, f32[512,512]{1,0:T(8,128)S(1)}) custom-call(s32[3]{0:T(128)S(1)} %pad_add_fusion.info, bf16[512,512]{1,0:T(8,128)(2,1)S(1)} %maximum_multiply_fusion.q, bf16[512,512]{1,0:T(8,128)(2,1)S(1)} %pad_maximum_fusion.3.kv.refs_0_), custom_call_target="tpu_custom_call" | custom-call | flops 1 | bytes 1 | tf_op jit(solution)/shard_map/attend_forward/pallas_call | solution.py:114
  27.5 3.0 %collective-permute-done.7.refs_3_ = bf16[288,512]{1,0:T(8,128)(2,1)} collective-permute-done((bf16[288,512]{1,0:T(8,128)(2,1)}, bf16[288,512]{1,0:T(8,128)(2,1)}, u32[]{:S(2)}, u32[]{:S(2)}) %collective-permute-start.7) | collective-permute-done | bytes 294944 | tf_op jit(solution)/shard_map/ppermute | solution.py:374
  30.5 1.6 %collective-permute-done.8.refs_4_ = bf16[288,512]{1,0:T(8,128)(2,1)} collective-permute-done((bf16[288,512]{1,0:T(8,128)(2,1)}, bf16[288,512]{1,0:T(8,128)(2,1)}, u32[]{:S(2)}, u32[]{:S(2)}) %collective-permute-start.8) | collective-permute-done | bytes 294944 | tf_op jit(solution)/shard_map/ppermute | solution.py:374
  32.2 2.1 %collective-permute-done.1.kv.refs_0_ = bf16[512,512]{1,0:T(8,128)(2,1)} collective-permute-done((bf16[512,512]{1,0:T(8,128)(2,1)S(1)}, bf16[512,512]{1,0:T(8,128)(2,1)}, u32[]{:S(2)}, u32[]{:S(2)}) %collective-permute-start.1) | collective-permute-done | bytes 524320 | tf_op jit(solution)/shard_map/ppermute | solution.py:365
  34.3 2.2 %collective-permute-start.14 = (bf16[512,512]{1,0:T(8,128)(2,1)}, bf16[512,512]{1,0:T(8,128)(2,1)}, u32[]{:S(2)}, u32[]{:S(2)}) collective-permute-start(bf16[512,512]{1,0:T(8,128)(2,1)} %collective-permute-done.1.kv.refs_0_), channel_id=1, source_target_pairs={{0,2},{2,4},{4,6},{1,3},{3,5},{5,7},{8,10},{10,12},{12,14},{9,11},... | collective-permute-start | bytes 1572872 | tf_op jit(solution)/shard_map/ppermute | solution.py:365
  36.5 1.3 collective-permute-start.10
  37.8 1.2 collective-permute-start.11
  39.5 2.5 %attend_forward.5 = (f32[16,512]{1,0:T(8,128)S(1)}, f32[16,512]{1,0:T(8,128)S(1)}, f32[512,512]{1,0:T(8,128)S(1)}) custom-call(s32[3]{0:T(128)S(1)} %pad_add_fusion.info, bf16[512,512]{1,0:T(8,128)(2,1)S(1)} %maximum_multiply_fusion.q, bf16[512,512]{1,0:T(8,128)(2,1)} %collective-permute-done.1.kv.refs_0_, f32[16,512]{1,0:T(8,128)S(1)} %get-tuple-element.91.refs_0_, ...), custom_call_target="tpu_custom_call" | custom-call | flops 1 | bytes 1 | tf_op jit(solution)/shard_map/attend_forward/pallas_call | solution.py:114
  42.0 1.0 copy-done.3
  43.0 1.6 %copy.14.theirs = bf16[256,2304]{1,0:T(8,128)(2,1)S(1)} copy(bf16[256,2304]{0,1:T(8,128)(2,1)} %collective-permute-done.9) | data formatting | bytes 2359296 | tf_op jit(solution)/shard_map/optimization_barrier | solution.py:405
  44.6 1.2 fusion
  46.0 1.4 %fusion.5 = (bf16[288,512]{1,0:T(8,128)(2,1)S(1)}, bf16[288,512]{1,0:T(8,128)(2,1)S(1)}, bf16[288,512]{1,0:T(8,128)(2,1)S(1)}, bf16[288,512]{1,0:T(8,128)(2,1)S(...) fusion(s32[]{:T(128)S(6)} %select_n.139, bf16[2304,256]{1,0:T(8,128)(2,1)S(1)} %bitcast.29, ...), kind=kLoop, calls=%fused_computation.35 | loop fusion | flops 3538944 | bytes 4128792 | tf_op jit(solution)/shard_map/concatenate | solution.py:424
  47.4 3.0 %collective-permute-done.12.refs_6_ = bf16[288,512]{1,0:T(8,128)(2,1)} collective-permute-done((bf16[288,512]{1,0:T(8,128)(2,1)}, bf16[288,512]{1,0:T(8,128)(2,1)}, u32[]{:S(2)}, u32[]{:S(2)}) %collective-permute-start.12) | collective-permute-done | bytes 294944 | tf_op jit(solution)/shard_map/ppermute | solution.py:374
  50.5 0.9 collective-permute-done.13.refs_7_
  51.4 2.9 %collective-permute-start.15 = (bf16[512,512]{1,0:T(8,128)(2,1)}, bf16[512,512]{1,0:T(8,128)(2,1)S(1)}, u32[]{:S(2)}, u32[]{:S(2)}) collective-permute-start(bf16[512,512]{1,0:T(8,128)(2,1)} %collective-permute-done.14.kv.refs_0_), channel_id=1, source_target_pairs={{0,2},{2,4},{4,6},{1,3},{3,5},{5,7},{8,10},{10,12},{12,14},{9,11},... | collective-permute-start | bytes 1572872 | tf_op jit(solution)/shard_map/ppermute | solution.py:365
  54.5 1.1 copy-done.4
  55.6 1.1 attend_forward.6
  56.7 3.1 %gradient_into_heads.1 = (bf16[2304,512]{1,0:T(8,128)(2,1)S(1)}, bf16[512,512]{1,0:T(8,128)(2,1)S(1)}) custom-call(s32[3]{0:T(128)S(1)} %pad_add_fusion.info, bf16[256,2304]{1,0:T(8,128)(2,1)S(1)} %bitcast.25, bf16[256,2304]{1,0:T(8,128)(2,1)S(1)} %copy.14.theirs, bf16[288,512]{1,0:T(8,128)(2,1)} %bitcast.8.refs_0_, bf16[288,512]{1,0:T(8,128)(2,1)} %bitcast.9.refs_1_, ...), custom_call_target="tpu_custom_call" | custom-call | flops 1 | bytes 1 | tf_op jit(solution)/shard_map/gradient_into_heads/pallas_call | solution.py:274
  59.9 4.5 %collective-permute-done.15.kv.refs_0_ = bf16[512,512]{1,0:T(8,128)(2,1)S(1)} collective-permute-done((bf16[512,512]{1,0:T(8,128)(2,1)}, bf16[512,512]{1,0:T(8,128)(2,1)S(1)}, u32[]{:S(2)}, u32[]{:S(2)}) %collective-permute-start.15) | collective-permute-done | bytes 524320 | tf_op jit(solution)/shard_map/ppermute | solution.py:365
  64.4 1.5 %attend_forward.7 = (bf16[512,512]{1,0:T(8,128)(2,1)S(1)}, f32[16,512]{1,0:T(8,128)S(1)}, bf16[576,512]{1,0:T(8,128)(2,1)S(1)}, bf16[576,512]{1,0:T(8,128)(2,1)S(1)}) custom-call(s32[3]{0:T(128)S(1)} %pad_add_fusion.info, bf16[512,512]{1,0:T(8,128)(2,1)S(1)} %maximum_multiply_fusion.q, bf16[512,512]{1,0:T(8,128)(2,1)S(1)} %collective-permute-done.15.kv.refs_0_, ...), custom_call_target="tpu_custom_call" | custom-call | flops 1 | bytes 1 | tf_op jit(solution)/shard_map/attend_forward/pallas_call | solution.py:114
  66.3 1.2 collective-permute-start.17
  67.6 0.9 attend_backward.4
  68.5 1.9 %collective-permute-start.18 = (bf16[512,512]{1,0:T(8,128)(2,1)S(1)}, bf16[512,512]{1,0:T(8,128)(2,1)S(1)}, u32[]{:S(2)}, u32[]{:S(2)}) collective-permute-start(bf16[512,512]{1,0:T(8,128)(2,1)S(1)} %get-tuple-element.120), channel_id=1, source_target_pairs={{2,0},{4,2},{6,4},{3,1},{5,3},{7,5},{10,8},{12,10},{14,12},{11,9},... | collective-permute-start | bytes 1572872 | tf_op jit(solution)/shard_map/ppermute | solution.py:368
  70.4 1.3 %attend_backward.5 = (bf16[512,512]{1,0:T(8,128)(2,1)S(1)}, f32[512,512]{1,0:T(8,128)S(1)}) custom-call(s32[3]{0:T(128)S(1)} %pad_add_fusion.info, bf16[512,512]{1,0:T(8,128)(2,1)S(1)} %maximum_multiply_fusion.q, bf16[512,512]{1,0:T(8,128)(2,1)S(1)} %get-tuple-element.117.da, f32[16,512]{1,0:T(8,128)S(1)} %get-tuple-element.118.lse_t, ...), custom_call_target="tpu_custom_call" | custom-call | flops 1 | bytes 1 | tf_op jit(solution)/shard_map/attend_backward/pallas_call | solution.py:215
  71.8 2.8 %attend_backward.6 = (bf16[512,512]{1,0:T(8,128)(2,1)S(1)}, f32[512,512]{1,0:T(8,128)S(1)}) custom-call(s32[3]{0:T(128)S(1)} %pad_add_fusion.info, bf16[512,512]{1,0:T(8,128)(2,1)S(1)} %maximum_multiply_fusion.q, bf16[512,512]{1,0:T(8,128)(2,1)S(1)} %get-tuple-element.117.da, f32[16,512]{1,0:T(8,128)S(1)} %get-tuple-element.118.lse_t, ...), custom_call_target="tpu_custom_call" | custom-call | flops 1 | bytes 1 | tf_op jit(solution)/shard_map/attend_backward/pallas_call | solution.py:215
  74.6 0.8 copy-done.7
  75.4 2.5 %attend_backward.7 = (f32[512,512]{1,0:T(8,128)S(1)}, bf16[512,512]{1,0:T(8,128)(2,1)S(1)}) custom-call(s32[3]{0:T(128)S(1)} %pad_add_fusion.info, bf16[512,512]{1,0:T(8,128)(2,1)S(1)} %maximum_multiply_fusion.q, bf16[512,512]{1,0:T(8,128)(2,1)S(1)} %get-tuple-element.117.da, f32[16,512]{1,0:T(8,128)S(1)} %get-tuple-element.118.lse_t, ...), custom_call_target="tpu_custom_call" | custom-call | flops 1 | bytes 1 | tf_op jit(solution)/shard_map/attend_backward/pallas_call | solution.py:215
  77.9 1.3 strip_product.1
  79.9 1.1 add_convert_fusion.3
  80.9 2.2 %collective-permute-start.22 = (bf16[512,512]{1,0:T(8,128)(2,1)}, bf16[512,512]{1,0:T(8,128)(2,1)}, u32[]{:S(2)}, u32[]{:S(2)}) collective-permute-start(bf16[512,512]{1,0:T(8,128)(2,1)} %add_convert_fusion.3), channel_id=1, source_target_pairs={{2,0},{4,2},{6,4},{3,1},{5,3},{7,5},{10,8},{12,10},{14,12},{11,9},... | collective-permute-start | bytes 1572872 | tf_op jit(solution)/shard_map/ppermute | solution.py:368
  83.1 0.9 add_convert_fusion.4
  84.1 1.1 collective-permute-start.19
  86.2 5.5 %collective-permute-start.21 = (bf16[256,512]{1,0:T(8,128)(2,1)}, bf16[256,512]{1,0:T(8,128)(2,1)}, u32[]{:S(2)}, u32[]{:S(2)}) collective-permute-start(bf16[256,512]{1,0:T(8,128)(2,1)} %get-tuple-element.169), channel_id=1, source_target_pairs={{0,1},{1,0},{2,3},{3,2},{4,5},{5,4},{6,7},{7,6},{8,9},{9,8},{10,11... | collective-permute-start | bytes 786440 | tf_op jit(solution)/shard_map/ppermute | solution.py:362
  91.6 1.7 %copy-done.2 = bf16[2304,512]{1,0:T(8,128)(2,1)S(1)} copy-done((bf16[2304,512]{1,0:T(8,128)(2,1)S(1)}, bf16[2304,512]{1,0:T(8,128)(2,1)}, u32[]{:S(2)}) %copy-start.2) | copy-done | bytes 2359320
  93.3 3.2 %layer_product.1 = (f32[256,2304]{1,0:T(8,128)S(1)}, bf16[256,2304]{1,0:T(8,128)(2,1)S(1)}) custom-call(bf16[512,512]{1,0:T(8,128)(2,1)S(1)} %get-tuple-element.134.refs_1_.w.x, bf16[2304,512]{1,0:T(8,128)(2,1)S(1)} %copy-done.2), custom_call_target="tpu_custom_call" | custom-call | flops 1 | bytes 1 | tf_op jit(solution)/shard_map/layer_product/pallas_call | solution.py:303
  96.5 1.9 %collective-permute-start.26 = (bf16[256,2304]{1,0:T(8,128)(2,1)S(1)}, bf16[256,2304]{1,0:T(8,128)(2,1)S(1)}, u32[]{:S(2)}, u32[]{:S(2)}) collective-permute-start(bf16[256,2304]{1,0:T(8,128)(2,1)S(1)} %get-tuple-element.142), channel_id=1, source_target_pairs={{0,1},{1,0},{2,3},{3,2},{4,5},{5,4},{6,7},{7,6},{8,9},{9,8},{10,11... | collective-permute-start | bytes 3538952 | tf_op jit(solution)/shard_map/ppermute | solution.py:362
  98.5 1.2 add_convert_fusion.2
  99.7 1.9 %collective-permute-start.27 = (bf16[512,512]{1,0:T(8,128)(2,1)S(1)}, bf16[512,512]{1,0:T(8,128)(2,1)S(1)}, u32[]{:S(2)}, u32[]{:S(2)}) collective-permute-start(bf16[512,512]{1,0:T(8,128)(2,1)S(1)} %add_convert_fusion.2), channel_id=1, source_target_pairs={{2,0},{4,2},{6,4},{3,1},{5,3},{7,5},{10,8},{12,10},{14,12},{11,9},... | collective-permute-start | bytes 1572872 | tf_op jit(solution)/shard_map/ppermute | solution.py:368
  101.6 1.0 convert_add_fusion.1
  102.6 1.0 convert_add_fusion
  104.0 1.5 %collective-permute-start.23 = (bf16[144,512]{1,0:T(8,128)(2,1)S(1)}, bf16[144,512]{1,0:T(8,128)(2,1)S(1)}, u32[]{:S(2)}, u32[]{:S(2)}) collective-permute-start(bf16[144,512]{1,0:T(8,128)(2,1)S(1)} %get-tuple-element.163), channel_id=1, source_target_pairs={{0,2},{2,4},{4,6},{6,0},{1,3},{3,5},{5,7},{7,1},{8,10},{10,12},{12... | collective-permute-start | bytes 442376 | tf_op jit(solution)/shard_map/ppermute | solution.py:371
  105.6 1.3 collective-permute-start.24
  106.8 1.4 %collective-permute-start.25 = (bf16[144,512]{1,0:T(8,128)(2,1)S(1)}, bf16[144,512]{1,0:T(8,128)(2,1)S(1)}, u32[]{:S(2)}, u32[]{:S(2)}) collective-permute-start(bf16[144,512]{1,0:T(8,128)(2,1)S(1)} %get-tuple-element.161), channel_id=1, source_target_pairs={{0,6},{2,0},{4,2},{6,4},{1,7},{3,1},{5,3},{7,5},{8,14},{10,8},{12,... | collective-permute-start | bytes 442376 | tf_op jit(solution)/shard_map/ppermute | solution.py:371
  108.2 2.0 %maximum_select_fusion.1 = bf16[256,1024]{1,0:T(8,128)(2,1)} fusion(bf16[256,512]{1,0:T(8,128)(2,1)} %collective-permute-done.21, bf16[256,512]{1,0:T(8,128)(2,1)S(1)} %get-tuple-element.168, pred[]{:T(512)S(6)} %eq.3), kind=kLoop, calls=%fused_computation.30 | loop fusion | flops 2359296 | bytes 1048577 | tf_op jit(solution)/shard_map/jit(_where)/select_n | solution.py:377
  110.2 1.2 add_convert_fusion
  111.4 11.1 %collective-permute-done.24 = bf16[144,512]{1,0:T(8,128)(2,1)S(1)} collective-permute-done((bf16[144,512]{1,0:T(8,128)(2,1)S(1)}, bf16[144,512]{1,0:T(8,128)(2,1)S(1)}, u32[]{:S(2)}, u32[]{:S(2)}) %collective-permute-start.24) | collective-permute-done | bytes 147488 | tf_op jit(solution)/shard_map/ppermute | solution.py:371
  122.5 5.2 %collective-permute-done.25 = bf16[144,512]{1,0:T(8,128)(2,1)S(1)} collective-permute-done((bf16[144,512]{1,0:T(8,128)(2,1)S(1)}, bf16[144,512]{1,0:T(8,128)(2,1)S(1)}, u32[]{:S(2)}, u32[]{:S(2)}) %collective-permute-start.25) | collective-permute-done | bytes 147488 | tf_op jit(solution)/shard_map/ppermute | solution.py:371
  127.8 0.9 collective-permute-start.29
  130.6 0.9 maximum_select_fusion.3
  (78 shorter events, 6.8 us)
Async XLA Ops:
  0.6 8.1 %copy-start = (bf16[1,256,2304]{2,1,0:T(8,128)(2,1)S(1)}, bf16[1,256,2304]{2,1,0:T(8,128)(2,1)}, u32[]{:S(2)}) copy-start(bf16[1,256,2304]{2,1,0:T(8,128)(2,1)} %param.9) | copy-start | bytes 3538948
  0.6 9.6 %collective-permute-start.3 = (bf16[72,1024]{1,0:T(8,128)(2,1)}, bf16[72,1024]{1,0:T(8,128)(2,1)S(1)}, u32[]{:S(2)}, u32[]{:S(2)}) collective-permute-start(bf16[72,1024]{1,0:T(8,128)(2,1)} %refs_0_.1), channel_id=1, source_target_pairs={{0,2},{2,4},{4,6},{6,0},{1,3},{3,5},{5,7},{7,1},{8,10},{10,12},{12... | collective-permute-start | bytes 442376 | tf_op jit(solution)/shard_map/ppermute | solution.py:371
  2.0 12.3 %collective-permute-start.4 = (bf16[72,1024]{1,0:T(8,128)(2,1)}, bf16[72,1024]{1,0:T(8,128)(2,1)S(1)}, u32[]{:S(2)}, u32[]{:S(2)}) collective-permute-start(bf16[72,1024]{1,0:T(8,128)(2,1)} %refs_0_.1), channel_id=1, source_target_pairs={{0,4},{2,6},{4,0},{6,2},{1,5},{3,7},{5,1},{7,3},{8,12},{10,14},{12... | collective-permute-start | bytes 442376 | tf_op jit(solution)/shard_map/ppermute | solution.py:371
  3.1 13.9 %collective-permute-start.5 = (bf16[72,1024]{1,0:T(8,128)(2,1)}, bf16[72,1024]{1,0:T(8,128)(2,1)S(1)}, u32[]{:S(2)}, u32[]{:S(2)}) collective-permute-start(bf16[72,1024]{1,0:T(8,128)(2,1)} %refs_0_.1), channel_id=1, source_target_pairs={{0,6},{2,0},{4,2},{6,4},{1,7},{3,1},{5,3},{7,5},{8,14},{10,8},{12,... | collective-permute-start | bytes 442376 | tf_op jit(solution)/shard_map/ppermute | solution.py:371
  7.1 9.9 %copy-start.9 = (bf16[72,1024]{1,0:T(8,128)(2,1)S(1)}, bf16[72,1024]{1,0:T(8,128)(2,1)}, u32[]{:S(2)}) copy-start(bf16[72,1024]{1,0:T(8,128)(2,1)} %refs_0_.1) | copy-start | bytes 442372
  7.1 11.2 %collective-permute-start = (bf16[256,512]{1,0:T(8,128)(2,1)S(1)}, bf16[256,512]{1,0:T(8,128)(2,1)}, u32[]{:S(2)}, u32[]{:S(2)}) collective-permute-start(bf16[256,512]{1,0:T(8,128)(2,1)S(1)} %pad_maximum_fusion.4), channel_id=1, source_target_pairs={{0,1},{1,0},{2,3},{3,2},{4,5},{5,4},{6,7},{7,6},{8,9},{9,8},{10,11... | collective-permute-start | bytes 786440 | tf_op jit(solution)/shard_map/ppermute | solution.py:362
  10.1 24.2 %collective-permute-start.9 = (bf16[256,2304]{0,1:T(8,128)(2,1)}, bf16[256,2304]{0,1:T(8,128)(2,1)}, u32[]{:S(2)}, u32[]{:S(2)}) collective-permute-start(bf16[256,2304]{0,1:T(8,128)(2,1)} %bitcast.27), channel_id=1, source_target_pairs={{0,1},{1,0},{2,3},{3,2},{4,5},{5,4},{6,7},{7,6},{8,9},{9,8},{10,11... | collective-permute-start | bytes 3538952 | tf_op jit(solution)/shard_map/ppermute | solution.py:362
  10.2 7.9 %copy-start.15 = (bf16[1,256,1024]{2,1,0:T(8,128)(2,1)S(1)}, bf16[1,256,1024]{2,1,0:T(8,128)(2,1)}, u32[]{:S(2)}) copy-start(bf16[1,256,1024]{2,1,0:T(8,128)(2,1)} %param.5) | copy-start | bytes 1572868
  10.2 8.1 %copy-start.16 = (bf16[256,256]{1,0:T(8,128)(2,1)S(1)}, bf16[256,256]{1,0:T(8,128)(2,1)}, u32[]{:S(2)}) copy-start(bf16[256,256]{1,0:T(8,128)(2,1)} %get-tuple-element.178) | copy-start | bytes 393220
  17.6 3.6 %collective-permute-start.6 = (bf16[4,72,512]{2,1,0:T(8,128)(2,1)S(1)}, bf16[4,72,512]{2,1,0:T(8,128)(2,1)S(1)}, u32[]{:S(2)}, u32[]{:S(2)}) collective-permute-start(bf16[4,72,512]{2,1,0:T(8,128)(2,1)S(1)} %get-tuple-element.83), channel_id=1, source_target_pairs={{0,1},{1,0},{2,3},{3,2},{4,5},{5,4},{6,7},{7,6},{8,9},{9,8},{10,11... | collective-permute-start | bytes 884744 | tf_op jit(solution)/shard_map/ppermute | solution.py:362
  18.2 7.1 %collective-permute-start.2 = (bf16[256,512]{1,0:T(8,128)(2,1)S(1)}, bf16[256,512]{1,0:T(8,128)(2,1)S(1)}, u32[]{:S(2)}, u32[]{:S(2)}) collective-permute-start(bf16[256,512]{1,0:T(8,128)(2,1)S(1)} %get-tuple-element.171), channel_id=1, source_target_pairs={{0,1},{1,0},{2,3},{3,2},{4,5},{5,4},{6,7},{7,6},{8,9},{9,8},{10,11... | collective-permute-start | bytes 786440 | tf_op jit(solution)/shard_map/ppermute | solution.py:362
  19.3 15.0 %collective-permute-start.1 = (bf16[512,512]{1,0:T(8,128)(2,1)S(1)}, bf16[512,512]{1,0:T(8,128)(2,1)}, u32[]{:S(2)}, u32[]{:S(2)}) collective-permute-start(bf16[512,512]{1,0:T(8,128)(2,1)S(1)} %pad_maximum_fusion.3.kv.refs_0_), channel_id=1, source_target_pairs={{0,2},{2,4},{4,6},{1,3},{3,5},{5,7},{8,10},{10,12},{12,14},{9,11},... | collective-permute-start | bytes 1572872 | tf_op jit(solution)/shard_map/ppermute | solution.py:365
  22.1 8.4 %collective-permute-start.7 = (bf16[288,512]{1,0:T(8,128)(2,1)}, bf16[288,512]{1,0:T(8,128)(2,1)}, u32[]{:S(2)}, u32[]{:S(2)}) collective-permute-start(bf16[288,512]{1,0:T(8,128)(2,1)} %bitcast.9.refs_1_), channel_id=1, source_target_pairs={{0,8},{8,0},{16,24},{24,16},{1,9},{9,1},{17,25},{25,17},{2,10},{10... | collective-permute-start | bytes 884744 | tf_op jit(solution)/shard_map/ppermute | solution.py:374
  24.1 8.1 %collective-permute-start.8 = (bf16[288,512]{1,0:T(8,128)(2,1)}, bf16[288,512]{1,0:T(8,128)(2,1)}, u32[]{:S(2)}, u32[]{:S(2)}) collective-permute-start(bf16[288,512]{1,0:T(8,128)(2,1)} %bitcast.8.refs_0_), channel_id=1, source_target_pairs={{0,16},{8,24},{16,0},{24,8},{1,17},{9,25},{17,1},{25,9},{2,18},{10... | collective-permute-start | bytes 884744 | tf_op jit(solution)/shard_map/ppermute | solution.py:374
  34.3 17.1 %collective-permute-start.14 = (bf16[512,512]{1,0:T(8,128)(2,1)}, bf16[512,512]{1,0:T(8,128)(2,1)}, u32[]{:S(2)}, u32[]{:S(2)}) collective-permute-start(bf16[512,512]{1,0:T(8,128)(2,1)} %collective-permute-done.1.kv.refs_0_), channel_id=1, source_target_pairs={{0,2},{2,4},{4,6},{1,3},{3,5},{5,7},{8,10},{10,12},{12,14},{9,11},... | collective-permute-start | bytes 1572872 | tf_op jit(solution)/shard_map/ppermute | solution.py:365
  36.5 10.9 %collective-permute-start.10 = (bf16[288,512]{1,0:T(8,128)(2,1)}, bf16[288,512]{1,0:T(8,128)(2,1)}, u32[]{:S(2)}, u32[]{:S(2)}) collective-permute-start(bf16[288,512]{1,0:T(8,128)(2,1)} %bitcast.8.refs_0_), channel_id=1, source_target_pairs={{0,8},{8,0},{16,24},{24,16},{1,9},{9,1},{17,25},{25,17},{2,10},{10... | collective-permute-start | bytes 884744 | tf_op jit(solution)/shard_map/ppermute | solution.py:374
  37.8 9.6 %collective-permute-start.11 = (bf16[288,512]{1,0:T(8,128)(2,1)}, bf16[288,512]{1,0:T(8,128)(2,1)}, u32[]{:S(2)}, u32[]{:S(2)}) collective-permute-start(bf16[288,512]{1,0:T(8,128)(2,1)} %bitcast.9.refs_1_), channel_id=1, source_target_pairs={{0,16},{8,24},{16,0},{24,8},{1,17},{9,25},{17,1},{25,9},{2,18},{10... | collective-permute-start | bytes 884744 | tf_op jit(solution)/shard_map/ppermute | solution.py:374
  39.1 11.4 %collective-permute-start.12 = (bf16[288,512]{1,0:T(8,128)(2,1)}, bf16[288,512]{1,0:T(8,128)(2,1)}, u32[]{:S(2)}, u32[]{:S(2)}) collective-permute-start(bf16[288,512]{1,0:T(8,128)(2,1)} %collective-permute-done.8.refs_4_), channel_id=1, source_target_pairs={{0,8},{8,0},{16,24},{24,16},{1,9},{9,1},{17,25},{25,17},{2,10},{10... | collective-permute-start | bytes 884744 | tf_op jit(solution)/shard_map/ppermute | solution.py:374
  39.3 12.1 %collective-permute-start.13 = (bf16[288,512]{1,0:T(8,128)(2,1)}, bf16[288,512]{1,0:T(8,128)(2,1)}, u32[]{:S(2)}, u32[]{:S(2)}) collective-permute-start(bf16[288,512]{1,0:T(8,128)(2,1)} %collective-permute-done.7.refs_3_), channel_id=1, source_target_pairs={{0,16},{8,24},{16,0},{24,8},{1,17},{9,25},{17,1},{25,9},{2,18},{10... | collective-permute-start | bytes 884744 | tf_op jit(solution)/shard_map/ppermute | solution.py:374
  42.0 1.0 copy-start.3
  44.6 1.5 %copy-start.10 = (bf16[1,256,2304]{1,2,0:T(8,128)(2,1)S(1)}, bf16[1,256,2304]{1,2,0:T(8,128)(2,1)}, u32[]{:S(2)}) copy-start(bf16[1,256,2304]{1,2,0:T(8,128)(2,1)} %copy.12) | copy-start | bytes 3538948
  51.4 13.0 %collective-permute-start.15 = (bf16[512,512]{1,0:T(8,128)(2,1)}, bf16[512,512]{1,0:T(8,128)(2,1)S(1)}, u32[]{:S(2)}, u32[]{:S(2)}) collective-permute-start(bf16[512,512]{1,0:T(8,128)(2,1)} %collective-permute-done.14.kv.refs_0_), channel_id=1, source_target_pairs={{0,2},{2,4},{4,6},{1,3},{3,5},{5,7},{8,10},{10,12},{12,14},{9,11},... | collective-permute-start | bytes 1572872 | tf_op jit(solution)/shard_map/ppermute | solution.py:365
  54.4 1.2 copy-start.4
  59.9 6.1 %copy-start.1 = (bf16[2304,512]{1,0:T(8,128)(2,1)}, bf16[2304,512]{1,0:T(8,128)(2,1)S(1)}, u32[]{:S(2)}) copy-start(bf16[2304,512]{1,0:T(8,128)(2,1)S(1)} %get-tuple-element.135.w) | copy-start | bytes 7077892
  66.0 13.9 %collective-permute-start.16 = (bf16[576,512]{1,0:T(8,128)(2,1)S(1)}, bf16[576,512]{1,0:T(8,128)(2,1)S(1)}, u32[]{:S(2)}, u32[]{:S(2)}) collective-permute-start(bf16[576,512]{1,0:T(8,128)(2,1)S(1)} %get-tuple-element.115), channel_id=1, source_target_pairs={{0,8},{8,0},{16,24},{24,16},{1,9},{9,1},{17,25},{25,17},{2,10},{10... | collective-permute-start | bytes 1769480 | tf_op jit(solution)/shard_map/ppermute | solution.py:374
  66.3 13.5 %collective-permute-start.17 = (bf16[576,512]{1,0:T(8,128)(2,1)S(1)}, bf16[576,512]{1,0:T(8,128)(2,1)S(1)}, u32[]{:S(2)}, u32[]{:S(2)}) collective-permute-start(bf16[576,512]{1,0:T(8,128)(2,1)S(1)} %get-tuple-element.116), channel_id=1, source_target_pairs={{0,16},{8,24},{16,0},{24,8},{1,17},{9,25},{17,1},{25,9},{2,18},{10... | collective-permute-start | bytes 1769480 | tf_op jit(solution)/shard_map/ppermute | solution.py:374
  68.5 11.4 %collective-permute-start.18 = (bf16[512,512]{1,0:T(8,128)(2,1)S(1)}, bf16[512,512]{1,0:T(8,128)(2,1)S(1)}, u32[]{:S(2)}, u32[]{:S(2)}) collective-permute-start(bf16[512,512]{1,0:T(8,128)(2,1)S(1)} %get-tuple-element.120), channel_id=1, source_target_pairs={{2,0},{4,2},{6,4},{3,1},{5,3},{7,5},{10,8},{12,10},{14,12},{11,9},... | collective-permute-start | bytes 1572872 | tf_op jit(solution)/shard_map/ppermute | solution.py:368
  74.5 0.8 copy-start.7
  77.9 1.3 %copy-start.5 = (f32[512,512]{1,0:T(8,128)}, f32[512,512]{1,0:T(8,128)S(1)}, u32[]{:S(2)}) copy-start(f32[512,512]{1,0:T(8,128)S(1)} %get-tuple-element.148) | copy-start | bytes 3145732
  79.9 4.2 %copy-start.11 = (bf16[576,512]{1,0:T(8,128)(2,1)}, bf16[576,512]{1,0:T(8,128)(2,1)S(1)}, u32[]{:S(2)}) copy-start(bf16[576,512]{1,0:T(8,128)(2,1)S(1)} %collective-permute-done.16) | copy-start | bytes 1769476
  79.9 4.2 %copy-start.13 = (bf16[576,512]{1,0:T(8,128)(2,1)}, bf16[576,512]{1,0:T(8,128)(2,1)S(1)}, u32[]{:S(2)}) copy-start(bf16[576,512]{1,0:T(8,128)(2,1)S(1)} %collective-permute-done.17) | copy-start | bytes 1769476
  80.9 15.6 %collective-permute-start.22 = (bf16[512,512]{1,0:T(8,128)(2,1)}, bf16[512,512]{1,0:T(8,128)(2,1)}, u32[]{:S(2)}, u32[]{:S(2)}) collective-permute-start(bf16[512,512]{1,0:T(8,128)(2,1)} %add_convert_fusion.3), channel_id=1, source_target_pairs={{2,0},{4,2},{6,4},{3,1},{5,3},{7,5},{10,8},{12,10},{14,12},{11,9},... | collective-permute-start | bytes 1572872 | tf_op jit(solution)/shard_map/ppermute | solution.py:368
  84.1 12.4 %collective-permute-start.19 = (bf16[288,512]{1,0:T(8,128)(2,1)}, bf16[288,512]{1,0:T(8,128)(2,1)}, u32[]{:S(2)}, u32[]{:S(2)}) collective-permute-start(bf16[288,512]{1,0:T(8,128)(2,1)} %get-tuple-element.154), channel_id=1, source_target_pairs={{0,8},{8,0},{16,24},{24,16},{1,9},{9,1},{17,25},{25,17},{2,10},{10... | collective-permute-start | bytes 884744 | tf_op jit(solution)/shard_map/ppermute | solution.py:374
  85.2 11.3 %collective-permute-start.20 = (bf16[288,512]{1,0:T(8,128)(2,1)S(1)}, bf16[288,512]{1,0:T(8,128)(2,1)}, u32[]{:S(2)}, u32[]{:S(2)}) collective-permute-start(bf16[288,512]{1,0:T(8,128)(2,1)S(1)} %get-tuple-element.153), channel_id=1, source_target_pairs={{0,16},{8,24},{16,0},{24,8},{1,17},{9,25},{17,1},{25,9},{2,18},{10... | collective-permute-start | bytes 884744 | tf_op jit(solution)/shard_map/ppermute | solution.py:374
  86.2 10.3 %collective-permute-start.21 = (bf16[256,512]{1,0:T(8,128)(2,1)}, bf16[256,512]{1,0:T(8,128)(2,1)}, u32[]{:S(2)}, u32[]{:S(2)}) collective-permute-start(bf16[256,512]{1,0:T(8,128)(2,1)} %get-tuple-element.169), channel_id=1, source_target_pairs={{0,1},{1,0},{2,3},{3,2},{4,5},{5,4},{6,7},{7,6},{8,9},{9,8},{10,11... | collective-permute-start | bytes 786440 | tf_op jit(solution)/shard_map/ppermute | solution.py:362
  91.6 1.7 %copy-start.2 = (bf16[2304,512]{1,0:T(8,128)(2,1)S(1)}, bf16[2304,512]{1,0:T(8,128)(2,1)}, u32[]{:S(2)}) copy-start(bf16[2304,512]{1,0:T(8,128)(2,1)} %copy-done.1) | copy-start | bytes 7077892
  93.3 5.2 %copy-start.8 = (bf16[512,512]{1,0:T(8,128)(2,1)S(1)}, bf16[512,512]{1,0:T(8,128)(2,1)}, u32[]{:S(2)}) copy-start(bf16[512,512]{1,0:T(8,128)(2,1)} %copy-done.7) | copy-start | bytes 1572868
  96.5 5.1 %copy-start.12 = (bf16[576,512]{1,0:T(8,128)(2,1)S(1)}, bf16[576,512]{1,0:T(8,128)(2,1)}, u32[]{:S(2)}) copy-start(bf16[576,512]{1,0:T(8,128)(2,1)} %copy-done.11) | copy-start | bytes 1769476
  96.5 6.1 %copy-start.14 = (bf16[576,512]{1,0:T(8,128)(2,1)S(1)}, bf16[576,512]{1,0:T(8,128)(2,1)}, u32[]{:S(2)}) copy-start(bf16[576,512]{1,0:T(8,128)(2,1)} %copy-done.13) | copy-start | bytes 1769476
  96.5 13.7 %collective-permute-start.26 = (bf16[256,2304]{1,0:T(8,128)(2,1)S(1)}, bf16[256,2304]{1,0:T(8,128)(2,1)S(1)}, u32[]{:S(2)}, u32[]{:S(2)}) collective-permute-start(bf16[256,2304]{1,0:T(8,128)(2,1)S(1)} %get-tuple-element.142), channel_id=1, source_target_pairs={{0,1},{1,0},{2,3},{3,2},{4,5},{5,4},{6,7},{7,6},{8,9},{9,8},{10,11... | collective-permute-start | bytes 3538952 | tf_op jit(solution)/shard_map/ppermute | solution.py:362
  99.7 28.1 %collective-permute-start.27 = (bf16[512,512]{1,0:T(8,128)(2,1)S(1)}, bf16[512,512]{1,0:T(8,128)(2,1)S(1)}, u32[]{:S(2)}, u32[]{:S(2)}) collective-permute-start(bf16[512,512]{1,0:T(8,128)(2,1)S(1)} %add_convert_fusion.2), channel_id=1, source_target_pairs={{2,0},{4,2},{6,4},{3,1},{5,3},{7,5},{10,8},{12,10},{14,12},{11,9},... | collective-permute-start | bytes 1572872 | tf_op jit(solution)/shard_map/ppermute | solution.py:368
  104.0 7.4 %collective-permute-start.23 = (bf16[144,512]{1,0:T(8,128)(2,1)S(1)}, bf16[144,512]{1,0:T(8,128)(2,1)S(1)}, u32[]{:S(2)}, u32[]{:S(2)}) collective-permute-start(bf16[144,512]{1,0:T(8,128)(2,1)S(1)} %get-tuple-element.163), channel_id=1, source_target_pairs={{0,2},{2,4},{4,6},{6,0},{1,3},{3,5},{5,7},{7,1},{8,10},{10,12},{12... | collective-permute-start | bytes 442376 | tf_op jit(solution)/shard_map/ppermute | solution.py:371
  105.6 17.0 %collective-permute-start.24 = (bf16[144,512]{1,0:T(8,128)(2,1)S(1)}, bf16[144,512]{1,0:T(8,128)(2,1)S(1)}, u32[]{:S(2)}, u32[]{:S(2)}) collective-permute-start(bf16[144,512]{1,0:T(8,128)(2,1)S(1)} %get-tuple-element.162), channel_id=1, source_target_pairs={{0,4},{2,6},{4,0},{6,2},{1,5},{3,7},{5,1},{7,3},{8,12},{10,14},{12... | collective-permute-start | bytes 442376 | tf_op jit(solution)/shard_map/ppermute | solution.py:371
  106.8 20.9 %collective-permute-start.25 = (bf16[144,512]{1,0:T(8,128)(2,1)S(1)}, bf16[144,512]{1,0:T(8,128)(2,1)S(1)}, u32[]{:S(2)}, u32[]{:S(2)}) collective-permute-start(bf16[144,512]{1,0:T(8,128)(2,1)S(1)} %get-tuple-element.161), channel_id=1, source_target_pairs={{0,6},{2,0},{4,2},{6,4},{1,7},{3,1},{5,3},{7,5},{8,14},{10,8},{12,... | collective-permute-start | bytes 442376 | tf_op jit(solution)/shard_map/ppermute | solution.py:371
  111.4 17.3 %copy-start.6 = (f32[512,512]{1,0:T(8,128)S(1)}, f32[512,512]{1,0:T(8,128)}, u32[]{:S(2)}) copy-start(f32[512,512]{1,0:T(8,128)} %copy-done.5) | copy-start | bytes 3145732
  127.8 1.9 %collective-permute-start.29 = (f32[72,512]{1,0:T(8,128)S(1)}, f32[72,512]{1,0:T(8,128)S(1)}, u32[]{:S(2)}, u32[]{:S(2)}) collective-permute-start(f32[72,512]{1,0:T(8,128)S(1)} %get-tuple-element.173), channel_id=1, source_target_pairs={{0,1},{1,0},{2,3},{3,2},{4,5},{5,4},{6,7},{7,6},{8,9},{9,8},{10,11... | collective-permute-start | bytes 442376 | tf_op jit(solution)/shard_map/ppermute | solution.py:362
  129.0 1.6 %collective-permute-start.28 = (bf16[256,512]{1,0:T(8,128)(2,1)S(1)}, bf16[256,512]{1,0:T(8,128)(2,1)S(1)}, u32[]{:S(2)}, u32[]{:S(2)}) collective-permute-start(bf16[256,512]{1,0:T(8,128)(2,1)S(1)} %slice.119), channel_id=1, source_target_pairs={{0,1},{1,0},{2,3},{3,2},{4,5},{5,4},{6,7},{7,6},{8,9},{9,8},{10,11... | collective-permute-start | bytes 786440 | tf_op jit(solution)/shard_map/ppermute | solution.py:362

commit v10 on v9

--- a/solution.py
+++ b/solution.py
@@ -285,6 +285,45 @@
     )(info, mine, theirs, *arrays)
 
 
+def plane_sum_kernel(info, rest, from_x, from_y, by_x1, by_y0, kept, farther, sent, total):
+    share, part = total.shape[0], kept.shape[0]
+    half = share // 2
+    total[:half, :] = (
+        rest[share : share + half, :] + from_x[half:, :].astype(F32) + by_y0[...].astype(F32)
+    )
+    total[half:, :] = (
+        rest[share + half :, :] + by_x1[...].astype(F32) + from_y[half:, :].astype(F32)
+    )
+
+    def block(k):
+        return total[pl.ds(pl.multiple_of((info[0] ^ k) * part, part), part), :]
+
+    kept[...] = block(0)
+    farther[...] = block(2)
+    sent[:part, :] = block(1).astype(BF16)
+    sent[part:, :] = block(3).astype(BF16)
+
+
+def plane_sum(info, rest, *arrived):
+    share = rest.shape[0] // 2
+    part, width = share // 4, rest.shape[1]
+    vmem = pl.BlockSpec(memory_space=pltpu.VMEM)
+    return pl.pallas_call(
+        plane_sum_kernel,
+        out_shape=(
+            jax.ShapeDtypeStruct((part, width), F32),
+            jax.ShapeDtypeStruct((part, width), F32),
+            jax.ShapeDtypeStruct((2 * part, width), BF16),
+        ),
+        in_specs=[pl.BlockSpec(memory_space=pltpu.SMEM)] + [vmem] * (1 + len(arrived)),
+        out_specs=(vmem, vmem, vmem),
+        scratch_shapes=[pltpu.VMEM((share, width), F32)],
+        cost_estimate=FILLER,
+        compiler_params=pltpu.CompilerParams(vmem_limit_bytes=16 * 1024 * 1024),
+        name="plane_sum",
+    )(info, rest, *arrived)
+
+
 def product_kernel(x, w, *outs):
     result = dot(x[...], w[...], NT if len(outs) == 2 else (((1,), (0,)), ((), ())))
     if len(outs) == 2:
@@ -472,27 +511,27 @@
     )
     passing = (terms[1].astype(F32) + got.astype(F32)).astype(BF16)
     coming = down(passing, 1)
-    mine = here + jnp.concatenate(
-        [
-            from_x[half:].astype(F32) + by_y0.astype(F32),
-            by_x1.astype(F32) + from_y[half:].astype(F32),
-        ],
-        0,
-    )
-
     layer_out = (part_mine + swap(part_sent).astype(F32)).astype(BF16)
     query_grad = in_order(dq[:tok], dq_theirs, 1)
-    if near:
-        final = lax.dynamic_slice_in_dim(mine, chip * part, part, 0)
-        got = []
-        for k in range(1, chips):
-            target = lax.rem(chip + k, chips)
-            sent = lax.dynamic_slice_in_dim(mine, target * part, part, 0).astype(BF16)
-            got.append(round_chips(sent, k))
-        *got, layer_out, query_grad, coming = together((*got, layer_out, query_grad, coming))
-        for x in got:
-            final = final + x.astype(F32)
-    else:
+    if chips == 4:
+
+        def pair(x, k):
+            return lax.ppermute(x, "chip", [(i, i ^ k) for i in range(chips)])
+
+        final, farther, sent = plane_sum(info, rest, from_x, from_y, by_x1, by_y0)
+        got = pair(sent, 1)
+        final = final + got[:part].astype(F32)
+        got = pair((farther + got[part:].astype(F32)).astype(BF16), 2)
+        got, layer_out, query_grad, coming = together((got, layer_out, query_grad, coming))
+        final = final + got.astype(F32)
+    else:
+        mine = here + jnp.concatenate(
+            [
+                from_x[half:].astype(F32) + by_y0.astype(F32),
+                by_x1.astype(F32) + from_y[half:].astype(F32),
+            ],
+            0,
+        )
         final = lax.psum_scatter(mine, "chip", scatter_dimension=0, tiled=True)
     total_tokens = rows_dp * chips * rows
     final = final * (1.0 / math.sqrt(total_tokens))

time: 132 us -> 125 us (0.947)
  other arithmetic: 17.3 us -> 9.82 us
  local copies, waits for them, and re-layouts: 10.2 us -> 6.72 us
  waiting for transfers between devices: 39.7 us -> 41.7 us
  starting transfers between devices: 40.1 us -> 41.6 us
    ppermute x0 -> x2, waiting for transfers between devices: none -> 16.7 us  [pair(): return lax.ppermute(x, 'chip', [(i, i ^ k) for i in range(chips)])]
    ppermute x6 -> x3, waiting for transfers between devices: 23 us -> 7.4 us  [round_chips(): return lax.ppermute(x, 'chip', [(i, (i + k) % chips) for i in range(chips)])]
    ppermute x6 -> x3, starting transfers between devices: 8 us -> 3.83 us  [round_chips(): return lax.ppermute(x, 'chip', [(i, (i + k) % chips) for i in range(chips)])]
    unnamed x35 -> x11, local copies, waits for them, and re-layouts: 6.27 us -> 3.55 us
    add x3 -> x0, other arithmetic: 2.35 us -> none  [the longest x1 1.04 us: on_device(): by_x1.astype(F32) + from_y[half:].astype(F32)]
    ppermute x8, starting transfers between devices: 10.7 us -> 13 us  [swap(): return lax.ppermute(x, 'core', [(0, 1), (1, 0)])]
    ppermute x0 -> x2, starting transfers between devices: none -> 1.8 us  [pair(): return lax.ppermute(x, 'chip', [(i, i ^ k) for i in range(chips)])]
    ppermute x3, starting transfers between devices: 6.03 us -> 7.48 us  [down(): return lax.ppermute(x, 'chip', [(i + k, i) for i in range(chips - k)])]
  transfers between devices with their start and end apart: 30 -> 29, of which waited for: 12 -> 13; matrix products, arithmetic and copies ran while one was open for 16% -> 11% of each run, Pallas kernels for 16% -> 18%
where the time goes in v10:
time: 125 us
  waiting for transfers between devices  41.7 us (33%)
  starting transfers between devices  41.6 us (33%)
  Pallas kernels  23.9 us (19%)
  other arithmetic  9.82 us (8%)
  local copies, waits for them, and re-layouts  6.72 us (5%)
    ppermute x2, waiting for transfers between devices, pair(): return lax.ppermute(x, 'chip', [(i, i ^ k) for i in range(chips)])  16.7 us
    ppermute x8, starting transfers between devices, swap(): return lax.ppermute(x, 'core', [(0, 1), (1, 0)])  13 us
    ppermute x10, waiting for transfers between devices, across(): return lax.ppermute(x, 'dp', [(i, i ^ k) for i in range(rows_dp)])  8.63 us
    ppermute x10, starting transfers between devices, across(): return lax.ppermute(x, 'dp', [(i, i ^ k) for i in range(rows_dp)])  8.48 us
    pallas_call x4, Pallas kernels, backward(): pl.pallas_call(functools.partial(backward_kernel, steps, rows, first, las...  7.61 us
    ppermute x3, starting transfers between devices, down(): return lax.ppermute(x, 'chip', [(i + k, i) for i in range(chips - k)])  7.48 us
    ppermute x3, waiting for transfers between devices, round_chips(): return lax.ppermute(x, 'chip', [(i, (i + k) % chips) for i in range(chips)])  7.4 us
    pallas_call x4, Pallas kernels, forward(): pl.pallas_call(functools.partial(forward_kernel, step, rows, first, last)...  7.25 us
  transfers between devices with their start and end apart: 29, of which 13 were waited for; matrix products, arithmetic and copies ran while one was open for 11% of the time, Pallas kernels for 18%

profile of v10, /device:TPU:9, one launch (start us, length us, event | category | flops | bytes accessed | tf_op | source)
XLA Modules:
  0.0 124.7 jit_solution(5656263921712329675)
XLA Ops:
  0.6 1.3 %collective-permute-start.3 = (bf16[72,1024]{1,0:T(8,128)(2,1)}, bf16[72,1024]{1,0:T(8,128)(2,1)S(1)}, u32[]{:S(2)}, u32[]{:S(2)}) collective-permute-start(bf16[72,1024]{1,0:T(8,128)(2,1)} %refs_0_.1), channel_id=1, source_target_pairs={{0,2},{2,4},{4,6},{6,0},{1,3},{3,5},{5,7},{7,1},{8,10},{10,12},{12... | collective-permute-start | bytes 442376 | tf_op jit(solution)/shard_map/ppermute | solution.py:410
  2.0 1.1 collective-permute-start.4
  3.1 1.4 %collective-permute-start.5 = (bf16[72,1024]{1,0:T(8,128)(2,1)}, bf16[72,1024]{1,0:T(8,128)(2,1)S(1)}, u32[]{:S(2)}, u32[]{:S(2)}) collective-permute-start(bf16[72,1024]{1,0:T(8,128)(2,1)} %refs_0_.1), channel_id=1, source_target_pairs={{0,6},{2,0},{4,2},{6,4},{1,7},{3,1},{5,3},{7,5},{8,14},{10,8},{12,... | collective-permute-start | bytes 442376 | tf_op jit(solution)/shard_map/ppermute | solution.py:410
  4.5 1.0 broadcast_select_fusion.5
  5.5 1.0 broadcast_select_fusion.4
  6.5 1.6 %collective-permute-start = (bf16[256,512]{1,0:T(8,128)(2,1)S(1)}, bf16[256,512]{1,0:T(8,128)(2,1)S(1)}, u32[]{:S(2)}, u32[]{:S(2)}) collective-permute-start(bf16[256,512]{1,0:T(8,128)(2,1)S(1)} %pad_maximum_fusion.4), channel_id=1, source_target_pairs={{0,1},{1,0},{2,3},{3,2},{4,5},{5,4},{6,7},{7,6},{8,9},{9,8},{10,11... | collective-permute-start | bytes 786440 | tf_op jit(solution)/shard_map/ppermute | solution.py:401
  8.1 1.4 %copy.12 = bf16[1,256,2304]{1,2,0:T(8,128)(2,1)} copy(bf16[1,256,2304]{2,1,0:T(8,128)(2,1)S(1)} %copy-done) | data formatting | bytes 2359296 | tf_op args[4]
  9.6 4.7 %collective-permute-done.4.refs_2_ = bf16[72,1024]{1,0:T(8,128)(2,1)S(1)} collective-permute-done((bf16[72,1024]{1,0:T(8,128)(2,1)}, bf16[72,1024]{1,0:T(8,128)(2,1)S(1)}, u32[]{:S(2)}, u32[]{:S(2)}) %collective-permute-start.4) | collective-permute-done | bytes 147488 | tf_op jit(solution)/shard_map/ppermute | solution.py:410
  14.3 2.7 %collective-permute-done.5.refs_3_ = bf16[72,1024]{1,0:T(8,128)(2,1)S(1)} collective-permute-done((bf16[72,1024]{1,0:T(8,128)(2,1)}, bf16[72,1024]{1,0:T(8,128)(2,1)S(1)}, u32[]{:S(2)}, u32[]{:S(2)}) %collective-permute-start.5) | collective-permute-done | bytes 147488 | tf_op jit(solution)/shard_map/ppermute | solution.py:410
  17.0 0.6 column_halves.1
  17.6 0.6 collective-permute-start.6
  18.3 1.9 %collective-permute-start.1 = (bf16[512,512]{1,0:T(8,128)(2,1)S(1)}, bf16[512,512]{1,0:T(8,128)(2,1)}, u32[]{:S(2)}, u32[]{:S(2)}) collective-permute-start(bf16[512,512]{1,0:T(8,128)(2,1)S(1)} %pad_maximum_fusion.3.kv.refs_0_), channel_id=1, source_target_pairs={{0,2},{2,4},{4,6},{1,3},{3,5},{5,7},{8,10},{10,12},{12,14},{9,11},... | collective-permute-start | bytes 1572872 | tf_op jit(solution)/shard_map/ppermute | solution.py:404
  20.4 0.7 copy.11
  21.2 1.2 collective-permute-start.7
  22.4 0.7 copy.10
  23.1 1.2 collective-permute-start.8
  24.5 2.1 %attend_forward.4 = (f32[16,512]{1,0:T(8,128)S(1)}, f32[16,512]{1,0:T(8,128)S(1)}, f32[512,512]{1,0:T(8,128)S(1)}) custom-call(s32[3]{0:T(128)S(1)} %pad_add_fusion.info, bf16[512,512]{1,0:T(8,128)(2,1)S(1)} %maximum_multiply_fusion.q, bf16[512,512]{1,0:T(8,128)(2,1)S(1)} %pad_maximum_fusion.3.kv.refs_0_), custom_call_target="tpu_custom_call" | custom-call | flops 1 | bytes 1 | tf_op jit(solution)/shard_map/attend_forward/pallas_call | solution.py:114
  26.6 3.0 %collective-permute-done.7.refs_3_ = bf16[288,512]{1,0:T(8,128)(2,1)} collective-permute-done((bf16[288,512]{1,0:T(8,128)(2,1)}, bf16[288,512]{1,0:T(8,128)(2,1)}, u32[]{:S(2)}, u32[]{:S(2)}) %collective-permute-start.7) | collective-permute-done | bytes 294944 | tf_op jit(solution)/shard_map/ppermute | solution.py:413
  29.6 1.6 %collective-permute-done.8.refs_4_ = bf16[288,512]{1,0:T(8,128)(2,1)} collective-permute-done((bf16[288,512]{1,0:T(8,128)(2,1)}, bf16[288,512]{1,0:T(8,128)(2,1)}, u32[]{:S(2)}, u32[]{:S(2)}) %collective-permute-start.8) | collective-permute-done | bytes 294944 | tf_op jit(solution)/shard_map/ppermute | solution.py:413
  31.2 2.1 %collective-permute-done.1.kv.refs_0_ = bf16[512,512]{1,0:T(8,128)(2,1)} collective-permute-done((bf16[512,512]{1,0:T(8,128)(2,1)S(1)}, bf16[512,512]{1,0:T(8,128)(2,1)}, u32[]{:S(2)}, u32[]{:S(2)}) %collective-permute-start.1) | collective-permute-done | bytes 524320 | tf_op jit(solution)/shard_map/ppermute | solution.py:404
  33.4 2.2 %collective-permute-start.14 = (bf16[512,512]{1,0:T(8,128)(2,1)}, bf16[512,512]{1,0:T(8,128)(2,1)}, u32[]{:S(2)}, u32[]{:S(2)}) collective-permute-start(bf16[512,512]{1,0:T(8,128)(2,1)} %collective-permute-done.1.kv.refs_0_), channel_id=1, source_target_pairs={{0,2},{2,4},{4,6},{1,3},{3,5},{5,7},{8,10},{10,12},{12,14},{9,11},... | collective-permute-start | bytes 1572872 | tf_op jit(solution)/shard_map/ppermute | solution.py:404
  35.6 1.3 %collective-permute-start.10 = (bf16[288,512]{1,0:T(8,128)(2,1)}, bf16[288,512]{1,0:T(8,128)(2,1)}, u32[]{:S(2)}, u32[]{:S(2)}) collective-permute-start(bf16[288,512]{1,0:T(8,128)(2,1)} %bitcast.8.refs_0_), channel_id=1, source_target_pairs={{0,8},{8,0},{16,24},{24,16},{1,9},{9,1},{17,25},{25,17},{2,10},{10... | collective-permute-start | bytes 884744 | tf_op jit(solution)/shard_map/ppermute | solution.py:413
  36.9 1.2 collective-permute-start.11
  38.1 0.3 collective-permute-start.12
  38.4 0.2 collective-permute-start.13
  38.6 2.5 %attend_forward.5 = (f32[16,512]{1,0:T(8,128)S(1)}, f32[16,512]{1,0:T(8,128)S(1)}, f32[512,512]{1,0:T(8,128)S(1)}) custom-call(s32[3]{0:T(128)S(1)} %pad_add_fusion.info, bf16[512,512]{1,0:T(8,128)(2,1)S(1)} %maximum_multiply_fusion.q, bf16[512,512]{1,0:T(8,128)(2,1)} %collective-permute-done.1.kv.refs_0_, f32[16,512]{1,0:T(8,128)S(1)} %get-tuple-element.92.refs_0_, ...), custom_call_target="tpu_custom_call" | custom-call | flops 1 | bytes 1 | tf_op jit(solution)/shard_map/attend_forward/pallas_call | solution.py:114
  41.1 1.0 copy-done.1
  42.1 1.6 %copy.14.theirs = bf16[256,2304]{1,0:T(8,128)(2,1)S(1)} copy(bf16[256,2304]{0,1:T(8,128)(2,1)} %collective-permute-done.9) | data formatting | bytes 2359296 | tf_op jit(solution)/shard_map/optimization_barrier | solution.py:444
  43.6 1.1 fusion
  44.7 1.6 %fusion.5 = (bf16[288,512]{1,0:T(8,128)(2,1)S(1)}, bf16[288,512]{1,0:T(8,128)(2,1)S(1)}, bf16[288,512]{1,0:T(8,128)(2,1)S(1)}, bf16[288,512]{1,0:T(8,128)(2,1)S(...) fusion(s32[]{:T(128)S(6)} %select_n.127, bf16[2304,256]{1,0:T(8,128)(2,1)} %bitcast.12, ...), kind=kLoop, calls=%fused_computation.32 | loop fusion | flops 3538944 | bytes 4128792 | tf_op jit(solution)/shard_map/concatenate | solution.py:463
  46.4 3.1 %collective-permute-done.12.refs_6_ = bf16[288,512]{1,0:T(8,128)(2,1)} collective-permute-done((bf16[288,512]{1,0:T(8,128)(2,1)}, bf16[288,512]{1,0:T(8,128)(2,1)}, u32[]{:S(2)}, u32[]{:S(2)}) %collective-permute-start.12) | collective-permute-done | bytes 294944 | tf_op jit(solution)/shard_map/ppermute | solution.py:413
  49.5 0.9 collective-permute-done.13.refs_7_
  50.4 2.8 %collective-permute-start.15 = (bf16[512,512]{1,0:T(8,128)(2,1)}, bf16[512,512]{1,0:T(8,128)(2,1)S(1)}, u32[]{:S(2)}, u32[]{:S(2)}) collective-permute-start(bf16[512,512]{1,0:T(8,128)(2,1)} %collective-permute-done.14.kv.refs_0_), channel_id=1, source_target_pairs={{0,2},{2,4},{4,6},{1,3},{3,5},{5,7},{8,10},{10,12},{12,14},{9,11},... | collective-permute-start | bytes 1572872 | tf_op jit(solution)/shard_map/ppermute | solution.py:404
  53.5 1.1 copy-done.2
  54.6 1.1 attend_forward.6
  55.8 3.1 %gradient_into_heads.1 = (bf16[2304,512]{1,0:T(8,128)(2,1)S(1)}, bf16[512,512]{1,0:T(8,128)(2,1)S(1)}) custom-call(s32[3]{0:T(128)S(1)} %pad_add_fusion.info, bf16[256,2304]{1,0:T(8,128)(2,1)S(1)} %bitcast.25, bf16[256,2304]{1,0:T(8,128)(2,1)S(1)} %copy.14.theirs, bf16[288,512]{1,0:T(8,128)(2,1)} %bitcast.8.refs_0_, bf16[288,512]{1,0:T(8,128)(2,1)} %bitcast.9.refs_1_, ...), custom_call_target="tpu_custom_call" | custom-call | flops 1 | bytes 1 | tf_op jit(solution)/shard_map/gradient_into_heads/pallas_call | solution.py:274
  58.9 4.6 %collective-permute-done.15.kv.refs_0_ = bf16[512,512]{1,0:T(8,128)(2,1)S(1)} collective-permute-done((bf16[512,512]{1,0:T(8,128)(2,1)}, bf16[512,512]{1,0:T(8,128)(2,1)S(1)}, u32[]{:S(2)}, u32[]{:S(2)}) %collective-permute-start.15) | collective-permute-done | bytes 524320 | tf_op jit(solution)/shard_map/ppermute | solution.py:404
  63.5 1.5 %attend_forward.7 = (bf16[512,512]{1,0:T(8,128)(2,1)S(1)}, f32[16,512]{1,0:T(8,128)S(1)}, bf16[576,512]{1,0:T(8,128)(2,1)S(1)}, bf16[576,512]{1,0:T(8,128)(2,1)S(1)}) custom-call(s32[3]{0:T(128)S(1)} %pad_add_fusion.info, bf16[512,512]{1,0:T(8,128)(2,1)S(1)} %maximum_multiply_fusion.q, bf16[512,512]{1,0:T(8,128)(2,1)S(1)} %collective-permute-done.15.kv.refs_0_, ...), custom_call_target="tpu_custom_call" | custom-call | flops 1 | bytes 1 | tf_op jit(solution)/shard_map/attend_forward/pallas_call | solution.py:114
  65.0 0.4 collective-permute-start.16
  65.4 1.2 collective-permute-start.17
  66.6 0.9 attend_backward.4
  67.5 1.9 %collective-permute-start.18 = (bf16[512,512]{1,0:T(8,128)(2,1)S(1)}, bf16[512,512]{1,0:T(8,128)(2,1)S(1)}, u32[]{:S(2)}, u32[]{:S(2)}) collective-permute-start(bf16[512,512]{1,0:T(8,128)(2,1)S(1)} %get-tuple-element.121), channel_id=1, source_target_pairs={{2,0},{4,2},{6,4},{3,1},{5,3},{7,5},{10,8},{12,10},{14,12},{11,9},... | collective-permute-start | bytes 1572872 | tf_op jit(solution)/shard_map/ppermute | solution.py:407
  69.4 1.3 %attend_backward.5 = (bf16[512,512]{1,0:T(8,128)(2,1)S(1)}, f32[512,512]{1,0:T(8,128)S(1)}) custom-call(s32[3]{0:T(128)S(1)} %pad_add_fusion.info, bf16[512,512]{1,0:T(8,128)(2,1)S(1)} %maximum_multiply_fusion.q, bf16[512,512]{1,0:T(8,128)(2,1)S(1)} %get-tuple-element.118.da, f32[16,512]{1,0:T(8,128)S(1)} %get-tuple-element.119.lse_t, ...), custom_call_target="tpu_custom_call" | custom-call | flops 1 | bytes 1 | tf_op jit(solution)/shard_map/attend_backward/pallas_call | solution.py:215
  70.8 2.8 %attend_backward.6 = (bf16[512,512]{1,0:T(8,128)(2,1)S(1)}, f32[512,512]{1,0:T(8,128)S(1)}) custom-call(s32[3]{0:T(128)S(1)} %pad_add_fusion.info, bf16[512,512]{1,0:T(8,128)(2,1)S(1)} %maximum_multiply_fusion.q, bf16[512,512]{1,0:T(8,128)(2,1)S(1)} %get-tuple-element.118.da, f32[16,512]{1,0:T(8,128)S(1)} %get-tuple-element.119.lse_t, ...), custom_call_target="tpu_custom_call" | custom-call | flops 1 | bytes 1 | tf_op jit(solution)/shard_map/attend_backward/pallas_call | solution.py:215
  73.6 2.5 %attend_backward.7 = (f32[512,512]{1,0:T(8,128)S(1)}, bf16[512,512]{1,0:T(8,128)(2,1)S(1)}) custom-call(s32[3]{0:T(128)S(1)} %pad_add_fusion.info, bf16[512,512]{1,0:T(8,128)(2,1)S(1)} %maximum_multiply_fusion.q, bf16[512,512]{1,0:T(8,128)(2,1)S(1)} %get-tuple-element.118.da, f32[16,512]{1,0:T(8,128)S(1)} %get-tuple-element.119.lse_t, ...), custom_call_target="tpu_custom_call" | custom-call | flops 1 | bytes 1 | tf_op jit(solution)/shard_map/attend_backward/pallas_call | solution.py:215
  76.2 1.3 %strip_product.1.rest = f32[1152,512]{1,0:T(8,128)S(1)} custom-call(bf16[1152,512]{1,0:T(8,128)(2,1)S(1)} %pad_maximum_fusion.x, bf16[512,512]{1,0:T(8,128)(2,1)S(1)} %get-tuple-element.135.refs_1_.w.x), custom_call_target="tpu_custom_call" | custom-call | flops 1 | bytes 1 | tf_op jit(solution)/shard_map/strip_product/pallas_call | solution.py:363
  77.5 1.4 %collective-permute-done.18 = bf16[512,512]{1,0:T(8,128)(2,1)S(1)} collective-permute-done((bf16[512,512]{1,0:T(8,128)(2,1)S(1)}, bf16[512,512]{1,0:T(8,128)(2,1)S(1)}, u32[]{:S(2)}, u32[]{:S(2)}) %collective-permute-start.18) | collective-permute-done | bytes 524320 | tf_op jit(solution)/shard_map/ppermute | solution.py:407
  79.0 2.2 %collective-permute-start.22 = (bf16[512,512]{1,0:T(8,128)(2,1)S(1)}, bf16[512,512]{1,0:T(8,128)(2,1)S(1)}, u32[]{:S(2)}, u32[]{:S(2)}) collective-permute-start(bf16[512,512]{1,0:T(8,128)(2,1)S(1)} %add_convert_fusion.3), channel_id=1, source_target_pairs={{2,0},{4,2},{6,4},{3,1},{5,3},{7,5},{10,8},{12,10},{14,12},{11,9},... | collective-permute-start | bytes 1572872 | tf_op jit(solution)/shard_map/ppermute | solution.py:407
  81.4 1.2 collective-permute-start.19
  82.6 0.2 collective-permute-start.20
  82.9 5.5 %collective-permute-start.21 = (bf16[256,512]{1,0:T(8,128)(2,1)S(1)}, bf16[256,512]{1,0:T(8,128)(2,1)S(1)}, u32[]{:S(2)}, u32[]{:S(2)}) collective-permute-start(bf16[256,512]{1,0:T(8,128)(2,1)S(1)} %get-tuple-element.168), channel_id=1, source_target_pairs={{0,1},{1,0},{2,3},{3,2},{4,5},{5,4},{6,7},{7,6},{8,9},{9,8},{10,11... | collective-permute-start | bytes 786440 | tf_op jit(solution)/shard_map/ppermute | solution.py:401
  88.4 3.2 %layer_product.1 = (f32[256,2304]{1,0:T(8,128)S(1)}, bf16[256,2304]{1,0:T(8,128)(2,1)S(1)}) custom-call(bf16[512,512]{1,0:T(8,128)(2,1)S(1)} %get-tuple-element.135.refs_1_.w.x, bf16[2304,512]{1,0:T(8,128)(2,1)S(1)} %get-tuple-element.136.w), custom_call_target="tpu_custom_call" | custom-call | flops 1 | bytes 1 | tf_op jit(solution)/shard_map/layer_product/pallas_call | solution.py:342
  91.6 4.3 %collective-permute-start.25 = (bf16[256,2304]{1,0:T(8,128)(2,1)S(1)}, bf16[256,2304]{1,0:T(8,128)(2,1)S(1)}, u32[]{:S(2)}, u32[]{:S(2)}) collective-permute-start(bf16[256,2304]{1,0:T(8,128)(2,1)S(1)} %get-tuple-element.145), channel_id=1, source_target_pairs={{0,1},{1,0},{2,3},{3,2},{4,5},{5,4},{6,7},{7,6},{8,9},{9,8},{10,11... | collective-permute-start | bytes 3538952 | tf_op jit(solution)/shard_map/ppermute | solution.py:401
  95.9 0.9 plane_sum.1
  97.0 3.4 %collective-permute-start.26 = (bf16[512,512]{1,0:T(8,128)(2,1)S(1)}, bf16[512,512]{1,0:T(8,128)(2,1)S(1)}, u32[]{:S(2)}, u32[]{:S(2)}) collective-permute-start(bf16[512,512]{1,0:T(8,128)(2,1)S(1)} %add_convert_fusion.2), channel_id=1, source_target_pairs={{2,0},{4,2},{6,4},{3,1},{5,3},{7,5},{10,8},{12,10},{14,12},{11,9},... | collective-permute-start | bytes 1572872 | tf_op jit(solution)/shard_map/ppermute | solution.py:407
  100.4 0.9 maximum_select_fusion.1
  101.3 4.2 %collective-permute-done.23 = bf16[288,512]{1,0:T(8,128)(2,1)S(1)} collective-permute-done((bf16[288,512]{1,0:T(8,128)(2,1)S(1)}, bf16[288,512]{1,0:T(8,128)(2,1)S(1)}, u32[]{:S(2)}, u32[]{:S(2)}) %collective-permute-start.23) | collective-permute-done | bytes 294944 | tf_op jit(solution)/shard_map/ppermute | solution.py:519
  105.5 1.7 %collective-permute-start.24 = (bf16[144,512]{1,0:T(8,128)(2,1)S(1)}, bf16[144,512]{1,0:T(8,128)(2,1)S(1)}, u32[]{:S(2)}, u32[]{:S(2)}) collective-permute-start(bf16[144,512]{1,0:T(8,128)(2,1)S(1)} %add_convert_fusion.6), channel_id=1, source_target_pairs={{0,4},{2,6},{4,0},{6,2},{1,5},{3,7},{5,1},{7,3},{8,12},{10,14},{12... | collective-permute-start | bytes 442376 | tf_op jit(solution)/shard_map/ppermute | solution.py:519
  107.3 1.2 add_convert_fusion
  108.5 12.6 %collective-permute-done.24 = bf16[144,512]{1,0:T(8,128)(2,1)S(1)} collective-permute-done((bf16[144,512]{1,0:T(8,128)(2,1)S(1)}, bf16[144,512]{1,0:T(8,128)(2,1)S(1)}, u32[]{:S(2)}, u32[]{:S(2)}) %collective-permute-start.24) | collective-permute-done | bytes 147488 | tf_op jit(solution)/shard_map/ppermute | solution.py:519
  121.2 0.8 collective-permute-start.28
  122.3 0.7 collective-permute-done.28
  123.0 0.7 maximum_select_fusion.2
  123.8 0.9 maximum_select_fusion.3
  (50 shorter events, 1.8 us)
Async XLA Ops:
  0.6 7.4 %copy-start = (bf16[1,256,2304]{2,1,0:T(8,128)(2,1)S(1)}, bf16[1,256,2304]{2,1,0:T(8,128)(2,1)}, u32[]{:S(2)}) copy-start(bf16[1,256,2304]{2,1,0:T(8,128)(2,1)} %param.9) | copy-start | bytes 3538948
  0.6 9.0 %collective-permute-start.3 = (bf16[72,1024]{1,0:T(8,128)(2,1)}, bf16[72,1024]{1,0:T(8,128)(2,1)S(1)}, u32[]{:S(2)}, u32[]{:S(2)}) collective-permute-start(bf16[72,1024]{1,0:T(8,128)(2,1)} %refs_0_.1), channel_id=1, source_target_pairs={{0,2},{2,4},{4,6},{6,0},{1,3},{3,5},{5,7},{7,1},{8,10},{10,12},{12... | collective-permute-start | bytes 442376 | tf_op jit(solution)/shard_map/ppermute | solution.py:410
  2.0 12.3 %collective-permute-start.4 = (bf16[72,1024]{1,0:T(8,128)(2,1)}, bf16[72,1024]{1,0:T(8,128)(2,1)S(1)}, u32[]{:S(2)}, u32[]{:S(2)}) collective-permute-start(bf16[72,1024]{1,0:T(8,128)(2,1)} %refs_0_.1), channel_id=1, source_target_pairs={{0,4},{2,6},{4,0},{6,2},{1,5},{3,7},{5,1},{7,3},{8,12},{10,14},{12... | collective-permute-start | bytes 442376 | tf_op jit(solution)/shard_map/ppermute | solution.py:410
  3.1 13.9 %collective-permute-start.5 = (bf16[72,1024]{1,0:T(8,128)(2,1)}, bf16[72,1024]{1,0:T(8,128)(2,1)S(1)}, u32[]{:S(2)}, u32[]{:S(2)}) collective-permute-start(bf16[72,1024]{1,0:T(8,128)(2,1)} %refs_0_.1), channel_id=1, source_target_pairs={{0,6},{2,0},{4,2},{6,4},{1,7},{3,1},{5,3},{7,5},{8,14},{10,8},{12,... | collective-permute-start | bytes 442376 | tf_op jit(solution)/shard_map/ppermute | solution.py:410
  6.5 10.5 %copy-start.3 = (bf16[72,1024]{1,0:T(8,128)(2,1)S(1)}, bf16[72,1024]{1,0:T(8,128)(2,1)}, u32[]{:S(2)}) copy-start(bf16[72,1024]{1,0:T(8,128)(2,1)} %refs_0_.1) | copy-start | bytes 442372
  6.5 11.8 %collective-permute-start = (bf16[256,512]{1,0:T(8,128)(2,1)S(1)}, bf16[256,512]{1,0:T(8,128)(2,1)S(1)}, u32[]{:S(2)}, u32[]{:S(2)}) collective-permute-start(bf16[256,512]{1,0:T(8,128)(2,1)S(1)} %pad_maximum_fusion.4), channel_id=1, source_target_pairs={{0,1},{1,0},{2,3},{3,2},{4,5},{5,4},{6,7},{7,6},{8,9},{9,8},{10,11... | collective-permute-start | bytes 786440 | tf_op jit(solution)/shard_map/ppermute | solution.py:401
  9.5 23.9 %collective-permute-start.9 = (bf16[256,2304]{0,1:T(8,128)(2,1)}, bf16[256,2304]{0,1:T(8,128)(2,1)}, u32[]{:S(2)}, u32[]{:S(2)}) collective-permute-start(bf16[256,2304]{0,1:T(8,128)(2,1)} %bitcast.10), channel_id=1, source_target_pairs={{0,1},{1,0},{2,3},{3,2},{4,5},{5,4},{6,7},{7,6},{8,9},{9,8},{10,11... | collective-permute-start | bytes 3538952 | tf_op jit(solution)/shard_map/ppermute | solution.py:401
  9.6 8.6 %copy-start.4 = (bf16[1,256,1024]{2,1,0:T(8,128)(2,1)S(1)}, bf16[1,256,1024]{2,1,0:T(8,128)(2,1)}, u32[]{:S(2)}) copy-start(bf16[1,256,1024]{2,1,0:T(8,128)(2,1)} %param.5) | copy-start | bytes 1572868
  17.6 2.7 %collective-permute-start.6 = (bf16[4,72,512]{2,1,0:T(8,128)(2,1)S(1)}, bf16[4,72,512]{2,1,0:T(8,128)(2,1)S(1)}, u32[]{:S(2)}, u32[]{:S(2)}) collective-permute-start(bf16[4,72,512]{2,1,0:T(8,128)(2,1)S(1)} %get-tuple-element.84), channel_id=1, source_target_pairs={{0,1},{1,0},{2,3},{3,2},{4,5},{5,4},{6,7},{7,6},{8,9},{9,8},{10,11... | collective-permute-start | bytes 884744 | tf_op jit(solution)/shard_map/ppermute | solution.py:401
  18.2 6.2 %collective-permute-start.2 = (bf16[256,512]{1,0:T(8,128)(2,1)S(1)}, bf16[256,512]{1,0:T(8,128)(2,1)S(1)}, u32[]{:S(2)}, u32[]{:S(2)}) collective-permute-start(bf16[256,512]{1,0:T(8,128)(2,1)S(1)} %get-tuple-element.170), channel_id=1, source_target_pairs={{0,1},{1,0},{2,3},{3,2},{4,5},{5,4},{6,7},{7,6},{8,9},{9,8},{10,11... | collective-permute-start | bytes 786440 | tf_op jit(solution)/shard_map/ppermute | solution.py:401
  18.3 15.0 %collective-permute-start.1 = (bf16[512,512]{1,0:T(8,128)(2,1)S(1)}, bf16[512,512]{1,0:T(8,128)(2,1)}, u32[]{:S(2)}, u32[]{:S(2)}) collective-permute-start(bf16[512,512]{1,0:T(8,128)(2,1)S(1)} %pad_maximum_fusion.3.kv.refs_0_), channel_id=1, source_target_pairs={{0,2},{2,4},{4,6},{1,3},{3,5},{5,7},{8,10},{10,12},{12,14},{9,11},... | collective-permute-start | bytes 1572872 | tf_op jit(solution)/shard_map/ppermute | solution.py:404
  21.2 8.4 %collective-permute-start.7 = (bf16[288,512]{1,0:T(8,128)(2,1)}, bf16[288,512]{1,0:T(8,128)(2,1)}, u32[]{:S(2)}, u32[]{:S(2)}) collective-permute-start(bf16[288,512]{1,0:T(8,128)(2,1)} %bitcast.9.refs_1_), channel_id=1, source_target_pairs={{0,8},{8,0},{16,24},{24,16},{1,9},{9,1},{17,25},{25,17},{2,10},{10... | collective-permute-start | bytes 884744 | tf_op jit(solution)/shard_map/ppermute | solution.py:413
  23.1 8.1 %collective-permute-start.8 = (bf16[288,512]{1,0:T(8,128)(2,1)}, bf16[288,512]{1,0:T(8,128)(2,1)}, u32[]{:S(2)}, u32[]{:S(2)}) collective-permute-start(bf16[288,512]{1,0:T(8,128)(2,1)} %bitcast.8.refs_0_), channel_id=1, source_target_pairs={{0,16},{8,24},{16,0},{24,8},{1,17},{9,25},{17,1},{25,9},{2,18},{10... | collective-permute-start | bytes 884744 | tf_op jit(solution)/shard_map/ppermute | solution.py:413
  33.4 17.1 %collective-permute-start.14 = (bf16[512,512]{1,0:T(8,128)(2,1)}, bf16[512,512]{1,0:T(8,128)(2,1)}, u32[]{:S(2)}, u32[]{:S(2)}) collective-permute-start(bf16[512,512]{1,0:T(8,128)(2,1)} %collective-permute-done.1.kv.refs_0_), channel_id=1, source_target_pairs={{0,2},{2,4},{4,6},{1,3},{3,5},{5,7},{8,10},{10,12},{12,14},{9,11},... | collective-permute-start | bytes 1572872 | tf_op jit(solution)/shard_map/ppermute | solution.py:404
  35.6 10.8 %collective-permute-start.10 = (bf16[288,512]{1,0:T(8,128)(2,1)}, bf16[288,512]{1,0:T(8,128)(2,1)}, u32[]{:S(2)}, u32[]{:S(2)}) collective-permute-start(bf16[288,512]{1,0:T(8,128)(2,1)} %bitcast.8.refs_0_), channel_id=1, source_target_pairs={{0,8},{8,0},{16,24},{24,16},{1,9},{9,1},{17,25},{25,17},{2,10},{10... | collective-permute-start | bytes 884744 | tf_op jit(solution)/shard_map/ppermute | solution.py:413
  36.9 9.5 %collective-permute-start.11 = (bf16[288,512]{1,0:T(8,128)(2,1)}, bf16[288,512]{1,0:T(8,128)(2,1)}, u32[]{:S(2)}, u32[]{:S(2)}) collective-permute-start(bf16[288,512]{1,0:T(8,128)(2,1)} %bitcast.9.refs_1_), channel_id=1, source_target_pairs={{0,16},{8,24},{16,0},{24,8},{1,17},{9,25},{17,1},{25,9},{2,18},{10... | collective-permute-start | bytes 884744 | tf_op jit(solution)/shard_map/ppermute | solution.py:413
  38.1 11.4 %collective-permute-start.12 = (bf16[288,512]{1,0:T(8,128)(2,1)}, bf16[288,512]{1,0:T(8,128)(2,1)}, u32[]{:S(2)}, u32[]{:S(2)}) collective-permute-start(bf16[288,512]{1,0:T(8,128)(2,1)} %collective-permute-done.8.refs_4_), channel_id=1, source_target_pairs={{0,8},{8,0},{16,24},{24,16},{1,9},{9,1},{17,25},{25,17},{2,10},{10... | collective-permute-start | bytes 884744 | tf_op jit(solution)/shard_map/ppermute | solution.py:413
  38.4 12.1 %collective-permute-start.13 = (bf16[288,512]{1,0:T(8,128)(2,1)}, bf16[288,512]{1,0:T(8,128)(2,1)}, u32[]{:S(2)}, u32[]{:S(2)}) collective-permute-start(bf16[288,512]{1,0:T(8,128)(2,1)} %collective-permute-done.7.refs_3_), channel_id=1, source_target_pairs={{0,16},{8,24},{16,0},{24,8},{1,17},{9,25},{17,1},{25,9},{2,18},{10... | collective-permute-start | bytes 884744 | tf_op jit(solution)/shard_map/ppermute | solution.py:413
  41.1 1.0 copy-start.1
  50.4 13.0 %collective-permute-start.15 = (bf16[512,512]{1,0:T(8,128)(2,1)}, bf16[512,512]{1,0:T(8,128)(2,1)S(1)}, u32[]{:S(2)}, u32[]{:S(2)}) collective-permute-start(bf16[512,512]{1,0:T(8,128)(2,1)} %collective-permute-done.14.kv.refs_0_), channel_id=1, source_target_pairs={{0,2},{2,4},{4,6},{1,3},{3,5},{5,7},{8,10},{10,12},{12,14},{9,11},... | collective-permute-start | bytes 1572872 | tf_op jit(solution)/shard_map/ppermute | solution.py:404
  53.4 1.2 copy-start.2
  65.0 13.9 %collective-permute-start.16 = (bf16[576,512]{1,0:T(8,128)(2,1)S(1)}, bf16[576,512]{1,0:T(8,128)(2,1)S(1)}, u32[]{:S(2)}, u32[]{:S(2)}) collective-permute-start(bf16[576,512]{1,0:T(8,128)(2,1)S(1)} %get-tuple-element.116), channel_id=1, source_target_pairs={{0,8},{8,0},{16,24},{24,16},{1,9},{9,1},{17,25},{25,17},{2,10},{10... | collective-permute-start | bytes 1769480 | tf_op jit(solution)/shard_map/ppermute | solution.py:413
  65.4 13.5 %collective-permute-start.17 = (bf16[576,512]{1,0:T(8,128)(2,1)S(1)}, bf16[576,512]{1,0:T(8,128)(2,1)S(1)}, u32[]{:S(2)}, u32[]{:S(2)}) collective-permute-start(bf16[576,512]{1,0:T(8,128)(2,1)S(1)} %get-tuple-element.117), channel_id=1, source_target_pairs={{0,16},{8,24},{16,0},{24,8},{1,17},{9,25},{17,1},{25,9},{2,18},{10... | collective-permute-start | bytes 1769480 | tf_op jit(solution)/shard_map/ppermute | solution.py:413
  67.5 11.4 %collective-permute-start.18 = (bf16[512,512]{1,0:T(8,128)(2,1)S(1)}, bf16[512,512]{1,0:T(8,128)(2,1)S(1)}, u32[]{:S(2)}, u32[]{:S(2)}) collective-permute-start(bf16[512,512]{1,0:T(8,128)(2,1)S(1)} %get-tuple-element.121), channel_id=1, source_target_pairs={{2,0},{4,2},{6,4},{3,1},{5,3},{7,5},{10,8},{12,10},{14,12},{11,9},... | collective-permute-start | bytes 1572872 | tf_op jit(solution)/shard_map/ppermute | solution.py:407
  79.0 12.6 %collective-permute-start.22 = (bf16[512,512]{1,0:T(8,128)(2,1)S(1)}, bf16[512,512]{1,0:T(8,128)(2,1)S(1)}, u32[]{:S(2)}, u32[]{:S(2)}) collective-permute-start(bf16[512,512]{1,0:T(8,128)(2,1)S(1)} %add_convert_fusion.3), channel_id=1, source_target_pairs={{2,0},{4,2},{6,4},{3,1},{5,3},{7,5},{10,8},{12,10},{14,12},{11,9},... | collective-permute-start | bytes 1572872 | tf_op jit(solution)/shard_map/ppermute | solution.py:407
  81.4 10.2 %collective-permute-start.19 = (bf16[288,512]{1,0:T(8,128)(2,1)S(1)}, bf16[288,512]{1,0:T(8,128)(2,1)S(1)}, u32[]{:S(2)}, u32[]{:S(2)}) collective-permute-start(bf16[288,512]{1,0:T(8,128)(2,1)S(1)} %get-tuple-element.156), channel_id=1, source_target_pairs={{0,8},{8,0},{16,24},{24,16},{1,9},{9,1},{17,25},{25,17},{2,10},{10... | collective-permute-start | bytes 884744 | tf_op jit(solution)/shard_map/ppermute | solution.py:413
  82.6 9.0 %collective-permute-start.20 = (bf16[288,512]{1,0:T(8,128)(2,1)S(1)}, bf16[288,512]{1,0:T(8,128)(2,1)S(1)}, u32[]{:S(2)}, u32[]{:S(2)}) collective-permute-start(bf16[288,512]{1,0:T(8,128)(2,1)S(1)} %get-tuple-element.155), channel_id=1, source_target_pairs={{0,16},{8,24},{16,0},{24,8},{1,17},{9,25},{17,1},{25,9},{2,18},{10... | collective-permute-start | bytes 884744 | tf_op jit(solution)/shard_map/ppermute | solution.py:413
  82.9 8.7 %collective-permute-start.21 = (bf16[256,512]{1,0:T(8,128)(2,1)S(1)}, bf16[256,512]{1,0:T(8,128)(2,1)S(1)}, u32[]{:S(2)}, u32[]{:S(2)}) collective-permute-start(bf16[256,512]{1,0:T(8,128)(2,1)S(1)} %get-tuple-element.168), channel_id=1, source_target_pairs={{0,1},{1,0},{2,3},{3,2},{4,5},{5,4},{6,7},{7,6},{8,9},{9,8},{10,11... | collective-permute-start | bytes 786440 | tf_op jit(solution)/shard_map/ppermute | solution.py:401
  91.6 15.6 %collective-permute-start.25 = (bf16[256,2304]{1,0:T(8,128)(2,1)S(1)}, bf16[256,2304]{1,0:T(8,128)(2,1)S(1)}, u32[]{:S(2)}, u32[]{:S(2)}) collective-permute-start(bf16[256,2304]{1,0:T(8,128)(2,1)S(1)} %get-tuple-element.145), channel_id=1, source_target_pairs={{0,1},{1,0},{2,3},{3,2},{4,5},{5,4},{6,7},{7,6},{8,9},{9,8},{10,11... | collective-permute-start | bytes 3538952 | tf_op jit(solution)/shard_map/ppermute | solution.py:401
  96.8 8.7 %collective-permute-start.23 = (bf16[288,512]{1,0:T(8,128)(2,1)S(1)}, bf16[288,512]{1,0:T(8,128)(2,1)S(1)}, u32[]{:S(2)}, u32[]{:S(2)}) collective-permute-start(bf16[288,512]{1,0:T(8,128)(2,1)S(1)} %get-tuple-element.143), channel_id=1, source_target_pairs={{0,2},{2,0},{4,6},{6,4},{1,3},{3,1},{5,7},{7,5},{8,10},{10,8},{12,... | collective-permute-start | bytes 884744 | tf_op jit(solution)/shard_map/ppermute | solution.py:519
  97.0 24.0 %collective-permute-start.26 = (bf16[512,512]{1,0:T(8,128)(2,1)S(1)}, bf16[512,512]{1,0:T(8,128)(2,1)S(1)}, u32[]{:S(2)}, u32[]{:S(2)}) collective-permute-start(bf16[512,512]{1,0:T(8,128)(2,1)S(1)} %add_convert_fusion.2), channel_id=1, source_target_pairs={{2,0},{4,2},{6,4},{3,1},{5,3},{7,5},{10,8},{12,10},{14,12},{11,9},... | collective-permute-start | bytes 1572872 | tf_op jit(solution)/shard_map/ppermute | solution.py:407
  105.5 15.5 %collective-permute-start.24 = (bf16[144,512]{1,0:T(8,128)(2,1)S(1)}, bf16[144,512]{1,0:T(8,128)(2,1)S(1)}, u32[]{:S(2)}, u32[]{:S(2)}) collective-permute-start(bf16[144,512]{1,0:T(8,128)(2,1)S(1)} %add_convert_fusion.6), channel_id=1, source_target_pairs={{0,4},{2,6},{4,0},{6,2},{1,5},{3,7},{5,1},{7,3},{8,12},{10,14},{12... | collective-permute-start | bytes 442376 | tf_op jit(solution)/shard_map/ppermute | solution.py:519
  121.2 1.9 %collective-permute-start.28 = (f32[72,512]{1,0:T(8,128)S(1)}, f32[72,512]{1,0:T(8,128)S(1)}, u32[]{:S(2)}, u32[]{:S(2)}) collective-permute-start(f32[72,512]{1,0:T(8,128)S(1)} %get-tuple-element.172), channel_id=1, source_target_pairs={{0,1},{1,0},{2,3},{3,2},{4,5},{5,4},{6,7},{7,6},{8,9},{9,8},{10,11... | collective-permute-start | bytes 442376 | tf_op jit(solution)/shard_map/ppermute | solution.py:401
  122.2 1.6 %collective-permute-start.27 = (bf16[256,512]{1,0:T(8,128)(2,1)S(1)}, bf16[256,512]{1,0:T(8,128)(2,1)S(1)}, u32[]{:S(2)}, u32[]{:S(2)}) collective-permute-start(bf16[256,512]{1,0:T(8,128)(2,1)S(1)} %slice.116), channel_id=1, source_target_pairs={{0,1},{1,0},{2,3},{3,2},{4,5},{5,4},{6,7},{7,6},{8,9},{9,8},{10,11... | collective-permute-start | bytes 786440 | tf_op jit(solution)/shard_map/ppermute | solution.py:401

commit v11 on v10

--- a/solution.py
+++ b/solution.py
@@ -251,38 +251,59 @@
     )(info, *pieces)
 
 
-def into_heads_kernel(places, info, mine, theirs, *refs):
-    *pieces, weight, out = refs
+def into_heads_kernel(places, based, info, turned, *refs):
+    *pieces, out = refs
+    total = None
+    if based:
+        base, *pieces = pieces
+        total = base[...]
     half = pieces[0].shape[0]
     for (k, at), ref in zip(places, pieces):
-        start = ((info[2] ^ k) * 2 + at) * half
-        weight[pl.ds(pl.multiple_of(start, half), half), :] = ref[...]
-    depth = weight.shape[0]
-    wide = 256
-    tok = mine.shape[0]
-    for at, grad in ((0, mine), (tok, theirs)):
-        total = dot(grad[:, :wide], weight[:wide, :])
-        for i in range(wide, depth, wide):
-            total = total + dot(grad[:, i : i + wide], weight[i : i + wide, :])
-        out[at : at + tok, :] = total.astype(BF16)
-
-
-def gradient_into_heads(info, mine, theirs, pieces):
+        start = pl.multiple_of(((info[2] ^ k) * 2 + at) * half, half)
+        term = dot(turned[pl.ds(start, half), :], ref[...], TN)
+        total = term if total is None else total + term
+    out[...] = total.astype(out.dtype)
+
+
+def gradient_into_heads(info, turned, pieces, base=None):
+    arrays = [x for x, _, _ in pieces]
+    based = base is not None
+    args = ([base] if based else []) + arrays
+    vmem = pl.BlockSpec(memory_space=pltpu.VMEM)
+    return pl.pallas_call(
+        functools.partial(into_heads_kernel, [(k, at) for _, k, at in pieces], based),
+        out_shape=jax.ShapeDtypeStruct(
+            (turned.shape[1], arrays[0].shape[1]), BF16 if based else F32
+        ),
+        in_specs=[pl.BlockSpec(memory_space=pltpu.SMEM)] + [vmem] * (1 + len(args)),
+        out_specs=vmem,
+        cost_estimate=FILLER,
+        compiler_params=pltpu.CompilerParams(vmem_limit_bytes=20 * 1024 * 1024),
+        name="gradient_into_heads",
+    )(info, turned, *args)
+
+
+def place_kernel(places, info, *refs):
+    *pieces, out = refs
+    half = pieces[0].shape[0]
+    for (k, at), ref in zip(places, pieces):
+        start = pl.multiple_of(((info[2] ^ k) * 2 + at) * half, half)
+        out[pl.ds(start, half), :] = ref[...]
+
+
+def placed(info, pieces):
     arrays = [x for x, _, _ in pieces]
     half, width = arrays[0].shape
     vmem = pl.BlockSpec(memory_space=pltpu.VMEM)
     return pl.pallas_call(
-        functools.partial(into_heads_kernel, [(k, at) for _, k, at in pieces]),
-        out_shape=(
-            jax.ShapeDtypeStruct((half * len(pieces), width), BF16),
-            jax.ShapeDtypeStruct((2 * mine.shape[0], width), BF16),
-        ),
-        in_specs=[pl.BlockSpec(memory_space=pltpu.SMEM)] + [vmem] * (2 + len(pieces)),
-        out_specs=(vmem, vmem),
-        cost_estimate=FILLER,
-        compiler_params=pltpu.CompilerParams(vmem_limit_bytes=20 * 1024 * 1024),
-        name="gradient_into_heads",
-    )(info, mine, theirs, *arrays)
+        functools.partial(place_kernel, [(k, at) for _, k, at in pieces]),
+        out_shape=jax.ShapeDtypeStruct((half * len(pieces), width), BF16),
+        in_specs=[pl.BlockSpec(memory_space=pltpu.SMEM)] + [vmem] * len(arrays),
+        out_specs=vmem,
+        cost_estimate=FILLER,
+        compiler_params=pltpu.CompilerParams(vmem_limit_bytes=8 * 1024 * 1024),
+        name="place_shares",
+    )(info, *arrays)
 
 
 def plane_sum_kernel(info, rest, from_x, from_y, by_x1, by_y0, kept, farther, sent, total):
@@ -448,8 +469,8 @@
 
     hop = up(hop, 1)
     state = forward(info, q, chunks[1], 1, state)
-    lower_x, upper_y, diagonal_x, diagonal_y, hop, state = together(
-        (across(lower, 1), across(upper, 2), across(lower_y, 1), across(upper_x, 2), hop, state)
+    diagonal_x, diagonal_y, hop, state, lower, upper = together(
+        (across(lower_y, 1), across(upper_x, 2), hop, state, lower, upper)
     )
     chunks.append(hop)
 
@@ -470,16 +491,18 @@
         jnp.concatenate([strip(3, half, half), strip(2, half, half)], 0),
         jnp.concatenate([strip(1, half, half), strip(2, 0, half), strip(0, 0, share)], 0),
     ]
-    weight, da = gradient_into_heads(
-        info,
-        g0,
-        grad_theirs,
-        [(lower, 0, 0), (upper, 0, 1), (lower_x, 1, 0), (upper_x, 1, 1), (lower_y, 2, 0)]
-        + [(upper_y, 2, 1), (diagonal_x, 3, 0), (diagonal_y, 3, 1)],
-    )
-    da, last_hop, state, *strips = together((da, last_hop, state, *strips))
+    early = [(lower, 0, 0), (upper, 0, 1), (upper_x, 1, 1), (lower_y, 2, 0)]
+    early += [(diagonal_x, 3, 0), (diagonal_y, 3, 1)]
+    da = gradient_into_heads(info, turned, early)
+    last_hop, lower_x, upper_y, da, state, *strips = together(
+        (last_hop, across(lower, 1), across(upper, 2), da, state, *strips)
+    )
     chunks.append(last_hop)
     att, lse_t, to_x, to_y = forward(info, q, last_hop, prior, state, strips[:2])
+    att, info = together((att, info))
+    late = [(lower_x, 1, 0), (upper_y, 2, 1)]
+    da = gradient_into_heads(info, turned, late, da)
+    weight = placed(info, early + late)
 
     carried = None
     terms = {}

time: 125 us -> 125 us (level)
  local copies, waits for them, and re-layouts: 6.72 us -> 1.6 us
  starting transfers between devices: 41.6 us -> 46.7 us
  other arithmetic: 9.82 us -> 11.6 us
    ppermute x3, starting transfers between devices: 6.99 us -> 12 us  [up(): return lax.ppermute(x, 'chip', [(i, i + k) for i in range(chips - k)])]
    unnamed x11 -> x7, local copies, waits for them, and re-layouts: 3.55 us -> 1.43 us
    ppermute x10, waiting for transfers between devices: 8.63 us -> 6.55 us  [across(): return lax.ppermute(x, 'dp', [(i, i ^ k) for i in range(rows_dp)])]
    ppermute x3, waiting for transfers between devices: 1.42 us -> 3.25 us  [down(): return lax.ppermute(x, 'chip', [(i + k, i) for i in range(chips - k)])]
    concatenate x2 -> x3, other arithmetic: 2.75 us -> 4.55 us  [on_device(): turned = jnp.concatenate([g0.T, grad_theirs.T], 1)]
    optimization_barrier x1 -> x0, local copies, waits for them, and re-layouts: 1.57 us -> none  [on_device(): together((hop, q, state, lower, upper, upper_x, lower_y, swap(g0)))]
    slice x3, local copies, waits for them, and re-layouts: 1.51 us -> 0.08 us  [on_device(): lower, upper = (ours[:half], ours[half:])]
    pallas_call x4, Pallas kernels: 7.61 us -> 6.35 us  [backward(): pl.pallas_call(functools.partial(backward_kernel, steps, rows, first, las...]
  transfers between devices with their start and end apart: 29 -> 29, of which waited for: 13 -> 13; matrix products, arithmetic and copies ran while one was open for 11% -> 10% of each run, Pallas kernels for 18% -> 17%
where the time goes in v11:
time: 125 us
  starting transfers between devices  46.7 us (37%)
  waiting for transfers between devices  40.9 us (33%)
  Pallas kernels  22.8 us (18%)
  other arithmetic  11.6 us (9%)
  local copies, waits for them, and re-layouts  1.6 us (1%)
    ppermute x2, waiting for transfers between devices, pair(): return lax.ppermute(x, 'chip', [(i, i ^ k) for i in range(chips)])  16.7 us
    ppermute x8, starting transfers between devices, swap(): return lax.ppermute(x, 'core', [(0, 1), (1, 0)])  13 us
    ppermute x3, starting transfers between devices, up(): return lax.ppermute(x, 'chip', [(i, i + k) for i in range(chips - k)])  12 us
    ppermute x10, starting transfers between devices, across(): return lax.ppermute(x, 'dp', [(i, i ^ k) for i in range(rows_dp)])  8.57 us
    ppermute x3, starting transfers between devices, down(): return lax.ppermute(x, 'chip', [(i + k, i) for i in range(chips - k)])  7.38 us
    ppermute x3, waiting for transfers between devices, up(): return lax.ppermute(x, 'chip', [(i, i + k) for i in range(chips - k)])  7.01 us
    ppermute x3, waiting for transfers between devices, round_chips(): return lax.ppermute(x, 'chip', [(i, (i + k) % chips) for i in range(chips)])  6.67 us
    ppermute x10, waiting for transfers between devices, across(): return lax.ppermute(x, 'dp', [(i, i ^ k) for i in range(rows_dp)])  6.55 us
  transfers between devices with their start and end apart: 29, of which 13 were waited for; matrix products, arithmetic and copies ran while one was open for 10% of the time, Pallas kernels for 17%

profile of v11, /device:TPU:9, one launch (start us, length us, event | category | flops | bytes accessed | tf_op | source)
XLA Modules:
  0.0 124.7 jit_solution(14056248288362606824)
XLA Ops:
  0.7 2.4 %collective-permute-start.4 = (bf16[72,1024]{1,0:T(8,128)(2,1)}, bf16[72,1024]{1,0:T(8,128)(2,1)S(1)}, u32[]{:S(2)}, u32[]{:S(2)}) collective-permute-start(bf16[72,1024]{1,0:T(8,128)(2,1)} %refs_0_.1), channel_id=1, source_target_pairs={{0,4},{2,6},{4,0},{6,2},{1,5},{3,7},{5,1},{7,3},{8,12},{10,14},{12... | collective-permute-start | bytes 442376 | tf_op jit(solution)/shard_map/ppermute | solution.py:431
  3.0 1.5 %collective-permute-start.5 = (bf16[72,1024]{1,0:T(8,128)(2,1)}, bf16[72,1024]{1,0:T(8,128)(2,1)S(1)}, u32[]{:S(2)}, u32[]{:S(2)}) collective-permute-start(bf16[72,1024]{1,0:T(8,128)(2,1)} %refs_0_.1), channel_id=1, source_target_pairs={{0,6},{2,0},{4,2},{6,4},{1,7},{3,1},{5,3},{7,5},{8,14},{10,8},{12,... | collective-permute-start | bytes 442376 | tf_op jit(solution)/shard_map/ppermute | solution.py:431
  4.5 1.0 broadcast_select_fusion.5
  5.5 1.0 broadcast_select_fusion.4
  6.5 1.6 %collective-permute-start = (bf16[256,512]{1,0:T(8,128)(2,1)S(1)}, bf16[256,512]{1,0:T(8,128)(2,1)S(1)}, u32[]{:S(2)}, u32[]{:S(2)}) collective-permute-start(bf16[256,512]{1,0:T(8,128)(2,1)S(1)} %pad_maximum_fusion.5), channel_id=1, source_target_pairs={{0,1},{1,0},{2,3},{3,2},{4,5},{5,4},{6,7},{7,6},{8,9},{9,8},{10,11... | collective-permute-start | bytes 786440 | tf_op jit(solution)/shard_map/ppermute | solution.py:422
  8.1 1.4 %copy.12 = bf16[1,256,2304]{1,2,0:T(8,128)(2,1)} copy(bf16[1,256,2304]{2,1,0:T(8,128)(2,1)S(1)} %copy-done.1) | data formatting | bytes 2359296 | tf_op args[4]
  9.6 0.9 collective-permute-done.4.refs_2_
  10.5 5.8 %collective-permute-done.3.refs_1_ = bf16[72,1024]{1,0:T(8,128)(2,1)S(1)} collective-permute-done((bf16[72,1024]{1,0:T(8,128)(2,1)}, bf16[72,1024]{1,0:T(8,128)(2,1)S(1)}, u32[]{:S(2)}, u32[]{:S(2)}) %collective-permute-start.3) | collective-permute-done | bytes 147488 | tf_op jit(solution)/shard_map/ppermute | solution.py:431
  16.3 0.6 column_halves.1
  16.9 0.6 collective-permute-start.6
  17.6 4.0 %collective-permute-start.1 = (bf16[512,512]{1,0:T(8,128)(2,1)S(1)}, bf16[512,512]{1,0:T(8,128)(2,1)S(1)}, u32[]{:S(2)}, u32[]{:S(2)}) collective-permute-start(bf16[512,512]{1,0:T(8,128)(2,1)S(1)} %pad_maximum_fusion.4.kv.refs_0_), channel_id=1, source_target_pairs={{0,2},{2,4},{4,6},{1,3},{3,5},{5,7},{8,10},{10,12},{12,14},{9,11},... | collective-permute-start | bytes 1572872 | tf_op jit(solution)/shard_map/ppermute | solution.py:425
  21.8 1.3 %collective-permute-start.8 = (bf16[288,512]{1,0:T(8,128)(2,1)S(1)}, bf16[288,512]{1,0:T(8,128)(2,1)S(1)}, u32[]{:S(2)}, u32[]{:S(2)}) collective-permute-start(bf16[288,512]{1,0:T(8,128)(2,1)S(1)} %bitcast.28), channel_id=1, source_target_pairs={{0,16},{8,24},{16,0},{24,8},{1,17},{9,25},{17,1},{25,9},{2,18},{10... | collective-permute-start | bytes 884744 | tf_op jit(solution)/shard_map/ppermute | solution.py:434
  23.2 1.2 collective-permute-start.7
  24.5 2.1 %attend_forward.4 = (f32[16,512]{1,0:T(8,128)S(1)}, f32[16,512]{1,0:T(8,128)S(1)}, f32[512,512]{1,0:T(8,128)S(1)}) custom-call(s32[3]{0:T(128)S(1)} %pad_add_fusion.info, bf16[512,512]{1,0:T(8,128)(2,1)S(1)} %maximum_multiply_fusion.q, bf16[512,512]{1,0:T(8,128)(2,1)S(1)} %pad_maximum_fusion.4.kv.refs_0_), custom_call_target="tpu_custom_call" | custom-call | flops 1 | bytes 1 | tf_op jit(solution)/shard_map/attend_forward/pallas_call | solution.py:114
  26.6 3.1 %collective-permute-done.8.refs_3_ = bf16[288,512]{1,0:T(8,128)(2,1)S(1)} collective-permute-done((bf16[288,512]{1,0:T(8,128)(2,1)S(1)}, bf16[288,512]{1,0:T(8,128)(2,1)S(1)}, u32[]{:S(2)}, u32[]{:S(2)}) %collective-permute-start.8) | collective-permute-done | bytes 294944 | tf_op jit(solution)/shard_map/ppermute | solution.py:434
  29.7 0.9 collective-permute-done.7.refs_2_
  30.6 1.9 %collective-permute-done.1.kv.refs_0_ = bf16[512,512]{1,0:T(8,128)(2,1)S(1)} collective-permute-done((bf16[512,512]{1,0:T(8,128)(2,1)S(1)}, bf16[512,512]{1,0:T(8,128)(2,1)S(1)}, u32[]{:S(2)}, u32[]{:S(2)}) %collective-permute-start.1) | collective-permute-done | bytes 524320 | tf_op jit(solution)/shard_map/ppermute | solution.py:425
  32.5 1.2 collective-permute-start.10
  33.7 1.2 collective-permute-start.11
  35.0 4.0 %collective-permute-start.12 = (bf16[512,512]{1,0:T(8,128)(2,1)S(1)}, bf16[512,512]{1,0:T(8,128)(2,1)S(1)}, u32[]{:S(2)}, u32[]{:S(2)}) collective-permute-start(bf16[512,512]{1,0:T(8,128)(2,1)S(1)} %collective-permute-done.1.kv.refs_0_), channel_id=1, source_target_pairs={{0,2},{2,4},{4,6},{1,3},{3,5},{5,7},{8,10},{10,12},{12,14},{9,11},... | collective-permute-start | bytes 1572872 | tf_op jit(solution)/shard_map/ppermute | solution.py:425
  39.0 1.9 %attend_forward.5 = (f32[16,512]{1,0:T(8,128)S(1)}, f32[16,512]{1,0:T(8,128)S(1)}, f32[512,512]{1,0:T(8,128)S(1)}) custom-call(s32[3]{0:T(128)S(1)} %pad_add_fusion.info, bf16[512,512]{1,0:T(8,128)(2,1)S(1)} %maximum_multiply_fusion.q, bf16[512,512]{1,0:T(8,128)(2,1)S(1)} %collective-permute-done.1.kv.refs_0_, f32[16,512]{1,0:T(8,128)S(1)} %get-tuple-element.91.refs_0_, ...), custom_call_target="tpu_custom_call" | custom-call | flops 1 | bytes 1 | tf_op jit(solution)/shard_map/attend_forward/pallas_call | solution.py:114
  40.9 1.7 %fusion.5 = (bf16[288,512]{1,0:T(8,128)(2,1)S(1)}, bf16[288,512]{1,0:T(8,128)(2,1)S(1)}, bf16[288,512]{1,0:T(8,128)(2,1)S(1)}, bf16[288,512]{1,0:T(8,128)(2,1)S(...) fusion(s32[]{:T(128)S(6)} %select_n.127, bf16[2304,256]{1,0:T(8,128)(2,1)} %bitcast.11, ...), kind=kLoop, calls=%fused_computation.33 | loop fusion | flops 3538944 | bytes 4128792 | tf_op jit(solution)/shard_map/concatenate | solution.py:484
  42.6 1.1 fusion
  43.7 1.8 %pad_maximum_fusion.turned = bf16[2304,512]{1,0:T(8,128)(2,1)S(1)} fusion(bf16[2304,256]{1,0:T(8,128)(2,1)} %bitcast.12, bf16[2304,256]{1,0:T(8,128)(2,1)} %bitcast.11), kind=kLoop, calls=%fused_computation.7 | loop fusion | flops 4718592 | bytes 4718592 | tf_op jit(solution)/shard_map/concatenate | solution.py:484
  45.5 2.9 %collective-permute-done.12.kv.refs_0_ = bf16[512,512]{1,0:T(8,128)(2,1)S(1)} collective-permute-done((bf16[512,512]{1,0:T(8,128)(2,1)S(1)}, bf16[512,512]{1,0:T(8,128)(2,1)S(1)}, u32[]{:S(2)}, u32[]{:S(2)}) %collective-permute-start.12) | collective-permute-done | bytes 524320 | tf_op jit(solution)/shard_map/ppermute | solution.py:425
  48.4 4.0 %collective-permute-start.13 = (bf16[512,512]{1,0:T(8,128)(2,1)S(1)}, bf16[512,512]{1,0:T(8,128)(2,1)S(1)}, u32[]{:S(2)}, u32[]{:S(2)}) collective-permute-start(bf16[512,512]{1,0:T(8,128)(2,1)S(1)} %collective-permute-done.12.kv.refs_0_), channel_id=1, source_target_pairs={{0,2},{2,4},{4,6},{1,3},{3,5},{5,7},{8,10},{10,12},{12,14},{9,11},... | collective-permute-start | bytes 1572872 | tf_op jit(solution)/shard_map/ppermute | solution.py:425
  52.4 0.3 collective-permute-start.14
  52.8 0.2 collective-permute-start.15
  53.1 0.6 attend_forward.6
  53.7 2.4 %gradient_into_heads.2.refs_0_ = f32[512,512]{1,0:T(8,128)S(1)} custom-call(s32[3]{0:T(128)S(1)} %pad_add_fusion.info, bf16[2304,512]{1,0:T(8,128)(2,1)S(1)} %pad_maximum_fusion.turned, bf16[288,512]{1,0:T(8,128)(2,1)S(1)} %bitcast.30, bf16[288,512]{1,0:T(8,128)(2,1)S(1)} %bitcast.26, bf16[288,512]{1,0:T(8,128)(2,1)S(1)} %collective-permute-done.7.refs_2_, ...), custom_call_target="tpu_custom_call" | custom-call | flops 1 | bytes 1 | tf_op jit(solution)/shard_map/gradient_into_heads/pallas_call | solution.py:273
  56.1 2.3 %collective-permute-done.14.refs_1_.refs_6_ = bf16[288,512]{1,0:T(8,128)(2,1)S(1)} collective-permute-done((bf16[288,512]{1,0:T(8,128)(2,1)S(1)}, bf16[288,512]{1,0:T(8,128)(2,1)S(1)}, u32[]{:S(2)}, u32[]{:S(2)}) %collective-permute-start.14) | collective-permute-done | bytes 294944 | tf_op jit(solution)/shard_map/ppermute | solution.py:434
  58.4 0.3 collective-permute-done.15.refs_2_.refs_7_
  58.6 2.2 %collective-permute-done.13.kv.refs_0_ = bf16[512,512]{1,0:T(8,128)(2,1)S(1)} collective-permute-done((bf16[512,512]{1,0:T(8,128)(2,1)S(1)}, bf16[512,512]{1,0:T(8,128)(2,1)S(1)}, u32[]{:S(2)}, u32[]{:S(2)}) %collective-permute-start.13) | collective-permute-done | bytes 524320 | tf_op jit(solution)/shard_map/ppermute | solution.py:425
  60.9 1.5 %attend_forward.7 = (bf16[512,512]{1,0:T(8,128)(2,1)S(1)}, f32[16,512]{1,0:T(8,128)S(1)}, bf16[576,512]{1,0:T(8,128)(2,1)S(1)}, bf16[576,512]{1,0:T(8,128)(2,1)S(1)}) custom-call(s32[3]{0:T(128)S(1)} %pad_add_fusion.info, bf16[512,512]{1,0:T(8,128)(2,1)S(1)} %maximum_multiply_fusion.q, bf16[512,512]{1,0:T(8,128)(2,1)S(1)} %collective-permute-done.13.kv.refs_0_, ...), custom_call_target="tpu_custom_call" | custom-call | flops 1 | bytes 1 | tf_op jit(solution)/shard_map/attend_forward/pallas_call | solution.py:114
  62.4 0.3 collective-permute-start.16
  62.7 0.2 collective-permute-start.17
  62.9 1.3 %gradient_into_heads.3.da = bf16[512,512]{1,0:T(8,128)(2,1)S(1)} custom-call(s32[3]{0:T(128)S(1)} %pad_add_fusion.info, bf16[2304,512]{1,0:T(8,128)(2,1)S(1)} %pad_maximum_fusion.turned, f32[512,512]{1,0:T(8,128)S(1)} %gradient_into_heads.2.refs_0_, bf16[288,512]{1,0:T(8,128)(2,1)S(1)} %collective-permute-done.14.refs_1_.refs_6_, ...), custom_call_target="tpu_custom_call" | custom-call | flops 1 | bytes 1 | tf_op jit(solution)/shard_map/gradient_into_heads/pallas_call | solution.py:273
  64.2 0.9 attend_backward.4
  65.1 2.1 %collective-permute-start.18 = (bf16[512,512]{1,0:T(8,128)(2,1)S(1)}, bf16[512,512]{1,0:T(8,128)(2,1)S(1)}, u32[]{:S(2)}, u32[]{:S(2)}) collective-permute-start(bf16[512,512]{1,0:T(8,128)(2,1)S(1)} %get-tuple-element.126), channel_id=1, source_target_pairs={{2,0},{4,2},{6,4},{3,1},{5,3},{7,5},{10,8},{12,10},{14,12},{11,9},... | collective-permute-start | bytes 1572872 | tf_op jit(solution)/shard_map/ppermute | solution.py:428
  67.2 0.6 attend_backward.5
  67.9 2.3 %attend_backward.6 = (bf16[512,512]{1,0:T(8,128)(2,1)S(1)}, f32[512,512]{1,0:T(8,128)S(1)}) custom-call(s32[3]{0:T(128)S(1)} %pad_add_fusion.info, bf16[512,512]{1,0:T(8,128)(2,1)S(1)} %maximum_multiply_fusion.q, bf16[512,512]{1,0:T(8,128)(2,1)S(1)} %gradient_into_heads.3.da, f32[16,512]{1,0:T(8,128)S(1)} %get-tuple-element.124.lse_t, ...), custom_call_target="tpu_custom_call" | custom-call | flops 1 | bytes 1 | tf_op jit(solution)/shard_map/attend_backward/pallas_call | solution.py:215
  70.2 2.5 %attend_backward.7 = (f32[512,512]{1,0:T(8,128)S(1)}, bf16[512,512]{1,0:T(8,128)(2,1)S(1)}) custom-call(s32[3]{0:T(128)S(1)} %pad_add_fusion.info, bf16[512,512]{1,0:T(8,128)(2,1)S(1)} %maximum_multiply_fusion.q, bf16[512,512]{1,0:T(8,128)(2,1)S(1)} %gradient_into_heads.3.da, f32[16,512]{1,0:T(8,128)S(1)} %get-tuple-element.124.lse_t, ...), custom_call_target="tpu_custom_call" | custom-call | flops 1 | bytes 1 | tf_op jit(solution)/shard_map/attend_backward/pallas_call | solution.py:215
  72.7 1.3 %strip_product.1.rest = f32[1152,512]{1,0:T(8,128)S(1)} custom-call(bf16[1152,512]{1,0:T(8,128)(2,1)S(1)} %pad_maximum_fusion.1.x, bf16[512,512]{1,0:T(8,128)(2,1)S(1)} %get-tuple-element.140.refs_1_.w.x), custom_call_target="tpu_custom_call" | custom-call | flops 1 | bytes 1 | tf_op jit(solution)/shard_map/strip_product/pallas_call | solution.py:384
  74.0 3.2 %collective-permute-done.18 = bf16[512,512]{1,0:T(8,128)(2,1)S(1)} collective-permute-done((bf16[512,512]{1,0:T(8,128)(2,1)S(1)}, bf16[512,512]{1,0:T(8,128)(2,1)S(1)}, u32[]{:S(2)}, u32[]{:S(2)}) %collective-permute-start.18) | collective-permute-done | bytes 524320 | tf_op jit(solution)/shard_map/ppermute | solution.py:428
  77.4 1.9 %collective-permute-start.22 = (bf16[512,512]{1,0:T(8,128)(2,1)S(1)}, bf16[512,512]{1,0:T(8,128)(2,1)S(1)}, u32[]{:S(2)}, u32[]{:S(2)}) collective-permute-start(bf16[512,512]{1,0:T(8,128)(2,1)S(1)} %add_convert_fusion.3), channel_id=1, source_target_pairs={{2,0},{4,2},{6,4},{3,1},{5,3},{7,5},{10,8},{12,10},{14,12},{11,9},... | collective-permute-start | bytes 1572872 | tf_op jit(solution)/shard_map/ppermute | solution.py:428
  79.3 0.2 add_convert_fusion.4
  79.5 1.3 %collective-permute-start.20 = (bf16[288,512]{1,0:T(8,128)(2,1)S(1)}, bf16[288,512]{1,0:T(8,128)(2,1)S(1)}, u32[]{:S(2)}, u32[]{:S(2)}) collective-permute-start(bf16[288,512]{1,0:T(8,128)(2,1)S(1)} %get-tuple-element.159), channel_id=1, source_target_pairs={{0,16},{8,24},{16,0},{24,8},{1,17},{9,25},{17,1},{25,9},{2,18},{10... | collective-permute-start | bytes 884744 | tf_op jit(solution)/shard_map/ppermute | solution.py:434
  80.8 1.2 collective-permute-start.19
  82.1 5.6 %collective-permute-start.21 = (bf16[256,512]{1,0:T(8,128)(2,1)S(1)}, bf16[256,512]{1,0:T(8,128)(2,1)S(1)}, u32[]{:S(2)}, u32[]{:S(2)}) collective-permute-start(bf16[256,512]{1,0:T(8,128)(2,1)S(1)} %get-tuple-element.172), channel_id=1, source_target_pairs={{0,1},{1,0},{2,3},{3,2},{4,5},{5,4},{6,7},{7,6},{8,9},{9,8},{10,11... | collective-permute-start | bytes 786440 | tf_op jit(solution)/shard_map/ppermute | solution.py:422
  87.6 0.7 place_shares.1.w
  88.3 3.2 %layer_product.1 = (f32[256,2304]{1,0:T(8,128)S(1)}, bf16[256,2304]{1,0:T(8,128)(2,1)S(1)}) custom-call(bf16[512,512]{1,0:T(8,128)(2,1)S(1)} %get-tuple-element.140.refs_1_.w.x, bf16[2304,512]{1,0:T(8,128)(2,1)S(1)} %place_shares.1.w), custom_call_target="tpu_custom_call" | custom-call | flops 1 | bytes 1 | tf_op jit(solution)/shard_map/layer_product/pallas_call | solution.py:363
  91.6 4.3 %collective-permute-start.25 = (bf16[256,2304]{1,0:T(8,128)(2,1)S(1)}, bf16[256,2304]{1,0:T(8,128)(2,1)S(1)}, u32[]{:S(2)}, u32[]{:S(2)}) collective-permute-start(bf16[256,2304]{1,0:T(8,128)(2,1)S(1)} %get-tuple-element.149), channel_id=1, source_target_pairs={{0,1},{1,0},{2,3},{3,2},{4,5},{5,4},{6,7},{7,6},{8,9},{9,8},{10,11... | collective-permute-start | bytes 3538952 | tf_op jit(solution)/shard_map/ppermute | solution.py:422
  95.9 0.9 plane_sum.1
  96.9 3.4 %collective-permute-start.26 = (bf16[512,512]{1,0:T(8,128)(2,1)S(1)}, bf16[512,512]{1,0:T(8,128)(2,1)S(1)}, u32[]{:S(2)}, u32[]{:S(2)}) collective-permute-start(bf16[512,512]{1,0:T(8,128)(2,1)S(1)} %add_convert_fusion.2), channel_id=1, source_target_pairs={{2,0},{4,2},{6,4},{3,1},{5,3},{7,5},{10,8},{12,10},{14,12},{11,9},... | collective-permute-start | bytes 1572872 | tf_op jit(solution)/shard_map/ppermute | solution.py:428
  100.3 0.9 maximum_select_fusion.1
  101.2 4.2 %collective-permute-done.23 = bf16[288,512]{1,0:T(8,128)(2,1)S(1)} collective-permute-done((bf16[288,512]{1,0:T(8,128)(2,1)S(1)}, bf16[288,512]{1,0:T(8,128)(2,1)S(1)}, u32[]{:S(2)}, u32[]{:S(2)}) %collective-permute-start.23) | collective-permute-done | bytes 294944 | tf_op jit(solution)/shard_map/ppermute | solution.py:542
  105.5 1.8 %collective-permute-start.24 = (bf16[144,512]{1,0:T(8,128)(2,1)S(1)}, bf16[144,512]{1,0:T(8,128)(2,1)S(1)}, u32[]{:S(2)}, u32[]{:S(2)}) collective-permute-start(bf16[144,512]{1,0:T(8,128)(2,1)S(1)} %add_convert_fusion.6), channel_id=1, source_target_pairs={{0,4},{2,6},{4,0},{6,2},{1,5},{3,7},{5,1},{7,3},{8,12},{10,14},{12... | collective-permute-start | bytes 442376 | tf_op jit(solution)/shard_map/ppermute | solution.py:542
  107.3 1.2 add_convert_fusion
  108.5 12.5 %collective-permute-done.24 = bf16[144,512]{1,0:T(8,128)(2,1)S(1)} collective-permute-done((bf16[144,512]{1,0:T(8,128)(2,1)S(1)}, bf16[144,512]{1,0:T(8,128)(2,1)S(1)}, u32[]{:S(2)}, u32[]{:S(2)}) %collective-permute-start.24) | collective-permute-done | bytes 147488 | tf_op jit(solution)/shard_map/ppermute | solution.py:542
  121.1 0.8 collective-permute-start.28
  121.9 0.2 add_convert_fusion.1
  122.2 0.7 collective-permute-done.28
  122.9 0.7 maximum_select_fusion.2
  123.8 0.9 maximum_select_fusion.3
  (48 shorter events, 1.4 us)
Async XLA Ops:
  0.6 15.7 %copy-start = (bf16[72,1024]{1,0:T(8,128)(2,1)S(1)}, bf16[72,1024]{1,0:T(8,128)(2,1)}, u32[]{:S(2)}) copy-start(bf16[72,1024]{1,0:T(8,128)(2,1)} %refs_0_.1) | copy-start | bytes 442372
  0.6 7.4 %copy-start.1 = (bf16[1,256,2304]{2,1,0:T(8,128)(2,1)S(1)}, bf16[1,256,2304]{2,1,0:T(8,128)(2,1)}, u32[]{:S(2)}) copy-start(bf16[1,256,2304]{2,1,0:T(8,128)(2,1)} %param.9) | copy-start | bytes 3538948
  0.7 9.8 %collective-permute-start.4 = (bf16[72,1024]{1,0:T(8,128)(2,1)}, bf16[72,1024]{1,0:T(8,128)(2,1)S(1)}, u32[]{:S(2)}, u32[]{:S(2)}) collective-permute-start(bf16[72,1024]{1,0:T(8,128)(2,1)} %refs_0_.1), channel_id=1, source_target_pairs={{0,4},{2,6},{4,0},{6,2},{1,5},{3,7},{5,1},{7,3},{8,12},{10,14},{12... | collective-permute-start | bytes 442376 | tf_op jit(solution)/shard_map/ppermute | solution.py:431
  3.0 13.3 %collective-permute-start.3 = (bf16[72,1024]{1,0:T(8,128)(2,1)}, bf16[72,1024]{1,0:T(8,128)(2,1)S(1)}, u32[]{:S(2)}, u32[]{:S(2)}) collective-permute-start(bf16[72,1024]{1,0:T(8,128)(2,1)} %refs_0_.1), channel_id=1, source_target_pairs={{0,2},{2,4},{4,6},{6,0},{1,3},{3,5},{5,7},{7,1},{8,10},{10,12},{12... | collective-permute-start | bytes 442376 | tf_op jit(solution)/shard_map/ppermute | solution.py:431
  3.0 13.3 %collective-permute-start.5 = (bf16[72,1024]{1,0:T(8,128)(2,1)}, bf16[72,1024]{1,0:T(8,128)(2,1)S(1)}, u32[]{:S(2)}, u32[]{:S(2)}) collective-permute-start(bf16[72,1024]{1,0:T(8,128)(2,1)} %refs_0_.1), channel_id=1, source_target_pairs={{0,6},{2,0},{4,2},{6,4},{1,7},{3,1},{5,3},{7,5},{8,14},{10,8},{12,... | collective-permute-start | bytes 442376 | tf_op jit(solution)/shard_map/ppermute | solution.py:431
  6.5 11.1 %collective-permute-start = (bf16[256,512]{1,0:T(8,128)(2,1)S(1)}, bf16[256,512]{1,0:T(8,128)(2,1)S(1)}, u32[]{:S(2)}, u32[]{:S(2)}) collective-permute-start(bf16[256,512]{1,0:T(8,128)(2,1)S(1)} %pad_maximum_fusion.5), channel_id=1, source_target_pairs={{0,1},{1,0},{2,3},{3,2},{4,5},{5,4},{6,7},{7,6},{8,9},{9,8},{10,11... | collective-permute-start | bytes 786440 | tf_op jit(solution)/shard_map/ppermute | solution.py:422
  9.5 23.0 %collective-permute-start.9 = (bf16[256,2304]{0,1:T(8,128)(2,1)}, bf16[256,2304]{0,1:T(8,128)(2,1)}, u32[]{:S(2)}, u32[]{:S(2)}) collective-permute-start(bf16[256,2304]{0,1:T(8,128)(2,1)} %bitcast.10), channel_id=1, source_target_pairs={{0,1},{1,0},{2,3},{3,2},{4,5},{5,4},{6,7},{7,6},{8,9},{9,8},{10,11... | collective-permute-start | bytes 3538952 | tf_op jit(solution)/shard_map/ppermute | solution.py:422
  9.6 7.8 %copy-start.2 = (bf16[1,256,1024]{2,1,0:T(8,128)(2,1)S(1)}, bf16[1,256,1024]{2,1,0:T(8,128)(2,1)}, u32[]{:S(2)}) copy-start(bf16[1,256,1024]{2,1,0:T(8,128)(2,1)} %param.5) | copy-start | bytes 1572868
  16.9 4.8 %collective-permute-start.6 = (bf16[4,72,512]{2,1,0:T(8,128)(2,1)S(1)}, bf16[4,72,512]{2,1,0:T(8,128)(2,1)S(1)}, u32[]{:S(2)}, u32[]{:S(2)}) collective-permute-start(bf16[4,72,512]{2,1,0:T(8,128)(2,1)S(1)} %get-tuple-element.86), channel_id=1, source_target_pairs={{0,1},{1,0},{2,3},{3,2},{4,5},{5,4},{6,7},{7,6},{8,9},{9,8},{10,11... | collective-permute-start | bytes 884744 | tf_op jit(solution)/shard_map/ppermute | solution.py:422
  17.5 6.9 %collective-permute-start.2 = (bf16[256,512]{1,0:T(8,128)(2,1)S(1)}, bf16[256,512]{1,0:T(8,128)(2,1)S(1)}, u32[]{:S(2)}, u32[]{:S(2)}) collective-permute-start(bf16[256,512]{1,0:T(8,128)(2,1)S(1)} %get-tuple-element.174), channel_id=1, source_target_pairs={{0,1},{1,0},{2,3},{3,2},{4,5},{5,4},{6,7},{7,6},{8,9},{9,8},{10,11... | collective-permute-start | bytes 786440 | tf_op jit(solution)/shard_map/ppermute | solution.py:422
  17.6 14.9 %collective-permute-start.1 = (bf16[512,512]{1,0:T(8,128)(2,1)S(1)}, bf16[512,512]{1,0:T(8,128)(2,1)S(1)}, u32[]{:S(2)}, u32[]{:S(2)}) collective-permute-start(bf16[512,512]{1,0:T(8,128)(2,1)S(1)} %pad_maximum_fusion.4.kv.refs_0_), channel_id=1, source_target_pairs={{0,2},{2,4},{4,6},{1,3},{3,5},{5,7},{8,10},{10,12},{12,14},{9,11},... | collective-permute-start | bytes 1572872 | tf_op jit(solution)/shard_map/ppermute | solution.py:425
  21.8 7.8 %collective-permute-start.8 = (bf16[288,512]{1,0:T(8,128)(2,1)S(1)}, bf16[288,512]{1,0:T(8,128)(2,1)S(1)}, u32[]{:S(2)}, u32[]{:S(2)}) collective-permute-start(bf16[288,512]{1,0:T(8,128)(2,1)S(1)} %bitcast.28), channel_id=1, source_target_pairs={{0,16},{8,24},{16,0},{24,8},{1,17},{9,25},{17,1},{25,9},{2,18},{10... | collective-permute-start | bytes 884744 | tf_op jit(solution)/shard_map/ppermute | solution.py:434
  23.2 7.5 %collective-permute-start.7 = (bf16[288,512]{1,0:T(8,128)(2,1)S(1)}, bf16[288,512]{1,0:T(8,128)(2,1)S(1)}, u32[]{:S(2)}, u32[]{:S(2)}) collective-permute-start(bf16[288,512]{1,0:T(8,128)(2,1)S(1)} %bitcast.24), channel_id=1, source_target_pairs={{0,8},{8,0},{16,24},{24,16},{1,9},{9,1},{17,25},{25,17},{2,10},{10... | collective-permute-start | bytes 884744 | tf_op jit(solution)/shard_map/ppermute | solution.py:434
  32.5 13.0 %collective-permute-start.10 = (bf16[288,512]{1,0:T(8,128)(2,1)S(1)}, bf16[288,512]{1,0:T(8,128)(2,1)S(1)}, u32[]{:S(2)}, u32[]{:S(2)}) collective-permute-start(bf16[288,512]{1,0:T(8,128)(2,1)S(1)} %collective-permute-done.8.refs_3_), channel_id=1, source_target_pairs={{0,8},{8,0},{16,24},{24,16},{1,9},{9,1},{17,25},{25,17},{2,10},{10... | collective-permute-start | bytes 884744 | tf_op jit(solution)/shard_map/ppermute | solution.py:434
  33.7 11.8 %collective-permute-start.11 = (bf16[288,512]{1,0:T(8,128)(2,1)S(1)}, bf16[288,512]{1,0:T(8,128)(2,1)S(1)}, u32[]{:S(2)}, u32[]{:S(2)}) collective-permute-start(bf16[288,512]{1,0:T(8,128)(2,1)S(1)} %collective-permute-done.7.refs_2_), channel_id=1, source_target_pairs={{0,16},{8,24},{16,0},{24,8},{1,17},{9,25},{17,1},{25,9},{2,18},{10... | collective-permute-start | bytes 884744 | tf_op jit(solution)/shard_map/ppermute | solution.py:434
  35.0 13.4 %collective-permute-start.12 = (bf16[512,512]{1,0:T(8,128)(2,1)S(1)}, bf16[512,512]{1,0:T(8,128)(2,1)S(1)}, u32[]{:S(2)}, u32[]{:S(2)}) collective-permute-start(bf16[512,512]{1,0:T(8,128)(2,1)S(1)} %collective-permute-done.1.kv.refs_0_), channel_id=1, source_target_pairs={{0,2},{2,4},{4,6},{1,3},{3,5},{5,7},{8,10},{10,12},{12,14},{9,11},... | collective-permute-start | bytes 1572872 | tf_op jit(solution)/shard_map/ppermute | solution.py:425
  48.4 12.5 %collective-permute-start.13 = (bf16[512,512]{1,0:T(8,128)(2,1)S(1)}, bf16[512,512]{1,0:T(8,128)(2,1)S(1)}, u32[]{:S(2)}, u32[]{:S(2)}) collective-permute-start(bf16[512,512]{1,0:T(8,128)(2,1)S(1)} %collective-permute-done.12.kv.refs_0_), channel_id=1, source_target_pairs={{0,2},{2,4},{4,6},{1,3},{3,5},{5,7},{8,10},{10,12},{12,14},{9,11},... | collective-permute-start | bytes 1572872 | tf_op jit(solution)/shard_map/ppermute | solution.py:425
  52.4 5.9 %collective-permute-start.14 = (bf16[288,512]{1,0:T(8,128)(2,1)S(1)}, bf16[288,512]{1,0:T(8,128)(2,1)S(1)}, u32[]{:S(2)}, u32[]{:S(2)}) collective-permute-start(bf16[288,512]{1,0:T(8,128)(2,1)S(1)} %bitcast.29), channel_id=1, source_target_pairs={{0,8},{8,0},{16,24},{24,16},{1,9},{9,1},{17,25},{25,17},{2,10},{10... | collective-permute-start | bytes 884744 | tf_op jit(solution)/shard_map/ppermute | solution.py:434
  52.8 5.9 %collective-permute-start.15 = (bf16[288,512]{1,0:T(8,128)(2,1)S(1)}, bf16[288,512]{1,0:T(8,128)(2,1)S(1)}, u32[]{:S(2)}, u32[]{:S(2)}) collective-permute-start(bf16[288,512]{1,0:T(8,128)(2,1)S(1)} %bitcast.25), channel_id=1, source_target_pairs={{0,16},{8,24},{16,0},{24,8},{1,17},{9,25},{17,1},{25,9},{2,18},{10... | collective-permute-start | bytes 884744 | tf_op jit(solution)/shard_map/ppermute | solution.py:434
  62.4 14.9 %collective-permute-start.16 = (bf16[576,512]{1,0:T(8,128)(2,1)S(1)}, bf16[576,512]{1,0:T(8,128)(2,1)S(1)}, u32[]{:S(2)}, u32[]{:S(2)}) collective-permute-start(bf16[576,512]{1,0:T(8,128)(2,1)S(1)} %get-tuple-element.119), channel_id=1, source_target_pairs={{0,8},{8,0},{16,24},{24,16},{1,9},{9,1},{17,25},{25,17},{2,10},{10... | collective-permute-start | bytes 1769480 | tf_op jit(solution)/shard_map/ppermute | solution.py:434
  62.7 14.5 %collective-permute-start.17 = (bf16[576,512]{1,0:T(8,128)(2,1)S(1)}, bf16[576,512]{1,0:T(8,128)(2,1)S(1)}, u32[]{:S(2)}, u32[]{:S(2)}) collective-permute-start(bf16[576,512]{1,0:T(8,128)(2,1)S(1)} %get-tuple-element.120), channel_id=1, source_target_pairs={{0,16},{8,24},{16,0},{24,8},{1,17},{9,25},{17,1},{25,9},{2,18},{10... | collective-permute-start | bytes 1769480 | tf_op jit(solution)/shard_map/ppermute | solution.py:434
  65.1 12.1 %collective-permute-start.18 = (bf16[512,512]{1,0:T(8,128)(2,1)S(1)}, bf16[512,512]{1,0:T(8,128)(2,1)S(1)}, u32[]{:S(2)}, u32[]{:S(2)}) collective-permute-start(bf16[512,512]{1,0:T(8,128)(2,1)S(1)} %get-tuple-element.126), channel_id=1, source_target_pairs={{2,0},{4,2},{6,4},{3,1},{5,3},{7,5},{10,8},{12,10},{14,12},{11,9},... | collective-permute-start | bytes 1572872 | tf_op jit(solution)/shard_map/ppermute | solution.py:428
  77.4 14.2 %collective-permute-start.22 = (bf16[512,512]{1,0:T(8,128)(2,1)S(1)}, bf16[512,512]{1,0:T(8,128)(2,1)S(1)}, u32[]{:S(2)}, u32[]{:S(2)}) collective-permute-start(bf16[512,512]{1,0:T(8,128)(2,1)S(1)} %add_convert_fusion.3), channel_id=1, source_target_pairs={{2,0},{4,2},{6,4},{3,1},{5,3},{7,5},{10,8},{12,10},{14,12},{11,9},... | collective-permute-start | bytes 1572872 | tf_op jit(solution)/shard_map/ppermute | solution.py:428
  79.5 12.1 %collective-permute-start.20 = (bf16[288,512]{1,0:T(8,128)(2,1)S(1)}, bf16[288,512]{1,0:T(8,128)(2,1)S(1)}, u32[]{:S(2)}, u32[]{:S(2)}) collective-permute-start(bf16[288,512]{1,0:T(8,128)(2,1)S(1)} %get-tuple-element.159), channel_id=1, source_target_pairs={{0,16},{8,24},{16,0},{24,8},{1,17},{9,25},{17,1},{25,9},{2,18},{10... | collective-permute-start | bytes 884744 | tf_op jit(solution)/shard_map/ppermute | solution.py:434
  80.8 10.8 %collective-permute-start.19 = (bf16[288,512]{1,0:T(8,128)(2,1)S(1)}, bf16[288,512]{1,0:T(8,128)(2,1)S(1)}, u32[]{:S(2)}, u32[]{:S(2)}) collective-permute-start(bf16[288,512]{1,0:T(8,128)(2,1)S(1)} %get-tuple-element.160), channel_id=1, source_target_pairs={{0,8},{8,0},{16,24},{24,16},{1,9},{9,1},{17,25},{25,17},{2,10},{10... | collective-permute-start | bytes 884744 | tf_op jit(solution)/shard_map/ppermute | solution.py:434
  82.1 9.5 %collective-permute-start.21 = (bf16[256,512]{1,0:T(8,128)(2,1)S(1)}, bf16[256,512]{1,0:T(8,128)(2,1)S(1)}, u32[]{:S(2)}, u32[]{:S(2)}) collective-permute-start(bf16[256,512]{1,0:T(8,128)(2,1)S(1)} %get-tuple-element.172), channel_id=1, source_target_pairs={{0,1},{1,0},{2,3},{3,2},{4,5},{5,4},{6,7},{7,6},{8,9},{9,8},{10,11... | collective-permute-start | bytes 786440 | tf_op jit(solution)/shard_map/ppermute | solution.py:422
  91.6 15.7 %collective-permute-start.25 = (bf16[256,2304]{1,0:T(8,128)(2,1)S(1)}, bf16[256,2304]{1,0:T(8,128)(2,1)S(1)}, u32[]{:S(2)}, u32[]{:S(2)}) collective-permute-start(bf16[256,2304]{1,0:T(8,128)(2,1)S(1)} %get-tuple-element.149), channel_id=1, source_target_pairs={{0,1},{1,0},{2,3},{3,2},{4,5},{5,4},{6,7},{7,6},{8,9},{9,8},{10,11... | collective-permute-start | bytes 3538952 | tf_op jit(solution)/shard_map/ppermute | solution.py:422
  96.7 8.7 %collective-permute-start.23 = (bf16[288,512]{1,0:T(8,128)(2,1)S(1)}, bf16[288,512]{1,0:T(8,128)(2,1)S(1)}, u32[]{:S(2)}, u32[]{:S(2)}) collective-permute-start(bf16[288,512]{1,0:T(8,128)(2,1)S(1)} %get-tuple-element.147), channel_id=1, source_target_pairs={{0,2},{2,0},{4,6},{6,4},{1,3},{3,1},{5,7},{7,5},{8,10},{10,8},{12,... | collective-permute-start | bytes 884744 | tf_op jit(solution)/shard_map/ppermute | solution.py:542
  96.9 24.1 %collective-permute-start.26 = (bf16[512,512]{1,0:T(8,128)(2,1)S(1)}, bf16[512,512]{1,0:T(8,128)(2,1)S(1)}, u32[]{:S(2)}, u32[]{:S(2)}) collective-permute-start(bf16[512,512]{1,0:T(8,128)(2,1)S(1)} %add_convert_fusion.2), channel_id=1, source_target_pairs={{2,0},{4,2},{6,4},{3,1},{5,3},{7,5},{10,8},{12,10},{14,12},{11,9},... | collective-permute-start | bytes 1572872 | tf_op jit(solution)/shard_map/ppermute | solution.py:428
  105.5 15.5 %collective-permute-start.24 = (bf16[144,512]{1,0:T(8,128)(2,1)S(1)}, bf16[144,512]{1,0:T(8,128)(2,1)S(1)}, u32[]{:S(2)}, u32[]{:S(2)}) collective-permute-start(bf16[144,512]{1,0:T(8,128)(2,1)S(1)} %add_convert_fusion.6), channel_id=1, source_target_pairs={{0,4},{2,6},{4,0},{6,2},{1,5},{3,7},{5,1},{7,3},{8,12},{10,14},{12... | collective-permute-start | bytes 442376 | tf_op jit(solution)/shard_map/ppermute | solution.py:542
  121.1 1.9 %collective-permute-start.28 = (f32[72,512]{1,0:T(8,128)S(1)}, f32[72,512]{1,0:T(8,128)S(1)}, u32[]{:S(2)}, u32[]{:S(2)}) collective-permute-start(f32[72,512]{1,0:T(8,128)S(1)} %get-tuple-element.176), channel_id=1, source_target_pairs={{0,1},{1,0},{2,3},{3,2},{4,5},{5,4},{6,7},{7,6},{8,9},{9,8},{10,11... | collective-permute-start | bytes 442376 | tf_op jit(solution)/shard_map/ppermute | solution.py:422
  122.1 1.6 %collective-permute-start.27 = (bf16[256,512]{1,0:T(8,128)(2,1)S(1)}, bf16[256,512]{1,0:T(8,128)(2,1)S(1)}, u32[]{:S(2)}, u32[]{:S(2)}) collective-permute-start(bf16[256,512]{1,0:T(8,128)(2,1)S(1)} %slice.116), channel_id=1, source_target_pairs={{0,1},{1,0},{2,3},{3,2},{4,5},{5,4},{6,7},{7,6},{8,9},{9,8},{10,11... | collective-permute-start | bytes 786440 | tf_op jit(solution)/shard_map/ppermute | solution.py:422

commit v12 on v11

--- a/solution.py
+++ b/solution.py
@@ -469,8 +469,9 @@
 
     hop = up(hop, 1)
     state = forward(info, q, chunks[1], 1, state)
-    diagonal_x, diagonal_y, hop, state, lower, upper = together(
-        (across(lower_y, 1), across(upper_x, 2), hop, state, lower, upper)
+    state, lower_y, upper_x = together((state, lower_y, upper_x))
+    diagonal_x, diagonal_y, hop, lower, upper = together(
+        (across(lower_y, 1), across(upper_x, 2), hop, lower, upper)
     )
     chunks.append(hop)
 

time: 125 us -> 126 us (level)
  starting transfers between devices: 46.7 us -> 48.3 us
    ppermute x3, waiting for transfers between devices: 7.01 us -> 3.78 us  [up(): return lax.ppermute(x, 'chip', [(i, i + k) for i in range(chips - k)])]
    ppermute x3, waiting for transfers between devices: 3.25 us -> 5.95 us  [down(): return lax.ppermute(x, 'chip', [(i + k, i) for i in range(chips - k)])]
    ppermute x10, starting transfers between devices: 8.57 us -> 10.7 us  [across(): return lax.ppermute(x, 'dp', [(i, i ^ k) for i in range(rows_dp)])]
  transfers between devices with their start and end apart: 29 -> 29, of which waited for: 13 -> 15; matrix products, arithmetic and copies ran while one was open for 10% -> 10% of each run, Pallas kernels for 17% -> 17%
where the time goes in v12:
time: 126 us
  starting transfers between devices  48.3 us (38%)
  waiting for transfers between devices  40.6 us (32%)
  Pallas kernels  22.8 us (18%)
  other arithmetic  11.6 us (9%)
  local copies, waits for them, and re-layouts  1.6 us (1%)
    ppermute x2, waiting for transfers between devices, pair(): return lax.ppermute(x, 'chip', [(i, i ^ k) for i in range(chips)])  17 us
    ppermute x8, starting transfers between devices, swap(): return lax.ppermute(x, 'core', [(0, 1), (1, 0)])  12.9 us
    ppermute x3, starting transfers between devices, up(): return lax.ppermute(x, 'chip', [(i, i + k) for i in range(chips - k)])  12 us
    ppermute x10, starting transfers between devices, across(): return lax.ppermute(x, 'dp', [(i, i ^ k) for i in range(rows_dp)])  10.7 us
    ppermute x3, starting transfers between devices, down(): return lax.ppermute(x, 'chip', [(i + k, i) for i in range(chips - k)])  7.38 us
    ppermute x3, waiting for transfers between devices, round_chips(): return lax.ppermute(x, 'chip', [(i, (i + k) % chips) for i in range(chips)])  6.67 us
    pallas_call x4, Pallas kernels, backward(): pl.pallas_call(functools.partial(backward_kernel, steps, rows, first, las...  6.36 us
    ppermute x10, waiting for transfers between devices, across(): return lax.ppermute(x, 'dp', [(i, i ^ k) for i in range(rows_dp)])  6.33 us
  transfers between devices with their start and end apart: 29, of which 15 were waited for; matrix products, arithmetic and copies ran while one was open for 10% of the time, Pallas kernels for 17%

profile of v12, /device:TPU:9, one launch (start us, length us, event | category | flops | bytes accessed | tf_op | source)
XLA Modules:
  0.0 125.9 jit_solution(3706424660020351924)
XLA Ops:
  0.7 2.4 %collective-permute-start.4 = (bf16[72,1024]{1,0:T(8,128)(2,1)}, bf16[72,1024]{1,0:T(8,128)(2,1)S(1)}, u32[]{:S(2)}, u32[]{:S(2)}) collective-permute-start(bf16[72,1024]{1,0:T(8,128)(2,1)} %refs_0_.1), channel_id=1, source_target_pairs={{0,4},{2,6},{4,0},{6,2},{1,5},{3,7},{5,1},{7,3},{8,12},{10,14},{12... | collective-permute-start | bytes 442376 | tf_op jit(solution)/shard_map/ppermute | solution.py:431
  3.0 1.5 %collective-permute-start.5 = (bf16[72,1024]{1,0:T(8,128)(2,1)}, bf16[72,1024]{1,0:T(8,128)(2,1)S(1)}, u32[]{:S(2)}, u32[]{:S(2)}) collective-permute-start(bf16[72,1024]{1,0:T(8,128)(2,1)} %refs_0_.1), channel_id=1, source_target_pairs={{0,6},{2,0},{4,2},{6,4},{1,7},{3,1},{5,3},{7,5},{8,14},{10,8},{12,... | collective-permute-start | bytes 442376 | tf_op jit(solution)/shard_map/ppermute | solution.py:431
  4.5 1.0 broadcast_select_fusion.5
  5.5 1.0 broadcast_select_fusion.4
  6.5 1.6 %collective-permute-start = (bf16[256,512]{1,0:T(8,128)(2,1)S(1)}, bf16[256,512]{1,0:T(8,128)(2,1)S(1)}, u32[]{:S(2)}, u32[]{:S(2)}) collective-permute-start(bf16[256,512]{1,0:T(8,128)(2,1)S(1)} %pad_maximum_fusion.5), channel_id=1, source_target_pairs={{0,1},{1,0},{2,3},{3,2},{4,5},{5,4},{6,7},{7,6},{8,9},{9,8},{10,11... | collective-permute-start | bytes 786440 | tf_op jit(solution)/shard_map/ppermute | solution.py:422
  8.1 1.4 %copy.12 = bf16[1,256,2304]{1,2,0:T(8,128)(2,1)} copy(bf16[1,256,2304]{2,1,0:T(8,128)(2,1)S(1)} %copy-done.1) | data formatting | bytes 2359296 | tf_op args[4]
  9.6 0.9 collective-permute-done.4.refs_2_
  10.5 5.8 %collective-permute-done.3.refs_1_ = bf16[72,1024]{1,0:T(8,128)(2,1)S(1)} collective-permute-done((bf16[72,1024]{1,0:T(8,128)(2,1)}, bf16[72,1024]{1,0:T(8,128)(2,1)S(1)}, u32[]{:S(2)}, u32[]{:S(2)}) %collective-permute-start.3) | collective-permute-done | bytes 147488 | tf_op jit(solution)/shard_map/ppermute | solution.py:431
  16.3 0.6 column_halves.1
  16.9 0.6 collective-permute-start.6
  17.6 4.0 %collective-permute-start.1 = (bf16[512,512]{1,0:T(8,128)(2,1)S(1)}, bf16[512,512]{1,0:T(8,128)(2,1)S(1)}, u32[]{:S(2)}, u32[]{:S(2)}) collective-permute-start(bf16[512,512]{1,0:T(8,128)(2,1)S(1)} %pad_maximum_fusion.4.kv.refs_0_), channel_id=1, source_target_pairs={{0,2},{2,4},{4,6},{1,3},{3,5},{5,7},{8,10},{10,12},{12,14},{9,11},... | collective-permute-start | bytes 1572872 | tf_op jit(solution)/shard_map/ppermute | solution.py:425
  21.8 1.3 %collective-permute-start.8 = (bf16[288,512]{1,0:T(8,128)(2,1)S(1)}, bf16[288,512]{1,0:T(8,128)(2,1)S(1)}, u32[]{:S(2)}, u32[]{:S(2)}) collective-permute-start(bf16[288,512]{1,0:T(8,128)(2,1)S(1)} %bitcast.28), channel_id=1, source_target_pairs={{0,16},{8,24},{16,0},{24,8},{1,17},{9,25},{17,1},{25,9},{2,18},{10... | collective-permute-start | bytes 884744 | tf_op jit(solution)/shard_map/ppermute | solution.py:434
  23.2 1.2 collective-permute-start.7
  24.5 2.1 %attend_forward.4 = (f32[16,512]{1,0:T(8,128)S(1)}, f32[16,512]{1,0:T(8,128)S(1)}, f32[512,512]{1,0:T(8,128)S(1)}) custom-call(s32[3]{0:T(128)S(1)} %pad_add_fusion.info, bf16[512,512]{1,0:T(8,128)(2,1)S(1)} %maximum_multiply_fusion.q, bf16[512,512]{1,0:T(8,128)(2,1)S(1)} %pad_maximum_fusion.4.kv.refs_0_), custom_call_target="tpu_custom_call" | custom-call | flops 1 | bytes 1 | tf_op jit(solution)/shard_map/attend_forward/pallas_call | solution.py:114
  26.6 3.1 %collective-permute-done.8.refs_3_ = bf16[288,512]{1,0:T(8,128)(2,1)S(1)} collective-permute-done((bf16[288,512]{1,0:T(8,128)(2,1)S(1)}, bf16[288,512]{1,0:T(8,128)(2,1)S(1)}, u32[]{:S(2)}, u32[]{:S(2)}) %collective-permute-start.8) | collective-permute-done | bytes 294944 | tf_op jit(solution)/shard_map/ppermute | solution.py:434
  29.7 0.9 collective-permute-done.7.refs_2_
  30.6 1.9 %collective-permute-done.1.kv.refs_0_ = bf16[512,512]{1,0:T(8,128)(2,1)S(1)} collective-permute-done((bf16[512,512]{1,0:T(8,128)(2,1)S(1)}, bf16[512,512]{1,0:T(8,128)(2,1)S(1)}, u32[]{:S(2)}, u32[]{:S(2)}) %collective-permute-start.1) | collective-permute-done | bytes 524320 | tf_op jit(solution)/shard_map/ppermute | solution.py:425
  32.5 4.0 %collective-permute-start.12 = (bf16[512,512]{1,0:T(8,128)(2,1)S(1)}, bf16[512,512]{1,0:T(8,128)(2,1)S(1)}, u32[]{:S(2)}, u32[]{:S(2)}) collective-permute-start(bf16[512,512]{1,0:T(8,128)(2,1)S(1)} %collective-permute-done.1.kv.refs_0_), channel_id=1, source_target_pairs={{0,2},{2,4},{4,6},{1,3},{3,5},{5,7},{8,10},{10,12},{12,14},{9,11},... | collective-permute-start | bytes 1572872 | tf_op jit(solution)/shard_map/ppermute | solution.py:425
  36.5 2.0 %attend_forward.5 = (f32[16,512]{1,0:T(8,128)S(1)}, f32[16,512]{1,0:T(8,128)S(1)}, f32[512,512]{1,0:T(8,128)S(1)}) custom-call(s32[3]{0:T(128)S(1)} %pad_add_fusion.info, bf16[512,512]{1,0:T(8,128)(2,1)S(1)} %maximum_multiply_fusion.q, bf16[512,512]{1,0:T(8,128)(2,1)S(1)} %collective-permute-done.1.kv.refs_0_, f32[16,512]{1,0:T(8,128)S(1)} %get-tuple-element.91.refs_0_, ...), custom_call_target="tpu_custom_call" | custom-call | flops 1 | bytes 1 | tf_op jit(solution)/shard_map/attend_forward/pallas_call | solution.py:114
  38.5 1.3 %collective-permute-start.10 = (bf16[288,512]{1,0:T(8,128)(2,1)S(1)}, bf16[288,512]{1,0:T(8,128)(2,1)S(1)}, u32[]{:S(2)}, u32[]{:S(2)}) collective-permute-start(bf16[288,512]{1,0:T(8,128)(2,1)S(1)} %collective-permute-done.8.refs_3_), channel_id=1, source_target_pairs={{0,8},{8,0},{16,24},{24,16},{1,9},{9,1},{17,25},{25,17},{2,10},{10... | collective-permute-start | bytes 884744 | tf_op jit(solution)/shard_map/ppermute | solution.py:434
  39.8 1.2 collective-permute-start.11
  41.0 1.6 %fusion.5 = (bf16[288,512]{1,0:T(8,128)(2,1)S(1)}, bf16[288,512]{1,0:T(8,128)(2,1)S(1)}, bf16[288,512]{1,0:T(8,128)(2,1)S(1)}, bf16[288,512]{1,0:T(8,128)(2,1)S(...) fusion(s32[]{:T(128)S(6)} %select_n.127, bf16[2304,256]{1,0:T(8,128)(2,1)} %bitcast.11, ...), kind=kLoop, calls=%fused_computation.33 | loop fusion | flops 3538944 | bytes 4128792 | tf_op jit(solution)/shard_map/concatenate | solution.py:485
  42.6 1.1 fusion
  43.7 1.8 %pad_maximum_fusion.turned = bf16[2304,512]{1,0:T(8,128)(2,1)S(1)} fusion(bf16[2304,256]{1,0:T(8,128)(2,1)} %bitcast.12, bf16[2304,256]{1,0:T(8,128)(2,1)} %bitcast.11), kind=kLoop, calls=%fused_computation.7 | loop fusion | flops 4718592 | bytes 4718592 | tf_op jit(solution)/shard_map/concatenate | solution.py:485
  45.6 0.8 collective-permute-done.11.refs_5_
  46.5 4.0 %collective-permute-start.13 = (bf16[512,512]{1,0:T(8,128)(2,1)S(1)}, bf16[512,512]{1,0:T(8,128)(2,1)S(1)}, u32[]{:S(2)}, u32[]{:S(2)}) collective-permute-start(bf16[512,512]{1,0:T(8,128)(2,1)S(1)} %collective-permute-done.12.kv.refs_0_), channel_id=1, source_target_pairs={{0,2},{2,4},{4,6},{1,3},{3,5},{5,7},{8,10},{10,12},{12,14},{9,11},... | collective-permute-start | bytes 1572872 | tf_op jit(solution)/shard_map/ppermute | solution.py:425
  50.5 1.3 %collective-permute-start.14 = (bf16[288,512]{1,0:T(8,128)(2,1)S(1)}, bf16[288,512]{1,0:T(8,128)(2,1)S(1)}, u32[]{:S(2)}, u32[]{:S(2)}) collective-permute-start(bf16[288,512]{1,0:T(8,128)(2,1)S(1)} %bitcast.29), channel_id=1, source_target_pairs={{0,8},{8,0},{16,24},{24,16},{1,9},{9,1},{17,25},{25,17},{2,10},{10... | collective-permute-start | bytes 884744 | tf_op jit(solution)/shard_map/ppermute | solution.py:434
  51.8 1.2 collective-permute-start.15
  53.2 0.6 attend_forward.6
  53.8 2.4 %gradient_into_heads.2.refs_0_ = f32[512,512]{1,0:T(8,128)S(1)} custom-call(s32[3]{0:T(128)S(1)} %pad_add_fusion.info, bf16[2304,512]{1,0:T(8,128)(2,1)S(1)} %pad_maximum_fusion.turned, bf16[288,512]{1,0:T(8,128)(2,1)S(1)} %bitcast.30, bf16[288,512]{1,0:T(8,128)(2,1)S(1)} %bitcast.26, bf16[288,512]{1,0:T(8,128)(2,1)S(1)} %collective-permute-done.7.refs_2_, ...), custom_call_target="tpu_custom_call" | custom-call | flops 1 | bytes 1 | tf_op jit(solution)/shard_map/gradient_into_heads/pallas_call | solution.py:273
  56.2 0.4 collective-permute-done.14.refs_1_.refs_6_
  56.6 1.1 collective-permute-done.15.refs_2_.refs_7_
  57.7 1.7 %collective-permute-done.13.kv.refs_0_ = bf16[512,512]{1,0:T(8,128)(2,1)S(1)} collective-permute-done((bf16[512,512]{1,0:T(8,128)(2,1)S(1)}, bf16[512,512]{1,0:T(8,128)(2,1)S(1)}, u32[]{:S(2)}, u32[]{:S(2)}) %collective-permute-start.13) | collective-permute-done | bytes 524320 | tf_op jit(solution)/shard_map/ppermute | solution.py:425
  59.4 1.5 %attend_forward.7 = (bf16[512,512]{1,0:T(8,128)(2,1)S(1)}, f32[16,512]{1,0:T(8,128)S(1)}, bf16[576,512]{1,0:T(8,128)(2,1)S(1)}, bf16[576,512]{1,0:T(8,128)(2,1)S(1)}) custom-call(s32[3]{0:T(128)S(1)} %pad_add_fusion.info, bf16[512,512]{1,0:T(8,128)(2,1)S(1)} %maximum_multiply_fusion.q, bf16[512,512]{1,0:T(8,128)(2,1)S(1)} %collective-permute-done.13.kv.refs_0_, ...), custom_call_target="tpu_custom_call" | custom-call | flops 1 | bytes 1 | tf_op jit(solution)/shard_map/attend_forward/pallas_call | solution.py:114
  61.0 1.4 %collective-permute-start.16 = (bf16[576,512]{1,0:T(8,128)(2,1)S(1)}, bf16[576,512]{1,0:T(8,128)(2,1)S(1)}, u32[]{:S(2)}, u32[]{:S(2)}) collective-permute-start(bf16[576,512]{1,0:T(8,128)(2,1)S(1)} %get-tuple-element.123), channel_id=1, source_target_pairs={{0,8},{8,0},{16,24},{24,16},{1,9},{9,1},{17,25},{25,17},{2,10},{10... | collective-permute-start | bytes 1769480 | tf_op jit(solution)/shard_map/ppermute | solution.py:434
  62.3 1.2 collective-permute-start.17
  63.6 1.3 %gradient_into_heads.3.da = bf16[512,512]{1,0:T(8,128)(2,1)S(1)} custom-call(s32[3]{0:T(128)S(1)} %pad_add_fusion.info, bf16[2304,512]{1,0:T(8,128)(2,1)S(1)} %pad_maximum_fusion.turned, f32[512,512]{1,0:T(8,128)S(1)} %gradient_into_heads.2.refs_0_, bf16[288,512]{1,0:T(8,128)(2,1)S(1)} %collective-permute-done.14.refs_1_.refs_6_, ...), custom_call_target="tpu_custom_call" | custom-call | flops 1 | bytes 1 | tf_op jit(solution)/shard_map/gradient_into_heads/pallas_call | solution.py:273
  64.9 0.9 attend_backward.4
  65.8 2.1 %collective-permute-start.18 = (bf16[512,512]{1,0:T(8,128)(2,1)S(1)}, bf16[512,512]{1,0:T(8,128)(2,1)S(1)}, u32[]{:S(2)}, u32[]{:S(2)}) collective-permute-start(bf16[512,512]{1,0:T(8,128)(2,1)S(1)} %get-tuple-element.130), channel_id=1, source_target_pairs={{2,0},{4,2},{6,4},{3,1},{5,3},{7,5},{10,8},{12,10},{14,12},{11,9},... | collective-permute-start | bytes 1572872 | tf_op jit(solution)/shard_map/ppermute | solution.py:428
  67.9 0.6 attend_backward.5
  68.5 2.3 %attend_backward.6 = (bf16[512,512]{1,0:T(8,128)(2,1)S(1)}, f32[512,512]{1,0:T(8,128)S(1)}) custom-call(s32[3]{0:T(128)S(1)} %pad_add_fusion.info, bf16[512,512]{1,0:T(8,128)(2,1)S(1)} %maximum_multiply_fusion.q, bf16[512,512]{1,0:T(8,128)(2,1)S(1)} %gradient_into_heads.3.da, f32[16,512]{1,0:T(8,128)S(1)} %get-tuple-element.128.lse_t, ...), custom_call_target="tpu_custom_call" | custom-call | flops 1 | bytes 1 | tf_op jit(solution)/shard_map/attend_backward/pallas_call | solution.py:215
  70.8 2.5 %attend_backward.7 = (f32[512,512]{1,0:T(8,128)S(1)}, bf16[512,512]{1,0:T(8,128)(2,1)S(1)}) custom-call(s32[3]{0:T(128)S(1)} %pad_add_fusion.info, bf16[512,512]{1,0:T(8,128)(2,1)S(1)} %maximum_multiply_fusion.q, bf16[512,512]{1,0:T(8,128)(2,1)S(1)} %gradient_into_heads.3.da, f32[16,512]{1,0:T(8,128)S(1)} %get-tuple-element.128.lse_t, ...), custom_call_target="tpu_custom_call" | custom-call | flops 1 | bytes 1 | tf_op jit(solution)/shard_map/attend_backward/pallas_call | solution.py:215
  73.4 1.3 %strip_product.1.rest = f32[1152,512]{1,0:T(8,128)S(1)} custom-call(bf16[1152,512]{1,0:T(8,128)(2,1)S(1)} %pad_maximum_fusion.1.x, bf16[512,512]{1,0:T(8,128)(2,1)S(1)} %get-tuple-element.144.refs_1_.w.x), custom_call_target="tpu_custom_call" | custom-call | flops 1 | bytes 1 | tf_op jit(solution)/shard_map/strip_product/pallas_call | solution.py:384
  74.7 3.8 %collective-permute-done.18 = bf16[512,512]{1,0:T(8,128)(2,1)S(1)} collective-permute-done((bf16[512,512]{1,0:T(8,128)(2,1)S(1)}, bf16[512,512]{1,0:T(8,128)(2,1)S(1)}, u32[]{:S(2)}, u32[]{:S(2)}) %collective-permute-start.18) | collective-permute-done | bytes 524320 | tf_op jit(solution)/shard_map/ppermute | solution.py:428
  78.6 1.9 %collective-permute-start.22 = (bf16[512,512]{1,0:T(8,128)(2,1)S(1)}, bf16[512,512]{1,0:T(8,128)(2,1)S(1)}, u32[]{:S(2)}, u32[]{:S(2)}) collective-permute-start(bf16[512,512]{1,0:T(8,128)(2,1)S(1)} %add_convert_fusion.3), channel_id=1, source_target_pairs={{2,0},{4,2},{6,4},{3,1},{5,3},{7,5},{10,8},{12,10},{14,12},{11,9},... | collective-permute-start | bytes 1572872 | tf_op jit(solution)/shard_map/ppermute | solution.py:428
  80.5 0.2 add_convert_fusion.4
  80.7 0.3 collective-permute-start.20
  81.0 0.2 collective-permute-start.19
  81.3 5.0 %collective-permute-start.21 = (bf16[256,512]{1,0:T(8,128)(2,1)S(1)}, bf16[256,512]{1,0:T(8,128)(2,1)S(1)}, u32[]{:S(2)}, u32[]{:S(2)}) collective-permute-start(bf16[256,512]{1,0:T(8,128)(2,1)S(1)} %get-tuple-element.176), channel_id=1, source_target_pairs={{0,1},{1,0},{2,3},{3,2},{4,5},{5,4},{6,7},{7,6},{8,9},{9,8},{10,11... | collective-permute-start | bytes 786440 | tf_op jit(solution)/shard_map/ppermute | solution.py:422
  86.3 0.7 place_shares.1.w
  87.0 3.2 %layer_product.1 = (f32[256,2304]{1,0:T(8,128)S(1)}, bf16[256,2304]{1,0:T(8,128)(2,1)S(1)}) custom-call(bf16[512,512]{1,0:T(8,128)(2,1)S(1)} %get-tuple-element.144.refs_1_.w.x, bf16[2304,512]{1,0:T(8,128)(2,1)S(1)} %place_shares.1.w), custom_call_target="tpu_custom_call" | custom-call | flops 1 | bytes 1 | tf_op jit(solution)/shard_map/layer_product/pallas_call | solution.py:363
  90.2 2.2 %collective-permute-done.22 = bf16[512,512]{1,0:T(8,128)(2,1)S(1)} collective-permute-done((bf16[512,512]{1,0:T(8,128)(2,1)S(1)}, bf16[512,512]{1,0:T(8,128)(2,1)S(1)}, u32[]{:S(2)}, u32[]{:S(2)}) %collective-permute-start.22) | collective-permute-done | bytes 524320 | tf_op jit(solution)/shard_map/ppermute | solution.py:428
  92.4 4.7 %collective-permute-start.25 = (bf16[256,2304]{1,0:T(8,128)(2,1)S(1)}, bf16[256,2304]{1,0:T(8,128)(2,1)S(1)}, u32[]{:S(2)}, u32[]{:S(2)}) collective-permute-start(bf16[256,2304]{1,0:T(8,128)(2,1)S(1)} %get-tuple-element.153), channel_id=1, source_target_pairs={{0,1},{1,0},{2,3},{3,2},{4,5},{5,4},{6,7},{7,6},{8,9},{9,8},{10,11... | collective-permute-start | bytes 3538952 | tf_op jit(solution)/shard_map/ppermute | solution.py:422
  97.1 0.9 plane_sum.1
  98.2 3.4 %collective-permute-start.26 = (bf16[512,512]{1,0:T(8,128)(2,1)S(1)}, bf16[512,512]{1,0:T(8,128)(2,1)S(1)}, u32[]{:S(2)}, u32[]{:S(2)}) collective-permute-start(bf16[512,512]{1,0:T(8,128)(2,1)S(1)} %add_convert_fusion.2), channel_id=1, source_target_pairs={{2,0},{4,2},{6,4},{3,1},{5,3},{7,5},{10,8},{12,10},{14,12},{11,9},... | collective-permute-start | bytes 1572872 | tf_op jit(solution)/shard_map/ppermute | solution.py:428
  101.5 0.9 maximum_select_fusion.1
  102.5 4.2 %collective-permute-done.23 = bf16[288,512]{1,0:T(8,128)(2,1)S(1)} collective-permute-done((bf16[288,512]{1,0:T(8,128)(2,1)S(1)}, bf16[288,512]{1,0:T(8,128)(2,1)S(1)}, u32[]{:S(2)}, u32[]{:S(2)}) %collective-permute-start.23) | collective-permute-done | bytes 294944 | tf_op jit(solution)/shard_map/ppermute | solution.py:543
  106.7 1.4 %collective-permute-start.24 = (bf16[144,512]{1,0:T(8,128)(2,1)S(1)}, bf16[144,512]{1,0:T(8,128)(2,1)S(1)}, u32[]{:S(2)}, u32[]{:S(2)}) collective-permute-start(bf16[144,512]{1,0:T(8,128)(2,1)S(1)} %add_convert_fusion.6), channel_id=1, source_target_pairs={{0,4},{2,6},{4,0},{6,2},{1,5},{3,7},{5,1},{7,3},{8,12},{10,14},{12... | collective-permute-start | bytes 442376 | tf_op jit(solution)/shard_map/ppermute | solution.py:543
  108.1 1.2 add_convert_fusion
  109.3 12.9 %collective-permute-done.24 = bf16[144,512]{1,0:T(8,128)(2,1)S(1)} collective-permute-done((bf16[144,512]{1,0:T(8,128)(2,1)S(1)}, bf16[144,512]{1,0:T(8,128)(2,1)S(1)}, u32[]{:S(2)}, u32[]{:S(2)}) %collective-permute-start.24) | collective-permute-done | bytes 147488 | tf_op jit(solution)/shard_map/ppermute | solution.py:543
  122.3 0.8 collective-permute-start.28
  123.5 0.7 collective-permute-done.28
  124.2 0.7 maximum_select_fusion.2
  125.0 0.9 maximum_select_fusion.3
  (48 shorter events, 1.7 us)
Async XLA Ops:
  0.6 15.7 %copy-start = (bf16[72,1024]{1,0:T(8,128)(2,1)S(1)}, bf16[72,1024]{1,0:T(8,128)(2,1)}, u32[]{:S(2)}) copy-start(bf16[72,1024]{1,0:T(8,128)(2,1)} %refs_0_.1) | copy-start | bytes 442372
  0.6 7.4 %copy-start.1 = (bf16[1,256,2304]{2,1,0:T(8,128)(2,1)S(1)}, bf16[1,256,2304]{2,1,0:T(8,128)(2,1)}, u32[]{:S(2)}) copy-start(bf16[1,256,2304]{2,1,0:T(8,128)(2,1)} %param.9) | copy-start | bytes 3538948
  0.7 9.8 %collective-permute-start.4 = (bf16[72,1024]{1,0:T(8,128)(2,1)}, bf16[72,1024]{1,0:T(8,128)(2,1)S(1)}, u32[]{:S(2)}, u32[]{:S(2)}) collective-permute-start(bf16[72,1024]{1,0:T(8,128)(2,1)} %refs_0_.1), channel_id=1, source_target_pairs={{0,4},{2,6},{4,0},{6,2},{1,5},{3,7},{5,1},{7,3},{8,12},{10,14},{12... | collective-permute-start | bytes 442376 | tf_op jit(solution)/shard_map/ppermute | solution.py:431
  3.0 13.3 %collective-permute-start.3 = (bf16[72,1024]{1,0:T(8,128)(2,1)}, bf16[72,1024]{1,0:T(8,128)(2,1)S(1)}, u32[]{:S(2)}, u32[]{:S(2)}) collective-permute-start(bf16[72,1024]{1,0:T(8,128)(2,1)} %refs_0_.1), channel_id=1, source_target_pairs={{0,2},{2,4},{4,6},{6,0},{1,3},{3,5},{5,7},{7,1},{8,10},{10,12},{12... | collective-permute-start | bytes 442376 | tf_op jit(solution)/shard_map/ppermute | solution.py:431
  3.0 13.3 %collective-permute-start.5 = (bf16[72,1024]{1,0:T(8,128)(2,1)}, bf16[72,1024]{1,0:T(8,128)(2,1)S(1)}, u32[]{:S(2)}, u32[]{:S(2)}) collective-permute-start(bf16[72,1024]{1,0:T(8,128)(2,1)} %refs_0_.1), channel_id=1, source_target_pairs={{0,6},{2,0},{4,2},{6,4},{1,7},{3,1},{5,3},{7,5},{8,14},{10,8},{12,... | collective-permute-start | bytes 442376 | tf_op jit(solution)/shard_map/ppermute | solution.py:431
  6.5 11.1 %collective-permute-start = (bf16[256,512]{1,0:T(8,128)(2,1)S(1)}, bf16[256,512]{1,0:T(8,128)(2,1)S(1)}, u32[]{:S(2)}, u32[]{:S(2)}) collective-permute-start(bf16[256,512]{1,0:T(8,128)(2,1)S(1)} %pad_maximum_fusion.5), channel_id=1, source_target_pairs={{0,1},{1,0},{2,3},{3,2},{4,5},{5,4},{6,7},{7,6},{8,9},{9,8},{10,11... | collective-permute-start | bytes 786440 | tf_op jit(solution)/shard_map/ppermute | solution.py:422
  9.5 23.0 %collective-permute-start.9 = (bf16[256,2304]{0,1:T(8,128)(2,1)}, bf16[256,2304]{0,1:T(8,128)(2,1)}, u32[]{:S(2)}, u32[]{:S(2)}) collective-permute-start(bf16[256,2304]{0,1:T(8,128)(2,1)} %bitcast.10), channel_id=1, source_target_pairs={{0,1},{1,0},{2,3},{3,2},{4,5},{5,4},{6,7},{7,6},{8,9},{9,8},{10,11... | collective-permute-start | bytes 3538952 | tf_op jit(solution)/shard_map/ppermute | solution.py:422
  9.6 7.8 %copy-start.2 = (bf16[1,256,1024]{2,1,0:T(8,128)(2,1)S(1)}, bf16[1,256,1024]{2,1,0:T(8,128)(2,1)}, u32[]{:S(2)}) copy-start(bf16[1,256,1024]{2,1,0:T(8,128)(2,1)} %param.5) | copy-start | bytes 1572868
  16.9 4.8 %collective-permute-start.6 = (bf16[4,72,512]{2,1,0:T(8,128)(2,1)S(1)}, bf16[4,72,512]{2,1,0:T(8,128)(2,1)S(1)}, u32[]{:S(2)}, u32[]{:S(2)}) collective-permute-start(bf16[4,72,512]{2,1,0:T(8,128)(2,1)S(1)} %get-tuple-element.88), channel_id=1, source_target_pairs={{0,1},{1,0},{2,3},{3,2},{4,5},{5,4},{6,7},{7,6},{8,9},{9,8},{10,11... | collective-permute-start | bytes 884744 | tf_op jit(solution)/shard_map/ppermute | solution.py:422
  17.5 6.9 %collective-permute-start.2 = (bf16[256,512]{1,0:T(8,128)(2,1)S(1)}, bf16[256,512]{1,0:T(8,128)(2,1)S(1)}, u32[]{:S(2)}, u32[]{:S(2)}) collective-permute-start(bf16[256,512]{1,0:T(8,128)(2,1)S(1)} %get-tuple-element.178), channel_id=1, source_target_pairs={{0,1},{1,0},{2,3},{3,2},{4,5},{5,4},{6,7},{7,6},{8,9},{9,8},{10,11... | collective-permute-start | bytes 786440 | tf_op jit(solution)/shard_map/ppermute | solution.py:422
  17.6 14.9 %collective-permute-start.1 = (bf16[512,512]{1,0:T(8,128)(2,1)S(1)}, bf16[512,512]{1,0:T(8,128)(2,1)S(1)}, u32[]{:S(2)}, u32[]{:S(2)}) collective-permute-start(bf16[512,512]{1,0:T(8,128)(2,1)S(1)} %pad_maximum_fusion.4.kv.refs_0_), channel_id=1, source_target_pairs={{0,2},{2,4},{4,6},{1,3},{3,5},{5,7},{8,10},{10,12},{12,14},{9,11},... | collective-permute-start | bytes 1572872 | tf_op jit(solution)/shard_map/ppermute | solution.py:425
  21.8 7.8 %collective-permute-start.8 = (bf16[288,512]{1,0:T(8,128)(2,1)S(1)}, bf16[288,512]{1,0:T(8,128)(2,1)S(1)}, u32[]{:S(2)}, u32[]{:S(2)}) collective-permute-start(bf16[288,512]{1,0:T(8,128)(2,1)S(1)} %bitcast.28), channel_id=1, source_target_pairs={{0,16},{8,24},{16,0},{24,8},{1,17},{9,25},{17,1},{25,9},{2,18},{10... | collective-permute-start | bytes 884744 | tf_op jit(solution)/shard_map/ppermute | solution.py:434
  23.2 7.5 %collective-permute-start.7 = (bf16[288,512]{1,0:T(8,128)(2,1)S(1)}, bf16[288,512]{1,0:T(8,128)(2,1)S(1)}, u32[]{:S(2)}, u32[]{:S(2)}) collective-permute-start(bf16[288,512]{1,0:T(8,128)(2,1)S(1)} %bitcast.24), channel_id=1, source_target_pairs={{0,8},{8,0},{16,24},{24,16},{1,9},{9,1},{17,25},{25,17},{2,10},{10... | collective-permute-start | bytes 884744 | tf_op jit(solution)/shard_map/ppermute | solution.py:434
  32.5 14.0 %collective-permute-start.12 = (bf16[512,512]{1,0:T(8,128)(2,1)S(1)}, bf16[512,512]{1,0:T(8,128)(2,1)S(1)}, u32[]{:S(2)}, u32[]{:S(2)}) collective-permute-start(bf16[512,512]{1,0:T(8,128)(2,1)S(1)} %collective-permute-done.1.kv.refs_0_), channel_id=1, source_target_pairs={{0,2},{2,4},{4,6},{1,3},{3,5},{5,7},{8,10},{10,12},{12,14},{9,11},... | collective-permute-start | bytes 1572872 | tf_op jit(solution)/shard_map/ppermute | solution.py:425
  38.5 7.1 %collective-permute-start.10 = (bf16[288,512]{1,0:T(8,128)(2,1)S(1)}, bf16[288,512]{1,0:T(8,128)(2,1)S(1)}, u32[]{:S(2)}, u32[]{:S(2)}) collective-permute-start(bf16[288,512]{1,0:T(8,128)(2,1)S(1)} %collective-permute-done.8.refs_3_), channel_id=1, source_target_pairs={{0,8},{8,0},{16,24},{24,16},{1,9},{9,1},{17,25},{25,17},{2,10},{10... | collective-permute-start | bytes 884744 | tf_op jit(solution)/shard_map/ppermute | solution.py:434
  39.8 6.6 %collective-permute-start.11 = (bf16[288,512]{1,0:T(8,128)(2,1)S(1)}, bf16[288,512]{1,0:T(8,128)(2,1)S(1)}, u32[]{:S(2)}, u32[]{:S(2)}) collective-permute-start(bf16[288,512]{1,0:T(8,128)(2,1)S(1)} %collective-permute-done.7.refs_2_), channel_id=1, source_target_pairs={{0,16},{8,24},{16,0},{24,8},{1,17},{9,25},{17,1},{25,9},{2,18},{10... | collective-permute-start | bytes 884744 | tf_op jit(solution)/shard_map/ppermute | solution.py:434
  46.5 12.9 %collective-permute-start.13 = (bf16[512,512]{1,0:T(8,128)(2,1)S(1)}, bf16[512,512]{1,0:T(8,128)(2,1)S(1)}, u32[]{:S(2)}, u32[]{:S(2)}) collective-permute-start(bf16[512,512]{1,0:T(8,128)(2,1)S(1)} %collective-permute-done.12.kv.refs_0_), channel_id=1, source_target_pairs={{0,2},{2,4},{4,6},{1,3},{3,5},{5,7},{8,10},{10,12},{12,14},{9,11},... | collective-permute-start | bytes 1572872 | tf_op jit(solution)/shard_map/ppermute | solution.py:425
  50.5 6.0 %collective-permute-start.14 = (bf16[288,512]{1,0:T(8,128)(2,1)S(1)}, bf16[288,512]{1,0:T(8,128)(2,1)S(1)}, u32[]{:S(2)}, u32[]{:S(2)}) collective-permute-start(bf16[288,512]{1,0:T(8,128)(2,1)S(1)} %bitcast.29), channel_id=1, source_target_pairs={{0,8},{8,0},{16,24},{24,16},{1,9},{9,1},{17,25},{25,17},{2,10},{10... | collective-permute-start | bytes 884744 | tf_op jit(solution)/shard_map/ppermute | solution.py:434
  51.8 5.9 %collective-permute-start.15 = (bf16[288,512]{1,0:T(8,128)(2,1)S(1)}, bf16[288,512]{1,0:T(8,128)(2,1)S(1)}, u32[]{:S(2)}, u32[]{:S(2)}) collective-permute-start(bf16[288,512]{1,0:T(8,128)(2,1)S(1)} %bitcast.25), channel_id=1, source_target_pairs={{0,16},{8,24},{16,0},{24,8},{1,17},{9,25},{17,1},{25,9},{2,18},{10... | collective-permute-start | bytes 884744 | tf_op jit(solution)/shard_map/ppermute | solution.py:434
  61.0 17.5 %collective-permute-start.16 = (bf16[576,512]{1,0:T(8,128)(2,1)S(1)}, bf16[576,512]{1,0:T(8,128)(2,1)S(1)}, u32[]{:S(2)}, u32[]{:S(2)}) collective-permute-start(bf16[576,512]{1,0:T(8,128)(2,1)S(1)} %get-tuple-element.123), channel_id=1, source_target_pairs={{0,8},{8,0},{16,24},{24,16},{1,9},{9,1},{17,25},{25,17},{2,10},{10... | collective-permute-start | bytes 1769480 | tf_op jit(solution)/shard_map/ppermute | solution.py:434
  62.3 16.1 %collective-permute-start.17 = (bf16[576,512]{1,0:T(8,128)(2,1)S(1)}, bf16[576,512]{1,0:T(8,128)(2,1)S(1)}, u32[]{:S(2)}, u32[]{:S(2)}) collective-permute-start(bf16[576,512]{1,0:T(8,128)(2,1)S(1)} %get-tuple-element.124), channel_id=1, source_target_pairs={{0,16},{8,24},{16,0},{24,8},{1,17},{9,25},{17,1},{25,9},{2,18},{10... | collective-permute-start | bytes 1769480 | tf_op jit(solution)/shard_map/ppermute | solution.py:434
  65.8 12.7 %collective-permute-start.18 = (bf16[512,512]{1,0:T(8,128)(2,1)S(1)}, bf16[512,512]{1,0:T(8,128)(2,1)S(1)}, u32[]{:S(2)}, u32[]{:S(2)}) collective-permute-start(bf16[512,512]{1,0:T(8,128)(2,1)S(1)} %get-tuple-element.130), channel_id=1, source_target_pairs={{2,0},{4,2},{6,4},{3,1},{5,3},{7,5},{10,8},{12,10},{14,12},{11,9},... | collective-permute-start | bytes 1572872 | tf_op jit(solution)/shard_map/ppermute | solution.py:428
  78.6 13.8 %collective-permute-start.22 = (bf16[512,512]{1,0:T(8,128)(2,1)S(1)}, bf16[512,512]{1,0:T(8,128)(2,1)S(1)}, u32[]{:S(2)}, u32[]{:S(2)}) collective-permute-start(bf16[512,512]{1,0:T(8,128)(2,1)S(1)} %add_convert_fusion.3), channel_id=1, source_target_pairs={{2,0},{4,2},{6,4},{3,1},{5,3},{7,5},{10,8},{12,10},{14,12},{11,9},... | collective-permute-start | bytes 1572872 | tf_op jit(solution)/shard_map/ppermute | solution.py:428
  80.7 9.5 %collective-permute-start.20 = (bf16[288,512]{1,0:T(8,128)(2,1)S(1)}, bf16[288,512]{1,0:T(8,128)(2,1)S(1)}, u32[]{:S(2)}, u32[]{:S(2)}) collective-permute-start(bf16[288,512]{1,0:T(8,128)(2,1)S(1)} %get-tuple-element.163), channel_id=1, source_target_pairs={{0,16},{8,24},{16,0},{24,8},{1,17},{9,25},{17,1},{25,9},{2,18},{10... | collective-permute-start | bytes 884744 | tf_op jit(solution)/shard_map/ppermute | solution.py:434
  81.0 9.2 %collective-permute-start.19 = (bf16[288,512]{1,0:T(8,128)(2,1)S(1)}, bf16[288,512]{1,0:T(8,128)(2,1)S(1)}, u32[]{:S(2)}, u32[]{:S(2)}) collective-permute-start(bf16[288,512]{1,0:T(8,128)(2,1)S(1)} %get-tuple-element.164), channel_id=1, source_target_pairs={{0,8},{8,0},{16,24},{24,16},{1,9},{9,1},{17,25},{25,17},{2,10},{10... | collective-permute-start | bytes 884744 | tf_op jit(solution)/shard_map/ppermute | solution.py:434
  81.3 8.9 %collective-permute-start.21 = (bf16[256,512]{1,0:T(8,128)(2,1)S(1)}, bf16[256,512]{1,0:T(8,128)(2,1)S(1)}, u32[]{:S(2)}, u32[]{:S(2)}) collective-permute-start(bf16[256,512]{1,0:T(8,128)(2,1)S(1)} %get-tuple-element.176), channel_id=1, source_target_pairs={{0,1},{1,0},{2,3},{3,2},{4,5},{5,4},{6,7},{7,6},{8,9},{9,8},{10,11... | collective-permute-start | bytes 786440 | tf_op jit(solution)/shard_map/ppermute | solution.py:422
  92.4 15.7 %collective-permute-start.25 = (bf16[256,2304]{1,0:T(8,128)(2,1)S(1)}, bf16[256,2304]{1,0:T(8,128)(2,1)S(1)}, u32[]{:S(2)}, u32[]{:S(2)}) collective-permute-start(bf16[256,2304]{1,0:T(8,128)(2,1)S(1)} %get-tuple-element.153), channel_id=1, source_target_pairs={{0,1},{1,0},{2,3},{3,2},{4,5},{5,4},{6,7},{7,6},{8,9},{9,8},{10,11... | collective-permute-start | bytes 3538952 | tf_op jit(solution)/shard_map/ppermute | solution.py:422
  97.9 8.7 %collective-permute-start.23 = (bf16[288,512]{1,0:T(8,128)(2,1)S(1)}, bf16[288,512]{1,0:T(8,128)(2,1)S(1)}, u32[]{:S(2)}, u32[]{:S(2)}) collective-permute-start(bf16[288,512]{1,0:T(8,128)(2,1)S(1)} %get-tuple-element.151), channel_id=1, source_target_pairs={{0,2},{2,0},{4,6},{6,4},{1,3},{3,1},{5,7},{7,5},{8,10},{10,8},{12,... | collective-permute-start | bytes 884744 | tf_op jit(solution)/shard_map/ppermute | solution.py:543
  98.2 24.1 %collective-permute-start.26 = (bf16[512,512]{1,0:T(8,128)(2,1)S(1)}, bf16[512,512]{1,0:T(8,128)(2,1)S(1)}, u32[]{:S(2)}, u32[]{:S(2)}) collective-permute-start(bf16[512,512]{1,0:T(8,128)(2,1)S(1)} %add_convert_fusion.2), channel_id=1, source_target_pairs={{2,0},{4,2},{6,4},{3,1},{5,3},{7,5},{10,8},{12,10},{14,12},{11,9},... | collective-permute-start | bytes 1572872 | tf_op jit(solution)/shard_map/ppermute | solution.py:428
  106.7 15.5 %collective-permute-start.24 = (bf16[144,512]{1,0:T(8,128)(2,1)S(1)}, bf16[144,512]{1,0:T(8,128)(2,1)S(1)}, u32[]{:S(2)}, u32[]{:S(2)}) collective-permute-start(bf16[144,512]{1,0:T(8,128)(2,1)S(1)} %add_convert_fusion.6), channel_id=1, source_target_pairs={{0,4},{2,6},{4,0},{6,2},{1,5},{3,7},{5,1},{7,3},{8,12},{10,14},{12... | collective-permute-start | bytes 442376 | tf_op jit(solution)/shard_map/ppermute | solution.py:543
  122.3 1.9 %collective-permute-start.28 = (f32[72,512]{1,0:T(8,128)S(1)}, f32[72,512]{1,0:T(8,128)S(1)}, u32[]{:S(2)}, u32[]{:S(2)}) collective-permute-start(f32[72,512]{1,0:T(8,128)S(1)} %get-tuple-element.180), channel_id=1, source_target_pairs={{0,1},{1,0},{2,3},{3,2},{4,5},{5,4},{6,7},{7,6},{8,9},{9,8},{10,11... | collective-permute-start | bytes 442376 | tf_op jit(solution)/shard_map/ppermute | solution.py:422
  123.3 1.6 %collective-permute-start.27 = (bf16[256,512]{1,0:T(8,128)(2,1)S(1)}, bf16[256,512]{1,0:T(8,128)(2,1)S(1)}, u32[]{:S(2)}, u32[]{:S(2)}) collective-permute-start(bf16[256,512]{1,0:T(8,128)(2,1)S(1)} %slice.116), channel_id=1, source_target_pairs={{0,1},{1,0},{2,3},{3,2},{4,5},{5,4},{6,7},{7,6},{8,9},{9,8},{10,11... | collective-permute-start | bytes 786440 | tf_op jit(solution)/shard_map/ppermute | solution.py:422
